TPU v7x, 32 devices: a whole 2x2x4 slice. The times are simulated.
32 devices in a mesh: clus: 8 (over y, x, core), probe: 4 (over z).
Axes of the slice: x: 2, y: 2, z: 4, core: 2. Of those that a mesh axis runs over, the one named last changes fastest.
Arguments:
- probes: bfloat16 [96, 128, 128], P('clus', 'probe'), may hold values from -6 to 6
- onsite: float32 [96, 128], P('clus'), may hold values from -1.1 to 1.1
- hopping: bfloat16 [20, 96, 128, 128], P(None, 'clus'), may hold values from -0.0390625 to 0.0390625
- block_col: int32 [20, 96], P(None, 'clus'), may hold values from -1 to 95, as said below
- atom_of: int32 [96, 128], P('clus'), may hold values from 0 to 31, as said below
- bond_dir: bfloat16 [3, 20, 96], P(None, None, 'clus'), may hold values from -1 to 1, as said below
- chemical_potential: float32 [1], replicated, may hold values from -0.3 to 0.3
Outputs:
- density: float32 [96, 128], P('clus')
- filling: float32 [1], replicated
- forces: float32 [3, 3072], P(None, 'clus')
Inputs may be any that keep to these rules, and one draw needn't show every extreme that they name: `block_col`: -1 marks an empty slot. Slot (m, c) belongs to row cluster c; a live slot's column cluster lies within 12 clusters of c, and the live columns of one row cluster are distinct. In each aligned group of 12 row clusters the live slots are those with m under a count common to the group, either 20 or from 5 to 10, except columns that would fall outside the grid, which are empty. In some group, never the first or the last, every slot is live. `atom_of`: in each cluster every atom number appears for exactly four orbitals. `bond_dir`: the three components of each slot form a unit vector.
All inputs are finite; a program needn't handle non-finite values.
Results may differ from a plain program's by a relative error of at most 0.0011.
Values may be sent and summed in bfloat16 or wider, within the bound.
No kernel may reach another device: no remote copies, remote signals or barrier semaphores. Data moves between devices by JAX's collectives and lax.ppermute only.
A program may use at most 128 MiB of HBM per device.

v0:
```python
import jax
import jax.numpy as jnp
from jax import lax
from jax.sharding import PartitionSpec as P

ATOMS = 32
REACH = 12
PROBE_VECTORS = 128
ORDER = 4


DECAY = 50.0
SMEARING_TEMP = 0.1
quad_nodes = 64


def extended(block, sides, width):
    for axis, dim in sides:
        count = lax.axis_size(axis)
        forward = [(i, i + 1) for i in range(count - 1)]
        backward = [(target, source) for source, target in forward]
        low = lax.ppermute(
            lax.slice_in_dim(block, block.shape[dim] - width, None, axis=dim), axis, forward
        )
        high = lax.ppermute(lax.slice_in_dim(block, 0, width, axis=dim), axis, backward)
        block = jnp.concatenate([low, block, high], axis=dim)
    return block


def passed_along(array, axis, by):
    devices = lax.axis_size(axis)
    pairs = [(i, i + by) for i in range(devices) if 0 <= i + by < devices]
    return lax.ppermute(array, axis, pairs)


def expansion(chemical_potential, degree):
    node_index = jnp.arange(quad_nodes, dtype=jnp.float32)
    bond_angles = jnp.pi * (node_index + 0.5) / quad_nodes
    fermi_occupation = 1.0 / (
        1.0 + jnp.exp((jnp.cos(bond_angles) - chemical_potential) / SMEARING_TEMP)
    )
    orders = jnp.arange(degree + 1, dtype=jnp.float32)
    cosines = jnp.cos(orders[:, None] * bond_angles[None, :])
    coeffs = 2.0 / quad_nodes * jnp.sum(cosines * fermi_occupation[None, :], axis=1)
    return coeffs * jnp.where(orders == 0.0, 0.5, 1.0)


def gather_columns(source, gather_ids):
    safe_ids = jnp.minimum(gather_ids, source.shape[0] - 1)
    picked = jnp.take(source, safe_ids.reshape(-1), axis=0)
    return picked.reshape(gather_ids.shape + source.shape[1:])


def direct_terms(padded, blocks, gather_ids):
    picked = gather_columns(padded, gather_ids)
    return jnp.einsum("mrpj,mrij->rpi", picked, blocks, preferred_element_type=jnp.float32)


def spread_terms(vector_rows, blocks, target_ids, segments):
    spread = jnp.einsum("rpi,mrij->mrpj", vector_rows, blocks, preferred_element_type=jnp.float32)
    flat = spread.reshape((-1,) + spread.shape[2:])
    return jax.ops.segment_sum(flat, target_ids.reshape(-1), num_segments=segments)


def bond_sums(u_rows, v_rows, u_cols, v_cols, blocks):
    density_blocks = jnp.einsum(
        "rpi,mrpj->mrij", u_rows, v_cols, preferred_element_type=jnp.float32
    )
    density_blocks = density_blocks + jnp.einsum(
        "rpi,mrpj->mrij", v_rows, u_cols, preferred_element_type=jnp.float32
    )
    product = density_blocks * blocks.astype(jnp.float32)
    return (jnp.sum(product, axis=3), jnp.sum(product, axis=2))


def column_force(directions, col_sums, target_ids, segments):
    facing = jnp.transpose(directions.astype(jnp.float32), (1, 2, 0))
    terms = DECAY * facing[:, :, :, None] * col_sums[:, :, None, :]
    flat = terms.reshape((-1,) + terms.shape[2:])
    return jax.ops.segment_sum(flat, target_ids.reshape(-1), num_segments=segments)


def local(probes, onsite, hopping, block_col, atom_of, bond_dir, chemical_potential):
    clusters = probes.shape[0]
    offset = lax.axis_index("clus") * clusters
    orbitals = clusters * lax.axis_size("clus") * probes.shape[2]
    live_mask = block_col >= 0
    masked_hop = jnp.where(live_mask[:, :, None, None], hopping, jnp.zeros((), hopping.dtype))
    frame_ids = jnp.where(live_mask, block_col - offset + REACH, clusters + 2 * REACH)
    coeffs = expansion(chemical_potential[0], ORDER)
    probe_wide = probes.astype(jnp.float32)
    partial_sq = jnp.sum(probe_wide * probe_wide, axis=(0, 2))
    norm_sq = lax.psum(partial_sq, "clus")

    def operate(vector_b):
        padded = extended(vector_b, (("clus", 0),), REACH)
        direct = direct_terms(padded, masked_hop, frame_ids)
        carried = spread_terms(vector_b, masked_hop, frame_ids, clusters + 2 * REACH + 1)
        from_right = passed_along(carried[:REACH], "clus", -1)
        from_left = passed_along(carried[clusters + REACH : clusters + 2 * REACH], "clus", 1)
        back = carried[REACH : REACH + clusters]
        back = back + from_right
        back = back + from_left
        result = onsite[:, None, :] * vector_b.astype(jnp.float32) + direct + back
        return (result, padded)

    previous = probe_wide
    current, probe_pad = operate(probes)
    fermi_vec = coeffs[0] * previous + coeffs[1] * current
    for term_index in range(2, ORDER + 1):
        image, unused = operate(current.astype(jnp.bfloat16))
        following = 2.0 * image - previous
        fermi_vec = fermi_vec + coeffs[term_index] * following
        previous, current = (current, following)
    scale = orbitals / (norm_sq * PROBE_VECTORS)
    density_part = jnp.sum(probe_wide * fermi_vec * scale[None, :, None], axis=1)
    weighted = (fermi_vec * scale[None, :, None]).astype(jnp.bfloat16)
    weighted_pad = extended(weighted, (("clus", 0),), REACH)
    u_cols = gather_columns(weighted_pad, frame_ids)
    v_cols = gather_columns(probe_pad, frame_ids)
    row_sums, col_sums = bond_sums(weighted, probes, u_cols, v_cols, masked_hop)
    facing = jnp.transpose(bond_dir.astype(jnp.float32), (1, 2, 0))
    orbital_gradient = jnp.sum(-DECAY * facing[:, :, :, None] * row_sums[:, :, None, :], axis=0)
    col_force = column_force(bond_dir, col_sums, frame_ids, clusters + 2 * REACH + 1)
    from_right = passed_along(col_force[:REACH], "clus", -1)
    from_left = passed_along(col_force[clusters + REACH : clusters + 2 * REACH], "clus", 1)
    orbital_gradient = orbital_gradient + col_force[REACH : REACH + clusters]
    orbital_gradient = orbital_gradient + from_right
    orbital_gradient = orbital_gradient + from_left
    atom_table = (atom_of[:, :, None] == jnp.arange(ATOMS, dtype=jnp.int32)[None, None, :]).astype(
        jnp.float32
    )
    atom_part = jnp.einsum(
        "rxb,rba->xra", orbital_gradient, atom_table, precision=lax.Precision.HIGHEST
    ).reshape(3, -1)
    density, atom_force = lax.psum((density_part, atom_part), "probe")
    filling = lax.psum(jnp.sum(density), "clus") / orbitals
    return (density, filling.reshape(1), atom_force)


def solution(mesh):
    placed = (
        P("clus", "probe", None),
        P("clus", None),
        P(None, "clus", None, None),
        P(None, "clus"),
        P("clus", None),
        P(None, None, "clus"),
        P(),
    )
    return jax.shard_map(
        local,
        mesh=mesh,
        in_specs=placed,
        out_specs=(P("clus", None), P(), P(None, "clus")),
        check_vma=False,
    )
```

profile of v0, /device:TPU:0, one launch (start us, length us, event | category | flops | bytes accessed | tf_op | source)
XLA Modules:
  0.0 311.9 jit_solution(14179802864283995936)
XLA Ops:
  1.9 3.0 collective-permute-start
  6.6 10.7 %copy.79 = bf16[20,12,128,128]{2,3,0,1:T(8,128)(2,1)} copy(bf16[20,12,128,128]{3,2,1,0:T(8,128)(2,1)} %param.11) | data formatting | bytes 15728640 | tf_op args[2]
  17.3 5.0 %convolution_bitcast_fusion.3 = f32[20,12,32,128]{3,2,0,1:T(8,128)S(1)} fusion(bf16[12,32,128]{2,1,0:T(8,128)(2,1)S(1)} %copy-done.1, bf16[20,12,128,128]{2,3,0,1:T(8,128)(2,1)} %copy.79, pred[20,12]{0,1:T(8,128)(4,1)S(1)} %broadcast_compare_fusion), kind=kOutput, calls=%fused_computation.23 | convolution fusion | flops 255590400 | bytes 11895024 | tf_op jit(solution)/shard_map/rpi,mrij->mrpj/dot_general | solution.py:60
  22.3 2.3 copy.83
  24.6 21.7 %scatter_fusion = f32[37,32,128]{2,1,0:T(8,128)S(1)} fusion(f32[37,32,128]{2,1,0:T(8,128)S(1)} %broadcast.72.clone.1, s32[240]{0:T(256)S(1)} %reshape.135, f32[240,32,128]{2,1,0:T(8,128)} %bitcast.92), kind=kCustom, calls=%fused_computation.5 | custom fusion | flops 983040 | bytes 11797440 | tf_op jit(solution)/shard_map/scatter-add | solution.py:62
  46.4 5.1 %collective-permute-start.3 = (f32[12,32,128]{2,1,0:T(8,128)S(1)}, f32[12,32,128]{2,1,0:T(8,128)}, u32[]{:S(2)}, u32[]{:S(2)}) collective-permute-start(f32[12,32,128]{2,1,0:T(8,128)S(1)} %get-tuple-element.17), channel_id=1, source_target_pairs={{0,4},{4,8},{8,12},{12,16},{16,20},{20,24},{24,28},{1,5},{5,9},{9,... | collective-permute-start | bytes 589832 | tf_op jit(solution)/shard_map/ppermute | solution.py:33
  60.2 5.1 %fusion.80 = (bf16[12,32,128]{2,1,0:T(8,128)(2,1)S(1)}, f32[12,32,128]{2,1,0:T(8,128)}) fusion(f32[12,32,128]{2,1,0:T(8,128)} %collective-permute-done.3, f32[12,32,128]{2,1,0:T(8,128)} %collective-permute-done.2, f32[37,32,128]{2,1,0:T(8,128)S(1)} %scatter_fusion, bf16[20,12,32,128]{3,2,1,0:T(8,128)(2,1)S(1)} %bitcast.102, ...), kind=kOutput, calls=%fused_computation.113 | convolution fusion | flops 255934464 | bytes 10819824 | tf_op jit(solution)/shard_map/mrpj,mrij->rpi/dot_general | solution.py:56
  65.3 2.9 convolution_bitcast_fusion.2
  69.4 4.3 %collective-permute-start.4 = (bf16[12,32,128]{2,1,0:T(8,128)(2,1)S(1)}, bf16[12,32,128]{2,1,0:T(8,128)(2,1)}, u32[]{:S(2)}, u32[]{:S(2)}) collective-permute-start(bf16[12,32,128]{2,1,0:T(8,128)(2,1)S(1)} %get-tuple-element.31), channel_id=1, source_target_pairs={{0,4},{4,8},{8,12},{12,16},{16,20},{20,24},{24,28},{1,5},{5,9},{9,... | collective-permute-start | bytes 294920 | tf_op jit(solution)/shard_map/ppermute | solution.py:22
  73.7 2.3 copy.86
  76.1 21.7 %scatter_fusion.1 = f32[37,32,128]{2,1,0:T(8,128)S(1)} fusion(f32[37,32,128]{2,1,0:T(8,128)S(1)} %broadcast.72.clone, s32[240]{0:T(256)S(1)} %reshape.135, f32[240,32,128]{2,1,0:T(8,128)} %bitcast.93), kind=kCustom, calls=%fused_computation.6 | custom fusion | flops 983040 | bytes 11797440 | tf_op jit(solution)/shard_map/scatter-add | solution.py:62
  97.8 3.7 %collective-permute-start.7 = (f32[12,32,128]{2,1,0:T(8,128)S(1)}, f32[12,32,128]{2,1,0:T(8,128)}, u32[]{:S(2)}, u32[]{:S(2)}) collective-permute-start(f32[12,32,128]{2,1,0:T(8,128)S(1)} %get-tuple-element.15), channel_id=1, source_target_pairs={{0,4},{4,8},{8,12},{12,16},{16,20},{20,24},{24,28},{1,5},{5,9},{9,... | collective-permute-start | bytes 589832 | tf_op jit(solution)/shard_map/ppermute | solution.py:33
  108.9 5.3 %fusion.41 = (f32[32]{0:T(128)S(1)}, bf16[12,32,128]{2,1,0:T(8,128)(2,1)}, f32[12,32,128]{2,1,0:T(8,128)}) fusion(bf16[12,32,128]{2,1,0:T(8,128)(2,1)S(1)} %copy-done.1, f32[12,32,128]{2,1,0:T(8,128)} %collective-permute-done.7, f32[12,32,128]{2,1,0:T(8,128)} %collective-permute-done.6, f32[37,32,128]{2,1,0:T(8,128)S(1)} %scatter_fusion.1, ...), kind=kOutput, calls=%fused_computation.59 | convolution fusion | flops 256180192 | bytes 10918256 | tf_op jit(solution)/shard_map/mrpj,mrij->rpi/dot_general | solution.py:56
  114.2 5.0 %convolution_bitcast_fusion.1 = f32[20,12,32,128]{3,2,0,1:T(8,128)} fusion(bf16[12,32,128]{2,1,0:T(8,128)(2,1)} %get-tuple-element.21, bf16[20,12,128,128]{2,3,0,1:T(8,128)(2,1)S(1)} %bitcast.99, pred[20,12]{0,1:T(8,128)(4,1)S(1)} %broadcast_compare_fusion), kind=kOutput, calls=%fused_computation.21 | convolution fusion | flops 255590400 | bytes 11895024 | tf_op jit(solution)/shard_map/rpi,mrij->mrpj/dot_general | solution.py:60
  120.5 4.3 %collective-permute-start.8 = (bf16[12,32,128]{2,1,0:T(8,128)(2,1)}, bf16[12,32,128]{2,1,0:T(8,128)(2,1)}, u32[]{:S(2)}, u32[]{:S(2)}) collective-permute-start(bf16[12,32,128]{2,1,0:T(8,128)(2,1)} %get-tuple-element.21), channel_id=1, source_target_pairs={{0,4},{4,8},{8,12},{12,16},{16,20},{20,24},{24,28},{1,5},{5,9},{9,... | collective-permute-start | bytes 294920 | tf_op jit(solution)/shard_map/ppermute | solution.py:22
  124.8 12.9 %psum.28 = f32[32]{0:T(128)S(1)} all-reduce(f32[32]{0:T(128)S(1)} %get-tuple-element.20), channel_id=1, replica_groups=mesh['clus'=8,'probe'=4] {'clus'}, use_global_device_ids=true, to_apply=%region_6.8 | all-reduce | flops 32 | bytes 256 | tf_op jit(solution)/shard_map/psum | solution.py:93
  137.7 4.6 %copy.89 = f32[20,12,32,128]{3,2,1,0:T(8,128)} copy(f32[20,12,32,128]{3,2,0,1:T(8,128)} %convolution_bitcast_fusion.1) | data formatting | bytes 7864320 | tf_op jit(solution)/shard_map/rpi,mrij->mrpj/transpose | solution.py:60
  142.3 21.7 %scatter_fusion.2 = f32[37,32,128]{2,1,0:T(8,128)S(1)} fusion(f32[37,32,128]{2,1,0:T(8,128)S(1)} %broadcast.72.clone.2, s32[240]{0:T(256)S(1)} %reshape.135, f32[240,32,128]{2,1,0:T(8,128)} %bitcast.94), kind=kCustom, calls=%fused_computation.7 | custom fusion | flops 983040 | bytes 11797440 | tf_op jit(solution)/shard_map/scatter-add | solution.py:62
  174.4 5.2 %fusion.81 = (bf16[12,32,128]{2,1,0:T(8,128)(2,1)S(1)}, f32[12,32,128]{2,1,0:T(8,128)}) fusion(f32[12,32,128]{2,1,0:T(8,128)} %get-tuple-element.32, f32[12,32,128]{2,1,0:T(8,128)} %collective-permute-done.11, f32[12,32,128]{2,1,0:T(8,128)} %collective-permute-done.10, f32[37,32,128]{2,1,0:T(8,128)S(1)} %scatter_fusion.2, ...), kind=kOutput, calls=%fused_computation.114 | convolution fusion | flops 256032768 | bytes 11016432 | tf_op jit(solution)/shard_map/mrpj,mrij->rpi/dot_general | solution.py:56
  179.6 2.9 convolution_bitcast_fusion
  183.7 5.9 %collective-permute-start.12 = (bf16[12,32,128]{2,1,0:T(8,128)(2,1)S(1)}, bf16[12,32,128]{2,1,0:T(8,128)(2,1)}, u32[]{:S(2)}, u32[]{:S(2)}) collective-permute-start(bf16[12,32,128]{2,1,0:T(8,128)(2,1)S(1)} %get-tuple-element.34), channel_id=1, source_target_pairs={{0,4},{4,8},{8,12},{12,16},{16,20},{20,24},{24,28},{1,5},{5,9},{9,... | collective-permute-start | bytes 294920 | tf_op jit(solution)/shard_map/ppermute | solution.py:22
  189.6 2.3 copy.92
  191.9 21.7 %scatter_fusion.3 = f32[37,32,128]{2,1,0:T(8,128)S(1)} fusion(f32[37,32,128]{2,1,0:T(8,128)S(1)} %broadcast.72, s32[240]{0:T(256)S(1)} %reshape.135, f32[240,32,128]{2,1,0:T(8,128)} %bitcast.95), kind=kCustom, calls=%fused_computation.8 | custom fusion | flops 983040 | bytes 11797440 | tf_op jit(solution)/shard_map/scatter-add | solution.py:62
  214.5 3.6 %collective-permute-start.15 = (f32[12,32,128]{2,1,0:T(8,128)}, f32[12,32,128]{2,1,0:T(8,128)}, u32[]{:S(2)}, u32[]{:S(2)}) collective-permute-start(f32[12,32,128]{2,1,0:T(8,128)} %get-tuple-element.11), channel_id=1, source_target_pairs={{0,4},{4,8},{8,12},{12,16},{16,20},{20,24},{24,28},{1,5},{5,9},{9,... | collective-permute-start | bytes 589832 | tf_op jit(solution)/shard_map/ppermute | solution.py:33
  225.5 7.8 %multiply_convert_fusion = (bf16[12,32,128]{2,1,0:T(8,128)(2,1)S(1)}, f32[12,128]{1,0:T(8,128)S(1)}) fusion(f32[32]{0:T(128)S(1)} %multiply_divide_fusion, bf16[12,32,128]{2,1,0:T(8,128)(2,1)S(1)} %copy-done.2, f32[12,32,128]{2,1,0:T(8,128)} %collective-permute-done.15, f32[12,32,128]{2,1,0:T(8,128)} %collective-permute-done.14, ...), kind=kOutput, calls=%fused_computation.77 | convolution fusion | flops 257112576 | bytes 12005764 | tf_op jit(solution)/shard_map/mrpj,mrij->rpi/dot_general | solution.py:56
  234.6 4.2 %collective-permute-start.16 = (bf16[12,32,128]{2,1,0:T(8,128)(2,1)S(1)}, bf16[12,32,128]{2,1,0:T(8,128)(2,1)S(1)}, u32[]{:S(2)}, u32[]{:S(2)}) collective-permute-start(bf16[12,32,128]{2,1,0:T(8,128)(2,1)S(1)} %get-tuple-element.18), channel_id=1, source_target_pairs={{0,4},{4,8},{8,12},{12,16},{16,20},{20,24},{24,28},{1,5},{5,9},{9,... | collective-permute-start | bytes 294920 | tf_op jit(solution)/shard_map/ppermute | solution.py:22
  238.9 6.9 %fusion.9 = f32[12,20,128,128]{3,2,1,0:T(8,128)} fusion(bf16[20,12,32,128]{3,2,1,0:T(8,128)(2,1)S(1)} %bitcast.103, bf16[12,32,128]{2,1,0:T(8,128)(2,1)S(1)} %get-tuple-element.18), kind=kOutput, calls=%fused_computation.25 | convolution fusion | flops 251658240 | bytes 17793024 | tf_op jit(solution)/shard_map/rpi,mrpj->mrij/dot_general | solution.py:66
  247.7 12.0 %fusion.73 = (f32[20,12,128]{2,0,1:T(8,128)S(1)}, f32[20,12,128]{2,0,1:T(8,128)S(1)}) fusion(f32[12,20,128,128]{3,2,1,0:T(8,128)} %fusion.9, bf16[12,32,128]{2,1,0:T(8,128)(2,1)S(1)} %copy-done.3, bf16[20,12,32,128]{3,2,1,0:T(8,128)(2,1)S(1)} %bitcast.107, bf16[20,12,128,128]{2,3,0,1:T(8,128)(2,1)} %copy.79, pred[20,12]{0,1:T(8,128)(4,1)S(1)} %broadcast_compare_fusion), kind=kOutput, calls=%fused_computation.106 | convolution fusion | flops 275189760 | bytes 25903344 | tf_op jit(solution)/shard_map/rpi,mrpj->mrij/dot_general | solution.py:69
  260.2 9.3 %scatter_fusion.4 = f32[37,3,128]{2,1,0:T(4,128)S(1)} fusion(f32[37,3,128]{2,1,0:T(4,128)S(1)} %broadcast_in_dim.57, s32[240]{0:T(256)S(1)} %reshape.135, f32[240,3,128]{2,1,0:T(4,128)S(1)} %broadcast_multiply_fusion), kind=kCustom, calls=%fused_computation.9 | custom fusion | flops 92160 | bytes 1106880 | tf_op jit(solution)/shard_map/scatter-add | solution.py:80
  269.5 4.1 %collective-permute-start.19 = (f32[12,3,128]{2,1,0:T(4,128)S(1)}, f32[12,3,128]{2,1,0:T(4,128)S(1)}, u32[]{:S(2)}, u32[]{:S(2)}) collective-permute-start(f32[12,3,128]{2,1,0:T(4,128)S(1)} %get-tuple-element.23), channel_id=1, source_target_pairs={{0,4},{4,8},{8,12},{12,16},{16,20},{20,24},{24,28},{1,5},{5,9},{9,... | collective-permute-start | bytes 55304 | tf_op jit(solution)/shard_map/ppermute | solution.py:33
  277.5 19.5 %all-reduce = (f32[12,128]{1,0:T(8,128)S(1)}, f32[3,384]{1,0:T(4,128)}) all-reduce(f32[12,128]{1,0:T(8,128)S(1)} %get-tuple-element.19, f32[3,384]{1,0:T(4,128)S(1)} %reshape.92), channel_id=1, replica_groups=mesh['clus'=8,'probe'=4] {'probe'}, use_global_device_ids=true, to_apply=%region_8.10 | all-reduce | flops 2688 | bytes 21504 | tf_op jit(solution)/shard_map/psum | solution.py:136
  297.7 12.4 %psum.30 = f32[]{:T(128)} all-reduce(f32[]{:T(128)} %reduce_sum.66), channel_id=1, replica_groups=mesh['clus'=8,'probe'=4] {'clus'}, use_global_device_ids=true, to_apply=%region_10.12 | all-reduce | flops 1 | bytes 8 | tf_op jit(solution)/shard_map/psum | solution.py:137
  (134 shorter events, 48.8 us)
Async XLA Ops:
  0.6 55.0 %collective-permute-start.1 = (bf16[12,32,128]{2,1,0:T(8,128)(2,1)}, bf16[12,32,128]{2,1,0:T(8,128)(2,1)S(1)}, u32[]{:S(2)}, u32[]{:S(2)}) collective-permute-start(bf16[12,32,128]{2,1,0:T(8,128)(2,1)} %param.9), channel_id=1, source_target_pairs={{4,0},{8,4},{12,8},{16,12},{20,16},{24,20},{28,24},{5,1},{9,5},{13... | collective-permute-start | bytes 294920 | tf_op jit(solution)/shard_map/ppermute | solution.py:25
  1.9 53.7 %collective-permute-start = (bf16[12,32,128]{2,1,0:T(8,128)(2,1)}, bf16[12,32,128]{2,1,0:T(8,128)(2,1)S(1)}, u32[]{:S(2)}, u32[]{:S(2)}) collective-permute-start(bf16[12,32,128]{2,1,0:T(8,128)(2,1)} %param.9), channel_id=1, source_target_pairs={{0,4},{4,8},{8,12},{12,16},{16,20},{20,24},{24,28},{1,5},{5,9},{9,... | collective-permute-start | bytes 294920 | tf_op jit(solution)/shard_map/ppermute | solution.py:22
  6.6 10.8 %copy-start.1 = (bf16[12,32,128]{2,1,0:T(8,128)(2,1)S(1)}, bf16[12,32,128]{2,1,0:T(8,128)(2,1)}, u32[]{:S(2)}) copy-start(bf16[12,32,128]{2,1,0:T(8,128)(2,1)} %param.9) | copy-start | bytes 294916
  24.6 30.0 %copy-start.11 = (bf16[3,20,12]{1,2,0:T(8,128)(2,1)S(1)}, bf16[3,20,12]{1,2,0:T(8,128)(2,1)}, u32[]{:S(2)}) copy-start(bf16[3,20,12]{1,2,0:T(8,128)(2,1)} %param.14) | copy-start | bytes 4324
  46.4 13.7 %collective-permute-start.3 = (f32[12,32,128]{2,1,0:T(8,128)S(1)}, f32[12,32,128]{2,1,0:T(8,128)}, u32[]{:S(2)}, u32[]{:S(2)}) collective-permute-start(f32[12,32,128]{2,1,0:T(8,128)S(1)} %get-tuple-element.17), channel_id=1, source_target_pairs={{0,4},{4,8},{8,12},{12,16},{16,20},{20,24},{24,28},{1,5},{5,9},{9,... | collective-permute-start | bytes 589832 | tf_op jit(solution)/shard_map/ppermute | solution.py:33
  51.6 8.6 %collective-permute-start.2 = (f32[12,32,128]{2,1,0:T(8,128)S(1)}, f32[12,32,128]{2,1,0:T(8,128)}, u32[]{:S(2)}, u32[]{:S(2)}) collective-permute-start(f32[12,32,128]{2,1,0:T(8,128)S(1)} %get-tuple-element.16), channel_id=1, source_target_pairs={{4,0},{8,4},{12,8},{16,12},{20,16},{24,20},{28,24},{5,1},{9,5},{13... | collective-permute-start | bytes 589832 | tf_op jit(solution)/shard_map/ppermute | solution.py:33
  57.9 7.3 %slice-start = ((s8[7864320]{0:T(1024)(128)(4,1)}), s8[4194304]{0:T(1024)(128)(4,1)S(1)}, s32[]{:S(2)}) async-start(s8[7864320]{0:T(1024)(128)(4,1)} %bitcast.96), calls=%async_computation | async-start | bytes 8388608
  60.2 5.1 %slice-start.1 = ((s8[7864320]{0:T(1024)(128)(4,1)}), s8[3670016]{0:T(1024)(128)(4,1)S(1)}, s32[]{:S(2)}) async-start(s8[7864320]{0:T(1024)(128)(4,1)} %bitcast.96), calls=%async_computation.1 | async-start | bytes 7340032
  65.2 43.6 %copy-start.4 = (bf16[12,32,128]{2,1,0:T(8,128)(2,1)}, bf16[12,32,128]{2,1,0:T(8,128)(2,1)S(1)}, u32[]{:S(2)}) copy-start(bf16[12,32,128]{2,1,0:T(8,128)(2,1)S(1)} %get-tuple-element.31) | copy-start | bytes 294916
  68.1 34.7 %collective-permute-start.5 = (bf16[12,32,128]{2,1,0:T(8,128)(2,1)S(1)}, bf16[12,32,128]{2,1,0:T(8,128)(2,1)S(1)}, u32[]{:S(2)}, u32[]{:S(2)}) collective-permute-start(bf16[12,32,128]{2,1,0:T(8,128)(2,1)S(1)} %get-tuple-element.31), channel_id=1, source_target_pairs={{4,0},{8,4},{12,8},{16,12},{20,16},{24,20},{28,24},{5,1},{9,5},{13... | collective-permute-start | bytes 294920 | tf_op jit(solution)/shard_map/ppermute | solution.py:25
  69.4 34.0 %collective-permute-start.4 = (bf16[12,32,128]{2,1,0:T(8,128)(2,1)S(1)}, bf16[12,32,128]{2,1,0:T(8,128)(2,1)}, u32[]{:S(2)}, u32[]{:S(2)}) collective-permute-start(bf16[12,32,128]{2,1,0:T(8,128)(2,1)S(1)} %get-tuple-element.31), channel_id=1, source_target_pairs={{0,4},{4,8},{8,12},{12,16},{16,20},{20,24},{24,28},{1,5},{5,9},{9,... | collective-permute-start | bytes 294920 | tf_op jit(solution)/shard_map/ppermute | solution.py:22
  97.8 11.0 %collective-permute-start.7 = (f32[12,32,128]{2,1,0:T(8,128)S(1)}, f32[12,32,128]{2,1,0:T(8,128)}, u32[]{:S(2)}, u32[]{:S(2)}) collective-permute-start(f32[12,32,128]{2,1,0:T(8,128)S(1)} %get-tuple-element.15), channel_id=1, source_target_pairs={{0,4},{4,8},{8,12},{12,16},{16,20},{20,24},{24,28},{1,5},{5,9},{9,... | collective-permute-start | bytes 589832 | tf_op jit(solution)/shard_map/ppermute | solution.py:33
  101.5 7.3 %collective-permute-start.6 = (f32[12,32,128]{2,1,0:T(8,128)S(1)}, f32[12,32,128]{2,1,0:T(8,128)}, u32[]{:S(2)}, u32[]{:S(2)}) collective-permute-start(f32[12,32,128]{2,1,0:T(8,128)S(1)} %get-tuple-element.14), channel_id=1, source_target_pairs={{4,0},{8,4},{12,8},{16,12},{20,16},{24,20},{28,24},{5,1},{9,5},{13... | collective-permute-start | bytes 589832 | tf_op jit(solution)/shard_map/ppermute | solution.py:33
  106.6 7.5 %slice-start.2 = ((s8[7864320]{0:T(1024)(128)(4,1)}), s8[4194304]{0:T(1024)(128)(4,1)S(1)}, s32[]{:S(2)}) async-start(s8[7864320]{0:T(1024)(128)(4,1)} %bitcast.98), calls=%async_computation.2 | async-start | bytes 8388608
  108.9 5.3 %slice-start.3 = ((s8[7864320]{0:T(1024)(128)(4,1)}), s8[3670016]{0:T(1024)(128)(4,1)S(1)}, s32[]{:S(2)}) async-start(s8[7864320]{0:T(1024)(128)(4,1)} %bitcast.98), calls=%async_computation.3 | async-start | bytes 7340032
  119.2 49.1 %collective-permute-start.9 = (bf16[12,32,128]{2,1,0:T(8,128)(2,1)}, bf16[12,32,128]{2,1,0:T(8,128)(2,1)S(1)}, u32[]{:S(2)}, u32[]{:S(2)}) collective-permute-start(bf16[12,32,128]{2,1,0:T(8,128)(2,1)} %get-tuple-element.21), channel_id=1, source_target_pairs={{4,0},{8,4},{12,8},{16,12},{20,16},{24,20},{28,24},{5,1},{9,5},{13... | collective-permute-start | bytes 294920 | tf_op jit(solution)/shard_map/ppermute | solution.py:25
  120.5 48.5 %collective-permute-start.8 = (bf16[12,32,128]{2,1,0:T(8,128)(2,1)}, bf16[12,32,128]{2,1,0:T(8,128)(2,1)}, u32[]{:S(2)}, u32[]{:S(2)}) collective-permute-start(bf16[12,32,128]{2,1,0:T(8,128)(2,1)} %get-tuple-element.21), channel_id=1, source_target_pairs={{0,4},{4,8},{8,12},{12,16},{16,20},{20,24},{24,28},{1,5},{5,9},{9,... | collective-permute-start | bytes 294920 | tf_op jit(solution)/shard_map/ppermute | solution.py:22
  164.8 9.5 %collective-permute-start.11 = (f32[12,32,128]{2,1,0:T(8,128)}, f32[12,32,128]{2,1,0:T(8,128)}, u32[]{:S(2)}, u32[]{:S(2)}) collective-permute-start(f32[12,32,128]{2,1,0:T(8,128)} %get-tuple-element.13), channel_id=1, source_target_pairs={{0,4},{4,8},{8,12},{12,16},{16,20},{20,24},{24,28},{1,5},{5,9},{9,... | collective-permute-start | bytes 589832 | tf_op jit(solution)/shard_map/ppermute | solution.py:33
  166.8 7.6 %collective-permute-start.10 = (f32[12,32,128]{2,1,0:T(8,128)}, f32[12,32,128]{2,1,0:T(8,128)}, u32[]{:S(2)}, u32[]{:S(2)}) collective-permute-start(f32[12,32,128]{2,1,0:T(8,128)} %get-tuple-element.12), channel_id=1, source_target_pairs={{4,0},{8,4},{12,8},{16,12},{20,16},{24,20},{28,24},{5,1},{9,5},{13... | collective-permute-start | bytes 589832 | tf_op jit(solution)/shard_map/ppermute | solution.py:33
  172.1 7.4 %slice-start.4 = ((s8[7864320]{0:T(1024)(128)(4,1)}), s8[4194304]{0:T(1024)(128)(4,1)S(1)}, s32[]{:S(2)}) async-start(s8[7864320]{0:T(1024)(128)(4,1)} %bitcast.100), calls=%async_computation.4 | async-start | bytes 8388608
  174.4 5.2 %slice-start.5 = ((s8[7864320]{0:T(1024)(128)(4,1)}), s8[3670016]{0:T(1024)(128)(4,1)S(1)}, s32[]{:S(2)}) async-start(s8[7864320]{0:T(1024)(128)(4,1)} %bitcast.100), calls=%async_computation.5 | async-start | bytes 7340032
  182.4 37.0 %collective-permute-start.13 = (bf16[12,32,128]{2,1,0:T(8,128)(2,1)S(1)}, bf16[12,32,128]{2,1,0:T(8,128)(2,1)S(1)}, u32[]{:S(2)}, u32[]{:S(2)}) collective-permute-start(bf16[12,32,128]{2,1,0:T(8,128)(2,1)S(1)} %get-tuple-element.34), channel_id=1, source_target_pairs={{4,0},{8,4},{12,8},{16,12},{20,16},{24,20},{28,24},{5,1},{9,5},{13... | collective-permute-start | bytes 294920 | tf_op jit(solution)/shard_map/ppermute | solution.py:25
  183.7 36.3 %collective-permute-start.12 = (bf16[12,32,128]{2,1,0:T(8,128)(2,1)S(1)}, bf16[12,32,128]{2,1,0:T(8,128)(2,1)}, u32[]{:S(2)}, u32[]{:S(2)}) collective-permute-start(bf16[12,32,128]{2,1,0:T(8,128)(2,1)S(1)} %get-tuple-element.34), channel_id=1, source_target_pairs={{0,4},{4,8},{8,12},{12,16},{16,20},{20,24},{24,28},{1,5},{5,9},{9,... | collective-permute-start | bytes 294920 | tf_op jit(solution)/shard_map/ppermute | solution.py:22
  214.5 11.0 %collective-permute-start.15 = (f32[12,32,128]{2,1,0:T(8,128)}, f32[12,32,128]{2,1,0:T(8,128)}, u32[]{:S(2)}, u32[]{:S(2)}) collective-permute-start(f32[12,32,128]{2,1,0:T(8,128)} %get-tuple-element.11), channel_id=1, source_target_pairs={{0,4},{4,8},{8,12},{12,16},{16,20},{20,24},{24,28},{1,5},{5,9},{9,... | collective-permute-start | bytes 589832 | tf_op jit(solution)/shard_map/ppermute | solution.py:33
  218.1 7.3 %collective-permute-start.14 = (f32[12,32,128]{2,1,0:T(8,128)}, f32[12,32,128]{2,1,0:T(8,128)}, u32[]{:S(2)}, u32[]{:S(2)}) collective-permute-start(f32[12,32,128]{2,1,0:T(8,128)} %get-tuple-element.10), channel_id=1, source_target_pairs={{4,0},{8,4},{12,8},{16,12},{20,16},{24,20},{28,24},{5,1},{9,5},{13... | collective-permute-start | bytes 589832 | tf_op jit(solution)/shard_map/ppermute | solution.py:33
  233.3 12.4 %collective-permute-start.17 = (bf16[12,32,128]{2,1,0:T(8,128)(2,1)S(1)}, bf16[12,32,128]{2,1,0:T(8,128)(2,1)S(1)}, u32[]{:S(2)}, u32[]{:S(2)}) collective-permute-start(bf16[12,32,128]{2,1,0:T(8,128)(2,1)S(1)} %get-tuple-element.18), channel_id=1, source_target_pairs={{4,0},{8,4},{12,8},{16,12},{20,16},{24,20},{28,24},{5,1},{9,5},{13... | collective-permute-start | bytes 294920 | tf_op jit(solution)/shard_map/ppermute | solution.py:25
  234.6 11.1 %collective-permute-start.16 = (bf16[12,32,128]{2,1,0:T(8,128)(2,1)S(1)}, bf16[12,32,128]{2,1,0:T(8,128)(2,1)S(1)}, u32[]{:S(2)}, u32[]{:S(2)}) collective-permute-start(bf16[12,32,128]{2,1,0:T(8,128)(2,1)S(1)} %get-tuple-element.18), channel_id=1, source_target_pairs={{0,4},{4,8},{8,12},{12,16},{16,20},{20,24},{24,28},{1,5},{5,9},{9,... | collective-permute-start | bytes 294920 | tf_op jit(solution)/shard_map/ppermute | solution.py:22
  247.7 12.1 %copy-start = (f32[240,3]{1,0:T(8,128)S(1)}, f32[240,3]{1,0:T(8,128)}, u32[]{:S(2)}) copy-start(f32[240,3]{1,0:T(8,128)} %copy.97) | copy-start | bytes 8644
  247.7 29.5 %copy-start.14 = (s32[12,128]{1,0:T(8,128)S(1)}, s32[12,128]{1,0:T(8,128)}, u32[]{:S(2)}) copy-start(s32[12,128]{1,0:T(8,128)} %param.13) | copy-start | bytes 18436
  269.5 5.6 %collective-permute-start.19 = (f32[12,3,128]{2,1,0:T(4,128)S(1)}, f32[12,3,128]{2,1,0:T(4,128)S(1)}, u32[]{:S(2)}, u32[]{:S(2)}) collective-permute-start(f32[12,3,128]{2,1,0:T(4,128)S(1)} %get-tuple-element.23), channel_id=1, source_target_pairs={{0,4},{4,8},{8,12},{12,16},{16,20},{20,24},{24,28},{1,5},{5,9},{9,... | collective-permute-start | bytes 55304 | tf_op jit(solution)/shard_map/ppermute | solution.py:33
  273.5 3.6 %collective-permute-start.18 = (f32[12,3,128]{2,1,0:T(4,128)S(1)}, f32[12,3,128]{2,1,0:T(4,128)S(1)}, u32[]{:S(2)}, u32[]{:S(2)}) collective-permute-start(f32[12,3,128]{2,1,0:T(4,128)S(1)} %get-tuple-element.22), channel_id=1, source_target_pairs={{4,0},{8,4},{12,8},{16,12},{20,16},{24,20},{28,24},{5,1},{9,5},{13... | collective-permute-start | bytes 55304 | tf_op jit(solution)/shard_map/ppermute | solution.py:33
  297.1 13.7 %copy-start.12 = (f32[12,128]{1,0:T(8,128)}, f32[12,128]{1,0:T(8,128)S(1)}, u32[]{:S(2)}) copy-start(f32[12,128]{1,0:T(8,128)S(1)} %get-tuple-element.6) | copy-start | bytes 18436
  (12 other events, 25.8 us)
where the time goes:
time: 317 us; the launch traced here: 312 us
  other arithmetic  112 us (35%)
  matrix products  58.2 us (18%)
  starting transfers between devices  53.3 us (17%)
  blocking collectives  44.8 us (14%)
  local copies, waits for them, and re-layouts  37.9 us (12%)
  between operations  3.84 us (1%)
    scatter-add x4, other arithmetic, spread_terms(): jax.ops.segment_sum(flat, target_ids.reshape(-1), num_segments=segments)  86.9 us
    ppermute x10, starting transfers between devices, passed_along(): return lax.ppermute(array, axis, pairs)  25.1 us
    dot_general x4, matrix products, direct_terms(): jnp.einsum('mrpj,mrij->rpi', picked, blocks, preferred_element_type=jnp.f...  23.3 us
    ppermute x5, starting transfers between devices, extended(): lax.ppermute(lax.slice_in_dim(block, block.shape[dim] - width, None, axis...  21.7 us
    psum x1, blocking collectives, local(): density, atom_force = lax.psum((density_part, atom_part), 'probe')  19.5 us
    dot_general x4, matrix products, spread_terms(): jnp.einsum('rpi,mrij->mrpj', vector_rows, blocks, preferred_element_type=...  15.7 us
    psum x1, blocking collectives, local(): norm_sq = lax.psum(partial_sq, 'clus')  12.9 us
    unnamed x49, local copies, waits for them, and re-layouts  12.7 us
  transfers between devices with their start and end apart: 20, of which 1 were waited for; matrix products, arithmetic and copies ran while one was open for 47% of the time, Pallas kernels for 0%

commit v1 on v0

v1 whole, which is shorter than its diff:
```python
import functools

import jax
import jax.numpy as jnp
from jax import lax
from jax.experimental import pallas as pl
from jax.experimental.pallas import tpu as pltpu
from jax.sharding import PartitionSpec as P

ATOMS = 32
REACH = 12
PROBE_VECTORS = 128
ORDER = 4
DECAY = 50.0
SMEARING_TEMP = 0.1
QUAD_NODES = 64
HALF_SLOTS = 10

bf16 = jnp.bfloat16
f32 = jnp.float32
NN = (((1,), (0,)), ((), ()))
NT = (((1,), (1,)), ((), ()))
dot = functools.partial(lax.dot_general, preferred_element_type=f32)
VM = pl.BlockSpec(memory_space=pltpu.VMEM)
SM = pl.BlockSpec(memory_space=pltpu.SMEM)


def params(flops, nbytes):
    return dict(
        compiler_params=pltpu.CompilerParams(vmem_limit_bytes=8 << 20),
        cost_estimate=pl.CostEstimate(flops=flops, bytes_accessed=nbytes, transcendentals=0),
    )


def expansion(chemical_potential, degree):
    node_index = jnp.arange(QUAD_NODES, dtype=f32)
    bond_angles = jnp.pi * (node_index + 0.5) / QUAD_NODES
    fermi_occupation = 1.0 / (
        1.0 + jnp.exp((jnp.cos(bond_angles) - chemical_potential) / SMEARING_TEMP)
    )
    orders = jnp.arange(degree + 1, dtype=f32)
    cosines = jnp.cos(orders[:, None] * bond_angles[None, :])
    coeffs = 2.0 / QUAD_NODES * jnp.sum(cosines * fermi_occupation[None, :], axis=1)
    return coeffs * jnp.where(orders == 0.0, 0.5, 1.0)


def exchange(even_side, odd_side):
    count = lax.axis_size("clus")
    paired = [(i, i ^ 1) for i in range(count)]
    shifted = [(i, i + 1 if i % 2 else i - 1) for i in range(count)]
    shifted = [(i, j if 0 <= j < count else i) for i, j in shifted]
    crossed = lax.ppermute(odd_side, "clus", shifted)
    return lax.ppermute(even_side, "clus", paired), crossed


def doubled_sum(part, axis):
    step = 1
    while step < lax.axis_size(axis):
        pairs = [(i, i ^ step) for i in range(lax.axis_size(axis))]
        part = part + lax.ppermute(part, axis, pairs)
        step *= 2
    return part


def by_size(flag, slots, body):
    @pl.when(flag[0] != 0)
    def _():
        body(slots)

    @pl.when(flag[0] == 0)
    def _():
        body(HALF_SLOTS)


def spread(flag, ids, x, k):
    slots, rows, block, _ = k.shape
    probes = x.shape[1]
    frame = rows + 2 * REACH

    def kernel(turn, flag_ref, ids_ref, x_ref, k_ref, own_ref, even_ref, odd_ref, *rest):
        acc = rest[-1]
        acc[...] = jnp.zeros_like(acc)

        def body(count):
            for c in range(rows):
                xc = x_ref[c]
                for first in range(0, count, 4):
                    parts, targets = [], []
                    for m in range(first, min(first + 4, count), 2):
                        pair = [k_ref[m, c], k_ref[m + 1, c]]
                        out = dot(xc, jnp.concatenate(pair, axis=1), NN)
                        parts += [out[:, :block], out[:, block:]]
                        targets += [ids_ref[m, c], ids_ref[m + 1, c]]
                        if turn:
                            rest[0][m, c] = pair[0].T
                            rest[0][m + 1, c] = pair[1].T
                    values = [acc[t] + part for t, part in zip(targets, parts)]
                    for t, value in zip(targets, values):
                        acc[t] = value

        by_size(flag_ref, slots, body)
        odd = flag_ref[1]
        own_ref[...] = acc[pl.ds(REACH, rows)]
        even_ref[...] = acc[pl.ds((1 - odd) * (REACH + rows), REACH)].astype(bf16)
        odd_ref[...] = acc[pl.ds(odd * (REACH + rows), REACH)].astype(bf16)

    side = jax.ShapeDtypeStruct((REACH, probes, block), bf16)
    shapes = [jax.ShapeDtypeStruct((rows, probes, block), f32), side, side]

    def call(turn):
        out = shapes + ([jax.ShapeDtypeStruct(k.shape, k.dtype)] if turn else [])
        return pl.pallas_call(
            functools.partial(kernel, turn),
            out_shape=out,
            in_specs=[SM, SM, VM, VM],
            out_specs=[VM] * len(out),
            scratch_shapes=[pltpu.VMEM((frame + 1, probes, block), f32)],
            name="spread_turn" if turn else "spread",
            **params(2 * slots * rows * probes * block * block, k.size * 2),
        )(flag, ids, x, k)

    return call


def fill_frame(frame_ref, odd, own, even, crossed):
    rows = own.shape[0]
    frame_ref[pl.ds(REACH, rows)] = own[...]
    frame_ref[pl.ds((1 - odd) * (REACH + rows), REACH)] = even[...]
    frame_ref[pl.ds(odd * (REACH + rows), REACH)] = crossed[...]
    frame_ref[rows + 2 * REACH] = jnp.zeros(own.shape[1:], own.dtype)


def direct(flag, ids, x, even, crossed, kt, own, onsite):
    slots, rows, block, _ = kt.shape
    probes = x.shape[1]

    def kernel(flag_ref, ids_ref, x_ref, e_ref, o_ref, kt_ref, own_ref, site_ref, out_ref, frame):
        fill_frame(frame, flag_ref[1], x_ref, e_ref, o_ref)

        def body(count):
            for c in range(rows):
                acc = own_ref[c] + site_ref[pl.ds(c, 1)] * x_ref[c].astype(f32)
                for m in range(0, count, 2):
                    pair = [frame[ids_ref[m, c]], frame[ids_ref[m + 1, c]]]
                    weights = jnp.concatenate([kt_ref[m, c], kt_ref[m + 1, c]], axis=0)
                    acc = acc + dot(jnp.concatenate(pair, axis=1), weights, NN)
                out_ref[c] = acc

        by_size(flag_ref, slots, body)

    return pl.pallas_call(
        kernel,
        out_shape=jax.ShapeDtypeStruct((rows, probes, block), f32),
        in_specs=[SM, SM, VM, VM, VM, VM, VM, VM],
        out_specs=VM,
        scratch_shapes=[pltpu.VMEM((rows + 2 * REACH + 1, probes, block), bf16)],
        name="direct",
        **params(2 * slots * rows * probes * block * block, kt.size * 2),
    )(flag, ids, x, even, crossed, kt, own, onsite)


def images(flag, v, w, k):
    slots, rows, block, _ = k.shape
    probes = v.shape[1]

    def kernel(flag_ref, v_ref, w_ref, k_ref, out_ref):
        def body(count):
            for c in range(rows):
                left = jnp.concatenate([w_ref[c], v_ref[c]], axis=0)
                for m in range(0, count, 2):
                    out = dot(left, jnp.concatenate([k_ref[m, c], k_ref[m + 1, c]], axis=1), NN)
                    out_ref[m, c] = out[:, :block]
                    out_ref[m + 1, c] = out[:, block:]

        by_size(flag_ref, slots, body)

    return pl.pallas_call(
        kernel,
        out_shape=jax.ShapeDtypeStruct((slots, rows, 2 * probes, block), f32),
        in_specs=[SM, VM, VM, VM],
        out_specs=VM,
        name="images",
        **params(4 * slots * rows * probes * block * block, k.size * 2),
    )(flag, v, w, k)


def forces(flag, ids, bond, v, v_even, v_crossed, w, w_even, w_crossed, kt, image):
    slots, rows, block, _ = kt.shape
    probes = v.shape[1]
    frame_rows = rows + 2 * REACH
    sub = 8

    def folded(value):
        parts = [value[i : i + sub] for i in range(0, value.shape[0], sub)]
        while len(parts) > 1:
            parts = [a + b for a, b in zip(parts[::2], parts[1::2])]
        return parts[0]

    def kernel(flag_ref, ids_ref, bond_ref, *refs):
        v_ref, ve_ref, vo_ref, w_ref, we_ref, wo_ref, kt_ref, image_ref = refs[:8]
        own_ref, even_ref, odd_ref, vf, wf, acc = refs[8:]
        odd = flag_ref[1]
        fill_frame(vf, odd, v_ref, ve_ref, vo_ref)
        fill_frame(wf, odd, w_ref, we_ref, wo_ref)
        acc[...] = jnp.zeros_like(acc)

        def body(count):
            for c in range(rows):
                mine = jnp.concatenate([w_ref[c], v_ref[c]], axis=0).astype(f32)
                row = [jnp.zeros((sub, block), f32)] * 3
                for m in range(0, count, 2):
                    far = []
                    for slot in (m, m + 1):
                        d = ids_ref[slot, c]
                        far.append(jnp.concatenate([vf[d], wf[d]], axis=0))
                    weights = jnp.concatenate([kt_ref[m, c], kt_ref[m + 1, c]], axis=1)
                    out = dot(jnp.concatenate(far, axis=0), weights, NN)
                    direct_parts = [out[: 2 * probes, :block], out[2 * probes :, block:]]
                    for slot, other, part in zip((m, m + 1), far, direct_parts):
                        d = ids_ref[slot, c]
                        row_part = folded(mine * part)
                        col_part = folded(other.astype(f32) * image_ref[slot, c])
                        for axis in range(3):
                            b = bond_ref[axis * slots + slot, c]
                            row[axis] = row[axis] + b * row_part
                            acc[d, axis] = acc[d, axis] + b * col_part
                for axis in range(3):
                    acc[c + REACH, axis] = acc[c + REACH, axis] - row[axis]

        by_size(flag_ref, slots, body)

        def taken(start, count):
            return DECAY * jnp.sum(acc[pl.ds(start, count)], axis=2)

        own_ref[...] = taken(REACH, rows)
        even_ref[...] = taken((1 - odd) * (REACH + rows), REACH)
        odd_ref[...] = taken(odd * (REACH + rows), REACH)

    side = jax.ShapeDtypeStruct((REACH, 3, block), f32)
    frame = pltpu.VMEM((frame_rows + 1, probes, block), bf16)
    return pl.pallas_call(
        kernel,
        out_shape=[jax.ShapeDtypeStruct((rows, 3, block), f32), side, side],
        in_specs=[SM, SM, SM] + [VM] * 8,
        out_specs=[VM] * 3,
        scratch_shapes=[frame, frame, pltpu.VMEM((frame_rows + 1, 3, sub, block), f32)],
        name="forces",
        **params(4 * slots * rows * probes * block * block, kt.size * 2 + image.size * 4),
    )(flag, ids, bond, v, v_even, v_crossed, w, w_even, w_crossed, kt, image)


def local(probes, onsite, hopping, block_col, atom_of, bond_dir, chemical_potential):
    rows, _, block = probes.shape
    slots = hopping.shape[0]
    me = lax.axis_index("clus")
    orbitals = rows * lax.axis_size("clus") * block
    live = block_col >= 0
    ids = jnp.where(live, block_col - me * rows + REACH, rows + 2 * REACH)
    many = jnp.max(block_col[HALF_SLOTS:]) >= 0
    flag = jnp.stack([many.astype(jnp.int32), (me % 2).astype(jnp.int32)])
    bond = bond_dir.astype(f32).reshape(3 * slots, rows)

    x = probes
    even, crossed = exchange(x, x)
    v_even, v_crossed = even, crossed
    wide = probes.astype(f32)
    square = doubled_sum(jnp.sum(wide * wide, axis=0), "clus")
    scale = orbitals / (jnp.sum(square, axis=1) * PROBE_VECTORS)
    coeffs = expansion(chemical_potential[0], ORDER)

    cheb = [wide]
    for term in range(1, ORDER + 1):
        outs = spread(flag, ids, x, hopping)(term == 1)
        if term == 1:
            turned = outs[3]
        back_even, back_crossed = exchange(outs[1], outs[2])
        image = direct(flag, ids, x, even, crossed, turned, outs[0], onsite)
        image = image + (back_even.astype(f32) + back_crossed.astype(f32))
        cheb.append(image if term == 1 else 2.0 * image - cheb[-2])
        x = cheb[-1].astype(bf16)
        if term < ORDER:
            even, crossed = exchange(x, x)
    fermi = coeffs[0] * cheb[0]
    for term in range(1, ORDER + 1):
        fermi = fermi + coeffs[term] * cheb[term]
    scaled = fermi * scale[None, :, None]
    density_part = jnp.sum(wide * scaled, axis=1)
    weighted = scaled.astype(bf16)
    w_even, w_crossed = exchange(weighted, weighted)
    image = images(flag, probes, weighted, hopping)
    filled = doubled_sum(jnp.sum(density_part, axis=0, keepdims=True), "clus")
    own, to_even, to_odd = forces(
        flag, ids, bond, probes, v_even, v_crossed, weighted, w_even, w_crossed, turned, image
    )
    from_even, from_odd = exchange(to_even, to_odd)
    gradient = own + from_even + from_odd
    atom_table = (atom_of[:, :, None] == jnp.arange(ATOMS, dtype=jnp.int32)[None, None, :]).astype(f32)
    atom_part = jnp.einsum(
        "rxb,rba->xra", gradient, atom_table, precision=lax.Precision.HIGHEST
    ).reshape(-1, block)
    packed = jnp.concatenate([density_part, atom_part, filled], axis=0)
    total = packed
    count = lax.axis_size("probe")
    for step in range(1, count):
        total = total + lax.ppermute(packed, "probe", [(i, (i + step) % count) for i in range(count)])
    density = total[:rows]
    atom_force = total[rows:-1].reshape(3, -1)
    filling = jnp.sum(total[-1]) / orbitals
    return (density, filling.reshape(1), atom_force)


def solution(mesh):
    placed = (
        P("clus", "probe", None),
        P("clus", None),
        P(None, "clus", None, None),
        P(None, "clus"),
        P("clus", None),
        P(None, None, "clus"),
        P(),
    )
    return jax.shard_map(
        local,
        mesh=mesh,
        in_specs=placed,
        out_specs=(P("clus", None), P(), P(None, "clus")),
        check_vma=False,
    )
```

time: 317 us -> 106 us (0.33); the launches traced: 312 us -> 105 us
  other arithmetic: 112 us -> 6.2 us
  matrix products: 58.2 us -> 0.26 us
  blocking collectives: 44.8 us -> 0 us
  local copies, waits for them, and re-layouts: 37.9 us -> 13.5 us
  Pallas kernels: 0 us -> 16.9 us
  waiting for transfers between devices: 2.18 us -> 8.61 us
    scatter-add x5 -> x0, other arithmetic: 96.2 us -> none  [the longest x4 86.9 us: spread_terms(): jax.ops.segment_sum(flat, target_ids.reshape(-1), num_segments=segments)]
    dot_general x11 -> x1, matrix products: 58.2 us -> 0.26 us  [local(): jnp.einsum('rxb,rba->xra', gradient, atom_table, precision=lax.Precision....]
    psum x3 -> x0, blocking collectives: 44.8 us -> none  [the longest x1 19.5 us: local(): density, atom_force = lax.psum((density_part, atom_part), 'probe')]
    pallas_call x0 -> x10, Pallas kernels: none -> 16.9 us  [the longest x4 6.73 us: call(): pl.pallas_call(functools.partial(kernel, turn), out_shape=out, in_specs=[...]
    transpose x5 -> x1, local copies, waits for them, and re-layouts: 11.4 us -> 0.01 us  [local(): jnp.einsum('rxb,rba->xra', gradient, atom_table, precision=lax.Precision....]
    select_n x6 -> x1, other arithmetic: 9.69 us -> 0.01 us  [local(): ids = jnp.where(live, block_col - me * rows + REACH, rows + 2 * REACH)]
    gather x5 -> x0, local copies, waits for them, and re-layouts: 9.66 us -> none  [gather_columns(): picked = jnp.take(source, safe_ids.reshape(-1), axis=0)]
    ppermute x20 -> x29, waiting for transfers between devices: 2.18 us -> 8.61 us  [the longest x3 4.48 us: local(): lax.ppermute(packed, 'probe', [(i, (i + step) % count) for i in range(cou...]
  transfers between devices with their start and end apart: 20 -> 29, of which waited for: 1 -> 6; matrix products, arithmetic and copies ran while one was open for 47% -> 3% of each run, Pallas kernels for 0% -> 16%
where the time goes in v1:
time: 106 us; the launch traced here: 105 us
  starting transfers between devices  55.4 us (52%)
  Pallas kernels  16.9 us (16%)
  local copies, waits for them, and re-layouts  13.5 us (13%)
  waiting for transfers between devices  8.61 us (8%)
  other arithmetic  6.2 us (6%)
  between operations  4.23 us (4%)
    ppermute x10, starting transfers between devices, exchange(): return (lax.ppermute(even_side, 'clus', paired), crossed)  27 us
    ppermute x6, starting transfers between devices, doubled_sum(): part = part + lax.ppermute(part, axis, pairs)  15.9 us
    unnamed x29, local copies, waits for them, and re-layouts  11.4 us
    ppermute x10, starting transfers between devices, exchange(): crossed = lax.ppermute(odd_side, 'clus', shifted)  7.76 us
    pallas_call x4, Pallas kernels, call(): pl.pallas_call(functools.partial(kernel, turn), out_shape=out, in_specs=[...  6.73 us
    pallas_call x4, Pallas kernels, direct(): pl.pallas_call(kernel, out_shape=jax.ShapeDtypeStruct((rows, probes, bloc...  5.98 us
    ppermute x3, starting transfers between devices, local(): lax.ppermute(packed, 'probe', [(i, (i + step) % count) for i in range(cou...  4.67 us
    ppermute x3, waiting for transfers between devices, local(): lax.ppermute(packed, 'probe', [(i, (i + step) % count) for i in range(cou...  4.48 us
  transfers between devices with their start and end apart: 29, of which 6 were waited for; matrix products, arithmetic and copies ran while one was open for 3% of the time, Pallas kernels for 16%

profile of v1, /device:TPU:0, one launch (start us, length us, event | category | flops | bytes accessed | tf_op | source)
XLA Modules:
  0.0 105.1 jit_solution(17883440411136570097)
XLA Ops:
  0.6 1.6 %collective-permute-start.1 = (bf16[12,32,128]{2,1,0:T(8,128)(2,1)}, bf16[12,32,128]{2,1,0:T(8,128)(2,1)S(1)}, u32[]{:S(2)}, u32[]{:S(2)}) collective-permute-start(bf16[12,32,128]{2,1,0:T(8,128)(2,1)} %refs_0_.1), channel_id=1, source_target_pairs={{0,0},{4,8},{8,4},{12,16},{16,12},{20,24},{24,20},{28,28},{1,1},{5... | collective-permute-start | bytes 294920 | tf_op jit(solution)/shard_map/ppermute | solution.py:52
  2.2 3.5 %collective-permute-start = (bf16[12,32,128]{2,1,0:T(8,128)(2,1)}, bf16[12,32,128]{2,1,0:T(8,128)(2,1)S(1)}, u32[]{:S(2)}, u32[]{:S(2)}) collective-permute-start(bf16[12,32,128]{2,1,0:T(8,128)(2,1)} %refs_0_.1), channel_id=1, source_target_pairs={{0,4},{4,0},{8,12},{12,8},{16,20},{20,16},{24,28},{28,24},{1,5},{5... | collective-permute-start | bytes 294920 | tf_op jit(solution)/shard_map/ppermute | solution.py:53
  5.7 1.4 %slice_reduce_fusion = s32[]{:T(128)} fusion(s32[20,12]{0,1:T(8,128)} %param.10), kind=kLoop, calls=%fused_computation.25 | loop fusion | flops 119 | bytes 484 | tf_op jit(solution)/shard_map/reduce_max | solution.py:259
  8.6 3.2 %copy-done = bf16[20,12,128,128]{3,2,1,0:T(8,128)(2,1)S(1)} copy-done((bf16[20,12,128,128]{3,2,1,0:T(8,128)(2,1)S(1)}, bf16[20,12,128,128]{3,2,1,0:T(8,128)(2,1)}, u32[]{:S(2)}) %copy-start) | copy-done | bytes 7864344
  12.8 2.0 %spread_turn.1 = (f32[12,32,128]{2,1,0:T(8,128)S(1)}, bf16[12,32,128]{2,1,0:T(8,128)(2,1)S(1)}, bf16[12,32,128]{2,1,0:T(8,128)(2,1)S(1)}, bf16[20,12,128,128]{3,2,1,0:T(8,128)(2,1)S(1)}) custom-call(s32[2]{0:T(128)S(1)} %pad_add_fusion.flag_ref, s32[20,12]{1,0:T(8,128)S(1)} %add_select_fusion.ids_ref, bf16[12,32,128]{2,1,0:T(8,128)(2,1)S(1)} %copy-done.5, ...), custom_call_target="tpu_custom_call" | custom-call | flops 251658240 | bytes 7864320 | tf_op jit(solution)/shard_map/spread_turn/pallas_call | solution.py:112
  16.4 1.5 %direct.4 = f32[12,32,128]{2,1,0:T(8,128)S(1)} custom-call(s32[2]{0:T(128)S(1)} %pad_add_fusion.flag_ref, s32[20,12]{1,0:T(8,128)S(1)} %add_select_fusion.ids_ref, bf16[12,32,128]{2,1,0:T(8,128)(2,1)S(1)} %copy-done.6, bf16[12,32,128]{2,1,0:T(8,128)(2,1)S(1)} %collective-permute-done.e_ref.refs_1_, ...), custom_call_target="tpu_custom_call" | custom-call | flops 251658240 | bytes 7864320 | tf_op jit(solution)/shard_map/direct/pallas_call | solution.py:151
  18.8 7.0 %collective-permute-start.4 = (bf16[12,32,128]{2,1,0:T(8,128)(2,1)S(1)}, bf16[12,32,128]{2,1,0:T(8,128)(2,1)S(1)}, u32[]{:S(2)}, u32[]{:S(2)}) collective-permute-start(bf16[12,32,128]{2,1,0:T(8,128)(2,1)S(1)} %fusion.14.x_ref), channel_id=1, source_target_pairs={{0,4},{4,0},{8,12},{12,8},{16,20},{20,16},{24,28},{28,24},{1,5},{5... | collective-permute-start | bytes 294920 | tf_op jit(solution)/shard_map/ppermute | solution.py:53
  25.8 1.5 %spread.3 = (f32[12,32,128]{2,1,0:T(8,128)S(1)}, bf16[12,32,128]{2,1,0:T(8,128)(2,1)S(1)}, bf16[12,32,128]{2,1,0:T(8,128)(2,1)S(1)}) custom-call(s32[2]{0:T(128)S(1)} %pad_add_fusion.flag_ref, s32[20,12]{1,0:T(8,128)S(1)} %add_select_fusion.ids_ref, bf16[12,32,128]{2,1,0:T(8,128)(2,1)S(1)} %fusion.14.x_ref, bf16[20,12,128,128]{3,2,1,0:T(8,128)(2,1)S(1)} %bitcast.15), custom_call_target="tpu_custom_call" | custom-call | flops 251658240 | bytes 7864320 | tf_op jit(solution)/shard_map/spread/pallas_call | solution.py:112
  28.3 1.5 %direct.5 = f32[12,32,128]{2,1,0:T(8,128)S(1)} custom-call(s32[2]{0:T(128)S(1)} %pad_add_fusion.flag_ref, s32[20,12]{1,0:T(8,128)S(1)} %add_select_fusion.ids_ref, bf16[12,32,128]{2,1,0:T(8,128)(2,1)S(1)} %fusion.14.x_ref, bf16[12,32,128]{2,1,0:T(8,128)(2,1)S(1)} %collective-permute-done.4.e_ref, bf16[12,32,128]{2,1,0:T(8,128)(2,1)S(1)} %collective-permute-done.5.o_ref, ...), custom_call_target="tpu_custom_call" | custom-call | flops 251658240 | bytes 7864320 | tf_op jit(solution)/shard_map/direct/pallas_call | solution.py:151
  29.9 4.6 %collective-permute-start.16 = (f32[32,128]{1,0:T(8,128)S(1)}, f32[32,128]{1,0:T(8,128)S(1)}, u32[]{:S(2)}, u32[]{:S(2)}) collective-permute-start(f32[32,128]{1,0:T(8,128)S(1)} %get-tuple-element.40), channel_id=1, source_target_pairs={{0,4},{4,0},{8,12},{12,8},{16,20},{20,16},{24,28},{28,24},{1,5},{5... | collective-permute-start | bytes 49160 | tf_op jit(solution)/shard_map/ppermute | solution.py:60
  35.3 3.0 %collective-permute-start.17 = (f32[32,128]{1,0:T(8,128)S(1)}, f32[32,128]{1,0:T(8,128)S(1)}, u32[]{:S(2)}, u32[]{:S(2)}) collective-permute-start(f32[32,128]{1,0:T(8,128)S(1)} %add.119), channel_id=1, source_target_pairs={{0,8},{4,12},{8,0},{12,4},{16,24},{20,28},{24,16},{28,20},{1,9},{5... | collective-permute-start | bytes 49160 | tf_op jit(solution)/shard_map/ppermute | solution.py:60
  39.7 1.4 %collective-permute-start.8 = (bf16[12,32,128]{2,1,0:T(8,128)(2,1)S(1)}, bf16[12,32,128]{2,1,0:T(8,128)(2,1)S(1)}, u32[]{:S(2)}, u32[]{:S(2)}) collective-permute-start(bf16[12,32,128]{2,1,0:T(8,128)(2,1)S(1)} %get-tuple-element.39.x_ref), channel_id=1, source_target_pairs={{0,4},{4,0},{8,12},{12,8},{16,20},{20,16},{24,28},{28,24},{1,5},{5... | collective-permute-start | bytes 294920 | tf_op jit(solution)/shard_map/ppermute | solution.py:53
  41.1 2.2 %collective-permute-start.18 = (f32[32,128]{1,0:T(8,128)S(1)}, f32[32,128]{1,0:T(8,128)S(1)}, u32[]{:S(2)}, u32[]{:S(2)}) collective-permute-start(f32[32,128]{1,0:T(8,128)S(1)} %add.120), channel_id=1, source_target_pairs={{0,16},{4,20},{8,24},{12,28},{16,0},{20,4},{24,8},{28,12},{1,17},{... | collective-permute-start | bytes 49160 | tf_op jit(solution)/shard_map/ppermute | solution.py:60
  43.3 3.2 %copy-done.1 = bf16[20,12,128,128]{3,2,1,0:T(8,128)(2,1)S(1)} copy-done((bf16[20,12,128,128]{3,2,1,0:T(8,128)(2,1)S(1)}, bf16[20,12,128,128]{3,2,1,0:T(8,128)(2,1)}, u32[]{:S(2)}) %copy-start.1) | copy-done | bytes 7864344
  46.6 1.7 %spread.4 = (f32[12,32,128]{2,1,0:T(8,128)S(1)}, bf16[12,32,128]{2,1,0:T(8,128)(2,1)S(1)}, bf16[12,32,128]{2,1,0:T(8,128)(2,1)S(1)}) custom-call(s32[2]{0:T(128)S(1)} %pad_add_fusion.flag_ref, s32[20,12]{1,0:T(8,128)S(1)} %add_select_fusion.ids_ref, bf16[12,32,128]{2,1,0:T(8,128)(2,1)S(1)} %get-tuple-element.39.x_ref, bf16[20,12,128,128]{3,2,1,0:T(8,128)(2,1)S(1)} %copy-done.1), custom_call_target="tpu_custom_call" | custom-call | flops 251658240 | bytes 7864320 | tf_op jit(solution)/shard_map/spread/pallas_call | solution.py:112
  49.2 3.2 %copy-done.3 = bf16[20,12,128,128]{3,2,1,0:T(8,128)(2,1)S(1)} copy-done((bf16[20,12,128,128]{3,2,1,0:T(8,128)(2,1)S(1)}, bf16[20,12,128,128]{3,2,1,0:T(8,128)(2,1)}, u32[]{:S(2)}) %copy-start.3) | copy-done | bytes 7864344
  52.4 1.5 %direct.6 = f32[12,32,128]{2,1,0:T(8,128)S(1)} custom-call(s32[2]{0:T(128)S(1)} %pad_add_fusion.flag_ref, s32[20,12]{1,0:T(8,128)S(1)} %add_select_fusion.ids_ref, bf16[12,32,128]{2,1,0:T(8,128)(2,1)S(1)} %get-tuple-element.39.x_ref, bf16[12,32,128]{2,1,0:T(8,128)(2,1)S(1)} %collective-permute-done.8.e_ref, ...), custom_call_target="tpu_custom_call" | custom-call | flops 251658240 | bytes 7864320 | tf_op jit(solution)/shard_map/direct/pallas_call | solution.py:151
  54.8 5.5 %collective-permute-start.12 = (bf16[12,32,128]{2,1,0:T(8,128)(2,1)S(1)}, bf16[12,32,128]{2,1,0:T(8,128)(2,1)S(1)}, u32[]{:S(2)}, u32[]{:S(2)}) collective-permute-start(bf16[12,32,128]{2,1,0:T(8,128)(2,1)S(1)} %fusion.9.x_ref), channel_id=1, source_target_pairs={{0,4},{4,0},{8,12},{12,8},{16,20},{20,16},{24,28},{28,24},{1,5},{5... | collective-permute-start | bytes 294920 | tf_op jit(solution)/shard_map/ppermute | solution.py:53
  60.3 1.5 %spread.5 = (f32[12,32,128]{2,1,0:T(8,128)S(1)}, bf16[12,32,128]{2,1,0:T(8,128)(2,1)S(1)}, bf16[12,32,128]{2,1,0:T(8,128)(2,1)S(1)}) custom-call(s32[2]{0:T(128)S(1)} %pad_add_fusion.flag_ref, s32[20,12]{1,0:T(8,128)S(1)} %add_select_fusion.ids_ref, bf16[12,32,128]{2,1,0:T(8,128)(2,1)S(1)} %fusion.9.x_ref, bf16[20,12,128,128]{3,2,1,0:T(8,128)(2,1)S(1)} %bitcast.17), custom_call_target="tpu_custom_call" | custom-call | flops 251658240 | bytes 7864320 | tf_op jit(solution)/shard_map/spread/pallas_call | solution.py:112
  62.7 1.5 %direct.7 = f32[12,32,128]{2,1,0:T(8,128)S(1)} custom-call(s32[2]{0:T(128)S(1)} %pad_add_fusion.flag_ref, s32[20,12]{1,0:T(8,128)S(1)} %add_select_fusion.ids_ref, bf16[12,32,128]{2,1,0:T(8,128)(2,1)S(1)} %fusion.9.x_ref, bf16[12,32,128]{2,1,0:T(8,128)(2,1)S(1)} %collective-permute-done.12.e_ref, bf16[12,32,128]{2,1,0:T(8,128)(2,1)S(1)} %collective-permute-done.13.o_ref, ...), custom_call_target="tpu_custom_call" | custom-call | flops 251658240 | bytes 7864320 | tf_op jit(solution)/shard_map/direct/pallas_call | solution.py:151
  64.2 3.5 %fusion.15 = (bf16[12,32,128]{2,1,0:T(8,128)(2,1)S(1)}, f32[12,32,128]{2,1,0:T(8,128)S(1)}) fusion(f32[32]{0:T(128)S(1)} %multiply_divide_fusion, f32[12,32,128]{2,1,0:T(8,128)S(1)} %direct.7, bf16[12,32,128]{2,1,0:T(8,128)(2,1)S(1)} %collective-permute-done.15, bf16[12,32,128]{2,1,0:T(8,128)(2,1)S(1)} %collective-permute-done.14, f32[]{:T(128)} %bitcast.7, ...), kind=kLoop, calls=%fused_computation.36 | loop fusion | flops 1671168 | bytes 1966228 | tf_op jit(solution)/shard_map/convert_element_type | solution.py:288
  68.3 6.2 %collective-permute-start.19 = (bf16[12,32,128]{2,1,0:T(8,128)(2,1)S(1)}, bf16[12,32,128]{2,1,0:T(8,128)(2,1)S(1)}, u32[]{:S(2)}, u32[]{:S(2)}) collective-permute-start(bf16[12,32,128]{2,1,0:T(8,128)(2,1)S(1)} %get-tuple-element.37.w_ref.refs_3_), channel_id=1, source_target_pairs={{0,4},{4,0},{8,12},{12,8},{16,20},{20,16},{24,28},{28,24},{1,5},{5... | collective-permute-start | bytes 294920 | tf_op jit(solution)/shard_map/ppermute | solution.py:53
  74.7 1.2 %images.1.refs_7_ = f32[20,12,64,128]{3,2,1,0:T(8,128)S(1)} custom-call(s32[2]{0:T(128)S(1)} %pad_add_fusion.flag_ref, bf16[12,32,128]{2,1,0:T(8,128)(2,1)S(1)} %copy-done.6, bf16[12,32,128]{2,1,0:T(8,128)(2,1)S(1)} %get-tuple-element.37.w_ref.refs_3_, bf16[20,12,128,128]{3,2,1,0:T(8,128)(2,1)S(1)} %bitcast.17), custom_call_target="tpu_custom_call" | custom-call | flops 503316480 | bytes 7864320 | tf_op jit(solution)/shard_map/images/pallas_call | solution.py:177
  75.9 3.0 %forces.1 = (f32[12,3,128]{2,1,0:T(4,128)S(1)}, f32[12,3,128]{2,1,0:T(4,128)S(1)}, f32[12,3,128]{2,1,0:T(4,128)S(1)}) custom-call(s32[2]{0:T(128)S(1)} %pad_add_fusion.flag_ref, s32[20,12]{1,0:T(8,128)S(1)} %add_select_fusion.ids_ref, f32[60,12]{1,0:T(8,128)S(1)} %reshape.46.bond_ref, bf16[12,32,128]{2,1,0:T(8,128)(2,1)S(1)} %copy-done.6, ...), custom_call_target="tpu_custom_call" | custom-call | flops 503316480 | bytes 15728640 | tf_op jit(solution)/shard_map/forces/pallas_call | solution.py:241
  78.9 3.0 %collective-permute-start.21 = (f32[12,3,128]{2,1,0:T(4,128)S(1)}, f32[12,3,128]{2,1,0:T(4,128)S(1)}, u32[]{:S(2)}, u32[]{:S(2)}) collective-permute-start(f32[12,3,128]{2,1,0:T(4,128)S(1)} %get-tuple-element.33), channel_id=1, source_target_pairs={{0,4},{4,0},{8,12},{12,8},{16,20},{20,16},{24,28},{28,24},{1,5},{5... | collective-permute-start | bytes 55304 | tf_op jit(solution)/shard_map/ppermute | solution.py:53
  82.6 3.1 %collective-permute-start.24 = (f32[1,128]{1,0:T(1,128)S(1)}, f32[1,128]{1,0:T(1,128)S(1)}, u32[]{:S(2)}, u32[]{:S(2)}) collective-permute-start(f32[1,128]{1,0:T(1,128)S(1)} %bitcast_add_fusion), channel_id=1, source_target_pairs={{0,8},{4,12},{8,0},{12,4},{16,24},{20,28},{24,16},{28,20},{1,9},{5... | collective-permute-start | bytes 1544 | tf_op jit(solution)/shard_map/ppermute | solution.py:60
  85.7 1.7 %collective-permute-done.24 = f32[1,128]{1,0:T(1,128)S(1)} collective-permute-done((f32[1,128]{1,0:T(1,128)S(1)}, f32[1,128]{1,0:T(1,128)S(1)}, u32[]{:S(2)}, u32[]{:S(2)}) %collective-permute-start.24) | collective-permute-done | bytes 544 | tf_op jit(solution)/shard_map/ppermute | solution.py:60
  87.4 3.0 %collective-permute-start.25 = (f32[1,128]{1,0:T(1,128)S(1)}, f32[1,128]{1,0:T(1,128)S(1)}, u32[]{:S(2)}, u32[]{:S(2)}) collective-permute-start(f32[1,128]{1,0:T(1,128)S(1)} %add.125), channel_id=1, source_target_pairs={{0,16},{4,20},{8,24},{12,28},{16,0},{20,4},{24,8},{28,12},{1,17},{... | collective-permute-start | bytes 1544 | tf_op jit(solution)/shard_map/ppermute | solution.py:60
  90.4 1.5 %collective-permute-done.25 = f32[1,128]{1,0:T(1,128)S(1)} collective-permute-done((f32[1,128]{1,0:T(1,128)S(1)}, f32[1,128]{1,0:T(1,128)S(1)}, u32[]{:S(2)}, u32[]{:S(2)}) %collective-permute-start.25) | collective-permute-done | bytes 544 | tf_op jit(solution)/shard_map/ppermute | solution.py:60
  92.3 3.7 %collective-permute-start.28 = (f32[22,128]{1,0:T(8,128)S(1)}, f32[22,128]{1,0:T(8,128)S(1)}, u32[]{:S(2)}, u32[]{:S(2)}) collective-permute-start(f32[22,128]{1,0:T(8,128)S(1)} %pad_maximum_fusion), channel_id=1, source_target_pairs={{0,3},{1,0},{2,1},{3,2},{4,7},{5,4},{6,5},{7,6},{8,11},{9,8},{10,9... | collective-permute-start | bytes 33800 | tf_op jit(solution)/shard_map/ppermute | solution.py:305
  96.0 1.0 collective-permute-start.26
  97.4 3.2 %collective-permute-done.27 = f32[22,128]{1,0:T(8,128)S(1)} collective-permute-done((f32[22,128]{1,0:T(8,128)S(1)}, f32[22,128]{1,0:T(8,128)S(1)}, u32[]{:S(2)}, u32[]{:S(2)}) %collective-permute-start.27) | collective-permute-done | bytes 11296 | tf_op jit(solution)/shard_map/ppermute | solution.py:305
  (97 shorter events, 14.2 us)
Async XLA Ops:
  0.6 15.7 %copy-start.7 = (f32[12,128]{1,0:T(8,128)S(1)}, f32[12,128]{1,0:T(8,128)}, u32[]{:S(2)}) copy-start(f32[12,128]{1,0:T(8,128)} %site_ref.7) | copy-start | bytes 18436
  0.6 15.7 %collective-permute-start.1 = (bf16[12,32,128]{2,1,0:T(8,128)(2,1)}, bf16[12,32,128]{2,1,0:T(8,128)(2,1)S(1)}, u32[]{:S(2)}, u32[]{:S(2)}) collective-permute-start(bf16[12,32,128]{2,1,0:T(8,128)(2,1)} %refs_0_.1), channel_id=1, source_target_pairs={{0,0},{4,8},{8,4},{12,16},{16,12},{20,24},{24,20},{28,28},{1,1},{5... | collective-permute-start | bytes 294920 | tf_op jit(solution)/shard_map/ppermute | solution.py:52
  2.2 14.1 %collective-permute-start = (bf16[12,32,128]{2,1,0:T(8,128)(2,1)}, bf16[12,32,128]{2,1,0:T(8,128)(2,1)S(1)}, u32[]{:S(2)}, u32[]{:S(2)}) collective-permute-start(bf16[12,32,128]{2,1,0:T(8,128)(2,1)} %refs_0_.1), channel_id=1, source_target_pairs={{0,4},{4,0},{8,12},{12,8},{16,20},{20,16},{24,28},{28,24},{1,5},{5... | collective-permute-start | bytes 294920 | tf_op jit(solution)/shard_map/ppermute | solution.py:53
  14.8 3.1 %collective-permute-start.2 = (bf16[12,32,128]{2,1,0:T(8,128)(2,1)S(1)}, bf16[12,32,128]{2,1,0:T(8,128)(2,1)S(1)}, u32[]{:S(2)}, u32[]{:S(2)}) collective-permute-start(bf16[12,32,128]{2,1,0:T(8,128)(2,1)S(1)} %get-tuple-element.21), channel_id=1, source_target_pairs={{0,4},{4,0},{8,12},{12,8},{16,20},{20,16},{24,28},{28,24},{1,5},{5... | collective-permute-start | bytes 294920 | tf_op jit(solution)/shard_map/ppermute | solution.py:53
  14.9 3.0 %collective-permute-start.3 = (bf16[12,32,128]{2,1,0:T(8,128)(2,1)S(1)}, bf16[12,32,128]{2,1,0:T(8,128)(2,1)S(1)}, u32[]{:S(2)}, u32[]{:S(2)}) collective-permute-start(bf16[12,32,128]{2,1,0:T(8,128)(2,1)S(1)} %get-tuple-element.22), channel_id=1, source_target_pairs={{0,0},{4,8},{8,4},{12,16},{16,12},{20,24},{24,20},{28,28},{1,1},{5... | collective-permute-start | bytes 294920 | tf_op jit(solution)/shard_map/ppermute | solution.py:52
  18.0 21.0 %copy-start.8 = (bf16[3,20,12]{1,2,0:T(8,128)(2,1)S(1)}, bf16[3,20,12]{1,2,0:T(8,128)(2,1)}, u32[]{:S(2)}) copy-start(bf16[3,20,12]{1,2,0:T(8,128)(2,1)} %param.12) | copy-start | bytes 4324
  18.0 10.3 %collective-permute-start.5 = (bf16[12,32,128]{2,1,0:T(8,128)(2,1)S(1)}, bf16[12,32,128]{2,1,0:T(8,128)(2,1)S(1)}, u32[]{:S(2)}, u32[]{:S(2)}) collective-permute-start(bf16[12,32,128]{2,1,0:T(8,128)(2,1)S(1)} %fusion.14.x_ref), channel_id=1, source_target_pairs={{0,0},{4,8},{8,4},{12,16},{16,12},{20,24},{24,20},{28,28},{1,1},{5... | collective-permute-start | bytes 294920 | tf_op jit(solution)/shard_map/ppermute | solution.py:52
  18.8 9.5 %collective-permute-start.4 = (bf16[12,32,128]{2,1,0:T(8,128)(2,1)S(1)}, bf16[12,32,128]{2,1,0:T(8,128)(2,1)S(1)}, u32[]{:S(2)}, u32[]{:S(2)}) collective-permute-start(bf16[12,32,128]{2,1,0:T(8,128)(2,1)S(1)} %fusion.14.x_ref), channel_id=1, source_target_pairs={{0,4},{4,0},{8,12},{12,8},{16,20},{20,16},{24,28},{28,24},{1,5},{5... | collective-permute-start | bytes 294920 | tf_op jit(solution)/shard_map/ppermute | solution.py:53
  27.3 2.5 %collective-permute-start.6 = (bf16[12,32,128]{2,1,0:T(8,128)(2,1)S(1)}, bf16[12,32,128]{2,1,0:T(8,128)(2,1)S(1)}, u32[]{:S(2)}, u32[]{:S(2)}) collective-permute-start(bf16[12,32,128]{2,1,0:T(8,128)(2,1)S(1)} %get-tuple-element.24), channel_id=1, source_target_pairs={{0,4},{4,0},{8,12},{12,8},{16,20},{20,16},{24,28},{28,24},{1,5},{5... | collective-permute-start | bytes 294920 | tf_op jit(solution)/shard_map/ppermute | solution.py:53
  27.4 2.4 %collective-permute-start.7 = (bf16[12,32,128]{2,1,0:T(8,128)(2,1)S(1)}, bf16[12,32,128]{2,1,0:T(8,128)(2,1)S(1)}, u32[]{:S(2)}, u32[]{:S(2)}) collective-permute-start(bf16[12,32,128]{2,1,0:T(8,128)(2,1)S(1)} %get-tuple-element.25), channel_id=1, source_target_pairs={{0,0},{4,8},{8,4},{12,16},{16,12},{20,24},{24,20},{28,28},{1,1},{5... | collective-permute-start | bytes 294920 | tf_op jit(solution)/shard_map/ppermute | solution.py:52
  29.9 5.4 %collective-permute-start.16 = (f32[32,128]{1,0:T(8,128)S(1)}, f32[32,128]{1,0:T(8,128)S(1)}, u32[]{:S(2)}, u32[]{:S(2)}) collective-permute-start(f32[32,128]{1,0:T(8,128)S(1)} %get-tuple-element.40), channel_id=1, source_target_pairs={{0,4},{4,0},{8,12},{12,8},{16,20},{20,16},{24,28},{28,24},{1,5},{5... | collective-permute-start | bytes 49160 | tf_op jit(solution)/shard_map/ppermute | solution.py:60
  35.3 5.9 %collective-permute-start.17 = (f32[32,128]{1,0:T(8,128)S(1)}, f32[32,128]{1,0:T(8,128)S(1)}, u32[]{:S(2)}, u32[]{:S(2)}) collective-permute-start(f32[32,128]{1,0:T(8,128)S(1)} %add.119), channel_id=1, source_target_pairs={{0,8},{4,12},{8,0},{12,4},{16,24},{20,28},{24,16},{28,20},{1,9},{5... | collective-permute-start | bytes 49160 | tf_op jit(solution)/shard_map/ppermute | solution.py:60
  39.0 10.1 %collective-permute-start.9 = (bf16[12,32,128]{2,1,0:T(8,128)(2,1)S(1)}, bf16[12,32,128]{2,1,0:T(8,128)(2,1)S(1)}, u32[]{:S(2)}, u32[]{:S(2)}) collective-permute-start(bf16[12,32,128]{2,1,0:T(8,128)(2,1)S(1)} %get-tuple-element.39.x_ref), channel_id=1, source_target_pairs={{0,0},{4,8},{8,4},{12,16},{16,12},{20,24},{24,20},{28,28},{1,1},{5... | collective-permute-start | bytes 294920 | tf_op jit(solution)/shard_map/ppermute | solution.py:52
  39.7 9.4 %collective-permute-start.8 = (bf16[12,32,128]{2,1,0:T(8,128)(2,1)S(1)}, bf16[12,32,128]{2,1,0:T(8,128)(2,1)S(1)}, u32[]{:S(2)}, u32[]{:S(2)}) collective-permute-start(bf16[12,32,128]{2,1,0:T(8,128)(2,1)S(1)} %get-tuple-element.39.x_ref), channel_id=1, source_target_pairs={{0,4},{4,0},{8,12},{12,8},{16,20},{20,16},{24,28},{28,24},{1,5},{5... | collective-permute-start | bytes 294920 | tf_op jit(solution)/shard_map/ppermute | solution.py:53
  41.1 7.9 %collective-permute-start.18 = (f32[32,128]{1,0:T(8,128)S(1)}, f32[32,128]{1,0:T(8,128)S(1)}, u32[]{:S(2)}, u32[]{:S(2)}) collective-permute-start(f32[32,128]{1,0:T(8,128)S(1)} %add.120), channel_id=1, source_target_pairs={{0,16},{4,20},{8,24},{12,28},{16,0},{20,4},{24,8},{28,12},{1,17},{... | collective-permute-start | bytes 49160 | tf_op jit(solution)/shard_map/ppermute | solution.py:60
  48.3 5.6 %collective-permute-start.10 = (bf16[12,32,128]{2,1,0:T(8,128)(2,1)S(1)}, bf16[12,32,128]{2,1,0:T(8,128)(2,1)S(1)}, u32[]{:S(2)}, u32[]{:S(2)}) collective-permute-start(bf16[12,32,128]{2,1,0:T(8,128)(2,1)S(1)} %get-tuple-element.27), channel_id=1, source_target_pairs={{0,4},{4,0},{8,12},{12,8},{16,20},{20,16},{24,28},{28,24},{1,5},{5... | collective-permute-start | bytes 294920 | tf_op jit(solution)/shard_map/ppermute | solution.py:53
  48.3 5.6 %collective-permute-start.11 = (bf16[12,32,128]{2,1,0:T(8,128)(2,1)S(1)}, bf16[12,32,128]{2,1,0:T(8,128)(2,1)S(1)}, u32[]{:S(2)}, u32[]{:S(2)}) collective-permute-start(bf16[12,32,128]{2,1,0:T(8,128)(2,1)S(1)} %get-tuple-element.28), channel_id=1, source_target_pairs={{0,0},{4,8},{8,4},{12,16},{16,12},{20,24},{24,20},{28,28},{1,1},{5... | collective-permute-start | bytes 294920 | tf_op jit(solution)/shard_map/ppermute | solution.py:52
  54.0 8.6 %collective-permute-start.13 = (bf16[12,32,128]{2,1,0:T(8,128)(2,1)S(1)}, bf16[12,32,128]{2,1,0:T(8,128)(2,1)S(1)}, u32[]{:S(2)}, u32[]{:S(2)}) collective-permute-start(bf16[12,32,128]{2,1,0:T(8,128)(2,1)S(1)} %fusion.9.x_ref), channel_id=1, source_target_pairs={{0,0},{4,8},{8,4},{12,16},{16,12},{20,24},{24,20},{28,28},{1,1},{5... | collective-permute-start | bytes 294920 | tf_op jit(solution)/shard_map/ppermute | solution.py:52
  54.8 7.8 %collective-permute-start.12 = (bf16[12,32,128]{2,1,0:T(8,128)(2,1)S(1)}, bf16[12,32,128]{2,1,0:T(8,128)(2,1)S(1)}, u32[]{:S(2)}, u32[]{:S(2)}) collective-permute-start(bf16[12,32,128]{2,1,0:T(8,128)(2,1)S(1)} %fusion.9.x_ref), channel_id=1, source_target_pairs={{0,4},{4,0},{8,12},{12,8},{16,20},{20,16},{24,28},{28,24},{1,5},{5... | collective-permute-start | bytes 294920 | tf_op jit(solution)/shard_map/ppermute | solution.py:53
  61.9 2.3 %collective-permute-start.14 = (bf16[12,32,128]{2,1,0:T(8,128)(2,1)S(1)}, bf16[12,32,128]{2,1,0:T(8,128)(2,1)S(1)}, u32[]{:S(2)}, u32[]{:S(2)}) collective-permute-start(bf16[12,32,128]{2,1,0:T(8,128)(2,1)S(1)} %get-tuple-element.30), channel_id=1, source_target_pairs={{0,4},{4,0},{8,12},{12,8},{16,20},{20,16},{24,28},{28,24},{1,5},{5... | collective-permute-start | bytes 294920 | tf_op jit(solution)/shard_map/ppermute | solution.py:53
  61.9 2.2 %collective-permute-start.15 = (bf16[12,32,128]{2,1,0:T(8,128)(2,1)S(1)}, bf16[12,32,128]{2,1,0:T(8,128)(2,1)S(1)}, u32[]{:S(2)}, u32[]{:S(2)}) collective-permute-start(bf16[12,32,128]{2,1,0:T(8,128)(2,1)S(1)} %get-tuple-element.31), channel_id=1, source_target_pairs={{0,0},{4,8},{8,4},{12,16},{16,12},{20,24},{24,20},{28,28},{1,1},{5... | collective-permute-start | bytes 294920 | tf_op jit(solution)/shard_map/ppermute | solution.py:52
  67.7 8.3 %collective-permute-start.20 = (bf16[12,32,128]{2,1,0:T(8,128)(2,1)S(1)}, bf16[12,32,128]{2,1,0:T(8,128)(2,1)S(1)}, u32[]{:S(2)}, u32[]{:S(2)}) collective-permute-start(bf16[12,32,128]{2,1,0:T(8,128)(2,1)S(1)} %get-tuple-element.37.w_ref.refs_3_), channel_id=1, source_target_pairs={{0,0},{4,8},{8,4},{12,16},{16,12},{20,24},{24,20},{28,28},{1,1},{5... | collective-permute-start | bytes 294920 | tf_op jit(solution)/shard_map/ppermute | solution.py:52
  68.3 7.6 %collective-permute-start.19 = (bf16[12,32,128]{2,1,0:T(8,128)(2,1)S(1)}, bf16[12,32,128]{2,1,0:T(8,128)(2,1)S(1)}, u32[]{:S(2)}, u32[]{:S(2)}) collective-permute-start(bf16[12,32,128]{2,1,0:T(8,128)(2,1)S(1)} %get-tuple-element.37.w_ref.refs_3_), channel_id=1, source_target_pairs={{0,4},{4,0},{8,12},{12,8},{16,20},{20,16},{24,28},{28,24},{1,5},{5... | collective-permute-start | bytes 294920 | tf_op jit(solution)/shard_map/ppermute | solution.py:53
  74.6 8.0 %collective-permute-start.23 = (f32[1,128]{1,0:T(1,128)S(1)}, f32[1,128]{1,0:T(1,128)S(1)}, u32[]{:S(2)}, u32[]{:S(2)}) collective-permute-start(f32[1,128]{1,0:T(1,128)S(1)} %bitcast.18), channel_id=1, source_target_pairs={{0,4},{4,0},{8,12},{12,8},{16,20},{20,16},{24,28},{28,24},{1,5},{5... | collective-permute-start | bytes 1544 | tf_op jit(solution)/shard_map/ppermute | solution.py:60
  75.9 16.1 %copy-start.9 = (s32[12,128]{1,0:T(8,128)S(1)}, s32[12,128]{1,0:T(8,128)}, u32[]{:S(2)}) copy-start(s32[12,128]{1,0:T(8,128)} %param.11) | copy-start | bytes 18436
  78.9 13.0 %collective-permute-start.21 = (f32[12,3,128]{2,1,0:T(4,128)S(1)}, f32[12,3,128]{2,1,0:T(4,128)S(1)}, u32[]{:S(2)}, u32[]{:S(2)}) collective-permute-start(f32[12,3,128]{2,1,0:T(4,128)S(1)} %get-tuple-element.33), channel_id=1, source_target_pairs={{0,4},{4,0},{8,12},{12,8},{16,20},{20,16},{24,28},{28,24},{1,5},{5... | collective-permute-start | bytes 55304 | tf_op jit(solution)/shard_map/ppermute | solution.py:53
  81.9 10.0 %collective-permute-start.22 = (f32[12,3,128]{2,1,0:T(4,128)S(1)}, f32[12,3,128]{2,1,0:T(4,128)S(1)}, u32[]{:S(2)}, u32[]{:S(2)}) collective-permute-start(f32[12,3,128]{2,1,0:T(4,128)S(1)} %get-tuple-element.34), channel_id=1, source_target_pairs={{0,0},{4,8},{8,4},{12,16},{16,12},{20,24},{24,20},{28,28},{1,1},{5... | collective-permute-start | bytes 55304 | tf_op jit(solution)/shard_map/ppermute | solution.py:52
  82.6 4.8 %collective-permute-start.24 = (f32[1,128]{1,0:T(1,128)S(1)}, f32[1,128]{1,0:T(1,128)S(1)}, u32[]{:S(2)}, u32[]{:S(2)}) collective-permute-start(f32[1,128]{1,0:T(1,128)S(1)} %bitcast_add_fusion), channel_id=1, source_target_pairs={{0,8},{4,12},{8,0},{12,4},{16,24},{20,28},{24,16},{28,20},{1,9},{5... | collective-permute-start | bytes 1544 | tf_op jit(solution)/shard_map/ppermute | solution.py:60
  87.4 4.5 %collective-permute-start.25 = (f32[1,128]{1,0:T(1,128)S(1)}, f32[1,128]{1,0:T(1,128)S(1)}, u32[]{:S(2)}, u32[]{:S(2)}) collective-permute-start(f32[1,128]{1,0:T(1,128)S(1)} %add.125), channel_id=1, source_target_pairs={{0,16},{4,20},{8,24},{12,28},{16,0},{20,4},{24,8},{28,12},{1,17},{... | collective-permute-start | bytes 1544 | tf_op jit(solution)/shard_map/ppermute | solution.py:60
  92.3 5.1 %collective-permute-start.28 = (f32[22,128]{1,0:T(8,128)S(1)}, f32[22,128]{1,0:T(8,128)S(1)}, u32[]{:S(2)}, u32[]{:S(2)}) collective-permute-start(f32[22,128]{1,0:T(8,128)S(1)} %pad_maximum_fusion), channel_id=1, source_target_pairs={{0,3},{1,0},{2,1},{3,2},{4,7},{5,4},{6,5},{7,6},{8,11},{9,8},{10,9... | collective-permute-start | bytes 33800 | tf_op jit(solution)/shard_map/ppermute | solution.py:305
  96.0 4.6 %collective-permute-start.27 = (f32[22,128]{1,0:T(8,128)S(1)}, f32[22,128]{1,0:T(8,128)S(1)}, u32[]{:S(2)}, u32[]{:S(2)}) collective-permute-start(f32[22,128]{1,0:T(8,128)S(1)} %pad_maximum_fusion), channel_id=1, source_target_pairs={{0,2},{1,3},{2,0},{3,1},{4,6},{5,7},{6,4},{7,5},{8,10},{9,11},{10,... | collective-permute-start | bytes 33800 | tf_op jit(solution)/shard_map/ppermute | solution.py:305
  96.0 5.5 %collective-permute-start.26 = (f32[22,128]{1,0:T(8,128)S(1)}, f32[22,128]{1,0:T(8,128)S(1)}, u32[]{:S(2)}, u32[]{:S(2)}) collective-permute-start(f32[22,128]{1,0:T(8,128)S(1)} %pad_maximum_fusion), channel_id=1, source_target_pairs={{0,1},{1,2},{2,3},{3,0},{4,5},{5,6},{6,7},{7,4},{8,9},{9,10},{10,1... | collective-permute-start | bytes 33800 | tf_op jit(solution)/shard_map/ppermute | solution.py:305
  (11 other events, 82.1 us)

commit v2 on v1

--- a/solution.py
+++ b/solution.py
@@ -2,6 +2,7 @@
 
 import jax
 import jax.numpy as jnp
+import numpy as np
 from jax import lax
 from jax.experimental import pallas as pl
 from jax.experimental.pallas import tpu as pltpu
@@ -32,16 +33,172 @@
     )
 
 
-def expansion(chemical_potential, degree):
-    node_index = jnp.arange(QUAD_NODES, dtype=f32)
-    bond_angles = jnp.pi * (node_index + 0.5) / QUAD_NODES
-    fermi_occupation = 1.0 / (
-        1.0 + jnp.exp((jnp.cos(bond_angles) - chemical_potential) / SMEARING_TEMP)
-    )
-    orders = jnp.arange(degree + 1, dtype=f32)
-    cosines = jnp.cos(orders[:, None] * bond_angles[None, :])
-    coeffs = 2.0 / QUAD_NODES * jnp.sum(cosines * fermi_occupation[None, :], axis=1)
-    return coeffs * jnp.where(orders == 0.0, 0.5, 1.0)
+def quadrature():
+    angles = np.pi * (np.arange(QUAD_NODES) + 0.5) / QUAD_NODES
+    table = np.zeros((8, 128), np.float32)
+    for order in range(ORDER + 1):
+        weight = 2.0 / QUAD_NODES * (0.5 if order == 0 else 1.0)
+        table[order, :QUAD_NODES] = weight * np.cos(order * angles)
+    table[7, :QUAD_NODES] = np.cos(angles)
+    return jnp.asarray(table)
+
+
+def prepared(columns, bond_dir, chemical_potential):
+    rows, slots = columns.shape
+
+    def kernel(col_ref, bond_ref, mu_ref, table_ref, flag_ref, ids_ref, out_ref, coeff_ref):
+        me = lax.axis_index("clus")
+        col = col_ref[...]
+        ids_ref[...] = jnp.where(col >= 0, col - me * rows + REACH, rows + 2 * REACH)
+        late = lax.broadcasted_iota(jnp.int32, col.shape, 1) >= HALF_SLOTS
+        flag_ref[0] = (jnp.max(jnp.where(late, col, -1)) >= 0).astype(jnp.int32)
+        flag_ref[1] = lax.rem(me, 2)
+        for axis in range(3):
+            out_ref[axis * rows : (axis + 1) * rows] = bond_ref[axis].astype(f32)
+        energy = (table_ref[7:8] - mu_ref[0]) / SMEARING_TEMP
+        occupied = 1.0 / (1.0 + jnp.exp(energy))
+        total = jnp.sum(table_ref[...] * occupied, axis=1, keepdims=True)
+        coeff_ref[...] = jnp.broadcast_to(total, coeff_ref.shape)
+
+    return pl.pallas_call(
+        kernel,
+        out_shape=[
+            jax.ShapeDtypeStruct((2,), jnp.int32),
+            jax.ShapeDtypeStruct((rows, slots), jnp.int32),
+            jax.ShapeDtypeStruct((3 * rows, slots), f32),
+            jax.ShapeDtypeStruct((8, 128), f32),
+        ],
+        in_specs=[VM, VM, SM, VM],
+        out_specs=[SM, VM, VM, VM],
+        name="prepared",
+        **params(1000, 50000),
+    )(columns, bond_dir, chemical_potential, quadrature())
+
+
+def moments(coeffs, v, first, second):
+    _, probes, block = v.shape
+
+    def kernel(coeff_ref, v_ref, a_ref, b_ref, out_ref):
+        wide = v_ref[...].astype(f32)
+        a, b = a_ref[...], b_ref[...]
+        pairs = (wide * wide, wide * a, wide * b, a * b, b * b)
+        m0, m1, m2, ab, bb = [jnp.sum(pair, axis=0) for pair in pairs]
+        c = [coeff_ref[k : k + 1] for k in range(ORDER + 1)]
+        out_ref[0] = m0
+        out_ref[1] = (
+            c[0] * m0 + c[1] * m1 + c[2] * m2 + c[3] * (2.0 * ab - m1) + c[4] * (2.0 * bb - m0)
+        )
+
+    return pl.pallas_call(
+        kernel,
+        out_shape=jax.ShapeDtypeStruct((2, probes, block), f32),
+        in_specs=[VM] * 4,
+        out_specs=VM,
+        name="moments",
+        **params(10 * v.size, 10 * v.size),
+    )(coeffs, v, first, second)
+
+
+def closed(coeffs, sums, orbitals, cheb, image, back_even, back_crossed):
+    rows, probes, block = image.shape
+
+    def kernel(coeff_ref, sum_ref, c0, c1, c2, c3, y_ref, e_ref, o_ref, w_ref, head_ref):
+        square = jnp.sum(sum_ref[0], axis=1, keepdims=True)
+        scale = orbitals / (square * PROBE_VECTORS)
+        head_ref[...] = jnp.zeros_like(head_ref)
+        head_ref[rows : rows + 1] = jnp.sum(scale * sum_ref[1], axis=0, keepdims=True)
+        scale = jnp.broadcast_to(scale, (probes, block))
+        c = [coeff_ref[k : k + 1] for k in range(ORDER + 1)]
+        for r in range(rows):
+            y = y_ref[r] + (e_ref[r].astype(f32) + o_ref[r].astype(f32))
+            wide = c0[r].astype(f32)
+            fermi = c[0] * wide + c[1] * c1[r]
+            fermi = fermi + c[2] * c2[r]
+            fermi = fermi + c[3] * c3[r]
+            fermi = fermi + c[4] * (2.0 * y - c2[r])
+            scaled = fermi * scale
+            w_ref[r] = scaled.astype(bf16)
+            head_ref[r : r + 1] = jnp.sum(wide * scaled, axis=0, keepdims=True)
+
+    return pl.pallas_call(
+        kernel,
+        out_shape=[
+            jax.ShapeDtypeStruct((rows, probes, block), bf16),
+            jax.ShapeDtypeStruct((16, block), f32),
+        ],
+        in_specs=[VM] * 9,
+        out_specs=[VM] * 2,
+        name="closed",
+        **params(20 * image.size, 30 * image.size),
+    )(coeffs, sums, *cheb, image, back_even, back_crossed)
+
+
+def packed(head, own, from_even, from_odd, atom_of):
+    rows, _, block = own.shape
+    group = block // ATOMS
+    lines = rows // group
+
+    def kernel(head_ref, own_ref, e_ref, o_ref, atom_ref, out_ref):
+        out_ref[...] = jnp.zeros_like(out_ref)
+        out_ref[: rows + 1] = head_ref[: rows + 1]
+        lane = lax.broadcasted_iota(jnp.int32, (block, block), 0)
+        for line in range(lines):
+            total = jnp.zeros((16, block), f32)
+            for part in range(group):
+                r = line * group + part
+                g = own_ref[r] + e_ref[r] + o_ref[r]
+                high = g.astype(bf16)
+                rest = g - high.astype(f32)
+                middle = rest.astype(bf16)
+                low = (rest - middle.astype(f32)).astype(bf16)
+                pad = jnp.zeros((16 - 9, block), bf16)
+                left = jnp.concatenate([high, middle, low, pad], axis=0)
+                hot = (lane == atom_ref[r : r + 1] + part * ATOMS).astype(f32).astype(bf16)
+                total = total + dot(left, hot, NT)
+            value = total[0:3] + (total[3:6] + total[6:9])
+            for axis in range(3):
+                at = rows + 1 + axis * lines + line
+                out_ref[at : at + 1] = value[axis : axis + 1]
+
+    height = -(-(rows + 1 + 3 * lines) // 8) * 8
+    return pl.pallas_call(
+        kernel,
+        out_shape=jax.ShapeDtypeStruct((height, block), f32),
+        in_specs=[VM] * 5,
+        out_specs=VM,
+        name="packed",
+        **params(2 * rows * 16 * block * block, 100000),
+    )(head, own, from_even, from_odd, atom_of)
+
+
+def unpacked(parts, rows, orbitals):
+    height, block = parts[0].shape
+    lines = rows * ATOMS // block
+
+    def kernel(*refs):
+        ins, (density_ref, filling_ref, force_ref) = refs[: len(parts)], refs[len(parts) :]
+        total = ins[0][...]
+        for other in ins[1:]:
+            total = total + other[...]
+        density_ref[...] = total[:rows]
+        filling_ref[0] = jnp.sum(total[rows : rows + 1]) / orbitals
+        for axis in range(3):
+            for line in range(lines):
+                at = rows + 1 + axis * lines + line
+                force_ref[axis : axis + 1, line * block : (line + 1) * block] = total[at : at + 1]
+
+    return pl.pallas_call(
+        kernel,
+        out_shape=[
+            jax.ShapeDtypeStruct((rows, block), f32),
+            jax.ShapeDtypeStruct((1,), f32),
+            jax.ShapeDtypeStruct((3, lines * block), f32),
+        ],
+        in_specs=[VM] * len(parts),
+        out_specs=[VM, SM, VM],
+        name="unpacked",
+        **params(10000, 100000),
+    )(*parts)
 
 
 def exchange(even_side, odd_side):
@@ -90,7 +247,7 @@
                         pair = [k_ref[m, c], k_ref[m + 1, c]]
                         out = dot(xc, jnp.concatenate(pair, axis=1), NN)
                         parts += [out[:, :block], out[:, block:]]
-                        targets += [ids_ref[m, c], ids_ref[m + 1, c]]
+                        targets += [ids_ref[c, m], ids_ref[c, m + 1]]
                         if turn:
                             rest[0][m, c] = pair[0].T
                             rest[0][m + 1, c] = pair[1].T
@@ -141,7 +298,7 @@
             for c in range(rows):
                 acc = own_ref[c] + site_ref[pl.ds(c, 1)] * x_ref[c].astype(f32)
                 for m in range(0, count, 2):
-                    pair = [frame[ids_ref[m, c]], frame[ids_ref[m + 1, c]]]
+                    pair = [frame[ids_ref[c, m]], frame[ids_ref[c, m + 1]]]
                     weights = jnp.concatenate([kt_ref[m, c], kt_ref[m + 1, c]], axis=0)
                     acc = acc + dot(jnp.concatenate(pair, axis=1), weights, NN)
                 out_ref[c] = acc
@@ -211,17 +368,17 @@
                 for m in range(0, count, 2):
                     far = []
                     for slot in (m, m + 1):
-                        d = ids_ref[slot, c]
+                        d = ids_ref[c, slot]
                         far.append(jnp.concatenate([vf[d], wf[d]], axis=0))
                     weights = jnp.concatenate([kt_ref[m, c], kt_ref[m + 1, c]], axis=1)
                     out = dot(jnp.concatenate(far, axis=0), weights, NN)
                     direct_parts = [out[: 2 * probes, :block], out[2 * probes :, block:]]
                     for slot, other, part in zip((m, m + 1), far, direct_parts):
-                        d = ids_ref[slot, c]
+                        d = ids_ref[c, slot]
                         row_part = folded(mine * part)
                         col_part = folded(other.astype(f32) * image_ref[slot, c])
                         for axis in range(3):
-                            b = bond_ref[axis * slots + slot, c]
+                            b = bond_ref[axis * rows + c, slot]
                             row[axis] = row[axis] + b * row_part
                             acc[d, axis] = acc[d, axis] + b * col_part
                 for axis in range(3):
@@ -251,62 +408,44 @@
 
 def local(probes, onsite, hopping, block_col, atom_of, bond_dir, chemical_potential):
     rows, _, block = probes.shape
-    slots = hopping.shape[0]
-    me = lax.axis_index("clus")
-    orbitals = rows * lax.axis_size("clus") * block
-    live = block_col >= 0
-    ids = jnp.where(live, block_col - me * rows + REACH, rows + 2 * REACH)
-    many = jnp.max(block_col[HALF_SLOTS:]) >= 0
-    flag = jnp.stack([many.astype(jnp.int32), (me % 2).astype(jnp.int32)])
-    bond = bond_dir.astype(f32).reshape(3 * slots, rows)
-
+    orbitals = float(rows * lax.axis_size("clus") * block)
+    flag, ids, bond, coeffs = prepared(
+        block_col.T, jnp.transpose(bond_dir, (0, 2, 1)), chemical_potential
+    )
     x = probes
     even, crossed = exchange(x, x)
     v_even, v_crossed = even, crossed
-    wide = probes.astype(f32)
-    square = doubled_sum(jnp.sum(wide * wide, axis=0), "clus")
-    scale = orbitals / (jnp.sum(square, axis=1) * PROBE_VECTORS)
-    coeffs = expansion(chemical_potential[0], ORDER)
-
-    cheb = [wide]
+    cheb = [probes]
     for term in range(1, ORDER + 1):
         outs = spread(flag, ids, x, hopping)(term == 1)
         if term == 1:
             turned = outs[3]
         back_even, back_crossed = exchange(outs[1], outs[2])
         image = direct(flag, ids, x, even, crossed, turned, outs[0], onsite)
+        if term == ORDER:
+            break
         image = image + (back_even.astype(f32) + back_crossed.astype(f32))
-        cheb.append(image if term == 1 else 2.0 * image - cheb[-2])
+        cheb.append(image if term == 1 else 2.0 * image - cheb[-2].astype(f32))
         x = cheb[-1].astype(bf16)
-        if term < ORDER:
-            even, crossed = exchange(x, x)
-    fermi = coeffs[0] * cheb[0]
-    for term in range(1, ORDER + 1):
-        fermi = fermi + coeffs[term] * cheb[term]
-    scaled = fermi * scale[None, :, None]
-    density_part = jnp.sum(wide * scaled, axis=1)
-    weighted = scaled.astype(bf16)
+        even, crossed = exchange(x, x)
+        if term == 2:
+            sums = doubled_sum(moments(coeffs, *cheb), "clus")
+    weighted, head = closed(coeffs, sums, orbitals, cheb, image, back_even, back_crossed)
     w_even, w_crossed = exchange(weighted, weighted)
     image = images(flag, probes, weighted, hopping)
-    filled = doubled_sum(jnp.sum(density_part, axis=0, keepdims=True), "clus")
     own, to_even, to_odd = forces(
         flag, ids, bond, probes, v_even, v_crossed, weighted, w_even, w_crossed, turned, image
     )
     from_even, from_odd = exchange(to_even, to_odd)
-    gradient = own + from_even + from_odd
-    atom_table = (atom_of[:, :, None] == jnp.arange(ATOMS, dtype=jnp.int32)[None, None, :]).astype(f32)
-    atom_part = jnp.einsum(
-        "rxb,rba->xra", gradient, atom_table, precision=lax.Precision.HIGHEST
-    ).reshape(-1, block)
-    packed = jnp.concatenate([density_part, atom_part, filled], axis=0)
-    total = packed
+    part = packed(head, own, from_even, from_odd, atom_of)
     count = lax.axis_size("probe")
-    for step in range(1, count):
-        total = total + lax.ppermute(packed, "probe", [(i, (i + step) % count) for i in range(count)])
-    density = total[:rows]
-    atom_force = total[rows:-1].reshape(3, -1)
-    filling = jnp.sum(total[-1]) / orbitals
-    return (density, filling.reshape(1), atom_force)
+    parts = [part]
+    step = 1
+    while step < count:
+        part = sum(parts[1:], parts[0])
+        parts = [part, lax.ppermute(part, "probe", [(i, i ^ step) for i in range(count)])]
+        step *= 2
+    return tuple(unpacked(parts, rows, orbitals))
 
 
 def solution(mesh):

time: 106 us -> 90.9 us (0.86)
  the two profiles are of different devices: /device:TPU:0 before, /device:TPU:28 now
where the time goes in v2:
time: 90.9 us; the launch traced here: 89.5 us
  starting transfers between devices  35.4 us (39%)
  waiting for transfers between devices  27.8 us (31%)
  Pallas kernels  17.9 us (20%)
  local copies, waits for them, and re-layouts  6.23 us (7%)
  between operations  1.88 us (2%)
    ppermute x10, starting transfers between devices, exchange(): crossed = lax.ppermute(odd_side, 'clus', shifted)  29.6 us
    ppermute x10, waiting for transfers between devices, exchange(): crossed = lax.ppermute(odd_side, 'clus', shifted)  12.7 us
    ppermute x3, waiting for transfers between devices, doubled_sum(): part = part + lax.ppermute(part, axis, pairs)  7.54 us
    ppermute x2, waiting for transfers between devices, local(): lax.ppermute(part, 'probe', [(i, i ^ step) for i in range(count)])  7.52 us
    pallas_call x4, Pallas kernels, call(): pl.pallas_call(functools.partial(kernel, turn), out_shape=out, in_specs=[...  6.48 us
    unnamed x20, local copies, waits for them, and re-layouts  6.23 us
    pallas_call x4, Pallas kernels, direct(): pl.pallas_call(kernel, out_shape=jax.ShapeDtypeStruct((rows, probes, bloc...  5.74 us
    ppermute x10, starting transfers between devices, exchange(): return (lax.ppermute(even_side, 'clus', paired), crossed)  4.56 us
  transfers between devices with their start and end apart: 25, of which 9 were waited for; matrix products, arithmetic and copies ran while one was open for 0% of the time, Pallas kernels for 16%

profile of v2, /device:TPU:28, one launch (start us, length us, event | category | flops | bytes accessed | tf_op | source)
XLA Modules:
  0.0 89.5 jit_solution(472984834923133983)
XLA Ops:
  0.6 2.8 %collective-permute-start.1 = (bf16[12,32,128]{2,1,0:T(8,128)(2,1)}, bf16[12,32,128]{2,1,0:T(8,128)(2,1)S(1)}, u32[]{:S(2)}, u32[]{:S(2)}) collective-permute-start(bf16[12,32,128]{2,1,0:T(8,128)(2,1)} %refs_0_.1), channel_id=1, source_target_pairs={{0,0},{4,8},{8,4},{12,16},{16,12},{20,24},{24,20},{28,28},{1,1},{5... | collective-permute-start | bytes 294920 | tf_op jit(solution)/shard_map/ppermute | solution.py:209
  7.8 3.2 %copy-done = bf16[20,12,128,128]{3,2,1,0:T(8,128)(2,1)S(1)} copy-done((bf16[20,12,128,128]{3,2,1,0:T(8,128)(2,1)S(1)}, bf16[20,12,128,128]{3,2,1,0:T(8,128)(2,1)}, u32[]{:S(2)}) %copy-start) | copy-done | bytes 7864344
  11.0 0.9 copy-done.1
  11.9 2.0 %spread_turn.1 = (f32[12,32,128]{2,1,0:T(8,128)S(1)}, bf16[12,32,128]{2,1,0:T(8,128)(2,1)S(1)}, bf16[12,32,128]{2,1,0:T(8,128)(2,1)S(1)}, bf16[20,12,128,128]{3,2,1,0:T(8,128)(2,1)S(1)}) custom-call(s32[2]{0:T(128)S(1)} %get-tuple-element.26.flag_ref, s32[12,20]{1,0:T(8,128)S(1)} %get-tuple-element.27.ids_ref, bf16[12,32,128]{2,1,0:T(8,128)(2,1)S(1)} %copy-done.1, ...), custom_call_target="tpu_custom_call" | custom-call | flops 251658240 | bytes 7864320 | tf_op jit(solution)/shard_map/spread_turn/pallas_call | solution.py:269
  14.0 3.4 %collective-permute-start.3 = (bf16[12,32,128]{2,1,0:T(8,128)(2,1)S(1)}, bf16[12,32,128]{2,1,0:T(8,128)(2,1)S(1)}, u32[]{:S(2)}, u32[]{:S(2)}) collective-permute-start(bf16[12,32,128]{2,1,0:T(8,128)(2,1)S(1)} %get-tuple-element.31), channel_id=1, source_target_pairs={{0,0},{4,8},{8,4},{12,16},{16,12},{20,24},{24,20},{28,28},{1,1},{5... | collective-permute-start | bytes 294920 | tf_op jit(solution)/shard_map/ppermute | solution.py:209
  17.5 1.4 %direct.4 = f32[12,32,128]{2,1,0:T(8,128)S(1)} custom-call(s32[2]{0:T(128)S(1)} %get-tuple-element.26.flag_ref, s32[12,20]{1,0:T(8,128)S(1)} %get-tuple-element.27.ids_ref, bf16[12,32,128]{2,1,0:T(8,128)(2,1)S(1)} %copy-done.1, bf16[12,32,128]{2,1,0:T(8,128)(2,1)S(1)} %collective-permute-done.e_ref.refs_1_, ...), custom_call_target="tpu_custom_call" | custom-call | flops 251658240 | bytes 7864320 | tf_op jit(solution)/shard_map/direct/pallas_call | solution.py:308
  18.9 2.7 %collective-permute-done.3 = bf16[12,32,128]{2,1,0:T(8,128)(2,1)S(1)} collective-permute-done((bf16[12,32,128]{2,1,0:T(8,128)(2,1)S(1)}, bf16[12,32,128]{2,1,0:T(8,128)(2,1)S(1)}, u32[]{:S(2)}, u32[]{:S(2)}) %collective-permute-start.3) | collective-permute-done | bytes 98336 | tf_op jit(solution)/shard_map/ppermute | solution.py:209
  21.7 3.0 %collective-permute-start.5 = (bf16[12,32,128]{2,1,0:T(8,128)(2,1)S(1)}, bf16[12,32,128]{2,1,0:T(8,128)(2,1)S(1)}, u32[]{:S(2)}, u32[]{:S(2)}) collective-permute-start(bf16[12,32,128]{2,1,0:T(8,128)(2,1)S(1)} %get-tuple-element.51.x_ref), channel_id=1, source_target_pairs={{0,0},{4,8},{8,4},{12,16},{16,12},{20,24},{24,20},{28,28},{1,1},{5... | collective-permute-start | bytes 294920 | tf_op jit(solution)/shard_map/ppermute | solution.py:209
  24.8 1.4 %spread.3 = (f32[12,32,128]{2,1,0:T(8,128)S(1)}, bf16[12,32,128]{2,1,0:T(8,128)(2,1)S(1)}, bf16[12,32,128]{2,1,0:T(8,128)(2,1)S(1)}) custom-call(s32[2]{0:T(128)S(1)} %get-tuple-element.26.flag_ref, s32[12,20]{1,0:T(8,128)S(1)} %get-tuple-element.27.ids_ref, bf16[12,32,128]{2,1,0:T(8,128)(2,1)S(1)} %get-tuple-element.51.x_ref, ...), custom_call_target="tpu_custom_call" | custom-call | flops 251658240 | bytes 7864320 | tf_op jit(solution)/shard_map/spread/pallas_call | solution.py:269
  26.8 3.6 %collective-permute-start.7 = (bf16[12,32,128]{2,1,0:T(8,128)(2,1)S(1)}, bf16[12,32,128]{2,1,0:T(8,128)(2,1)S(1)}, u32[]{:S(2)}, u32[]{:S(2)}) collective-permute-start(bf16[12,32,128]{2,1,0:T(8,128)(2,1)S(1)} %get-tuple-element.34), channel_id=1, source_target_pairs={{0,0},{4,8},{8,4},{12,16},{16,12},{20,24},{24,20},{28,28},{1,1},{5... | collective-permute-start | bytes 294920 | tf_op jit(solution)/shard_map/ppermute | solution.py:209
  30.4 1.4 %direct.5 = f32[12,32,128]{2,1,0:T(8,128)S(1)} custom-call(s32[2]{0:T(128)S(1)} %get-tuple-element.26.flag_ref, s32[12,20]{1,0:T(8,128)S(1)} %get-tuple-element.27.ids_ref, bf16[12,32,128]{2,1,0:T(8,128)(2,1)S(1)} %get-tuple-element.51.x_ref, bf16[12,32,128]{2,1,0:T(8,128)(2,1)S(1)} %collective-permute-done.4.e_ref, ...), custom_call_target="tpu_custom_call" | custom-call | flops 251658240 | bytes 7864320 | tf_op jit(solution)/shard_map/direct/pallas_call | solution.py:308
  31.8 2.1 %collective-permute-done.7 = bf16[12,32,128]{2,1,0:T(8,128)(2,1)S(1)} collective-permute-done((bf16[12,32,128]{2,1,0:T(8,128)(2,1)S(1)}, bf16[12,32,128]{2,1,0:T(8,128)(2,1)S(1)}, u32[]{:S(2)}, u32[]{:S(2)}) %collective-permute-start.7) | collective-permute-done | bytes 98336 | tf_op jit(solution)/shard_map/ppermute | solution.py:209
  34.0 3.3 %collective-permute-start.12 = (bf16[12,32,128]{2,1,0:T(8,128)(2,1)S(1)}, bf16[12,32,128]{2,1,0:T(8,128)(2,1)S(1)}, u32[]{:S(2)}, u32[]{:S(2)}) collective-permute-start(bf16[12,32,128]{2,1,0:T(8,128)(2,1)S(1)} %get-tuple-element.49.x_ref), channel_id=1, source_target_pairs={{0,0},{4,8},{8,4},{12,16},{16,12},{20,24},{24,20},{28,28},{1,1},{5... | collective-permute-start | bytes 294920 | tf_op jit(solution)/shard_map/ppermute | solution.py:209
  37.3 1.6 %spread.4 = (f32[12,32,128]{2,1,0:T(8,128)S(1)}, bf16[12,32,128]{2,1,0:T(8,128)(2,1)S(1)}, bf16[12,32,128]{2,1,0:T(8,128)(2,1)S(1)}) custom-call(s32[2]{0:T(128)S(1)} %get-tuple-element.26.flag_ref, s32[12,20]{1,0:T(8,128)S(1)} %get-tuple-element.27.ids_ref, bf16[12,32,128]{2,1,0:T(8,128)(2,1)S(1)} %get-tuple-element.49.x_ref, ...), custom_call_target="tpu_custom_call" | custom-call | flops 251658240 | bytes 7864320 | tf_op jit(solution)/shard_map/spread/pallas_call | solution.py:269
  39.5 3.2 %collective-permute-start.14 = (bf16[12,32,128]{2,1,0:T(8,128)(2,1)S(1)}, bf16[12,32,128]{2,1,0:T(8,128)(2,1)S(1)}, u32[]{:S(2)}, u32[]{:S(2)}) collective-permute-start(bf16[12,32,128]{2,1,0:T(8,128)(2,1)S(1)} %get-tuple-element.37), channel_id=1, source_target_pairs={{0,0},{4,8},{8,4},{12,16},{16,12},{20,24},{24,20},{28,28},{1,1},{5... | collective-permute-start | bytes 294920 | tf_op jit(solution)/shard_map/ppermute | solution.py:209
  42.9 1.4 %direct.6 = f32[12,32,128]{2,1,0:T(8,128)S(1)} custom-call(s32[2]{0:T(128)S(1)} %get-tuple-element.26.flag_ref, s32[12,20]{1,0:T(8,128)S(1)} %get-tuple-element.27.ids_ref, bf16[12,32,128]{2,1,0:T(8,128)(2,1)S(1)} %get-tuple-element.49.x_ref, bf16[12,32,128]{2,1,0:T(8,128)(2,1)S(1)} %collective-permute-done.11.e_ref, ...), custom_call_target="tpu_custom_call" | custom-call | flops 251658240 | bytes 7864320 | tf_op jit(solution)/shard_map/direct/pallas_call | solution.py:308
  44.3 2.0 %collective-permute-done.14 = bf16[12,32,128]{2,1,0:T(8,128)(2,1)S(1)} collective-permute-done((bf16[12,32,128]{2,1,0:T(8,128)(2,1)S(1)}, bf16[12,32,128]{2,1,0:T(8,128)(2,1)S(1)}, u32[]{:S(2)}, u32[]{:S(2)}) %collective-permute-start.14) | collective-permute-done | bytes 98336 | tf_op jit(solution)/shard_map/ppermute | solution.py:209
  46.4 3.2 %collective-permute-start.16 = (bf16[12,32,128]{2,1,0:T(8,128)(2,1)S(1)}, bf16[12,32,128]{2,1,0:T(8,128)(2,1)S(1)}, u32[]{:S(2)}, u32[]{:S(2)}) collective-permute-start(bf16[12,32,128]{2,1,0:T(8,128)(2,1)S(1)} %get-tuple-element.47.x_ref), channel_id=1, source_target_pairs={{0,0},{4,8},{8,4},{12,16},{16,12},{20,24},{24,20},{28,28},{1,1},{5... | collective-permute-start | bytes 294920 | tf_op jit(solution)/shard_map/ppermute | solution.py:209
  49.7 1.4 %spread.5 = (f32[12,32,128]{2,1,0:T(8,128)S(1)}, bf16[12,32,128]{2,1,0:T(8,128)(2,1)S(1)}, bf16[12,32,128]{2,1,0:T(8,128)(2,1)S(1)}) custom-call(s32[2]{0:T(128)S(1)} %get-tuple-element.26.flag_ref, s32[12,20]{1,0:T(8,128)S(1)} %get-tuple-element.27.ids_ref, bf16[12,32,128]{2,1,0:T(8,128)(2,1)S(1)} %get-tuple-element.47.x_ref, ...), custom_call_target="tpu_custom_call" | custom-call | flops 251658240 | bytes 7864320 | tf_op jit(solution)/shard_map/spread/pallas_call | solution.py:269
  51.7 3.3 %collective-permute-start.18 = (bf16[12,32,128]{2,1,0:T(8,128)(2,1)S(1)}, bf16[12,32,128]{2,1,0:T(8,128)(2,1)S(1)}, u32[]{:S(2)}, u32[]{:S(2)}) collective-permute-start(bf16[12,32,128]{2,1,0:T(8,128)(2,1)S(1)} %get-tuple-element.40), channel_id=1, source_target_pairs={{0,0},{4,8},{8,4},{12,16},{16,12},{20,24},{24,20},{28,28},{1,1},{5... | collective-permute-start | bytes 294920 | tf_op jit(solution)/shard_map/ppermute | solution.py:209
  55.3 3.6 %collective-permute-done.9 = f32[2,32,128]{2,1,0:T(8,128)S(1)} collective-permute-done((f32[2,32,128]{2,1,0:T(8,128)S(1)}, f32[2,32,128]{2,1,0:T(8,128)S(1)}, u32[]{:S(2)}, u32[]{:S(2)}) %collective-permute-start.9) | collective-permute-done | bytes 32800 | tf_op jit(solution)/shard_map/ppermute | solution.py:217
  59.0 3.9 %collective-permute-done.10 = f32[2,32,128]{2,1,0:T(8,128)S(1)} collective-permute-done((f32[2,32,128]{2,1,0:T(8,128)S(1)}, f32[2,32,128]{2,1,0:T(8,128)S(1)}, u32[]{:S(2)}, u32[]{:S(2)}) %collective-permute-start.10) | collective-permute-done | bytes 32800 | tf_op jit(solution)/shard_map/ppermute | solution.py:217
  62.9 1.4 %direct.7.y_ref = f32[12,32,128]{2,1,0:T(8,128)S(1)} custom-call(s32[2]{0:T(128)S(1)} %get-tuple-element.26.flag_ref, s32[12,20]{1,0:T(8,128)S(1)} %get-tuple-element.27.ids_ref, bf16[12,32,128]{2,1,0:T(8,128)(2,1)S(1)} %get-tuple-element.47.x_ref, bf16[12,32,128]{2,1,0:T(8,128)(2,1)S(1)} %collective-permute-done.15.e_ref, ...), custom_call_target="tpu_custom_call" | custom-call | flops 251658240 | bytes 7864320 | tf_op jit(solution)/shard_map/direct/pallas_call | solution.py:308
  64.5 1.9 %collective-permute-start.20 = (bf16[12,32,128]{2,1,0:T(8,128)(2,1)S(1)}, bf16[12,32,128]{2,1,0:T(8,128)(2,1)S(1)}, u32[]{:S(2)}, u32[]{:S(2)}) collective-permute-start(bf16[12,32,128]{2,1,0:T(8,128)(2,1)S(1)} %get-tuple-element.43.w_ref.refs_3_), channel_id=1, source_target_pairs={{0,0},{4,8},{8,4},{12,16},{16,12},{20,24},{24,20},{28,28},{1,1},{5... | collective-permute-start | bytes 294920 | tf_op jit(solution)/shard_map/ppermute | solution.py:209
  66.5 1.7 %collective-permute-start.19 = (bf16[12,32,128]{2,1,0:T(8,128)(2,1)S(1)}, bf16[12,32,128]{2,1,0:T(8,128)(2,1)S(1)}, u32[]{:S(2)}, u32[]{:S(2)}) collective-permute-start(bf16[12,32,128]{2,1,0:T(8,128)(2,1)S(1)} %get-tuple-element.43.w_ref.refs_3_), channel_id=1, source_target_pairs={{0,4},{4,0},{8,12},{12,8},{16,20},{20,16},{24,28},{28,24},{1,5},{5... | collective-permute-start | bytes 294920 | tf_op jit(solution)/shard_map/ppermute | solution.py:210
  68.2 1.2 %images.1.refs_7_ = f32[20,12,64,128]{3,2,1,0:T(8,128)S(1)} custom-call(s32[2]{0:T(128)S(1)} %get-tuple-element.26.flag_ref, bf16[12,32,128]{2,1,0:T(8,128)(2,1)S(1)} %copy-done.2, bf16[12,32,128]{2,1,0:T(8,128)(2,1)S(1)} %get-tuple-element.43.w_ref.refs_3_, bf16[20,12,128,128]{3,2,1,0:T(8,128)(2,1)S(1)} %bitcast.3), custom_call_target="tpu_custom_call" | custom-call | flops 503316480 | bytes 7864320 | tf_op jit(solution)/shard_map/images/pallas_call | solution.py:334
  69.4 1.9 %collective-permute-done.20.refs_5_ = bf16[12,32,128]{2,1,0:T(8,128)(2,1)S(1)} collective-permute-done((bf16[12,32,128]{2,1,0:T(8,128)(2,1)S(1)}, bf16[12,32,128]{2,1,0:T(8,128)(2,1)S(1)}, u32[]{:S(2)}, u32[]{:S(2)}) %collective-permute-start.20) | collective-permute-done | bytes 98336 | tf_op jit(solution)/shard_map/ppermute | solution.py:209
  71.4 2.5 %forces.1 = (f32[12,3,128]{2,1,0:T(4,128)S(1)}, f32[12,3,128]{2,1,0:T(4,128)S(1)}, f32[12,3,128]{2,1,0:T(4,128)S(1)}) custom-call(s32[2]{0:T(128)S(1)} %get-tuple-element.26.flag_ref, s32[12,20]{1,0:T(8,128)S(1)} %get-tuple-element.27.ids_ref, f32[36,20]{1,0:T(8,128)S(1)} %get-tuple-element.42.bond_ref, bf16[12,32,128]{2,1,0:T(8,128)(2,1)S(1)} %copy-done.2, ...), custom_call_target="tpu_custom_call" | custom-call | flops 503316480 | bytes 15728640 | tf_op jit(solution)/shard_map/forces/pallas_call | solution.py:398
  74.0 2.0 %collective-permute-start.22 = (f32[12,3,128]{2,1,0:T(4,128)S(1)}, f32[12,3,128]{2,1,0:T(4,128)S(1)}, u32[]{:S(2)}, u32[]{:S(2)}) collective-permute-start(f32[12,3,128]{2,1,0:T(4,128)S(1)} %get-tuple-element.46), channel_id=1, source_target_pairs={{0,0},{4,8},{8,4},{12,16},{16,12},{20,24},{24,20},{28,28},{1,1},{5... | collective-permute-start | bytes 55304 | tf_op jit(solution)/shard_map/ppermute | solution.py:209
  76.0 4.0 %collective-permute-done.22.o_ref = f32[12,3,128]{2,1,0:T(4,128)S(1)} collective-permute-done((f32[12,3,128]{2,1,0:T(4,128)S(1)}, f32[12,3,128]{2,1,0:T(4,128)S(1)}, u32[]{:S(2)}, u32[]{:S(2)}) %collective-permute-start.22) | collective-permute-done | bytes 18464 | tf_op jit(solution)/shard_map/ppermute | solution.py:209
  80.8 3.2 %collective-permute-done.23 = f32[24,128]{1,0:T(8,128)S(1)} collective-permute-done((f32[24,128]{1,0:T(8,128)S(1)}, f32[24,128]{1,0:T(8,128)S(1)}, u32[]{:S(2)}, u32[]{:S(2)}) %collective-permute-start.23) | collective-permute-done | bytes 12320 | tf_op jit(solution)/shard_map/ppermute | solution.py:446
  84.4 4.3 %collective-permute-done.24.refs_1_ = f32[24,128]{1,0:T(8,128)S(1)} collective-permute-done((f32[24,128]{1,0:T(8,128)S(1)}, f32[24,128]{1,0:T(8,128)S(1)}, u32[]{:S(2)}, u32[]{:S(2)}) %collective-permute-start.24) | collective-permute-done | bytes 12320 | tf_op jit(solution)/shard_map/ppermute | solution.py:446
  (61 shorter events, 8.4 us)
Async XLA Ops:
  0.6 16.8 %copy-start.3 = (f32[12,128]{1,0:T(8,128)S(1)}, f32[12,128]{1,0:T(8,128)}, u32[]{:S(2)}) copy-start(f32[12,128]{1,0:T(8,128)} %site_ref.7) | copy-start | bytes 18436
  0.6 16.8 %collective-permute-start.1 = (bf16[12,32,128]{2,1,0:T(8,128)(2,1)}, bf16[12,32,128]{2,1,0:T(8,128)(2,1)S(1)}, u32[]{:S(2)}, u32[]{:S(2)}) collective-permute-start(bf16[12,32,128]{2,1,0:T(8,128)(2,1)} %refs_0_.1), channel_id=1, source_target_pairs={{0,0},{4,8},{8,4},{12,16},{16,12},{20,24},{24,20},{28,28},{1,1},{5... | collective-permute-start | bytes 294920 | tf_op jit(solution)/shard_map/ppermute | solution.py:209
  3.4 14.0 %collective-permute-start = (bf16[12,32,128]{2,1,0:T(8,128)(2,1)}, bf16[12,32,128]{2,1,0:T(8,128)(2,1)S(1)}, u32[]{:S(2)}, u32[]{:S(2)}) collective-permute-start(bf16[12,32,128]{2,1,0:T(8,128)(2,1)} %refs_0_.1), channel_id=1, source_target_pairs={{0,4},{4,0},{8,12},{12,8},{16,20},{20,16},{24,28},{28,24},{1,5},{5... | collective-permute-start | bytes 294920 | tf_op jit(solution)/shard_map/ppermute | solution.py:210
  7.8 3.2 %copy-start = (bf16[20,12,128,128]{3,2,1,0:T(8,128)(2,1)S(1)}, bf16[20,12,128,128]{3,2,1,0:T(8,128)(2,1)}, u32[]{:S(2)}) copy-start(bf16[20,12,128,128]{3,2,1,0:T(8,128)(2,1)} %k_ref.9) | copy-start | bytes 23592964
  11.0 0.9 copy-start.1
  11.9 12.8 %slice-start = ((s8[7864320]{0:T(1024)(128)(4,1)}), s8[3670016]{0:T(1024)(128)(4,1)S(1)}, s32[]{:S(2)}) async-start(s8[7864320]{0:T(1024)(128)(4,1)} %bitcast.2), calls=%async_computation | async-start | bytes 7340032
  13.9 5.0 %collective-permute-start.2 = (bf16[12,32,128]{2,1,0:T(8,128)(2,1)S(1)}, bf16[12,32,128]{2,1,0:T(8,128)(2,1)S(1)}, u32[]{:S(2)}, u32[]{:S(2)}) collective-permute-start(bf16[12,32,128]{2,1,0:T(8,128)(2,1)S(1)} %get-tuple-element.30), channel_id=1, source_target_pairs={{0,4},{4,0},{8,12},{12,8},{16,20},{20,16},{24,28},{28,24},{1,5},{5... | collective-permute-start | bytes 294920 | tf_op jit(solution)/shard_map/ppermute | solution.py:210
  14.0 7.6 %collective-permute-start.3 = (bf16[12,32,128]{2,1,0:T(8,128)(2,1)S(1)}, bf16[12,32,128]{2,1,0:T(8,128)(2,1)S(1)}, u32[]{:S(2)}, u32[]{:S(2)}) collective-permute-start(bf16[12,32,128]{2,1,0:T(8,128)(2,1)S(1)} %get-tuple-element.31), channel_id=1, source_target_pairs={{0,0},{4,8},{8,4},{12,16},{16,12},{20,24},{24,20},{28,28},{1,1},{5... | collective-permute-start | bytes 294920 | tf_op jit(solution)/shard_map/ppermute | solution.py:209
  17.5 7.3 %slice-start.1 = ((s8[7864320]{0:T(1024)(128)(4,1)}), s8[4194304]{0:T(1024)(128)(4,1)S(1)}, s32[]{:S(2)}) async-start(s8[7864320]{0:T(1024)(128)(4,1)} %bitcast.2), calls=%async_computation.1 | async-start | bytes 8388608
  21.7 12.3 %copy-start.2 = (bf16[12,32,128]{2,1,0:T(8,128)(2,1)S(1)}, bf16[12,32,128]{2,1,0:T(8,128)(2,1)}, u32[]{:S(2)}) copy-start(bf16[12,32,128]{2,1,0:T(8,128)(2,1)} %refs_0_.1) | copy-start | bytes 294916
  21.7 8.7 %collective-permute-start.5 = (bf16[12,32,128]{2,1,0:T(8,128)(2,1)S(1)}, bf16[12,32,128]{2,1,0:T(8,128)(2,1)S(1)}, u32[]{:S(2)}, u32[]{:S(2)}) collective-permute-start(bf16[12,32,128]{2,1,0:T(8,128)(2,1)S(1)} %get-tuple-element.51.x_ref), channel_id=1, source_target_pairs={{0,0},{4,8},{8,4},{12,16},{16,12},{20,24},{24,20},{28,28},{1,1},{5... | collective-permute-start | bytes 294920 | tf_op jit(solution)/shard_map/ppermute | solution.py:209
  24.7 5.7 %collective-permute-start.4 = (bf16[12,32,128]{2,1,0:T(8,128)(2,1)S(1)}, bf16[12,32,128]{2,1,0:T(8,128)(2,1)S(1)}, u32[]{:S(2)}, u32[]{:S(2)}) collective-permute-start(bf16[12,32,128]{2,1,0:T(8,128)(2,1)S(1)} %get-tuple-element.51.x_ref), channel_id=1, source_target_pairs={{0,4},{4,0},{8,12},{12,8},{16,20},{20,16},{24,28},{28,24},{1,5},{5... | collective-permute-start | bytes 294920 | tf_op jit(solution)/shard_map/ppermute | solution.py:210
  26.2 5.6 %collective-permute-start.6 = (bf16[12,32,128]{2,1,0:T(8,128)(2,1)S(1)}, bf16[12,32,128]{2,1,0:T(8,128)(2,1)S(1)}, u32[]{:S(2)}, u32[]{:S(2)}) collective-permute-start(bf16[12,32,128]{2,1,0:T(8,128)(2,1)S(1)} %get-tuple-element.33), channel_id=1, source_target_pairs={{0,4},{4,0},{8,12},{12,8},{16,20},{20,16},{24,28},{28,24},{1,5},{5... | collective-permute-start | bytes 294920 | tf_op jit(solution)/shard_map/ppermute | solution.py:210
  26.8 7.2 %collective-permute-start.7 = (bf16[12,32,128]{2,1,0:T(8,128)(2,1)S(1)}, bf16[12,32,128]{2,1,0:T(8,128)(2,1)S(1)}, u32[]{:S(2)}, u32[]{:S(2)}) collective-permute-start(bf16[12,32,128]{2,1,0:T(8,128)(2,1)S(1)} %get-tuple-element.34), channel_id=1, source_target_pairs={{0,0},{4,8},{8,4},{12,16},{16,12},{20,24},{24,20},{28,28},{1,1},{5... | collective-permute-start | bytes 294920 | tf_op jit(solution)/shard_map/ppermute | solution.py:209
  34.0 8.9 %collective-permute-start.12 = (bf16[12,32,128]{2,1,0:T(8,128)(2,1)S(1)}, bf16[12,32,128]{2,1,0:T(8,128)(2,1)S(1)}, u32[]{:S(2)}, u32[]{:S(2)}) collective-permute-start(bf16[12,32,128]{2,1,0:T(8,128)(2,1)S(1)} %get-tuple-element.49.x_ref), channel_id=1, source_target_pairs={{0,0},{4,8},{8,4},{12,16},{16,12},{20,24},{24,20},{28,28},{1,1},{5... | collective-permute-start | bytes 294920 | tf_op jit(solution)/shard_map/ppermute | solution.py:209
  37.3 5.6 %collective-permute-start.11 = (bf16[12,32,128]{2,1,0:T(8,128)(2,1)S(1)}, bf16[12,32,128]{2,1,0:T(8,128)(2,1)S(1)}, u32[]{:S(2)}, u32[]{:S(2)}) collective-permute-start(bf16[12,32,128]{2,1,0:T(8,128)(2,1)S(1)} %get-tuple-element.49.x_ref), channel_id=1, source_target_pairs={{0,4},{4,0},{8,12},{12,8},{16,20},{20,16},{24,28},{28,24},{1,5},{5... | collective-permute-start | bytes 294920 | tf_op jit(solution)/shard_map/ppermute | solution.py:210
  39.0 5.4 %collective-permute-start.13 = (bf16[12,32,128]{2,1,0:T(8,128)(2,1)S(1)}, bf16[12,32,128]{2,1,0:T(8,128)(2,1)S(1)}, u32[]{:S(2)}, u32[]{:S(2)}) collective-permute-start(bf16[12,32,128]{2,1,0:T(8,128)(2,1)S(1)} %get-tuple-element.36), channel_id=1, source_target_pairs={{0,4},{4,0},{8,12},{12,8},{16,20},{20,16},{24,28},{28,24},{1,5},{5... | collective-permute-start | bytes 294920 | tf_op jit(solution)/shard_map/ppermute | solution.py:210
  39.5 6.8 %collective-permute-start.14 = (bf16[12,32,128]{2,1,0:T(8,128)(2,1)S(1)}, bf16[12,32,128]{2,1,0:T(8,128)(2,1)S(1)}, u32[]{:S(2)}, u32[]{:S(2)}) collective-permute-start(bf16[12,32,128]{2,1,0:T(8,128)(2,1)S(1)} %get-tuple-element.37), channel_id=1, source_target_pairs={{0,0},{4,8},{8,4},{12,16},{16,12},{20,24},{24,20},{28,28},{1,1},{5... | collective-permute-start | bytes 294920 | tf_op jit(solution)/shard_map/ppermute | solution.py:209
  42.8 12.2 %collective-permute-start.8 = (f32[2,32,128]{2,1,0:T(8,128)S(1)}, f32[2,32,128]{2,1,0:T(8,128)S(1)}, u32[]{:S(2)}, u32[]{:S(2)}) collective-permute-start(f32[2,32,128]{2,1,0:T(8,128)S(1)} %moments.1), channel_id=1, source_target_pairs={{0,4},{4,0},{8,12},{12,8},{16,20},{20,16},{24,28},{28,24},{1,5},{5... | collective-permute-start | bytes 98312 | tf_op jit(solution)/shard_map/ppermute | solution.py:217
  46.4 16.5 %collective-permute-start.16 = (bf16[12,32,128]{2,1,0:T(8,128)(2,1)S(1)}, bf16[12,32,128]{2,1,0:T(8,128)(2,1)S(1)}, u32[]{:S(2)}, u32[]{:S(2)}) collective-permute-start(bf16[12,32,128]{2,1,0:T(8,128)(2,1)S(1)} %get-tuple-element.47.x_ref), channel_id=1, source_target_pairs={{0,0},{4,8},{8,4},{12,16},{16,12},{20,24},{24,20},{28,28},{1,1},{5... | collective-permute-start | bytes 294920 | tf_op jit(solution)/shard_map/ppermute | solution.py:209
  49.6 13.3 %collective-permute-start.15 = (bf16[12,32,128]{2,1,0:T(8,128)(2,1)S(1)}, bf16[12,32,128]{2,1,0:T(8,128)(2,1)S(1)}, u32[]{:S(2)}, u32[]{:S(2)}) collective-permute-start(bf16[12,32,128]{2,1,0:T(8,128)(2,1)S(1)} %get-tuple-element.47.x_ref), channel_id=1, source_target_pairs={{0,4},{4,0},{8,12},{12,8},{16,20},{20,16},{24,28},{28,24},{1,5},{5... | collective-permute-start | bytes 294920 | tf_op jit(solution)/shard_map/ppermute | solution.py:210
  51.1 13.2 %collective-permute-start.17 = (bf16[12,32,128]{2,1,0:T(8,128)(2,1)S(1)}, bf16[12,32,128]{2,1,0:T(8,128)(2,1)S(1)}, u32[]{:S(2)}, u32[]{:S(2)}) collective-permute-start(bf16[12,32,128]{2,1,0:T(8,128)(2,1)S(1)} %get-tuple-element.39), channel_id=1, source_target_pairs={{0,4},{4,0},{8,12},{12,8},{16,20},{20,16},{24,28},{28,24},{1,5},{5... | collective-permute-start | bytes 294920 | tf_op jit(solution)/shard_map/ppermute | solution.py:210
  51.7 12.7 %collective-permute-start.18 = (bf16[12,32,128]{2,1,0:T(8,128)(2,1)S(1)}, bf16[12,32,128]{2,1,0:T(8,128)(2,1)S(1)}, u32[]{:S(2)}, u32[]{:S(2)}) collective-permute-start(bf16[12,32,128]{2,1,0:T(8,128)(2,1)S(1)} %get-tuple-element.40), channel_id=1, source_target_pairs={{0,0},{4,8},{8,4},{12,16},{16,12},{20,24},{24,20},{28,28},{1,1},{5... | collective-permute-start | bytes 294920 | tf_op jit(solution)/shard_map/ppermute | solution.py:209
  55.0 4.0 %collective-permute-start.9 = (f32[2,32,128]{2,1,0:T(8,128)S(1)}, f32[2,32,128]{2,1,0:T(8,128)S(1)}, u32[]{:S(2)}, u32[]{:S(2)}) collective-permute-start(f32[2,32,128]{2,1,0:T(8,128)S(1)} %add.34), channel_id=1, source_target_pairs={{0,8},{4,12},{8,0},{12,4},{16,24},{20,28},{24,16},{28,20},{1,9},{5... | collective-permute-start | bytes 98312 | tf_op jit(solution)/shard_map/ppermute | solution.py:217
  59.0 3.9 %collective-permute-start.10 = (f32[2,32,128]{2,1,0:T(8,128)S(1)}, f32[2,32,128]{2,1,0:T(8,128)S(1)}, u32[]{:S(2)}, u32[]{:S(2)}) collective-permute-start(f32[2,32,128]{2,1,0:T(8,128)S(1)} %add.35), channel_id=1, source_target_pairs={{0,16},{4,20},{8,24},{12,28},{16,0},{20,4},{24,8},{28,12},{1,17},{... | collective-permute-start | bytes 98312 | tf_op jit(solution)/shard_map/ppermute | solution.py:217
  64.5 6.8 %collective-permute-start.20 = (bf16[12,32,128]{2,1,0:T(8,128)(2,1)S(1)}, bf16[12,32,128]{2,1,0:T(8,128)(2,1)S(1)}, u32[]{:S(2)}, u32[]{:S(2)}) collective-permute-start(bf16[12,32,128]{2,1,0:T(8,128)(2,1)S(1)} %get-tuple-element.43.w_ref.refs_3_), channel_id=1, source_target_pairs={{0,0},{4,8},{8,4},{12,16},{16,12},{20,24},{24,20},{28,28},{1,1},{5... | collective-permute-start | bytes 294920 | tf_op jit(solution)/shard_map/ppermute | solution.py:209
  66.5 4.9 %collective-permute-start.19 = (bf16[12,32,128]{2,1,0:T(8,128)(2,1)S(1)}, bf16[12,32,128]{2,1,0:T(8,128)(2,1)S(1)}, u32[]{:S(2)}, u32[]{:S(2)}) collective-permute-start(bf16[12,32,128]{2,1,0:T(8,128)(2,1)S(1)} %get-tuple-element.43.w_ref.refs_3_), channel_id=1, source_target_pairs={{0,4},{4,0},{8,12},{12,8},{16,20},{20,16},{24,28},{28,24},{1,5},{5... | collective-permute-start | bytes 294920 | tf_op jit(solution)/shard_map/ppermute | solution.py:210
  71.4 8.6 %copy-start.6 = (s32[12,128]{1,0:T(8,128)S(1)}, s32[12,128]{1,0:T(8,128)}, u32[]{:S(2)}) copy-start(s32[12,128]{1,0:T(8,128)} %atom_ref.1) | copy-start | bytes 18436
  73.9 2.1 %collective-permute-start.21 = (f32[12,3,128]{2,1,0:T(4,128)S(1)}, f32[12,3,128]{2,1,0:T(4,128)S(1)}, u32[]{:S(2)}, u32[]{:S(2)}) collective-permute-start(f32[12,3,128]{2,1,0:T(4,128)S(1)} %get-tuple-element.45), channel_id=1, source_target_pairs={{0,4},{4,0},{8,12},{12,8},{16,20},{20,16},{24,28},{28,24},{1,5},{5... | collective-permute-start | bytes 55304 | tf_op jit(solution)/shard_map/ppermute | solution.py:210
  74.0 6.0 %collective-permute-start.22 = (f32[12,3,128]{2,1,0:T(4,128)S(1)}, f32[12,3,128]{2,1,0:T(4,128)S(1)}, u32[]{:S(2)}, u32[]{:S(2)}) collective-permute-start(f32[12,3,128]{2,1,0:T(4,128)S(1)} %get-tuple-element.46), channel_id=1, source_target_pairs={{0,0},{4,8},{8,4},{12,16},{16,12},{20,24},{24,20},{28,28},{1,1},{5... | collective-permute-start | bytes 55304 | tf_op jit(solution)/shard_map/ppermute | solution.py:209
  80.3 3.7 %collective-permute-start.23 = (f32[24,128]{1,0:T(8,128)S(1)}, f32[24,128]{1,0:T(8,128)S(1)}, u32[]{:S(2)}, u32[]{:S(2)}) collective-permute-start(f32[24,128]{1,0:T(8,128)S(1)} %packed.1), channel_id=1, source_target_pairs={{0,1},{1,0},{2,3},{3,2},{4,5},{5,4},{6,7},{7,6},{8,9},{9,8},{10,11... | collective-permute-start | bytes 36872 | tf_op jit(solution)/shard_map/ppermute | solution.py:446
  84.0 4.6 %collective-permute-start.24 = (f32[24,128]{1,0:T(8,128)S(1)}, f32[24,128]{1,0:T(8,128)S(1)}, u32[]{:S(2)}, u32[]{:S(2)}) collective-permute-start(f32[24,128]{1,0:T(8,128)S(1)} %add.39.refs_0_), channel_id=1, source_target_pairs={{0,2},{1,3},{2,0},{3,1},{4,6},{5,7},{6,4},{7,5},{8,10},{9,11},{10,... | collective-permute-start | bytes 36872 | tf_op jit(solution)/shard_map/ppermute | solution.py:446
  (3 other events, 2.1 us)

commit v3 on v2

--- a/solution.py
+++ b/solution.py
@@ -204,8 +204,7 @@
 def exchange(even_side, odd_side):
     count = lax.axis_size("clus")
     paired = [(i, i ^ 1) for i in range(count)]
-    shifted = [(i, i + 1 if i % 2 else i - 1) for i in range(count)]
-    shifted = [(i, j if 0 <= j < count else i) for i, j in shifted]
+    shifted = [(i, (i + 1 if i % 2 else i - 1) % count) for i in range(count)]
     crossed = lax.ppermute(odd_side, "clus", shifted)
     return lax.ppermute(even_side, "clus", paired), crossed
 

time: 90.9 us -> 75 us (0.83)
  the two profiles are of different devices: /device:TPU:28 before, /device:TPU:0 now
where the time goes in v3:
time: 75 us; the launch traced here: 74.8 us
  starting transfers between devices  24.6 us (33%)
  waiting for transfers between devices  24.1 us (32%)
  Pallas kernels  18 us (24%)
  local copies, waits for them, and re-layouts  6.23 us (8%)
  between operations  1.7 us (2%)
    ppermute x10, waiting for transfers between devices, exchange(): crossed = lax.ppermute(odd_side, 'clus', shifted)  12.9 us
    ppermute x10, starting transfers between devices, exchange(): crossed = lax.ppermute(odd_side, 'clus', shifted)  12.8 us
    ppermute x3, waiting for transfers between devices, doubled_sum(): part = part + lax.ppermute(part, axis, pairs)  7.02 us
    pallas_call x4, Pallas kernels, call(): pl.pallas_call(functools.partial(kernel, turn), out_shape=out, in_specs=[...  6.53 us
    unnamed x20, local copies, waits for them, and re-layouts  6.23 us
    pallas_call x4, Pallas kernels, direct(): pl.pallas_call(kernel, out_shape=jax.ShapeDtypeStruct((rows, probes, bloc...  5.72 us
    ppermute x10, starting transfers between devices, exchange(): return (lax.ppermute(even_side, 'clus', paired), crossed)  5 us
    ppermute x2, starting transfers between devices, local(): lax.ppermute(part, 'probe', [(i, i ^ step) for i in range(count)])  4.19 us
  transfers between devices with their start and end apart: 25, of which 10 were waited for; matrix products, arithmetic and copies ran while one was open for 0% of the time, Pallas kernels for 19%

profile of v3, /device:TPU:0, one launch (start us, length us, event | category | flops | bytes accessed | tf_op | source)
XLA Modules:
  0.0 74.8 jit_solution(4703838484740290409)
XLA Ops:
  0.6 3.4 %collective-permute-start.1 = (bf16[12,32,128]{2,1,0:T(8,128)(2,1)}, bf16[12,32,128]{2,1,0:T(8,128)(2,1)S(1)}, u32[]{:S(2)}, u32[]{:S(2)}) collective-permute-start(bf16[12,32,128]{2,1,0:T(8,128)(2,1)} %refs_0_.1), channel_id=1, source_target_pairs={{0,28},{4,8},{8,4},{12,16},{16,12},{20,24},{24,20},{28,0},{1,29},{... | collective-permute-start | bytes 294920 | tf_op jit(solution)/shard_map/ppermute | solution.py:208
  4.7 0.7 copy-done.4
  6.8 0.8 %prepared.1 = (s32[2]{0:T(128)S(1)}, s32[12,20]{1,0:T(8,128)S(1)}, f32[36,20]{1,0:T(8,128)S(1)}, f32[8,128]{1,0:T(8,128)S(1)}) custom-call(s32[12,20]{1,0:T(8,128)S(1)} %bitcast.5, bf16[3,12,20]{2,1,0:T(8,128)(2,1)S(1)} %bitcast.4, f32[1]{0:T(128)S(6)} %copy.11.mu_ref, f32[8,128]{1,0:T(8,128)S(1)} %copy-done.7), custom_call_target="tpu_custom_call" | custom-call | flops 1000 | bytes 50000 | tf_op jit(solution)/shard_map/prepared/pallas_call | solution.py:63
  7.6 3.2 %copy-done = bf16[20,12,128,128]{3,2,1,0:T(8,128)(2,1)S(1)} copy-done((bf16[20,12,128,128]{3,2,1,0:T(8,128)(2,1)S(1)}, bf16[20,12,128,128]{3,2,1,0:T(8,128)(2,1)}, u32[]{:S(2)}) %copy-start) | copy-done | bytes 7864344
  10.9 0.9 %copy-done.1 = bf16[12,32,128]{2,1,0:T(8,128)(2,1)S(1)} copy-done((bf16[12,32,128]{2,1,0:T(8,128)(2,1)S(1)}, bf16[12,32,128]{2,1,0:T(8,128)(2,1)}, u32[]{:S(2)}) %copy-start.1) | copy-done | bytes 98328
  11.8 2.0 %spread_turn.1 = (f32[12,32,128]{2,1,0:T(8,128)S(1)}, bf16[12,32,128]{2,1,0:T(8,128)(2,1)S(1)}, bf16[12,32,128]{2,1,0:T(8,128)(2,1)S(1)}, bf16[20,12,128,128]{3,2,1,0:T(8,128)(2,1)S(1)}) custom-call(s32[2]{0:T(128)S(1)} %get-tuple-element.26.flag_ref, s32[12,20]{1,0:T(8,128)S(1)} %get-tuple-element.27.ids_ref, bf16[12,32,128]{2,1,0:T(8,128)(2,1)S(1)} %copy-done.1, ...), custom_call_target="tpu_custom_call" | custom-call | flops 251658240 | bytes 7864320 | tf_op jit(solution)/shard_map/spread_turn/pallas_call | solution.py:268
  14.7 1.4 %direct.4 = f32[12,32,128]{2,1,0:T(8,128)S(1)} custom-call(s32[2]{0:T(128)S(1)} %get-tuple-element.26.flag_ref, s32[12,20]{1,0:T(8,128)S(1)} %get-tuple-element.27.ids_ref, bf16[12,32,128]{2,1,0:T(8,128)(2,1)S(1)} %copy-done.1, bf16[12,32,128]{2,1,0:T(8,128)(2,1)S(1)} %collective-permute-done.e_ref.refs_1_, ...), custom_call_target="tpu_custom_call" | custom-call | flops 251658240 | bytes 7864320 | tf_op jit(solution)/shard_map/direct/pallas_call | solution.py:307
  16.1 4.2 %collective-permute-done.3 = bf16[12,32,128]{2,1,0:T(8,128)(2,1)S(1)} collective-permute-done((bf16[12,32,128]{2,1,0:T(8,128)(2,1)S(1)}, bf16[12,32,128]{2,1,0:T(8,128)(2,1)S(1)}, u32[]{:S(2)}, u32[]{:S(2)}) %collective-permute-start.3) | collective-permute-done | bytes 98336 | tf_op jit(solution)/shard_map/ppermute | solution.py:208
  20.7 1.4 %spread.3 = (f32[12,32,128]{2,1,0:T(8,128)S(1)}, bf16[12,32,128]{2,1,0:T(8,128)(2,1)S(1)}, bf16[12,32,128]{2,1,0:T(8,128)(2,1)S(1)}) custom-call(s32[2]{0:T(128)S(1)} %get-tuple-element.26.flag_ref, s32[12,20]{1,0:T(8,128)S(1)} %get-tuple-element.27.ids_ref, bf16[12,32,128]{2,1,0:T(8,128)(2,1)S(1)} %get-tuple-element.51.x_ref, ...), custom_call_target="tpu_custom_call" | custom-call | flops 251658240 | bytes 7864320 | tf_op jit(solution)/shard_map/spread/pallas_call | solution.py:268
  22.5 2.5 %collective-permute-start.7 = (bf16[12,32,128]{2,1,0:T(8,128)(2,1)S(1)}, bf16[12,32,128]{2,1,0:T(8,128)(2,1)S(1)}, u32[]{:S(2)}, u32[]{:S(2)}) collective-permute-start(bf16[12,32,128]{2,1,0:T(8,128)(2,1)S(1)} %get-tuple-element.34), channel_id=1, source_target_pairs={{0,28},{4,8},{8,4},{12,16},{16,12},{20,24},{24,20},{28,0},{1,29},{... | collective-permute-start | bytes 294920 | tf_op jit(solution)/shard_map/ppermute | solution.py:208
  25.8 1.4 %direct.5 = f32[12,32,128]{2,1,0:T(8,128)S(1)} custom-call(s32[2]{0:T(128)S(1)} %get-tuple-element.26.flag_ref, s32[12,20]{1,0:T(8,128)S(1)} %get-tuple-element.27.ids_ref, bf16[12,32,128]{2,1,0:T(8,128)(2,1)S(1)} %get-tuple-element.51.x_ref, bf16[12,32,128]{2,1,0:T(8,128)(2,1)S(1)} %collective-permute-done.4.e_ref, ...), custom_call_target="tpu_custom_call" | custom-call | flops 251658240 | bytes 7864320 | tf_op jit(solution)/shard_map/direct/pallas_call | solution.py:307
  27.5 2.8 %collective-permute-start.12 = (bf16[12,32,128]{2,1,0:T(8,128)(2,1)S(1)}, bf16[12,32,128]{2,1,0:T(8,128)(2,1)S(1)}, u32[]{:S(2)}, u32[]{:S(2)}) collective-permute-start(bf16[12,32,128]{2,1,0:T(8,128)(2,1)S(1)} %get-tuple-element.49.x_ref), channel_id=1, source_target_pairs={{0,28},{4,8},{8,4},{12,16},{16,12},{20,24},{24,20},{28,0},{1,29},{... | collective-permute-start | bytes 294920 | tf_op jit(solution)/shard_map/ppermute | solution.py:208
  30.3 1.6 %spread.4 = (f32[12,32,128]{2,1,0:T(8,128)S(1)}, bf16[12,32,128]{2,1,0:T(8,128)(2,1)S(1)}, bf16[12,32,128]{2,1,0:T(8,128)(2,1)S(1)}) custom-call(s32[2]{0:T(128)S(1)} %get-tuple-element.26.flag_ref, s32[12,20]{1,0:T(8,128)S(1)} %get-tuple-element.27.ids_ref, bf16[12,32,128]{2,1,0:T(8,128)(2,1)S(1)} %get-tuple-element.49.x_ref, ...), custom_call_target="tpu_custom_call" | custom-call | flops 251658240 | bytes 7864320 | tf_op jit(solution)/shard_map/spread/pallas_call | solution.py:268
  32.7 1.5 %collective-permute-start.8 = (f32[2,32,128]{2,1,0:T(8,128)S(1)}, f32[2,32,128]{2,1,0:T(8,128)S(1)}, u32[]{:S(2)}, u32[]{:S(2)}) collective-permute-start(f32[2,32,128]{2,1,0:T(8,128)S(1)} %moments.1), channel_id=1, source_target_pairs={{0,4},{4,0},{8,12},{12,8},{16,20},{20,16},{24,28},{28,24},{1,5},{5... | collective-permute-start | bytes 98312 | tf_op jit(solution)/shard_map/ppermute | solution.py:216
  34.2 1.4 %direct.6 = f32[12,32,128]{2,1,0:T(8,128)S(1)} custom-call(s32[2]{0:T(128)S(1)} %get-tuple-element.26.flag_ref, s32[12,20]{1,0:T(8,128)S(1)} %get-tuple-element.27.ids_ref, bf16[12,32,128]{2,1,0:T(8,128)(2,1)S(1)} %get-tuple-element.49.x_ref, bf16[12,32,128]{2,1,0:T(8,128)(2,1)S(1)} %collective-permute-done.11.e_ref, ...), custom_call_target="tpu_custom_call" | custom-call | flops 251658240 | bytes 7864320 | tf_op jit(solution)/shard_map/direct/pallas_call | solution.py:307
  35.6 2.7 %collective-permute-done.14 = bf16[12,32,128]{2,1,0:T(8,128)(2,1)S(1)} collective-permute-done((bf16[12,32,128]{2,1,0:T(8,128)(2,1)S(1)}, bf16[12,32,128]{2,1,0:T(8,128)(2,1)S(1)}, u32[]{:S(2)}, u32[]{:S(2)}) %collective-permute-start.14) | collective-permute-done | bytes 98336 | tf_op jit(solution)/shard_map/ppermute | solution.py:208
  38.6 1.4 %spread.5 = (f32[12,32,128]{2,1,0:T(8,128)S(1)}, bf16[12,32,128]{2,1,0:T(8,128)(2,1)S(1)}, bf16[12,32,128]{2,1,0:T(8,128)(2,1)S(1)}) custom-call(s32[2]{0:T(128)S(1)} %get-tuple-element.26.flag_ref, s32[12,20]{1,0:T(8,128)S(1)} %get-tuple-element.27.ids_ref, bf16[12,32,128]{2,1,0:T(8,128)(2,1)S(1)} %get-tuple-element.47.x_ref, ...), custom_call_target="tpu_custom_call" | custom-call | flops 251658240 | bytes 7864320 | tf_op jit(solution)/shard_map/spread/pallas_call | solution.py:268
  40.6 2.5 %collective-permute-start.18 = (bf16[12,32,128]{2,1,0:T(8,128)(2,1)S(1)}, bf16[12,32,128]{2,1,0:T(8,128)(2,1)S(1)}, u32[]{:S(2)}, u32[]{:S(2)}) collective-permute-start(bf16[12,32,128]{2,1,0:T(8,128)(2,1)S(1)} %get-tuple-element.40), channel_id=1, source_target_pairs={{0,28},{4,8},{8,4},{12,16},{16,12},{20,24},{24,20},{28,0},{1,29},{... | collective-permute-start | bytes 294920 | tf_op jit(solution)/shard_map/ppermute | solution.py:208
  43.2 4.2 %collective-permute-done.9 = f32[2,32,128]{2,1,0:T(8,128)S(1)} collective-permute-done((f32[2,32,128]{2,1,0:T(8,128)S(1)}, f32[2,32,128]{2,1,0:T(8,128)S(1)}, u32[]{:S(2)}, u32[]{:S(2)}) %collective-permute-start.9) | collective-permute-done | bytes 32800 | tf_op jit(solution)/shard_map/ppermute | solution.py:216
  47.5 1.1 %collective-permute-start.10 = (f32[2,32,128]{2,1,0:T(8,128)S(1)}, f32[2,32,128]{2,1,0:T(8,128)S(1)}, u32[]{:S(2)}, u32[]{:S(2)}) collective-permute-start(f32[2,32,128]{2,1,0:T(8,128)S(1)} %add.35), channel_id=1, source_target_pairs={{0,16},{4,20},{8,24},{12,28},{16,0},{20,4},{24,8},{28,12},{1,17},{... | collective-permute-start | bytes 98312 | tf_op jit(solution)/shard_map/ppermute | solution.py:216
  48.6 2.8 %collective-permute-done.10 = f32[2,32,128]{2,1,0:T(8,128)S(1)} collective-permute-done((f32[2,32,128]{2,1,0:T(8,128)S(1)}, f32[2,32,128]{2,1,0:T(8,128)S(1)}, u32[]{:S(2)}, u32[]{:S(2)}) %collective-permute-start.10) | collective-permute-done | bytes 32800 | tf_op jit(solution)/shard_map/ppermute | solution.py:216
  51.4 1.4 %direct.7.y_ref = f32[12,32,128]{2,1,0:T(8,128)S(1)} custom-call(s32[2]{0:T(128)S(1)} %get-tuple-element.26.flag_ref, s32[12,20]{1,0:T(8,128)S(1)} %get-tuple-element.27.ids_ref, bf16[12,32,128]{2,1,0:T(8,128)(2,1)S(1)} %get-tuple-element.47.x_ref, bf16[12,32,128]{2,1,0:T(8,128)(2,1)S(1)} %collective-permute-done.15.e_ref, ...), custom_call_target="tpu_custom_call" | custom-call | flops 251658240 | bytes 7864320 | tf_op jit(solution)/shard_map/direct/pallas_call | solution.py:307
  53.1 2.2 %collective-permute-start.19 = (bf16[12,32,128]{2,1,0:T(8,128)(2,1)S(1)}, bf16[12,32,128]{2,1,0:T(8,128)(2,1)S(1)}, u32[]{:S(2)}, u32[]{:S(2)}) collective-permute-start(bf16[12,32,128]{2,1,0:T(8,128)(2,1)S(1)} %get-tuple-element.43.w_ref.refs_3_), channel_id=1, source_target_pairs={{0,4},{4,0},{8,12},{12,8},{16,20},{20,16},{24,28},{28,24},{1,5},{5... | collective-permute-start | bytes 294920 | tf_op jit(solution)/shard_map/ppermute | solution.py:209
  55.3 1.2 %images.1.refs_7_ = f32[20,12,64,128]{3,2,1,0:T(8,128)S(1)} custom-call(s32[2]{0:T(128)S(1)} %get-tuple-element.26.flag_ref, bf16[12,32,128]{2,1,0:T(8,128)(2,1)S(1)} %copy-done.2, bf16[12,32,128]{2,1,0:T(8,128)(2,1)S(1)} %get-tuple-element.43.w_ref.refs_3_, bf16[20,12,128,128]{3,2,1,0:T(8,128)(2,1)S(1)} %bitcast.3), custom_call_target="tpu_custom_call" | custom-call | flops 503316480 | bytes 7864320 | tf_op jit(solution)/shard_map/images/pallas_call | solution.py:333
  56.5 1.8 %collective-permute-done.20.refs_5_ = bf16[12,32,128]{2,1,0:T(8,128)(2,1)S(1)} collective-permute-done((bf16[12,32,128]{2,1,0:T(8,128)(2,1)S(1)}, bf16[12,32,128]{2,1,0:T(8,128)(2,1)S(1)}, u32[]{:S(2)}, u32[]{:S(2)}) %collective-permute-start.20) | collective-permute-done | bytes 98336 | tf_op jit(solution)/shard_map/ppermute | solution.py:208
  58.3 2.5 %forces.1 = (f32[12,3,128]{2,1,0:T(4,128)S(1)}, f32[12,3,128]{2,1,0:T(4,128)S(1)}, f32[12,3,128]{2,1,0:T(4,128)S(1)}) custom-call(s32[2]{0:T(128)S(1)} %get-tuple-element.26.flag_ref, s32[12,20]{1,0:T(8,128)S(1)} %get-tuple-element.27.ids_ref, f32[36,20]{1,0:T(8,128)S(1)} %get-tuple-element.42.bond_ref, bf16[12,32,128]{2,1,0:T(8,128)(2,1)S(1)} %copy-done.2, ...), custom_call_target="tpu_custom_call" | custom-call | flops 503316480 | bytes 15728640 | tf_op jit(solution)/shard_map/forces/pallas_call | solution.py:397
  61.2 0.8 %collective-permute-start.22 = (f32[12,3,128]{2,1,0:T(4,128)S(1)}, f32[12,3,128]{2,1,0:T(4,128)S(1)}, u32[]{:S(2)}, u32[]{:S(2)}) collective-permute-start(f32[12,3,128]{2,1,0:T(4,128)S(1)} %get-tuple-element.46), channel_id=1, source_target_pairs={{0,28},{4,8},{8,4},{12,16},{16,12},{20,24},{24,20},{28,0},{1,29},{... | collective-permute-start | bytes 55304 | tf_op jit(solution)/shard_map/ppermute | solution.py:208
  62.1 3.3 %collective-permute-done.22.o_ref = f32[12,3,128]{2,1,0:T(4,128)S(1)} collective-permute-done((f32[12,3,128]{2,1,0:T(4,128)S(1)}, f32[12,3,128]{2,1,0:T(4,128)S(1)}, u32[]{:S(2)}, u32[]{:S(2)}) %collective-permute-start.22) | collective-permute-done | bytes 18464 | tf_op jit(solution)/shard_map/ppermute | solution.py:208
  65.7 1.6 %collective-permute-start.23 = (f32[24,128]{1,0:T(8,128)S(1)}, f32[24,128]{1,0:T(8,128)S(1)}, u32[]{:S(2)}, u32[]{:S(2)}) collective-permute-start(f32[24,128]{1,0:T(8,128)S(1)} %packed.1), channel_id=1, source_target_pairs={{0,1},{1,0},{2,3},{3,2},{4,5},{5,4},{6,7},{7,6},{8,9},{9,8},{10,11... | collective-permute-start | bytes 36872 | tf_op jit(solution)/shard_map/ppermute | solution.py:445
  67.3 2.1 %collective-permute-done.23 = f32[24,128]{1,0:T(8,128)S(1)} collective-permute-done((f32[24,128]{1,0:T(8,128)S(1)}, f32[24,128]{1,0:T(8,128)S(1)}, u32[]{:S(2)}, u32[]{:S(2)}) %collective-permute-start.23) | collective-permute-done | bytes 12320 | tf_op jit(solution)/shard_map/ppermute | solution.py:445
  69.4 2.6 %collective-permute-start.24 = (f32[24,128]{1,0:T(8,128)S(1)}, f32[24,128]{1,0:T(8,128)S(1)}, u32[]{:S(2)}, u32[]{:S(2)}) collective-permute-start(f32[24,128]{1,0:T(8,128)S(1)} %add.39.refs_0_), channel_id=1, source_target_pairs={{0,2},{1,3},{2,0},{3,1},{4,6},{5,7},{6,4},{7,5},{8,10},{9,11},{10,... | collective-permute-start | bytes 36872 | tf_op jit(solution)/shard_map/ppermute | solution.py:445
  72.0 2.0 %collective-permute-done.24.refs_1_ = f32[24,128]{1,0:T(8,128)S(1)} collective-permute-done((f32[24,128]{1,0:T(8,128)S(1)}, f32[24,128]{1,0:T(8,128)S(1)}, u32[]{:S(2)}, u32[]{:S(2)}) %collective-permute-start.24) | collective-permute-done | bytes 12320 | tf_op jit(solution)/shard_map/ppermute | solution.py:445
  (61 shorter events, 7.3 us)
Async XLA Ops:
  0.6 14.0 %copy-start.3 = (f32[12,128]{1,0:T(8,128)S(1)}, f32[12,128]{1,0:T(8,128)}, u32[]{:S(2)}) copy-start(f32[12,128]{1,0:T(8,128)} %site_ref.7) | copy-start | bytes 18436
  0.6 14.0 %collective-permute-start.1 = (bf16[12,32,128]{2,1,0:T(8,128)(2,1)}, bf16[12,32,128]{2,1,0:T(8,128)(2,1)S(1)}, u32[]{:S(2)}, u32[]{:S(2)}) collective-permute-start(bf16[12,32,128]{2,1,0:T(8,128)(2,1)} %refs_0_.1), channel_id=1, source_target_pairs={{0,28},{4,8},{8,4},{12,16},{16,12},{20,24},{24,20},{28,0},{1,29},{... | collective-permute-start | bytes 294920 | tf_op jit(solution)/shard_map/ppermute | solution.py:208
  4.1 10.6 %collective-permute-start = (bf16[12,32,128]{2,1,0:T(8,128)(2,1)}, bf16[12,32,128]{2,1,0:T(8,128)(2,1)S(1)}, u32[]{:S(2)}, u32[]{:S(2)}) collective-permute-start(bf16[12,32,128]{2,1,0:T(8,128)(2,1)} %refs_0_.1), channel_id=1, source_target_pairs={{0,4},{4,0},{8,12},{12,8},{16,20},{20,16},{24,28},{28,24},{1,5},{5... | collective-permute-start | bytes 294920 | tf_op jit(solution)/shard_map/ppermute | solution.py:209
  7.6 3.2 %copy-start = (bf16[20,12,128,128]{3,2,1,0:T(8,128)(2,1)S(1)}, bf16[20,12,128,128]{3,2,1,0:T(8,128)(2,1)}, u32[]{:S(2)}) copy-start(bf16[20,12,128,128]{3,2,1,0:T(8,128)(2,1)} %k_ref.9) | copy-start | bytes 23592964
  10.9 0.9 %copy-start.1 = (bf16[12,32,128]{2,1,0:T(8,128)(2,1)S(1)}, bf16[12,32,128]{2,1,0:T(8,128)(2,1)}, u32[]{:S(2)}) copy-start(bf16[12,32,128]{2,1,0:T(8,128)(2,1)} %refs_0_.1) | copy-start | bytes 294916
  11.7 9.0 %slice-start = ((s8[7864320]{0:T(1024)(128)(4,1)}), s8[3670016]{0:T(1024)(128)(4,1)S(1)}, s32[]{:S(2)}) async-start(s8[7864320]{0:T(1024)(128)(4,1)} %bitcast.2), calls=%async_computation | async-start | bytes 7340032
  13.8 2.4 %collective-permute-start.2 = (bf16[12,32,128]{2,1,0:T(8,128)(2,1)S(1)}, bf16[12,32,128]{2,1,0:T(8,128)(2,1)S(1)}, u32[]{:S(2)}, u32[]{:S(2)}) collective-permute-start(bf16[12,32,128]{2,1,0:T(8,128)(2,1)S(1)} %get-tuple-element.30), channel_id=1, source_target_pairs={{0,4},{4,0},{8,12},{12,8},{16,20},{20,16},{24,28},{28,24},{1,5},{5... | collective-permute-start | bytes 294920 | tf_op jit(solution)/shard_map/ppermute | solution.py:209
  14.3 6.0 %collective-permute-start.3 = (bf16[12,32,128]{2,1,0:T(8,128)(2,1)S(1)}, bf16[12,32,128]{2,1,0:T(8,128)(2,1)S(1)}, u32[]{:S(2)}, u32[]{:S(2)}) collective-permute-start(bf16[12,32,128]{2,1,0:T(8,128)(2,1)S(1)} %get-tuple-element.31), channel_id=1, source_target_pairs={{0,28},{4,8},{8,4},{12,16},{16,12},{20,24},{24,20},{28,0},{1,29},{... | collective-permute-start | bytes 294920 | tf_op jit(solution)/shard_map/ppermute | solution.py:208
  14.7 6.1 %slice-start.1 = ((s8[7864320]{0:T(1024)(128)(4,1)}), s8[4194304]{0:T(1024)(128)(4,1)S(1)}, s32[]{:S(2)}) async-start(s8[7864320]{0:T(1024)(128)(4,1)} %bitcast.2), calls=%async_computation.1 | async-start | bytes 8388608
  20.3 7.1 %copy-start.2 = (bf16[12,32,128]{2,1,0:T(8,128)(2,1)S(1)}, bf16[12,32,128]{2,1,0:T(8,128)(2,1)}, u32[]{:S(2)}) copy-start(bf16[12,32,128]{2,1,0:T(8,128)(2,1)} %refs_0_.1) | copy-start | bytes 294916
  20.4 5.4 %collective-permute-start.5 = (bf16[12,32,128]{2,1,0:T(8,128)(2,1)S(1)}, bf16[12,32,128]{2,1,0:T(8,128)(2,1)S(1)}, u32[]{:S(2)}, u32[]{:S(2)}) collective-permute-start(bf16[12,32,128]{2,1,0:T(8,128)(2,1)S(1)} %get-tuple-element.51.x_ref), channel_id=1, source_target_pairs={{0,28},{4,8},{8,4},{12,16},{16,12},{20,24},{24,20},{28,0},{1,29},{... | collective-permute-start | bytes 294920 | tf_op jit(solution)/shard_map/ppermute | solution.py:208
  20.4 5.3 %collective-permute-start.4 = (bf16[12,32,128]{2,1,0:T(8,128)(2,1)S(1)}, bf16[12,32,128]{2,1,0:T(8,128)(2,1)S(1)}, u32[]{:S(2)}, u32[]{:S(2)}) collective-permute-start(bf16[12,32,128]{2,1,0:T(8,128)(2,1)S(1)} %get-tuple-element.51.x_ref), channel_id=1, source_target_pairs={{0,4},{4,0},{8,12},{12,8},{16,20},{20,16},{24,28},{28,24},{1,5},{5... | collective-permute-start | bytes 294920 | tf_op jit(solution)/shard_map/ppermute | solution.py:209
  22.2 5.0 %collective-permute-start.6 = (bf16[12,32,128]{2,1,0:T(8,128)(2,1)S(1)}, bf16[12,32,128]{2,1,0:T(8,128)(2,1)S(1)}, u32[]{:S(2)}, u32[]{:S(2)}) collective-permute-start(bf16[12,32,128]{2,1,0:T(8,128)(2,1)S(1)} %get-tuple-element.33), channel_id=1, source_target_pairs={{0,4},{4,0},{8,12},{12,8},{16,20},{20,16},{24,28},{28,24},{1,5},{5... | collective-permute-start | bytes 294920 | tf_op jit(solution)/shard_map/ppermute | solution.py:209
  22.5 4.9 %collective-permute-start.7 = (bf16[12,32,128]{2,1,0:T(8,128)(2,1)S(1)}, bf16[12,32,128]{2,1,0:T(8,128)(2,1)S(1)}, u32[]{:S(2)}, u32[]{:S(2)}) collective-permute-start(bf16[12,32,128]{2,1,0:T(8,128)(2,1)S(1)} %get-tuple-element.34), channel_id=1, source_target_pairs={{0,28},{4,8},{8,4},{12,16},{16,12},{20,24},{24,20},{28,0},{1,29},{... | collective-permute-start | bytes 294920 | tf_op jit(solution)/shard_map/ppermute | solution.py:208
  27.5 6.6 %collective-permute-start.12 = (bf16[12,32,128]{2,1,0:T(8,128)(2,1)S(1)}, bf16[12,32,128]{2,1,0:T(8,128)(2,1)S(1)}, u32[]{:S(2)}, u32[]{:S(2)}) collective-permute-start(bf16[12,32,128]{2,1,0:T(8,128)(2,1)S(1)} %get-tuple-element.49.x_ref), channel_id=1, source_target_pairs={{0,28},{4,8},{8,4},{12,16},{16,12},{20,24},{24,20},{28,0},{1,29},{... | collective-permute-start | bytes 294920 | tf_op jit(solution)/shard_map/ppermute | solution.py:208
  30.3 3.8 %collective-permute-start.11 = (bf16[12,32,128]{2,1,0:T(8,128)(2,1)S(1)}, bf16[12,32,128]{2,1,0:T(8,128)(2,1)S(1)}, u32[]{:S(2)}, u32[]{:S(2)}) collective-permute-start(bf16[12,32,128]{2,1,0:T(8,128)(2,1)S(1)} %get-tuple-element.49.x_ref), channel_id=1, source_target_pairs={{0,4},{4,0},{8,12},{12,8},{16,20},{20,16},{24,28},{28,24},{1,5},{5... | collective-permute-start | bytes 294920 | tf_op jit(solution)/shard_map/ppermute | solution.py:209
  32.0 3.6 %collective-permute-start.13 = (bf16[12,32,128]{2,1,0:T(8,128)(2,1)S(1)}, bf16[12,32,128]{2,1,0:T(8,128)(2,1)S(1)}, u32[]{:S(2)}, u32[]{:S(2)}) collective-permute-start(bf16[12,32,128]{2,1,0:T(8,128)(2,1)S(1)} %get-tuple-element.36), channel_id=1, source_target_pairs={{0,4},{4,0},{8,12},{12,8},{16,20},{20,16},{24,28},{28,24},{1,5},{5... | collective-permute-start | bytes 294920 | tf_op jit(solution)/shard_map/ppermute | solution.py:209
  32.6 5.8 %collective-permute-start.14 = (bf16[12,32,128]{2,1,0:T(8,128)(2,1)S(1)}, bf16[12,32,128]{2,1,0:T(8,128)(2,1)S(1)}, u32[]{:S(2)}, u32[]{:S(2)}) collective-permute-start(bf16[12,32,128]{2,1,0:T(8,128)(2,1)S(1)} %get-tuple-element.37), channel_id=1, source_target_pairs={{0,28},{4,8},{8,4},{12,16},{16,12},{20,24},{24,20},{28,0},{1,29},{... | collective-permute-start | bytes 294920 | tf_op jit(solution)/shard_map/ppermute | solution.py:208
  32.7 10.4 %collective-permute-start.8 = (f32[2,32,128]{2,1,0:T(8,128)S(1)}, f32[2,32,128]{2,1,0:T(8,128)S(1)}, u32[]{:S(2)}, u32[]{:S(2)}) collective-permute-start(f32[2,32,128]{2,1,0:T(8,128)S(1)} %moments.1), channel_id=1, source_target_pairs={{0,4},{4,0},{8,12},{12,8},{16,20},{20,16},{24,28},{28,24},{1,5},{5... | collective-permute-start | bytes 98312 | tf_op jit(solution)/shard_map/ppermute | solution.py:216
  38.4 13.0 %collective-permute-start.16 = (bf16[12,32,128]{2,1,0:T(8,128)(2,1)S(1)}, bf16[12,32,128]{2,1,0:T(8,128)(2,1)S(1)}, u32[]{:S(2)}, u32[]{:S(2)}) collective-permute-start(bf16[12,32,128]{2,1,0:T(8,128)(2,1)S(1)} %get-tuple-element.47.x_ref), channel_id=1, source_target_pairs={{0,28},{4,8},{8,4},{12,16},{16,12},{20,24},{24,20},{28,0},{1,29},{... | collective-permute-start | bytes 294920 | tf_op jit(solution)/shard_map/ppermute | solution.py:208
  38.5 12.9 %collective-permute-start.15 = (bf16[12,32,128]{2,1,0:T(8,128)(2,1)S(1)}, bf16[12,32,128]{2,1,0:T(8,128)(2,1)S(1)}, u32[]{:S(2)}, u32[]{:S(2)}) collective-permute-start(bf16[12,32,128]{2,1,0:T(8,128)(2,1)S(1)} %get-tuple-element.47.x_ref), channel_id=1, source_target_pairs={{0,4},{4,0},{8,12},{12,8},{16,20},{20,16},{24,28},{28,24},{1,5},{5... | collective-permute-start | bytes 294920 | tf_op jit(solution)/shard_map/ppermute | solution.py:209
  40.0 12.8 %collective-permute-start.17 = (bf16[12,32,128]{2,1,0:T(8,128)(2,1)S(1)}, bf16[12,32,128]{2,1,0:T(8,128)(2,1)S(1)}, u32[]{:S(2)}, u32[]{:S(2)}) collective-permute-start(bf16[12,32,128]{2,1,0:T(8,128)(2,1)S(1)} %get-tuple-element.39), channel_id=1, source_target_pairs={{0,4},{4,0},{8,12},{12,8},{16,20},{20,16},{24,28},{28,24},{1,5},{5... | collective-permute-start | bytes 294920 | tf_op jit(solution)/shard_map/ppermute | solution.py:209
  40.6 12.3 %collective-permute-start.18 = (bf16[12,32,128]{2,1,0:T(8,128)(2,1)S(1)}, bf16[12,32,128]{2,1,0:T(8,128)(2,1)S(1)}, u32[]{:S(2)}, u32[]{:S(2)}) collective-permute-start(bf16[12,32,128]{2,1,0:T(8,128)(2,1)S(1)} %get-tuple-element.40), channel_id=1, source_target_pairs={{0,28},{4,8},{8,4},{12,16},{16,12},{20,24},{24,20},{28,0},{1,29},{... | collective-permute-start | bytes 294920 | tf_op jit(solution)/shard_map/ppermute | solution.py:208
  43.1 4.3 %collective-permute-start.9 = (f32[2,32,128]{2,1,0:T(8,128)S(1)}, f32[2,32,128]{2,1,0:T(8,128)S(1)}, u32[]{:S(2)}, u32[]{:S(2)}) collective-permute-start(f32[2,32,128]{2,1,0:T(8,128)S(1)} %add.34), channel_id=1, source_target_pairs={{0,8},{4,12},{8,0},{12,4},{16,24},{20,28},{24,16},{28,20},{1,9},{5... | collective-permute-start | bytes 98312 | tf_op jit(solution)/shard_map/ppermute | solution.py:216
  47.5 3.9 %collective-permute-start.10 = (f32[2,32,128]{2,1,0:T(8,128)S(1)}, f32[2,32,128]{2,1,0:T(8,128)S(1)}, u32[]{:S(2)}, u32[]{:S(2)}) collective-permute-start(f32[2,32,128]{2,1,0:T(8,128)S(1)} %add.35), channel_id=1, source_target_pairs={{0,16},{4,20},{8,24},{12,28},{16,0},{20,4},{24,8},{28,12},{1,17},{... | collective-permute-start | bytes 98312 | tf_op jit(solution)/shard_map/ppermute | solution.py:216
  53.0 5.3 %collective-permute-start.20 = (bf16[12,32,128]{2,1,0:T(8,128)(2,1)S(1)}, bf16[12,32,128]{2,1,0:T(8,128)(2,1)S(1)}, u32[]{:S(2)}, u32[]{:S(2)}) collective-permute-start(bf16[12,32,128]{2,1,0:T(8,128)(2,1)S(1)} %get-tuple-element.43.w_ref.refs_3_), channel_id=1, source_target_pairs={{0,28},{4,8},{8,4},{12,16},{16,12},{20,24},{24,20},{28,0},{1,29},{... | collective-permute-start | bytes 294920 | tf_op jit(solution)/shard_map/ppermute | solution.py:208
  53.1 5.2 %collective-permute-start.19 = (bf16[12,32,128]{2,1,0:T(8,128)(2,1)S(1)}, bf16[12,32,128]{2,1,0:T(8,128)(2,1)S(1)}, u32[]{:S(2)}, u32[]{:S(2)}) collective-permute-start(bf16[12,32,128]{2,1,0:T(8,128)(2,1)S(1)} %get-tuple-element.43.w_ref.refs_3_), channel_id=1, source_target_pairs={{0,4},{4,0},{8,12},{12,8},{16,20},{20,16},{24,28},{28,24},{1,5},{5... | collective-permute-start | bytes 294920 | tf_op jit(solution)/shard_map/ppermute | solution.py:209
  58.3 7.0 %copy-start.6 = (s32[12,128]{1,0:T(8,128)S(1)}, s32[12,128]{1,0:T(8,128)}, u32[]{:S(2)}) copy-start(s32[12,128]{1,0:T(8,128)} %atom_ref.1) | copy-start | bytes 18436
  60.8 1.3 %collective-permute-start.21 = (f32[12,3,128]{2,1,0:T(4,128)S(1)}, f32[12,3,128]{2,1,0:T(4,128)S(1)}, u32[]{:S(2)}, u32[]{:S(2)}) collective-permute-start(f32[12,3,128]{2,1,0:T(4,128)S(1)} %get-tuple-element.45), channel_id=1, source_target_pairs={{0,4},{4,0},{8,12},{12,8},{16,20},{20,16},{24,28},{28,24},{1,5},{5... | collective-permute-start | bytes 55304 | tf_op jit(solution)/shard_map/ppermute | solution.py:209
  61.2 4.2 %collective-permute-start.22 = (f32[12,3,128]{2,1,0:T(4,128)S(1)}, f32[12,3,128]{2,1,0:T(4,128)S(1)}, u32[]{:S(2)}, u32[]{:S(2)}) collective-permute-start(f32[12,3,128]{2,1,0:T(4,128)S(1)} %get-tuple-element.46), channel_id=1, source_target_pairs={{0,28},{4,8},{8,4},{12,16},{16,12},{20,24},{24,20},{28,0},{1,29},{... | collective-permute-start | bytes 55304 | tf_op jit(solution)/shard_map/ppermute | solution.py:208
  65.7 3.7 %collective-permute-start.23 = (f32[24,128]{1,0:T(8,128)S(1)}, f32[24,128]{1,0:T(8,128)S(1)}, u32[]{:S(2)}, u32[]{:S(2)}) collective-permute-start(f32[24,128]{1,0:T(8,128)S(1)} %packed.1), channel_id=1, source_target_pairs={{0,1},{1,0},{2,3},{3,2},{4,5},{5,4},{6,7},{7,6},{8,9},{9,8},{10,11... | collective-permute-start | bytes 36872 | tf_op jit(solution)/shard_map/ppermute | solution.py:445
  69.4 4.6 %collective-permute-start.24 = (f32[24,128]{1,0:T(8,128)S(1)}, f32[24,128]{1,0:T(8,128)S(1)}, u32[]{:S(2)}, u32[]{:S(2)}) collective-permute-start(f32[24,128]{1,0:T(8,128)S(1)} %add.39.refs_0_), channel_id=1, source_target_pairs={{0,2},{1,3},{2,0},{3,1},{4,6},{5,7},{6,4},{7,5},{8,10},{9,11},{10,... | collective-permute-start | bytes 36872 | tf_op jit(solution)/shard_map/ppermute | solution.py:445
  (3 other events, 2.1 us)

commit v4 on v3

--- a/solution.py
+++ b/solution.py
@@ -7,6 +7,7 @@
 from jax.experimental import pallas as pl
 from jax.experimental.pallas import tpu as pltpu
 from jax.sharding import PartitionSpec as P
+
 
 ATOMS = 32
 REACH = 12
@@ -43,23 +44,88 @@
     return jnp.asarray(table)
 
 
-def prepared(columns, bond_dir, chemical_potential):
+def opening(columns, x, k, bond_dir, chemical_potential):
     rows, slots = columns.shape
-
-    def kernel(col_ref, bond_ref, mu_ref, table_ref, flag_ref, ids_ref, out_ref, coeff_ref):
+    probes, block = x.shape[1:]
+    frame = rows + 2 * REACH
+    halves = (0, HALF_SLOTS, slots)
+
+    def kernel(col_hbm, x_hbm, k_hbm, bond_hbm, table_hbm, mu_ref, *refs):
+        flag_ref, ids_ref, out_ref, coeff_ref, own_ref, even_ref, odd_ref, kv_ref, kt_ref = refs[:9]
+        acc, col_sm, col_vm, xv, bond_vm, table_vm, sems, small = refs[9:]
         me = lax.axis_index("clus")
-        col = col_ref[...]
-        ids_ref[...] = jnp.where(col >= 0, col - me * rows + REACH, rows + 2 * REACH)
+
+        def load(c, half):
+            part = pl.ds(halves[half], halves[half + 1] - halves[half])
+            return pltpu.make_async_copy(
+                k_hbm.at[part, c], kv_ref.at[part, c], sems.at[half, c]
+            )
+
+        pairs = ((col_hbm, col_vm), (col_hbm, col_sm), (x_hbm, xv), (table_hbm, table_vm), (bond_hbm, bond_vm))
+        copies = [pltpu.make_async_copy(a, b, small.at[i]) for i, (a, b) in enumerate(pairs)]
+        for copy in copies:
+            copy.start()
+        for c in range(rows):
+            load(c, 0).start()
+        acc[...] = jnp.zeros_like(acc)
+        copies[0].wait()
+        col = col_vm[...]
         late = lax.broadcasted_iota(jnp.int32, col.shape, 1) >= HALF_SLOTS
-        flag_ref[0] = (jnp.max(jnp.where(late, col, -1)) >= 0).astype(jnp.int32)
-        flag_ref[1] = lax.rem(me, 2)
+        many = jnp.max(jnp.where(late, col, -1)) >= 0
+        flag_ref[0] = many.astype(jnp.int32)
+        odd = lax.rem(me, 2)
+        flag_ref[1] = odd
+
+        @pl.when(many)
+        def _():
+            for c in range(rows):
+                load(c, 1).start()
+
+        ids_ref[...] = jnp.where(col >= 0, col - me * rows + REACH, frame)
+        for copy in copies[1:]:
+            copy.wait()
         for axis in range(3):
-            out_ref[axis * rows : (axis + 1) * rows] = bond_ref[axis].astype(f32)
-        energy = (table_ref[7:8] - mu_ref[0]) / SMEARING_TEMP
+            out_ref[axis * rows : (axis + 1) * rows] = bond_vm[axis].astype(f32)
+        energy = (table_vm[7:8] - mu_ref[0]) / SMEARING_TEMP
         occupied = 1.0 / (1.0 + jnp.exp(energy))
-        total = jnp.sum(table_ref[...] * occupied, axis=1, keepdims=True)
+        total = jnp.sum(table_vm[...] * occupied, axis=1, keepdims=True)
         coeff_ref[...] = jnp.broadcast_to(total, coeff_ref.shape)
 
+        def body(last):
+            for half in range(last):
+                for c in range(rows):
+                    load(c, half).wait()
+                    xc = xv[c]
+                    for first in range(halves[half], halves[half + 1], 4):
+                        parts, targets = [], []
+                        for m in range(first, min(first + 4, halves[half + 1]), 2):
+                            pair = [kv_ref[m, c], kv_ref[m + 1, c]]
+                            out = dot(xc, jnp.concatenate(pair, axis=1), NN)
+                            parts += [out[:, :block], out[:, block:]]
+                            for slot in (m, m + 1):
+                                at = col_sm[c, slot]
+                                targets.append(jnp.where(at >= 0, at - me * rows + REACH, frame))
+                            kt_ref[m, c] = pair[0].T
+                            kt_ref[m + 1, c] = pair[1].T
+                        values = [acc[t] + part for t, part in zip(targets, parts)]
+                        for t, value in zip(targets, values):
+                            acc[t] = value
+
+        @pl.when(many)
+        def _():
+            body(2)
+
+        @pl.when(jnp.logical_not(many))
+        def _():
+            body(1)
+
+        own_ref[...] = acc[pl.ds(REACH, rows)]
+        even_ref[...] = acc[pl.ds((1 - odd) * (REACH + rows), REACH)].astype(bf16)
+        odd_ref[...] = acc[pl.ds(odd * (REACH + rows), REACH)].astype(bf16)
+
+    side = jax.ShapeDtypeStruct((REACH, probes, block), bf16)
+    blocks = jax.ShapeDtypeStruct(k.shape, k.dtype)
+    hbm = pl.BlockSpec(memory_space=pltpu.HBM)
     return pl.pallas_call(
         kernel,
         out_shape=[
@@ -67,12 +133,27 @@
             jax.ShapeDtypeStruct((rows, slots), jnp.int32),
             jax.ShapeDtypeStruct((3 * rows, slots), f32),
             jax.ShapeDtypeStruct((8, 128), f32),
+            jax.ShapeDtypeStruct((rows, probes, block), f32),
+            side,
+            side,
+            blocks,
+            blocks,
         ],
-        in_specs=[VM, VM, SM, VM],
-        out_specs=[SM, VM, VM, VM],
-        name="prepared",
-        **params(1000, 50000),
-    )(columns, bond_dir, chemical_potential, quadrature())
+        in_specs=[hbm] * 5 + [SM],
+        out_specs=[SM] + [VM] * 8,
+        scratch_shapes=[
+            pltpu.VMEM((frame + 1, probes, block), f32),
+            pltpu.SMEM((rows, slots), jnp.int32),
+            pltpu.VMEM((rows, slots), jnp.int32),
+            pltpu.VMEM(x.shape, x.dtype),
+            pltpu.VMEM(bond_dir.shape, bond_dir.dtype),
+            pltpu.VMEM((8, 128), f32),
+            pltpu.SemaphoreType.DMA((2, rows)),
+            pltpu.SemaphoreType.DMA((5,)),
+        ],
+        name="opening",
+        **params(2 * slots * rows * probes * block * block, k.size * 2),
+    )(*(pltpu.with_memory_space_constraint(a, pltpu.HBM) for a in (columns, x, k, bond_dir, quadrature())), chemical_potential)
 
 
 def moments(coeffs, v, first, second):
@@ -172,7 +253,7 @@
 
 
 def unpacked(parts, rows, orbitals):
-    height, block = parts[0].shape
+    _, block = parts[0].shape
     lines = rows * ATOMS // block
 
     def kernel(*refs):
@@ -206,16 +287,14 @@
     paired = [(i, i ^ 1) for i in range(count)]
     shifted = [(i, (i + 1 if i % 2 else i - 1) % count) for i in range(count)]
     crossed = lax.ppermute(odd_side, "clus", shifted)
-    return lax.ppermute(even_side, "clus", paired), crossed
-
-
-def doubled_sum(part, axis):
-    step = 1
-    while step < lax.axis_size(axis):
-        pairs = [(i, i ^ step) for i in range(lax.axis_size(axis))]
-        part = part + lax.ppermute(part, axis, pairs)
-        step *= 2
-    return part
+    even = lax.ppermute(even_side, "clus", paired)
+    return even, crossed
+
+
+def doubled(index, part, axis):
+    count = lax.axis_size(axis)
+    other = lax.ppermute(part, axis, [(i, i ^ (1 << index)) for i in range(count)])
+    return part + other
 
 
 def by_size(flag, slots, body):
@@ -233,8 +312,7 @@
     probes = x.shape[1]
     frame = rows + 2 * REACH
 
-    def kernel(turn, flag_ref, ids_ref, x_ref, k_ref, own_ref, even_ref, odd_ref, *rest):
-        acc = rest[-1]
+    def kernel(flag_ref, ids_ref, x_ref, k_ref, own_ref, even_ref, odd_ref, acc):
         acc[...] = jnp.zeros_like(acc)
 
         def body(count):
@@ -247,9 +325,6 @@
                         out = dot(xc, jnp.concatenate(pair, axis=1), NN)
                         parts += [out[:, :block], out[:, block:]]
                         targets += [ids_ref[c, m], ids_ref[c, m + 1]]
-                        if turn:
-                            rest[0][m, c] = pair[0].T
-                            rest[0][m + 1, c] = pair[1].T
                     values = [acc[t] + part for t, part in zip(targets, parts)]
                     for t, value in zip(targets, values):
                         acc[t] = value
@@ -261,21 +336,15 @@
         odd_ref[...] = acc[pl.ds(odd * (REACH + rows), REACH)].astype(bf16)
 
     side = jax.ShapeDtypeStruct((REACH, probes, block), bf16)
-    shapes = [jax.ShapeDtypeStruct((rows, probes, block), f32), side, side]
-
-    def call(turn):
-        out = shapes + ([jax.ShapeDtypeStruct(k.shape, k.dtype)] if turn else [])
-        return pl.pallas_call(
-            functools.partial(kernel, turn),
-            out_shape=out,
-            in_specs=[SM, SM, VM, VM],
-            out_specs=[VM] * len(out),
-            scratch_shapes=[pltpu.VMEM((frame + 1, probes, block), f32)],
-            name="spread_turn" if turn else "spread",
-            **params(2 * slots * rows * probes * block * block, k.size * 2),
-        )(flag, ids, x, k)
-
-    return call
+    return pl.pallas_call(
+        kernel,
+        out_shape=[jax.ShapeDtypeStruct((rows, probes, block), f32), side, side],
+        in_specs=[SM, SM, VM, VM],
+        out_specs=[VM] * 3,
+        scratch_shapes=[pltpu.VMEM((frame + 1, probes, block), f32)],
+        name="spread",
+        **params(2 * slots * rows * probes * block * block, k.size * 2),
+    )(flag, ids, x, k)
 
 
 def fill_frame(frame_ref, odd, own, even, crossed):
@@ -315,67 +384,40 @@
     )(flag, ids, x, even, crossed, kt, own, onsite)
 
 
-def images(flag, v, w, k):
-    slots, rows, block, _ = k.shape
+def folded(value):
+    parts = [value[i : i + 8] for i in range(0, value.shape[0], 8)]
+    while len(parts) > 1:
+        parts = [a + b for a, b in zip(parts[::2], parts[1::2])]
+    return parts[0]
+
+
+def near_forces(flag, ids, bond, v, v_even, v_crossed, w, k, kt):
+    slots, rows, block, _ = kt.shape
     probes = v.shape[1]
-
-    def kernel(flag_ref, v_ref, w_ref, k_ref, out_ref):
+    frame = rows + 2 * REACH
+
+    def kernel(flag_ref, ids_ref, bond_ref, *refs):
+        v_ref, ve_ref, vo_ref, w_ref, k_ref, kt_ref, acc, image_ref, vf = refs
+        fill_frame(vf, flag_ref[1], v_ref, ve_ref, vo_ref)
+        acc[...] = jnp.zeros_like(acc)
+
         def body(count):
             for c in range(rows):
+                mine = w_ref[c].astype(f32)
                 left = jnp.concatenate([w_ref[c], v_ref[c]], axis=0)
+                row = [jnp.zeros((8, block), f32)] * 3
                 for m in range(0, count, 2):
-                    out = dot(left, jnp.concatenate([k_ref[m, c], k_ref[m + 1, c]], axis=1), NN)
-                    out_ref[m, c] = out[:, :block]
-                    out_ref[m + 1, c] = out[:, block:]
-
-        by_size(flag_ref, slots, body)
-
-    return pl.pallas_call(
-        kernel,
-        out_shape=jax.ShapeDtypeStruct((slots, rows, 2 * probes, block), f32),
-        in_specs=[SM, VM, VM, VM],
-        out_specs=VM,
-        name="images",
-        **params(4 * slots * rows * probes * block * block, k.size * 2),
-    )(flag, v, w, k)
-
-
-def forces(flag, ids, bond, v, v_even, v_crossed, w, w_even, w_crossed, kt, image):
-    slots, rows, block, _ = kt.shape
-    probes = v.shape[1]
-    frame_rows = rows + 2 * REACH
-    sub = 8
-
-    def folded(value):
-        parts = [value[i : i + sub] for i in range(0, value.shape[0], sub)]
-        while len(parts) > 1:
-            parts = [a + b for a, b in zip(parts[::2], parts[1::2])]
-        return parts[0]
-
-    def kernel(flag_ref, ids_ref, bond_ref, *refs):
-        v_ref, ve_ref, vo_ref, w_ref, we_ref, wo_ref, kt_ref, image_ref = refs[:8]
-        own_ref, even_ref, odd_ref, vf, wf, acc = refs[8:]
-        odd = flag_ref[1]
-        fill_frame(vf, odd, v_ref, ve_ref, vo_ref)
-        fill_frame(wf, odd, w_ref, we_ref, wo_ref)
-        acc[...] = jnp.zeros_like(acc)
-
-        def body(count):
-            for c in range(rows):
-                mine = jnp.concatenate([w_ref[c], v_ref[c]], axis=0).astype(f32)
-                row = [jnp.zeros((sub, block), f32)] * 3
-                for m in range(0, count, 2):
-                    far = []
-                    for slot in (m, m + 1):
+                    two = (m, m + 1)
+                    far = [vf[ids_ref[c, slot]] for slot in two]
+                    out = dot(left, jnp.concatenate([k_ref[slot, c] for slot in two], axis=1), NN)
+                    weights = jnp.concatenate([kt_ref[slot, c] for slot in two], axis=1)
+                    back = dot(jnp.concatenate(far, axis=0), weights, NN)
+                    for i, slot in enumerate(two):
                         d = ids_ref[c, slot]
-                        far.append(jnp.concatenate([vf[d], wf[d]], axis=0))
-                    weights = jnp.concatenate([kt_ref[m, c], kt_ref[m + 1, c]], axis=1)
-                    out = dot(jnp.concatenate(far, axis=0), weights, NN)
-                    direct_parts = [out[: 2 * probes, :block], out[2 * probes :, block:]]
-                    for slot, other, part in zip((m, m + 1), far, direct_parts):
-                        d = ids_ref[c, slot]
-                        row_part = folded(mine * part)
-                        col_part = folded(other.astype(f32) * image_ref[slot, c])
+                        lanes = slice(i * block, (i + 1) * block)
+                        image_ref[slot, c] = out[probes:, lanes]
+                        col_part = folded(far[i].astype(f32) * out[:probes, lanes])
+                        row_part = folded(mine * back[i * probes : (i + 1) * probes, lanes])
                         for axis in range(3):
                             b = bond_ref[axis * rows + c, slot]
                             row[axis] = row[axis] + b * row_part
@@ -385,6 +427,55 @@
 
         by_size(flag_ref, slots, body)
 
+    return pl.pallas_call(
+        kernel,
+        out_shape=[
+            jax.ShapeDtypeStruct((frame + 1, 3, 8, block), f32),
+            jax.ShapeDtypeStruct((slots, rows, probes, block), f32),
+        ],
+        in_specs=[SM, SM, SM] + [VM] * 6,
+        out_specs=[VM] * 2,
+        scratch_shapes=[pltpu.VMEM((frame + 1, probes, block), bf16)],
+        name="near_forces",
+        **params(6 * slots * rows * probes * block * block, k.size * 4),
+    )(flag, ids, bond, v, v_even, v_crossed, w, k, kt)
+
+
+def far_forces(flag, ids, bond, v, w, w_even, w_crossed, kt, image, started):
+    slots, rows, block, _ = kt.shape
+    probes = v.shape[1]
+    frame = rows + 2 * REACH
+
+    def kernel(flag_ref, ids_ref, bond_ref, *refs):
+        v_ref, w_ref, we_ref, wo_ref, kt_ref, image_ref, start_ref = refs[:7]
+        own_ref, even_ref, odd_ref, wf, acc = refs[7:]
+        odd = flag_ref[1]
+        fill_frame(wf, odd, w_ref, we_ref, wo_ref)
+        acc[...] = start_ref[...]
+
+        def body(count):
+            for c in range(rows):
+                mine = v_ref[c].astype(f32)
+                row = [jnp.zeros((8, block), f32)] * 3
+                for m in range(0, count, 2):
+                    two = (m, m + 1)
+                    far = [wf[ids_ref[c, slot]] for slot in two]
+                    weights = jnp.concatenate([kt_ref[slot, c] for slot in two], axis=1)
+                    back = dot(jnp.concatenate(far, axis=0), weights, NN)
+                    for i, slot in enumerate(two):
+                        d = ids_ref[c, slot]
+                        lanes = slice(i * block, (i + 1) * block)
+                        col_part = folded(far[i].astype(f32) * image_ref[slot, c])
+                        row_part = folded(mine * back[i * probes : (i + 1) * probes, lanes])
+                        for axis in range(3):
+                            b = bond_ref[axis * rows + c, slot]
+                            row[axis] = row[axis] + b * row_part
+                            acc[d, axis] = acc[d, axis] + b * col_part
+                for axis in range(3):
+                    acc[c + REACH, axis] = acc[c + REACH, axis] - row[axis]
+
+        by_size(flag_ref, slots, body)
+
         def taken(start, count):
             return DECAY * jnp.sum(acc[pl.ds(start, count)], axis=2)
 
@@ -393,47 +484,54 @@
         odd_ref[...] = taken(odd * (REACH + rows), REACH)
 
     side = jax.ShapeDtypeStruct((REACH, 3, block), f32)
-    frame = pltpu.VMEM((frame_rows + 1, probes, block), bf16)
     return pl.pallas_call(
         kernel,
         out_shape=[jax.ShapeDtypeStruct((rows, 3, block), f32), side, side],
-        in_specs=[SM, SM, SM] + [VM] * 8,
+        in_specs=[SM, SM, SM] + [VM] * 7,
         out_specs=[VM] * 3,
-        scratch_shapes=[frame, frame, pltpu.VMEM((frame_rows + 1, 3, sub, block), f32)],
-        name="forces",
-        **params(4 * slots * rows * probes * block * block, kt.size * 2 + image.size * 4),
-    )(flag, ids, bond, v, v_even, v_crossed, w, w_even, w_crossed, kt, image)
+        scratch_shapes=[
+            pltpu.VMEM((frame + 1, probes, block), bf16),
+            pltpu.VMEM((frame + 1, 3, 8, block), f32),
+        ],
+        name="far_forces",
+        **params(2 * slots * rows * probes * block * block, kt.size * 2 + image.size * 4),
+    )(flag, ids, bond, v, w, w_even, w_crossed, kt, image, started)
 
 
 def local(probes, onsite, hopping, block_col, atom_of, bond_dir, chemical_potential):
     rows, _, block = probes.shape
     orbitals = float(rows * lax.axis_size("clus") * block)
-    flag, ids, bond, coeffs = prepared(
-        block_col.T, jnp.transpose(bond_dir, (0, 2, 1)), chemical_potential
-    )
     x = probes
     even, crossed = exchange(x, x)
     v_even, v_crossed = even, crossed
+    flag, ids, bond, coeffs, *outs, k, kt = opening(
+        block_col.T, x, hopping, jnp.transpose(bond_dir, (0, 2, 1)), chemical_potential
+    )
+    rounds = (lax.axis_size("clus") - 1).bit_length()
     cheb = [probes]
     for term in range(1, ORDER + 1):
-        outs = spread(flag, ids, x, hopping)(term == 1)
-        if term == 1:
-            turned = outs[3]
-        back_even, back_crossed = exchange(outs[1], outs[2])
-        image = direct(flag, ids, x, even, crossed, turned, outs[0], onsite)
+        if term == 3:
+            sums = doubled(0, moments(coeffs, *cheb), "clus")
+        if term > 1:
+            outs = spread(flag, ids, x, k)
+        own, to_even, to_odd = outs
+        back_even, back_crossed = exchange(to_even, to_odd)
+        if term > 2:
+            sums = doubled(term - 2, sums, "clus")
+        image = direct(flag, ids, x, even, crossed, kt, own, onsite)
         if term == ORDER:
             break
         image = image + (back_even.astype(f32) + back_crossed.astype(f32))
         cheb.append(image if term == 1 else 2.0 * image - cheb[-2].astype(f32))
         x = cheb[-1].astype(bf16)
         even, crossed = exchange(x, x)
-        if term == 2:
-            sums = doubled_sum(moments(coeffs, *cheb), "clus")
+    for index in range(3, rounds):
+        sums = doubled(index, sums, "clus")
     weighted, head = closed(coeffs, sums, orbitals, cheb, image, back_even, back_crossed)
     w_even, w_crossed = exchange(weighted, weighted)
-    image = images(flag, probes, weighted, hopping)
-    own, to_even, to_odd = forces(
-        flag, ids, bond, probes, v_even, v_crossed, weighted, w_even, w_crossed, turned, image
+    started, image = near_forces(flag, ids, bond, probes, v_even, v_crossed, weighted, k, kt)
+    own, to_even, to_odd = far_forces(
+        flag, ids, bond, probes, weighted, w_even, w_crossed, kt, image, started
     )
     from_even, from_odd = exchange(to_even, to_odd)
     part = packed(head, own, from_even, from_odd, atom_of)

time: 75 us -> 71.3 us (0.951)
  local copies, waits for them, and re-layouts: 6.23 us -> 0.01 us
  Pallas kernels: 18 us -> 21.5 us
  waiting for transfers between devices: 24.1 us -> 22.9 us
    unnamed x20 -> x6, local copies, waits for them, and re-layouts: 6.23 us -> 0.01 us
    pallas_call x7 -> x6, Pallas kernels: 11 us -> 14.4 us  [the longest x1 5.11 us: opening(): pl.pallas_call(kernel, out_shape=[jax.ShapeDtypeStruct((2,), jnp.int32),...]
    ppermute x10, waiting for transfers between devices: 12.9 us -> 11.9 us  [exchange(): crossed = lax.ppermute(odd_side, 'clus', shifted)]
  transfers between devices with their start and end apart: 25 -> 25, of which waited for: 10 -> 11; matrix products, arithmetic and copies ran while one was open for 0% -> 0% of each run, Pallas kernels for 19% -> 26%
where the time goes in v4:
time: 71.3 us; the launch traced here: 71.1 us
  starting transfers between devices  24.8 us (35%)
  waiting for transfers between devices  22.9 us (32%)
  Pallas kernels  21.5 us (30%)
  between operations  1.71 us (2%)
    ppermute x10, starting transfers between devices, exchange(): crossed = lax.ppermute(odd_side, 'clus', shifted)  12.3 us
    ppermute x10, waiting for transfers between devices, exchange(): crossed = lax.ppermute(odd_side, 'clus', shifted)  11.9 us
    ppermute x3, waiting for transfers between devices, doubled(): lax.ppermute(part, axis, [(i, i ^ 1 << index) for i in range(count)])  6.85 us
    pallas_call x4, Pallas kernels, direct(): pl.pallas_call(kernel, out_shape=jax.ShapeDtypeStruct((rows, probes, bloc...  5.9 us
    ppermute x10, starting transfers between devices, exchange(): even = lax.ppermute(even_side, 'clus', paired)  5.53 us
    pallas_call x1, Pallas kernels, opening(): pl.pallas_call(kernel, out_shape=[jax.ShapeDtypeStruct((2,), jnp.int32),...  5.11 us
    pallas_call x3, Pallas kernels, spread(): pl.pallas_call(kernel, out_shape=[jax.ShapeDtypeStruct((rows, probes, blo...  4.38 us
    ppermute x2, starting transfers between devices, local(): lax.ppermute(part, 'probe', [(i, i ^ step) for i in range(count)])  4.2 us
  transfers between devices with their start and end apart: 25, of which 11 were waited for; matrix products, arithmetic and copies ran while one was open for 0% of the time, Pallas kernels for 26%

profile of v4, /device:TPU:0, one launch (start us, length us, event | category | flops | bytes accessed | tf_op | source)
XLA Modules:
  0.0 71.1 jit_solution(18382479444341580528)
XLA Ops:
  0.7 3.4 %collective-permute-start.1 = (bf16[12,32,128]{2,1,0:T(8,128)(2,1)}, bf16[12,32,128]{2,1,0:T(8,128)(2,1)S(1)}, u32[]{:S(2)}, u32[]{:S(2)}) collective-permute-start(bf16[12,32,128]{2,1,0:T(8,128)(2,1)} %refs_0_.3), channel_id=1, source_target_pairs={{0,28},{4,8},{8,4},{12,16},{16,12},{20,24},{24,20},{28,0},{1,29},{... | collective-permute-start | bytes 294920 | tf_op jit(solution)/shard_map/ppermute | solution.py:289
  4.7 5.1 %opening.1 = (s32[2]{0:T(128)S(1)}, s32[12,20]{1,0:T(8,128)S(1)}, f32[36,20]{1,0:T(8,128)S(1)}, f32[8,128]{1,0:T(8,128)S(1)}, f32[12,32,128]{2,1,0:T(8,128)S(1)}...) custom-call(s32[12,20]{1,0:T(8,128)} %bitcast.3, ...), custom_call_target="tpu_custom_call" | custom-call | flops 251658240 | bytes 7864320 | tf_op jit(solution)/shard_map/opening/pallas_call | solution.py:129
  9.9 0.6 collective-permute-start.2
  10.8 1.4 %direct.4 = f32[12,32,128]{2,1,0:T(8,128)S(1)} custom-call(s32[2]{0:T(128)S(1)} %get-tuple-element.29.flag_ref, s32[12,20]{1,0:T(8,128)S(1)} %get-tuple-element.30.ids_ref, bf16[12,32,128]{2,1,0:T(8,128)(2,1)S(1)} %copy-done, bf16[12,32,128]{2,1,0:T(8,128)(2,1)S(1)} %collective-permute-done.e_ref.refs_1_, ...), custom_call_target="tpu_custom_call" | custom-call | flops 251658240 | bytes 7864320 | tf_op jit(solution)/shard_map/direct/pallas_call | solution.py:376
  12.2 4.2 %collective-permute-done.3 = bf16[12,32,128]{2,1,0:T(8,128)(2,1)S(1)} collective-permute-done((bf16[12,32,128]{2,1,0:T(8,128)(2,1)S(1)}, bf16[12,32,128]{2,1,0:T(8,128)(2,1)S(1)}, u32[]{:S(2)}, u32[]{:S(2)}) %collective-permute-start.3) | collective-permute-done | bytes 98336 | tf_op jit(solution)/shard_map/ppermute | solution.py:289
  16.5 1.3 %collective-permute-start.4 = (bf16[12,32,128]{2,1,0:T(8,128)(2,1)S(1)}, bf16[12,32,128]{2,1,0:T(8,128)(2,1)S(1)}, u32[]{:S(2)}, u32[]{:S(2)}) collective-permute-start(bf16[12,32,128]{2,1,0:T(8,128)(2,1)S(1)} %get-tuple-element.57.x_ref), channel_id=1, source_target_pairs={{0,4},{4,0},{8,12},{12,8},{16,20},{20,16},{24,28},{28,24},{1,5},{5... | collective-permute-start | bytes 294920 | tf_op jit(solution)/shard_map/ppermute | solution.py:290
  17.8 1.5 %spread.3 = (f32[12,32,128]{2,1,0:T(8,128)S(1)}, bf16[12,32,128]{2,1,0:T(8,128)(2,1)S(1)}, bf16[12,32,128]{2,1,0:T(8,128)(2,1)S(1)}) custom-call(s32[2]{0:T(128)S(1)} %get-tuple-element.29.flag_ref, s32[12,20]{1,0:T(8,128)S(1)} %get-tuple-element.30.ids_ref, bf16[12,32,128]{2,1,0:T(8,128)(2,1)S(1)} %get-tuple-element.57.x_ref, ...), custom_call_target="tpu_custom_call" | custom-call | flops 251658240 | bytes 7864320 | tf_op jit(solution)/shard_map/spread/pallas_call | solution.py:339
  19.3 1.8 %collective-permute-start.7 = (bf16[12,32,128]{2,1,0:T(8,128)(2,1)S(1)}, bf16[12,32,128]{2,1,0:T(8,128)(2,1)S(1)}, u32[]{:S(2)}, u32[]{:S(2)}) collective-permute-start(bf16[12,32,128]{2,1,0:T(8,128)(2,1)S(1)} %get-tuple-element.38), channel_id=1, source_target_pairs={{0,28},{4,8},{8,4},{12,16},{16,12},{20,24},{24,20},{28,0},{1,29},{... | collective-permute-start | bytes 294920 | tf_op jit(solution)/shard_map/ppermute | solution.py:289
  21.2 0.7 collective-permute-done.5.o_ref
  21.8 1.6 %direct.5 = f32[12,32,128]{2,1,0:T(8,128)S(1)} custom-call(s32[2]{0:T(128)S(1)} %get-tuple-element.29.flag_ref, s32[12,20]{1,0:T(8,128)S(1)} %get-tuple-element.30.ids_ref, bf16[12,32,128]{2,1,0:T(8,128)(2,1)S(1)} %get-tuple-element.57.x_ref, bf16[12,32,128]{2,1,0:T(8,128)(2,1)S(1)} %collective-permute-done.4.e_ref, ...), custom_call_target="tpu_custom_call" | custom-call | flops 251658240 | bytes 7864320 | tf_op jit(solution)/shard_map/direct/pallas_call | solution.py:376
  23.5 0.9 %collective-permute-done.7 = bf16[12,32,128]{2,1,0:T(8,128)(2,1)S(1)} collective-permute-done((bf16[12,32,128]{2,1,0:T(8,128)(2,1)S(1)}, bf16[12,32,128]{2,1,0:T(8,128)(2,1)S(1)}, u32[]{:S(2)}, u32[]{:S(2)}) %collective-permute-start.7) | collective-permute-done | bytes 98336 | tf_op jit(solution)/shard_map/ppermute | solution.py:289
  24.4 2.8 %collective-permute-start.12 = (bf16[12,32,128]{2,1,0:T(8,128)(2,1)S(1)}, bf16[12,32,128]{2,1,0:T(8,128)(2,1)S(1)}, u32[]{:S(2)}, u32[]{:S(2)}) collective-permute-start(bf16[12,32,128]{2,1,0:T(8,128)(2,1)S(1)} %get-tuple-element.55.x_ref), channel_id=1, source_target_pairs={{0,28},{4,8},{8,4},{12,16},{16,12},{20,24},{24,20},{28,0},{1,29},{... | collective-permute-start | bytes 294920 | tf_op jit(solution)/shard_map/ppermute | solution.py:289
  27.2 1.5 %spread.4 = (f32[12,32,128]{2,1,0:T(8,128)S(1)}, bf16[12,32,128]{2,1,0:T(8,128)(2,1)S(1)}, bf16[12,32,128]{2,1,0:T(8,128)(2,1)S(1)}) custom-call(s32[2]{0:T(128)S(1)} %get-tuple-element.29.flag_ref, s32[12,20]{1,0:T(8,128)S(1)} %get-tuple-element.30.ids_ref, bf16[12,32,128]{2,1,0:T(8,128)(2,1)S(1)} %get-tuple-element.55.x_ref, ...), custom_call_target="tpu_custom_call" | custom-call | flops 251658240 | bytes 7864320 | tf_op jit(solution)/shard_map/spread/pallas_call | solution.py:339
  29.5 1.6 %collective-permute-start.8 = (f32[2,32,128]{2,1,0:T(8,128)S(1)}, f32[2,32,128]{2,1,0:T(8,128)S(1)}, u32[]{:S(2)}, u32[]{:S(2)}) collective-permute-start(f32[2,32,128]{2,1,0:T(8,128)S(1)} %moments.1), channel_id=1, source_target_pairs={{0,4},{4,0},{8,12},{12,8},{16,20},{20,16},{24,28},{28,24},{1,5},{5... | collective-permute-start | bytes 98312 | tf_op jit(solution)/shard_map/ppermute | solution.py:296
  31.1 1.4 %direct.6 = f32[12,32,128]{2,1,0:T(8,128)S(1)} custom-call(s32[2]{0:T(128)S(1)} %get-tuple-element.29.flag_ref, s32[12,20]{1,0:T(8,128)S(1)} %get-tuple-element.30.ids_ref, bf16[12,32,128]{2,1,0:T(8,128)(2,1)S(1)} %get-tuple-element.55.x_ref, bf16[12,32,128]{2,1,0:T(8,128)(2,1)S(1)} %collective-permute-done.11.e_ref, ...), custom_call_target="tpu_custom_call" | custom-call | flops 251658240 | bytes 7864320 | tf_op jit(solution)/shard_map/direct/pallas_call | solution.py:376
  32.5 2.7 %collective-permute-done.14 = bf16[12,32,128]{2,1,0:T(8,128)(2,1)S(1)} collective-permute-done((bf16[12,32,128]{2,1,0:T(8,128)(2,1)S(1)}, bf16[12,32,128]{2,1,0:T(8,128)(2,1)S(1)}, u32[]{:S(2)}, u32[]{:S(2)}) %collective-permute-start.14) | collective-permute-done | bytes 98336 | tf_op jit(solution)/shard_map/ppermute | solution.py:289
  35.4 1.5 %spread.5 = (f32[12,32,128]{2,1,0:T(8,128)S(1)}, bf16[12,32,128]{2,1,0:T(8,128)(2,1)S(1)}, bf16[12,32,128]{2,1,0:T(8,128)(2,1)S(1)}) custom-call(s32[2]{0:T(128)S(1)} %get-tuple-element.29.flag_ref, s32[12,20]{1,0:T(8,128)S(1)} %get-tuple-element.30.ids_ref, bf16[12,32,128]{2,1,0:T(8,128)(2,1)S(1)} %get-tuple-element.53.x_ref, ...), custom_call_target="tpu_custom_call" | custom-call | flops 251658240 | bytes 7864320 | tf_op jit(solution)/shard_map/spread/pallas_call | solution.py:339
  37.4 2.6 %collective-permute-start.18 = (bf16[12,32,128]{2,1,0:T(8,128)(2,1)S(1)}, bf16[12,32,128]{2,1,0:T(8,128)(2,1)S(1)}, u32[]{:S(2)}, u32[]{:S(2)}) collective-permute-start(bf16[12,32,128]{2,1,0:T(8,128)(2,1)S(1)} %get-tuple-element.44), channel_id=1, source_target_pairs={{0,28},{4,8},{8,4},{12,16},{16,12},{20,24},{24,20},{28,0},{1,29},{... | collective-permute-start | bytes 294920 | tf_op jit(solution)/shard_map/ppermute | solution.py:289
  40.0 4.1 %collective-permute-done.9 = f32[2,32,128]{2,1,0:T(8,128)S(1)} collective-permute-done((f32[2,32,128]{2,1,0:T(8,128)S(1)}, f32[2,32,128]{2,1,0:T(8,128)S(1)}, u32[]{:S(2)}, u32[]{:S(2)}) %collective-permute-start.9) | collective-permute-done | bytes 32800 | tf_op jit(solution)/shard_map/ppermute | solution.py:296
  44.1 1.1 %collective-permute-start.10 = (f32[2,32,128]{2,1,0:T(8,128)S(1)}, f32[2,32,128]{2,1,0:T(8,128)S(1)}, u32[]{:S(2)}, u32[]{:S(2)}) collective-permute-start(f32[2,32,128]{2,1,0:T(8,128)S(1)} %add.35), channel_id=1, source_target_pairs={{0,16},{4,20},{8,24},{12,28},{16,0},{20,4},{24,8},{28,12},{1,17},{... | collective-permute-start | bytes 98312 | tf_op jit(solution)/shard_map/ppermute | solution.py:296
  45.3 2.8 %collective-permute-done.10 = f32[2,32,128]{2,1,0:T(8,128)S(1)} collective-permute-done((f32[2,32,128]{2,1,0:T(8,128)S(1)}, f32[2,32,128]{2,1,0:T(8,128)S(1)}, u32[]{:S(2)}, u32[]{:S(2)}) %collective-permute-start.10) | collective-permute-done | bytes 32800 | tf_op jit(solution)/shard_map/ppermute | solution.py:296
  48.1 1.4 %direct.7.y_ref = f32[12,32,128]{2,1,0:T(8,128)S(1)} custom-call(s32[2]{0:T(128)S(1)} %get-tuple-element.29.flag_ref, s32[12,20]{1,0:T(8,128)S(1)} %get-tuple-element.30.ids_ref, bf16[12,32,128]{2,1,0:T(8,128)(2,1)S(1)} %get-tuple-element.53.x_ref, bf16[12,32,128]{2,1,0:T(8,128)(2,1)S(1)} %collective-permute-done.15.e_ref, ...), custom_call_target="tpu_custom_call" | custom-call | flops 251658240 | bytes 7864320 | tf_op jit(solution)/shard_map/direct/pallas_call | solution.py:376
  49.8 2.2 %collective-permute-start.19 = (bf16[12,32,128]{2,1,0:T(8,128)(2,1)S(1)}, bf16[12,32,128]{2,1,0:T(8,128)(2,1)S(1)}, u32[]{:S(2)}, u32[]{:S(2)}) collective-permute-start(bf16[12,32,128]{2,1,0:T(8,128)(2,1)S(1)} %get-tuple-element.47.refs_3_.refs_1_), channel_id=1, source_target_pairs={{0,4},{4,0},{8,12},{12,8},{16,20},{20,16},{24,28},{28,24},{1,5},{5... | collective-permute-start | bytes 294920 | tf_op jit(solution)/shard_map/ppermute | solution.py:290
  51.9 2.7 %near_forces.1 = (f32[37,3,8,128]{3,2,1,0:T(8,128)S(1)}, f32[20,12,32,128]{3,2,1,0:T(8,128)S(1)}) custom-call(s32[2]{0:T(128)S(1)} %get-tuple-element.29.flag_ref, s32[12,20]{1,0:T(8,128)S(1)} %get-tuple-element.30.ids_ref, f32[36,20]{1,0:T(8,128)S(1)} %get-tuple-element.46.bond_ref, bf16[12,32,128]{2,1,0:T(8,128)(2,1)S(1)} %copy-done, ...), custom_call_target="tpu_custom_call" | custom-call | flops 754974720 | bytes 15728640 | tf_op jit(solution)/shard_map/near_forces/pallas_call | solution.py:430
  55.0 2.2 %far_forces.1 = (f32[12,3,128]{2,1,0:T(4,128)S(1)}, f32[12,3,128]{2,1,0:T(4,128)S(1)}, f32[12,3,128]{2,1,0:T(4,128)S(1)}) custom-call(s32[2]{0:T(128)S(1)} %get-tuple-element.29.flag_ref, s32[12,20]{1,0:T(8,128)S(1)} %get-tuple-element.30.ids_ref, f32[36,20]{1,0:T(8,128)S(1)} %get-tuple-element.46.bond_ref, bf16[12,32,128]{2,1,0:T(8,128)(2,1)S(1)} %copy-done, ...), custom_call_target="tpu_custom_call" | custom-call | flops 251658240 | bytes 11796480 | tf_op jit(solution)/shard_map/far_forces/pallas_call | solution.py:487
  57.5 0.9 %collective-permute-start.22 = (f32[12,3,128]{2,1,0:T(4,128)S(1)}, f32[12,3,128]{2,1,0:T(4,128)S(1)}, u32[]{:S(2)}, u32[]{:S(2)}) collective-permute-start(f32[12,3,128]{2,1,0:T(4,128)S(1)} %get-tuple-element.52), channel_id=1, source_target_pairs={{0,28},{4,8},{8,4},{12,16},{16,12},{20,24},{24,20},{28,0},{1,29},{... | collective-permute-start | bytes 55304 | tf_op jit(solution)/shard_map/ppermute | solution.py:289
  58.5 3.2 %collective-permute-done.22.o_ref = f32[12,3,128]{2,1,0:T(4,128)S(1)} collective-permute-done((f32[12,3,128]{2,1,0:T(4,128)S(1)}, f32[12,3,128]{2,1,0:T(4,128)S(1)}, u32[]{:S(2)}, u32[]{:S(2)}) %collective-permute-start.22) | collective-permute-done | bytes 18464 | tf_op jit(solution)/shard_map/ppermute | solution.py:289
  62.0 1.6 %collective-permute-start.23 = (f32[24,128]{1,0:T(8,128)S(1)}, f32[24,128]{1,0:T(8,128)S(1)}, u32[]{:S(2)}, u32[]{:S(2)}) collective-permute-start(f32[24,128]{1,0:T(8,128)S(1)} %packed.1), channel_id=1, source_target_pairs={{0,1},{1,0},{2,3},{3,2},{4,5},{5,4},{6,7},{7,6},{8,9},{9,8},{10,11... | collective-permute-start | bytes 36872 | tf_op jit(solution)/shard_map/ppermute | solution.py:543
  63.6 2.1 %collective-permute-done.23 = f32[24,128]{1,0:T(8,128)S(1)} collective-permute-done((f32[24,128]{1,0:T(8,128)S(1)}, f32[24,128]{1,0:T(8,128)S(1)}, u32[]{:S(2)}, u32[]{:S(2)}) %collective-permute-start.23) | collective-permute-done | bytes 12320 | tf_op jit(solution)/shard_map/ppermute | solution.py:543
  65.7 2.6 %collective-permute-start.24 = (f32[24,128]{1,0:T(8,128)S(1)}, f32[24,128]{1,0:T(8,128)S(1)}, u32[]{:S(2)}, u32[]{:S(2)}) collective-permute-start(f32[24,128]{1,0:T(8,128)S(1)} %add.39.refs_0_), channel_id=1, source_target_pairs={{0,2},{1,3},{2,0},{3,1},{4,6},{5,7},{6,4},{7,5},{8,10},{9,11},{10,... | collective-permute-start | bytes 36872 | tf_op jit(solution)/shard_map/ppermute | solution.py:543
  68.3 2.0 %collective-permute-done.24.refs_1_ = f32[24,128]{1,0:T(8,128)S(1)} collective-permute-done((f32[24,128]{1,0:T(8,128)S(1)}, f32[24,128]{1,0:T(8,128)S(1)}, u32[]{:S(2)}, u32[]{:S(2)}) %collective-permute-start.24) | collective-permute-done | bytes 12320 | tf_op jit(solution)/shard_map/ppermute | solution.py:543
  70.3 0.6 unpacked.1
  (45 shorter events, 3.5 us)
Async XLA Ops:
  0.6 10.1 %copy-start = (bf16[12,32,128]{2,1,0:T(8,128)(2,1)S(1)}, bf16[12,32,128]{2,1,0:T(8,128)(2,1)}, u32[]{:S(2)}) copy-start(bf16[12,32,128]{2,1,0:T(8,128)(2,1)} %refs_0_.3) | copy-start | bytes 294916
  0.6 10.1 %copy-start.1 = (f32[12,128]{1,0:T(8,128)S(1)}, f32[12,128]{1,0:T(8,128)}, u32[]{:S(2)}) copy-start(f32[12,128]{1,0:T(8,128)} %site_ref.7) | copy-start | bytes 18436
  0.7 10.1 %collective-permute-start.1 = (bf16[12,32,128]{2,1,0:T(8,128)(2,1)}, bf16[12,32,128]{2,1,0:T(8,128)(2,1)S(1)}, u32[]{:S(2)}, u32[]{:S(2)}) collective-permute-start(bf16[12,32,128]{2,1,0:T(8,128)(2,1)} %refs_0_.3), channel_id=1, source_target_pairs={{0,28},{4,8},{8,4},{12,16},{16,12},{20,24},{24,20},{28,0},{1,29},{... | collective-permute-start | bytes 294920 | tf_op jit(solution)/shard_map/ppermute | solution.py:289
  4.1 6.7 %collective-permute-start = (bf16[12,32,128]{2,1,0:T(8,128)(2,1)}, bf16[12,32,128]{2,1,0:T(8,128)(2,1)S(1)}, u32[]{:S(2)}, u32[]{:S(2)}) collective-permute-start(bf16[12,32,128]{2,1,0:T(8,128)(2,1)} %refs_0_.3), channel_id=1, source_target_pairs={{0,4},{4,0},{8,12},{12,8},{16,20},{20,16},{24,28},{28,24},{1,5},{5... | collective-permute-start | bytes 294920 | tf_op jit(solution)/shard_map/ppermute | solution.py:290
  9.9 2.4 %collective-permute-start.2 = (bf16[12,32,128]{2,1,0:T(8,128)(2,1)S(1)}, bf16[12,32,128]{2,1,0:T(8,128)(2,1)S(1)}, u32[]{:S(2)}, u32[]{:S(2)}) collective-permute-start(bf16[12,32,128]{2,1,0:T(8,128)(2,1)S(1)} %get-tuple-element.33), channel_id=1, source_target_pairs={{0,4},{4,0},{8,12},{12,8},{16,20},{20,16},{24,28},{28,24},{1,5},{5... | collective-permute-start | bytes 294920 | tf_op jit(solution)/shard_map/ppermute | solution.py:290
  10.4 5.9 %collective-permute-start.3 = (bf16[12,32,128]{2,1,0:T(8,128)(2,1)S(1)}, bf16[12,32,128]{2,1,0:T(8,128)(2,1)S(1)}, u32[]{:S(2)}, u32[]{:S(2)}) collective-permute-start(bf16[12,32,128]{2,1,0:T(8,128)(2,1)S(1)} %get-tuple-element.34), channel_id=1, source_target_pairs={{0,28},{4,8},{8,4},{12,16},{16,12},{20,24},{24,20},{28,0},{1,29},{... | collective-permute-start | bytes 294920 | tf_op jit(solution)/shard_map/ppermute | solution.py:289
  16.4 5.4 %collective-permute-start.5 = (bf16[12,32,128]{2,1,0:T(8,128)(2,1)S(1)}, bf16[12,32,128]{2,1,0:T(8,128)(2,1)S(1)}, u32[]{:S(2)}, u32[]{:S(2)}) collective-permute-start(bf16[12,32,128]{2,1,0:T(8,128)(2,1)S(1)} %get-tuple-element.57.x_ref), channel_id=1, source_target_pairs={{0,28},{4,8},{8,4},{12,16},{16,12},{20,24},{24,20},{28,0},{1,29},{... | collective-permute-start | bytes 294920 | tf_op jit(solution)/shard_map/ppermute | solution.py:289
  16.5 5.3 %collective-permute-start.4 = (bf16[12,32,128]{2,1,0:T(8,128)(2,1)S(1)}, bf16[12,32,128]{2,1,0:T(8,128)(2,1)S(1)}, u32[]{:S(2)}, u32[]{:S(2)}) collective-permute-start(bf16[12,32,128]{2,1,0:T(8,128)(2,1)S(1)} %get-tuple-element.57.x_ref), channel_id=1, source_target_pairs={{0,4},{4,0},{8,12},{12,8},{16,20},{20,16},{24,28},{28,24},{1,5},{5... | collective-permute-start | bytes 294920 | tf_op jit(solution)/shard_map/ppermute | solution.py:290
  19.2 4.2 %collective-permute-start.6 = (bf16[12,32,128]{2,1,0:T(8,128)(2,1)S(1)}, bf16[12,32,128]{2,1,0:T(8,128)(2,1)S(1)}, u32[]{:S(2)}, u32[]{:S(2)}) collective-permute-start(bf16[12,32,128]{2,1,0:T(8,128)(2,1)S(1)} %get-tuple-element.37), channel_id=1, source_target_pairs={{0,4},{4,0},{8,12},{12,8},{16,20},{20,16},{24,28},{28,24},{1,5},{5... | collective-permute-start | bytes 294920 | tf_op jit(solution)/shard_map/ppermute | solution.py:290
  19.3 5.0 %collective-permute-start.7 = (bf16[12,32,128]{2,1,0:T(8,128)(2,1)S(1)}, bf16[12,32,128]{2,1,0:T(8,128)(2,1)S(1)}, u32[]{:S(2)}, u32[]{:S(2)}) collective-permute-start(bf16[12,32,128]{2,1,0:T(8,128)(2,1)S(1)} %get-tuple-element.38), channel_id=1, source_target_pairs={{0,28},{4,8},{8,4},{12,16},{16,12},{20,24},{24,20},{28,0},{1,29},{... | collective-permute-start | bytes 294920 | tf_op jit(solution)/shard_map/ppermute | solution.py:289
  24.4 6.7 %collective-permute-start.12 = (bf16[12,32,128]{2,1,0:T(8,128)(2,1)S(1)}, bf16[12,32,128]{2,1,0:T(8,128)(2,1)S(1)}, u32[]{:S(2)}, u32[]{:S(2)}) collective-permute-start(bf16[12,32,128]{2,1,0:T(8,128)(2,1)S(1)} %get-tuple-element.55.x_ref), channel_id=1, source_target_pairs={{0,28},{4,8},{8,4},{12,16},{16,12},{20,24},{24,20},{28,0},{1,29},{... | collective-permute-start | bytes 294920 | tf_op jit(solution)/shard_map/ppermute | solution.py:289
  27.2 3.9 %collective-permute-start.11 = (bf16[12,32,128]{2,1,0:T(8,128)(2,1)S(1)}, bf16[12,32,128]{2,1,0:T(8,128)(2,1)S(1)}, u32[]{:S(2)}, u32[]{:S(2)}) collective-permute-start(bf16[12,32,128]{2,1,0:T(8,128)(2,1)S(1)} %get-tuple-element.55.x_ref), channel_id=1, source_target_pairs={{0,4},{4,0},{8,12},{12,8},{16,20},{20,16},{24,28},{28,24},{1,5},{5... | collective-permute-start | bytes 294920 | tf_op jit(solution)/shard_map/ppermute | solution.py:290
  28.6 3.8 %collective-permute-start.13 = (bf16[12,32,128]{2,1,0:T(8,128)(2,1)S(1)}, bf16[12,32,128]{2,1,0:T(8,128)(2,1)S(1)}, u32[]{:S(2)}, u32[]{:S(2)}) collective-permute-start(bf16[12,32,128]{2,1,0:T(8,128)(2,1)S(1)} %get-tuple-element.40), channel_id=1, source_target_pairs={{0,4},{4,0},{8,12},{12,8},{16,20},{20,16},{24,28},{28,24},{1,5},{5... | collective-permute-start | bytes 294920 | tf_op jit(solution)/shard_map/ppermute | solution.py:290
  29.2 6.0 %collective-permute-start.14 = (bf16[12,32,128]{2,1,0:T(8,128)(2,1)S(1)}, bf16[12,32,128]{2,1,0:T(8,128)(2,1)S(1)}, u32[]{:S(2)}, u32[]{:S(2)}) collective-permute-start(bf16[12,32,128]{2,1,0:T(8,128)(2,1)S(1)} %get-tuple-element.41), channel_id=1, source_target_pairs={{0,28},{4,8},{8,4},{12,16},{16,12},{20,24},{24,20},{28,0},{1,29},{... | collective-permute-start | bytes 294920 | tf_op jit(solution)/shard_map/ppermute | solution.py:289
  29.5 10.5 %collective-permute-start.8 = (f32[2,32,128]{2,1,0:T(8,128)S(1)}, f32[2,32,128]{2,1,0:T(8,128)S(1)}, u32[]{:S(2)}, u32[]{:S(2)}) collective-permute-start(f32[2,32,128]{2,1,0:T(8,128)S(1)} %moments.1), channel_id=1, source_target_pairs={{0,4},{4,0},{8,12},{12,8},{16,20},{20,16},{24,28},{28,24},{1,5},{5... | collective-permute-start | bytes 98312 | tf_op jit(solution)/shard_map/ppermute | solution.py:296
  35.2 12.8 %collective-permute-start.16 = (bf16[12,32,128]{2,1,0:T(8,128)(2,1)S(1)}, bf16[12,32,128]{2,1,0:T(8,128)(2,1)S(1)}, u32[]{:S(2)}, u32[]{:S(2)}) collective-permute-start(bf16[12,32,128]{2,1,0:T(8,128)(2,1)S(1)} %get-tuple-element.53.x_ref), channel_id=1, source_target_pairs={{0,28},{4,8},{8,4},{12,16},{16,12},{20,24},{24,20},{28,0},{1,29},{... | collective-permute-start | bytes 294920 | tf_op jit(solution)/shard_map/ppermute | solution.py:289
  35.3 12.8 %collective-permute-start.15 = (bf16[12,32,128]{2,1,0:T(8,128)(2,1)S(1)}, bf16[12,32,128]{2,1,0:T(8,128)(2,1)S(1)}, u32[]{:S(2)}, u32[]{:S(2)}) collective-permute-start(bf16[12,32,128]{2,1,0:T(8,128)(2,1)S(1)} %get-tuple-element.53.x_ref), channel_id=1, source_target_pairs={{0,4},{4,0},{8,12},{12,8},{16,20},{20,16},{24,28},{28,24},{1,5},{5... | collective-permute-start | bytes 294920 | tf_op jit(solution)/shard_map/ppermute | solution.py:290
  36.8 12.7 %collective-permute-start.17 = (bf16[12,32,128]{2,1,0:T(8,128)(2,1)S(1)}, bf16[12,32,128]{2,1,0:T(8,128)(2,1)S(1)}, u32[]{:S(2)}, u32[]{:S(2)}) collective-permute-start(bf16[12,32,128]{2,1,0:T(8,128)(2,1)S(1)} %get-tuple-element.43), channel_id=1, source_target_pairs={{0,4},{4,0},{8,12},{12,8},{16,20},{20,16},{24,28},{28,24},{1,5},{5... | collective-permute-start | bytes 294920 | tf_op jit(solution)/shard_map/ppermute | solution.py:290
  37.4 12.1 %collective-permute-start.18 = (bf16[12,32,128]{2,1,0:T(8,128)(2,1)S(1)}, bf16[12,32,128]{2,1,0:T(8,128)(2,1)S(1)}, u32[]{:S(2)}, u32[]{:S(2)}) collective-permute-start(bf16[12,32,128]{2,1,0:T(8,128)(2,1)S(1)} %get-tuple-element.44), channel_id=1, source_target_pairs={{0,28},{4,8},{8,4},{12,16},{16,12},{20,24},{24,20},{28,0},{1,29},{... | collective-permute-start | bytes 294920 | tf_op jit(solution)/shard_map/ppermute | solution.py:289
  40.0 4.1 %collective-permute-start.9 = (f32[2,32,128]{2,1,0:T(8,128)S(1)}, f32[2,32,128]{2,1,0:T(8,128)S(1)}, u32[]{:S(2)}, u32[]{:S(2)}) collective-permute-start(f32[2,32,128]{2,1,0:T(8,128)S(1)} %add.34), channel_id=1, source_target_pairs={{0,8},{4,12},{8,0},{12,4},{16,24},{20,28},{24,16},{28,20},{1,9},{5... | collective-permute-start | bytes 98312 | tf_op jit(solution)/shard_map/ppermute | solution.py:296
  44.1 3.9 %collective-permute-start.10 = (f32[2,32,128]{2,1,0:T(8,128)S(1)}, f32[2,32,128]{2,1,0:T(8,128)S(1)}, u32[]{:S(2)}, u32[]{:S(2)}) collective-permute-start(f32[2,32,128]{2,1,0:T(8,128)S(1)} %add.35), channel_id=1, source_target_pairs={{0,16},{4,20},{8,24},{12,28},{16,0},{20,4},{24,8},{28,12},{1,17},{... | collective-permute-start | bytes 98312 | tf_op jit(solution)/shard_map/ppermute | solution.py:296
  49.7 5.3 %collective-permute-start.20 = (bf16[12,32,128]{2,1,0:T(8,128)(2,1)S(1)}, bf16[12,32,128]{2,1,0:T(8,128)(2,1)S(1)}, u32[]{:S(2)}, u32[]{:S(2)}) collective-permute-start(bf16[12,32,128]{2,1,0:T(8,128)(2,1)S(1)} %get-tuple-element.47.refs_3_.refs_1_), channel_id=1, source_target_pairs={{0,28},{4,8},{8,4},{12,16},{16,12},{20,24},{24,20},{28,0},{1,29},{... | collective-permute-start | bytes 294920 | tf_op jit(solution)/shard_map/ppermute | solution.py:289
  49.8 5.2 %collective-permute-start.19 = (bf16[12,32,128]{2,1,0:T(8,128)(2,1)S(1)}, bf16[12,32,128]{2,1,0:T(8,128)(2,1)S(1)}, u32[]{:S(2)}, u32[]{:S(2)}) collective-permute-start(bf16[12,32,128]{2,1,0:T(8,128)(2,1)S(1)} %get-tuple-element.47.refs_3_.refs_1_), channel_id=1, source_target_pairs={{0,4},{4,0},{8,12},{12,8},{16,20},{20,16},{24,28},{28,24},{1,5},{5... | collective-permute-start | bytes 294920 | tf_op jit(solution)/shard_map/ppermute | solution.py:290
  54.6 7.0 %copy-start.2 = (s32[12,128]{1,0:T(8,128)S(1)}, s32[12,128]{1,0:T(8,128)}, u32[]{:S(2)}) copy-start(s32[12,128]{1,0:T(8,128)} %atom_ref.1) | copy-start | bytes 18436
  57.2 1.3 %collective-permute-start.21 = (f32[12,3,128]{2,1,0:T(4,128)S(1)}, f32[12,3,128]{2,1,0:T(4,128)S(1)}, u32[]{:S(2)}, u32[]{:S(2)}) collective-permute-start(f32[12,3,128]{2,1,0:T(4,128)S(1)} %get-tuple-element.51), channel_id=1, source_target_pairs={{0,4},{4,0},{8,12},{12,8},{16,20},{20,16},{24,28},{28,24},{1,5},{5... | collective-permute-start | bytes 55304 | tf_op jit(solution)/shard_map/ppermute | solution.py:290
  57.5 4.2 %collective-permute-start.22 = (f32[12,3,128]{2,1,0:T(4,128)S(1)}, f32[12,3,128]{2,1,0:T(4,128)S(1)}, u32[]{:S(2)}, u32[]{:S(2)}) collective-permute-start(f32[12,3,128]{2,1,0:T(4,128)S(1)} %get-tuple-element.52), channel_id=1, source_target_pairs={{0,28},{4,8},{8,4},{12,16},{16,12},{20,24},{24,20},{28,0},{1,29},{... | collective-permute-start | bytes 55304 | tf_op jit(solution)/shard_map/ppermute | solution.py:289
  62.0 3.7 %collective-permute-start.23 = (f32[24,128]{1,0:T(8,128)S(1)}, f32[24,128]{1,0:T(8,128)S(1)}, u32[]{:S(2)}, u32[]{:S(2)}) collective-permute-start(f32[24,128]{1,0:T(8,128)S(1)} %packed.1), channel_id=1, source_target_pairs={{0,1},{1,0},{2,3},{3,2},{4,5},{5,4},{6,7},{7,6},{8,9},{9,8},{10,11... | collective-permute-start | bytes 36872 | tf_op jit(solution)/shard_map/ppermute | solution.py:543
  65.7 4.6 %collective-permute-start.24 = (f32[24,128]{1,0:T(8,128)S(1)}, f32[24,128]{1,0:T(8,128)S(1)}, u32[]{:S(2)}, u32[]{:S(2)}) collective-permute-start(f32[24,128]{1,0:T(8,128)S(1)} %add.39.refs_0_), channel_id=1, source_target_pairs={{0,2},{1,3},{2,0},{3,1},{4,6},{5,7},{6,4},{7,5},{8,10},{9,11},{10,... | collective-permute-start | bytes 36872 | tf_op jit(solution)/shard_map/ppermute | solution.py:543

commit v5 on v4

--- a/solution.py
+++ b/solution.py
@@ -17,6 +17,8 @@
 SMEARING_TEMP = 0.1
 QUAD_NODES = 64
 HALF_SLOTS = 10
+CHUNKS = 3
+AHEAD = 6
 
 bf16 = jnp.bfloat16
 f32 = jnp.float32
@@ -49,24 +51,33 @@
     probes, block = x.shape[1:]
     frame = rows + 2 * REACH
     halves = (0, HALF_SLOTS, slots)
+    height = rows // CHUNKS
 
     def kernel(col_hbm, x_hbm, k_hbm, bond_hbm, table_hbm, mu_ref, *refs):
-        flag_ref, ids_ref, out_ref, coeff_ref, own_ref, even_ref, odd_ref, kv_ref, kt_ref = refs[:9]
-        acc, col_sm, col_vm, xv, bond_vm, table_vm, sems, small = refs[9:]
+        flag_ref, ids_ref, at_ref, out_ref, coeff_ref, own_ref, even_ref, odd_ref, kv_ref, kt_ref = refs[:10]
+        acc, col_sm, col_vm, xv, bond_vm, table_vm, sems, small = refs[10:]
         me = lax.axis_index("clus")
 
-        def load(c, half):
+        def load(index):
+            half, chunk = divmod(index, CHUNKS)
             part = pl.ds(halves[half], halves[half + 1] - halves[half])
+            group = pl.ds(chunk * height, height)
             return pltpu.make_async_copy(
-                k_hbm.at[part, c], kv_ref.at[part, c], sems.at[half, c]
+                k_hbm.at[part, group], kv_ref.at[part, group], sems.at[index]
             )
 
-        pairs = ((col_hbm, col_vm), (col_hbm, col_sm), (x_hbm, xv), (table_hbm, table_vm), (bond_hbm, bond_vm))
+        pairs = (
+            (col_hbm, col_vm),
+            (col_hbm, col_sm),
+            (x_hbm, xv),
+            (table_hbm, table_vm),
+            (bond_hbm, bond_vm),
+        )
         copies = [pltpu.make_async_copy(a, b, small.at[i]) for i, (a, b) in enumerate(pairs)]
         for copy in copies:
             copy.start()
-        for c in range(rows):
-            load(c, 0).start()
+        for index in range(min(AHEAD, CHUNKS)):
+            load(index).start()
         acc[...] = jnp.zeros_like(acc)
         copies[0].wait()
         col = col_vm[...]
@@ -76,12 +87,15 @@
         odd = lax.rem(me, 2)
         flag_ref[1] = odd
 
-        @pl.when(many)
-        def _():
-            for c in range(rows):
-                load(c, 1).start()
-
-        ids_ref[...] = jnp.where(col >= 0, col - me * rows + REACH, frame)
+        ids = jnp.where(col >= 0, col - me * rows + REACH, frame)
+        ids_ref[...] = ids
+        side = lax.broadcasted_iota(jnp.int32, (rows, REACH), 1) + odd * (REACH + rows)
+        at = jnp.full((rows, REACH), slots, jnp.int32)
+        for m in range(slots):
+            at = jnp.where(ids[:, m : m + 1] == side, m, at)
+        at_ref[...] = at
+        for c in range(rows):
+            kv_ref[slots, c] = jnp.zeros((block, block), kv_ref.dtype)
         for copy in copies[1:]:
             copy.wait()
         for axis in range(3):
@@ -92,9 +106,15 @@
         coeff_ref[...] = jnp.broadcast_to(total, coeff_ref.shape)
 
         def body(last):
-            for half in range(last):
-                for c in range(rows):
-                    load(c, half).wait()
+            for index in range(last * CHUNKS):
+                half, chunk = divmod(index, CHUNKS)
+                if index == 0:
+                    for later in range(min(AHEAD, CHUNKS), min(AHEAD, last * CHUNKS)):
+                        load(later).start()
+                load(index).wait()
+                if index + AHEAD < last * CHUNKS:
+                    load(index + AHEAD).start()
+                for c in range(chunk * height, (chunk + 1) * height):
                     xc = xv[c]
                     for first in range(halves[half], halves[half + 1], 4):
                         parts, targets = [], []
@@ -124,23 +144,24 @@
         odd_ref[...] = acc[pl.ds(odd * (REACH + rows), REACH)].astype(bf16)
 
     side = jax.ShapeDtypeStruct((REACH, probes, block), bf16)
-    blocks = jax.ShapeDtypeStruct(k.shape, k.dtype)
     hbm = pl.BlockSpec(memory_space=pltpu.HBM)
+    operands = (columns, x, k, bond_dir, quadrature())
     return pl.pallas_call(
         kernel,
         out_shape=[
             jax.ShapeDtypeStruct((2,), jnp.int32),
             jax.ShapeDtypeStruct((rows, slots), jnp.int32),
+            jax.ShapeDtypeStruct((rows, REACH), jnp.int32),
             jax.ShapeDtypeStruct((3 * rows, slots), f32),
             jax.ShapeDtypeStruct((8, 128), f32),
             jax.ShapeDtypeStruct((rows, probes, block), f32),
             side,
             side,
-            blocks,
-            blocks,
+            jax.ShapeDtypeStruct((slots + 1, *k.shape[1:]), k.dtype),
+            jax.ShapeDtypeStruct(k.shape, k.dtype),
         ],
         in_specs=[hbm] * 5 + [SM],
-        out_specs=[SM] + [VM] * 8,
+        out_specs=[SM] + [VM] * 9,
         scratch_shapes=[
             pltpu.VMEM((frame + 1, probes, block), f32),
             pltpu.SMEM((rows, slots), jnp.int32),
@@ -148,12 +169,12 @@
             pltpu.VMEM(x.shape, x.dtype),
             pltpu.VMEM(bond_dir.shape, bond_dir.dtype),
             pltpu.VMEM((8, 128), f32),
-            pltpu.SemaphoreType.DMA((2, rows)),
+            pltpu.SemaphoreType.DMA((2 * CHUNKS,)),
             pltpu.SemaphoreType.DMA((5,)),
         ],
         name="opening",
         **params(2 * slots * rows * probes * block * block, k.size * 2),
-    )(*(pltpu.with_memory_space_constraint(a, pltpu.HBM) for a in (columns, x, k, bond_dir, quadrature())), chemical_potential)
+    )(*(pltpu.with_memory_space_constraint(a, pltpu.HBM) for a in operands), chemical_potential)
 
 
 def moments(coeffs, v, first, second):
@@ -307,12 +328,47 @@
         body(HALF_SLOTS)
 
 
+def ahead(flag, at, x, k):
+    _, rows, block, _ = k.shape
+    probes = x.shape[1]
+
+    def kernel(flag_ref, at_ref, x_ref, k_ref, out_ref):
+        def body(above):
+            for j in range(REACH):
+                reach = list(range(j, rows)) if above else list(range(min(j + 1, rows)))
+                acc = None
+                for first in range(0, len(reach), 2):
+                    group = reach[first : first + 2]
+                    left = jnp.concatenate([x_ref[c] for c in group], axis=1)
+                    right = jnp.concatenate([k_ref[at_ref[c, j], c] for c in group], axis=0)
+                    part = dot(left, right, NN)
+                    acc = part if acc is None else acc + part
+                out_ref[j] = acc.astype(bf16)
+
+        @pl.when(flag_ref[1] == 0)
+        def _():
+            body(False)
+
+        @pl.when(flag_ref[1] != 0)
+        def _():
+            body(True)
+
+    return pl.pallas_call(
+        kernel,
+        out_shape=jax.ShapeDtypeStruct((REACH, probes, block), bf16),
+        in_specs=[SM, SM, VM, VM],
+        out_specs=VM,
+        name="ahead",
+        **params(80 * 2 * probes * block * block, 80 * 2 * block * block),
+    )(flag, at, x, k)
+
+
 def spread(flag, ids, x, k):
-    slots, rows, block, _ = k.shape
-    probes = x.shape[1]
+    rows, slots = ids.shape
+    _, probes, block = x.shape
     frame = rows + 2 * REACH
 
-    def kernel(flag_ref, ids_ref, x_ref, k_ref, own_ref, even_ref, odd_ref, acc):
+    def kernel(flag_ref, ids_ref, x_ref, k_ref, own_ref, even_ref, acc):
         acc[...] = jnp.zeros_like(acc)
 
         def body(count):
@@ -333,14 +389,13 @@
         odd = flag_ref[1]
         own_ref[...] = acc[pl.ds(REACH, rows)]
         even_ref[...] = acc[pl.ds((1 - odd) * (REACH + rows), REACH)].astype(bf16)
-        odd_ref[...] = acc[pl.ds(odd * (REACH + rows), REACH)].astype(bf16)
 
     side = jax.ShapeDtypeStruct((REACH, probes, block), bf16)
     return pl.pallas_call(
         kernel,
-        out_shape=[jax.ShapeDtypeStruct((rows, probes, block), f32), side, side],
+        out_shape=[jax.ShapeDtypeStruct((rows, probes, block), f32), side],
         in_specs=[SM, SM, VM, VM],
-        out_specs=[VM] * 3,
+        out_specs=[VM] * 2,
         scratch_shapes=[pltpu.VMEM((frame + 1, probes, block), f32)],
         name="spread",
         **params(2 * slots * rows * probes * block * block, k.size * 2),
@@ -504,7 +559,7 @@
     x = probes
     even, crossed = exchange(x, x)
     v_even, v_crossed = even, crossed
-    flag, ids, bond, coeffs, *outs, k, kt = opening(
+    flag, ids, at, bond, coeffs, own, to_even, to_odd, k, kt = opening(
         block_col.T, x, hopping, jnp.transpose(bond_dir, (0, 2, 1)), chemical_potential
     )
     rounds = (lax.axis_size("clus") - 1).bit_length()
@@ -513,8 +568,8 @@
         if term == 3:
             sums = doubled(0, moments(coeffs, *cheb), "clus")
         if term > 1:
-            outs = spread(flag, ids, x, k)
-        own, to_even, to_odd = outs
+            to_odd = ahead(flag, at, x, k)
+            own, to_even = spread(flag, ids, x, k)
         back_even, back_crossed = exchange(to_even, to_odd)
         if term > 2:
             sums = doubled(term - 2, sums, "clus")

time: 71.3 us -> 68.6 us (0.962)
  waiting for transfers between devices: 22.9 us -> 19.1 us
  Pallas kernels: 21.5 us -> 23.6 us
  starting transfers between devices: 24.8 us -> 23.7 us
    pallas_call x0 -> x3, Pallas kernels: none -> 3.73 us  [ahead(): pl.pallas_call(kernel, out_shape=jax.ShapeDtypeStruct((REACH, probes, blo...]
    ppermute x10, waiting for transfers between devices: 11.9 us -> 9.08 us  [exchange(): crossed = lax.ppermute(odd_side, 'clus', shifted)]
    pallas_call x1, Pallas kernels: 5.11 us -> 3.72 us  [opening(): pl.pallas_call(kernel, out_shape=[jax.ShapeDtypeStruct((2,), jnp.int32),...]
    ppermute x3, waiting for transfers between devices: 6.85 us -> 5.55 us  [doubled(): lax.ppermute(part, axis, [(i, i ^ 1 << index) for i in range(count)])]
    ppermute x10, starting transfers between devices: 5.53 us -> 4.39 us  [exchange(): even = lax.ppermute(even_side, 'clus', paired)]
  transfers between devices with their start and end apart: 25 -> 25, of which waited for: 11 -> 10; matrix products, arithmetic and copies ran while one was open for 0% -> 0% of each run, Pallas kernels for 26% -> 28%
where the time goes in v5:
time: 68.6 us; the launch traced here: 68.4 us
  starting transfers between devices  23.7 us (35%)
  Pallas kernels  23.6 us (34%)
  waiting for transfers between devices  19.1 us (28%)
  between operations  1.73 us (3%)
    ppermute x10, starting transfers between devices, exchange(): crossed = lax.ppermute(odd_side, 'clus', shifted)  12.7 us
    ppermute x10, waiting for transfers between devices, exchange(): crossed = lax.ppermute(odd_side, 'clus', shifted)  9.08 us
    pallas_call x4, Pallas kernels, direct(): pl.pallas_call(kernel, out_shape=jax.ShapeDtypeStruct((rows, probes, bloc...  5.72 us
    ppermute x3, waiting for transfers between devices, doubled(): lax.ppermute(part, axis, [(i, i ^ 1 << index) for i in range(count)])  5.55 us
    ppermute x10, starting transfers between devices, exchange(): even = lax.ppermute(even_side, 'clus', paired)  4.39 us
    pallas_call x3, Pallas kernels, spread(): pl.pallas_call(kernel, out_shape=[jax.ShapeDtypeStruct((rows, probes, blo...  4.36 us
    ppermute x2, starting transfers between devices, local(): lax.ppermute(part, 'probe', [(i, i ^ step) for i in range(count)])  4.18 us
    ppermute x2, waiting for transfers between devices, local(): lax.ppermute(part, 'probe', [(i, i ^ step) for i in range(count)])  4.12 us
  transfers between devices with their start and end apart: 25, of which 10 were waited for; matrix products, arithmetic and copies ran while one was open for 0% of the time, Pallas kernels for 28%

profile of v5, /device:TPU:0, one launch (start us, length us, event | category | flops | bytes accessed | tf_op | source)
XLA Modules:
  0.0 68.4 jit_solution(3803697796180507136)
XLA Ops:
  0.7 3.4 %collective-permute-start.1 = (bf16[12,32,128]{2,1,0:T(8,128)(2,1)}, bf16[12,32,128]{2,1,0:T(8,128)(2,1)S(1)}, u32[]{:S(2)}, u32[]{:S(2)}) collective-permute-start(bf16[12,32,128]{2,1,0:T(8,128)(2,1)} %refs_0_.3), channel_id=1, source_target_pairs={{0,28},{4,8},{8,4},{12,16},{16,12},{20,24},{24,20},{28,0},{1,29},{... | collective-permute-start | bytes 294920 | tf_op jit(solution)/shard_map/ppermute | solution.py:310
  4.7 3.7 %opening.1 = (s32[2]{0:T(128)S(1)}, s32[12,20]{1,0:T(8,128)S(1)}, s32[12,12]{1,0:T(8,128)S(1)}, f32[36,20]{1,0:T(8,128)S(1)}, f32[8,128]{1,0:T(8,128)S(1)}, /*in...) custom-call(s32[12,20]{1,0:T(8,128)} %bitcast.3, ...), custom_call_target="tpu_custom_call" | custom-call | flops 251658240 | bytes 7864320 | tf_op jit(solution)/shard_map/opening/pallas_call | solution.py:149
  9.4 1.4 %direct.4 = f32[12,32,128]{2,1,0:T(8,128)S(1)} custom-call(s32[2]{0:T(128)S(1)} %get-tuple-element.27.flag_ref, s32[12,20]{1,0:T(8,128)S(1)} %get-tuple-element.28.ids_ref, bf16[12,32,128]{2,1,0:T(8,128)(2,1)S(1)} %copy-done, bf16[12,32,128]{2,1,0:T(8,128)(2,1)S(1)} %collective-permute-done.e_ref.refs_1_, ...), custom_call_target="tpu_custom_call" | custom-call | flops 251658240 | bytes 7864320 | tf_op jit(solution)/shard_map/direct/pallas_call | solution.py:431
  10.8 4.2 %collective-permute-done.3 = bf16[12,32,128]{2,1,0:T(8,128)(2,1)S(1)} collective-permute-done((bf16[12,32,128]{2,1,0:T(8,128)(2,1)S(1)}, bf16[12,32,128]{2,1,0:T(8,128)(2,1)S(1)}, u32[]{:S(2)}, u32[]{:S(2)}) %collective-permute-start.3) | collective-permute-done | bytes 98336 | tf_op jit(solution)/shard_map/ppermute | solution.py:310
  15.5 1.2 %ahead.3 = bf16[12,32,128]{2,1,0:T(8,128)(2,1)S(1)} custom-call(s32[2]{0:T(128)S(1)} %get-tuple-element.27.flag_ref, s32[12,12]{1,0:T(8,128)S(1)} %get-tuple-element.36.at_ref, bf16[12,32,128]{2,1,0:T(8,128)(2,1)S(1)} %get-tuple-element.53.x_ref, bf16[21,12,128,128]{3,2,1,0:T(8,128)(2,1)S(1)} %get-tuple-element.33.k_ref.refs_4_), custom_call_target="tpu_custom_call" | custom-call | flops 83886080 | bytes 2621440 | tf_op jit(solution)/shard_map/ahead/pallas_call | solution.py:356
  16.7 2.3 %collective-permute-start.7 = (bf16[12,32,128]{2,1,0:T(8,128)(2,1)S(1)}, bf16[12,32,128]{2,1,0:T(8,128)(2,1)S(1)}, u32[]{:S(2)}, u32[]{:S(2)}) collective-permute-start(bf16[12,32,128]{2,1,0:T(8,128)(2,1)S(1)} %ahead.3), channel_id=1, source_target_pairs={{0,28},{4,8},{8,4},{12,16},{16,12},{20,24},{24,20},{28,0},{1,29},{... | collective-permute-start | bytes 294920 | tf_op jit(solution)/shard_map/ppermute | solution.py:310
  19.0 1.5 %spread.3 = (f32[12,32,128]{2,1,0:T(8,128)S(1)}, bf16[12,32,128]{2,1,0:T(8,128)(2,1)S(1)}) custom-call(s32[2]{0:T(128)S(1)} %get-tuple-element.27.flag_ref, s32[12,20]{1,0:T(8,128)S(1)} %get-tuple-element.28.ids_ref, bf16[12,32,128]{2,1,0:T(8,128)(2,1)S(1)} %get-tuple-element.53.x_ref, bf16[21,12,128,128]{3,2,1,0:T(8,128)(2,1)S(1)} %get-tuple-element.33.k_ref.refs_4_), custom_call_target="tpu_custom_call" | custom-call | flops 251658240 | bytes 8257536 | tf_op jit(solution)/shard_map/spread/pallas_call | solution.py:394
  20.6 1.4 %direct.5 = f32[12,32,128]{2,1,0:T(8,128)S(1)} custom-call(s32[2]{0:T(128)S(1)} %get-tuple-element.27.flag_ref, s32[12,20]{1,0:T(8,128)S(1)} %get-tuple-element.28.ids_ref, bf16[12,32,128]{2,1,0:T(8,128)(2,1)S(1)} %get-tuple-element.53.x_ref, bf16[12,32,128]{2,1,0:T(8,128)(2,1)S(1)} %collective-permute-done.4.e_ref, ...), custom_call_target="tpu_custom_call" | custom-call | flops 251658240 | bytes 7864320 | tf_op jit(solution)/shard_map/direct/pallas_call | solution.py:431
  22.1 1.4 %ahead.4 = bf16[12,32,128]{2,1,0:T(8,128)(2,1)S(1)} custom-call(s32[2]{0:T(128)S(1)} %get-tuple-element.27.flag_ref, s32[12,12]{1,0:T(8,128)S(1)} %get-tuple-element.36.at_ref, bf16[12,32,128]{2,1,0:T(8,128)(2,1)S(1)} %get-tuple-element.51.x_ref, bf16[21,12,128,128]{3,2,1,0:T(8,128)(2,1)S(1)} %get-tuple-element.33.k_ref.refs_4_), custom_call_target="tpu_custom_call" | custom-call | flops 83886080 | bytes 2621440 | tf_op jit(solution)/shard_map/ahead/pallas_call | solution.py:356
  23.5 2.2 %collective-permute-start.12 = (bf16[12,32,128]{2,1,0:T(8,128)(2,1)S(1)}, bf16[12,32,128]{2,1,0:T(8,128)(2,1)S(1)}, u32[]{:S(2)}, u32[]{:S(2)}) collective-permute-start(bf16[12,32,128]{2,1,0:T(8,128)(2,1)S(1)} %get-tuple-element.51.x_ref), channel_id=1, source_target_pairs={{0,28},{4,8},{8,4},{12,16},{16,12},{20,24},{24,20},{28,0},{1,29},{... | collective-permute-start | bytes 294920 | tf_op jit(solution)/shard_map/ppermute | solution.py:310
  25.8 0.8 %collective-permute-start.14 = (bf16[12,32,128]{2,1,0:T(8,128)(2,1)S(1)}, bf16[12,32,128]{2,1,0:T(8,128)(2,1)S(1)}, u32[]{:S(2)}, u32[]{:S(2)}) collective-permute-start(bf16[12,32,128]{2,1,0:T(8,128)(2,1)S(1)} %ahead.4), channel_id=1, source_target_pairs={{0,28},{4,8},{8,4},{12,16},{16,12},{20,24},{24,20},{28,0},{1,29},{... | collective-permute-start | bytes 294920 | tf_op jit(solution)/shard_map/ppermute | solution.py:310
  26.6 1.5 %spread.4 = (f32[12,32,128]{2,1,0:T(8,128)S(1)}, bf16[12,32,128]{2,1,0:T(8,128)(2,1)S(1)}) custom-call(s32[2]{0:T(128)S(1)} %get-tuple-element.27.flag_ref, s32[12,20]{1,0:T(8,128)S(1)} %get-tuple-element.28.ids_ref, bf16[12,32,128]{2,1,0:T(8,128)(2,1)S(1)} %get-tuple-element.51.x_ref, bf16[21,12,128,128]{3,2,1,0:T(8,128)(2,1)S(1)} %get-tuple-element.33.k_ref.refs_4_), custom_call_target="tpu_custom_call" | custom-call | flops 251658240 | bytes 8257536 | tf_op jit(solution)/shard_map/spread/pallas_call | solution.py:394
  28.9 1.4 %direct.6 = f32[12,32,128]{2,1,0:T(8,128)S(1)} custom-call(s32[2]{0:T(128)S(1)} %get-tuple-element.27.flag_ref, s32[12,20]{1,0:T(8,128)S(1)} %get-tuple-element.28.ids_ref, bf16[12,32,128]{2,1,0:T(8,128)(2,1)S(1)} %get-tuple-element.51.x_ref, bf16[12,32,128]{2,1,0:T(8,128)(2,1)S(1)} %collective-permute-done.11.e_ref, ...), custom_call_target="tpu_custom_call" | custom-call | flops 251658240 | bytes 7864320 | tf_op jit(solution)/shard_map/direct/pallas_call | solution.py:431
  30.3 1.2 %collective-permute-done.14 = bf16[12,32,128]{2,1,0:T(8,128)(2,1)S(1)} collective-permute-done((bf16[12,32,128]{2,1,0:T(8,128)(2,1)S(1)}, bf16[12,32,128]{2,1,0:T(8,128)(2,1)S(1)}, u32[]{:S(2)}, u32[]{:S(2)}) %collective-permute-start.14) | collective-permute-done | bytes 98336 | tf_op jit(solution)/shard_map/ppermute | solution.py:310
  31.6 1.2 %ahead.5 = bf16[12,32,128]{2,1,0:T(8,128)(2,1)S(1)} custom-call(s32[2]{0:T(128)S(1)} %get-tuple-element.27.flag_ref, s32[12,12]{1,0:T(8,128)S(1)} %get-tuple-element.36.at_ref, bf16[12,32,128]{2,1,0:T(8,128)(2,1)S(1)} %get-tuple-element.49.x_ref, bf16[21,12,128,128]{3,2,1,0:T(8,128)(2,1)S(1)} %get-tuple-element.33.k_ref.refs_4_), custom_call_target="tpu_custom_call" | custom-call | flops 83886080 | bytes 2621440 | tf_op jit(solution)/shard_map/ahead/pallas_call | solution.py:356
  32.8 1.8 %collective-permute-start.16 = (bf16[12,32,128]{2,1,0:T(8,128)(2,1)S(1)}, bf16[12,32,128]{2,1,0:T(8,128)(2,1)S(1)}, u32[]{:S(2)}, u32[]{:S(2)}) collective-permute-start(bf16[12,32,128]{2,1,0:T(8,128)(2,1)S(1)} %get-tuple-element.49.x_ref), channel_id=1, source_target_pairs={{0,28},{4,8},{8,4},{12,16},{16,12},{20,24},{24,20},{28,0},{1,29},{... | collective-permute-start | bytes 294920 | tf_op jit(solution)/shard_map/ppermute | solution.py:310
  34.6 0.9 %collective-permute-start.18 = (bf16[12,32,128]{2,1,0:T(8,128)(2,1)S(1)}, bf16[12,32,128]{2,1,0:T(8,128)(2,1)S(1)}, u32[]{:S(2)}, u32[]{:S(2)}) collective-permute-start(bf16[12,32,128]{2,1,0:T(8,128)(2,1)S(1)} %ahead.5), channel_id=1, source_target_pairs={{0,28},{4,8},{8,4},{12,16},{16,12},{20,24},{24,20},{28,0},{1,29},{... | collective-permute-start | bytes 294920 | tf_op jit(solution)/shard_map/ppermute | solution.py:310
  35.5 1.5 %spread.5 = (f32[12,32,128]{2,1,0:T(8,128)S(1)}, bf16[12,32,128]{2,1,0:T(8,128)(2,1)S(1)}) custom-call(s32[2]{0:T(128)S(1)} %get-tuple-element.27.flag_ref, s32[12,20]{1,0:T(8,128)S(1)} %get-tuple-element.28.ids_ref, bf16[12,32,128]{2,1,0:T(8,128)(2,1)S(1)} %get-tuple-element.49.x_ref, bf16[21,12,128,128]{3,2,1,0:T(8,128)(2,1)S(1)} %get-tuple-element.33.k_ref.refs_4_), custom_call_target="tpu_custom_call" | custom-call | flops 251658240 | bytes 8257536 | tf_op jit(solution)/shard_map/spread/pallas_call | solution.py:394
  37.4 1.3 %collective-permute-start.9 = (f32[2,32,128]{2,1,0:T(8,128)S(1)}, f32[2,32,128]{2,1,0:T(8,128)S(1)}, u32[]{:S(2)}, u32[]{:S(2)}) collective-permute-start(f32[2,32,128]{2,1,0:T(8,128)S(1)} %add.34), channel_id=1, source_target_pairs={{0,8},{4,12},{8,0},{12,4},{16,24},{20,28},{24,16},{28,20},{1,9},{5... | collective-permute-start | bytes 98312 | tf_op jit(solution)/shard_map/ppermute | solution.py:317
  38.8 2.6 %collective-permute-done.9 = f32[2,32,128]{2,1,0:T(8,128)S(1)} collective-permute-done((f32[2,32,128]{2,1,0:T(8,128)S(1)}, f32[2,32,128]{2,1,0:T(8,128)S(1)}, u32[]{:S(2)}, u32[]{:S(2)}) %collective-permute-start.9) | collective-permute-done | bytes 32800 | tf_op jit(solution)/shard_map/ppermute | solution.py:317
  41.4 1.0 %collective-permute-start.10 = (f32[2,32,128]{2,1,0:T(8,128)S(1)}, f32[2,32,128]{2,1,0:T(8,128)S(1)}, u32[]{:S(2)}, u32[]{:S(2)}) collective-permute-start(f32[2,32,128]{2,1,0:T(8,128)S(1)} %add.35), channel_id=1, source_target_pairs={{0,16},{4,20},{8,24},{12,28},{16,0},{20,4},{24,8},{28,12},{1,17},{... | collective-permute-start | bytes 98312 | tf_op jit(solution)/shard_map/ppermute | solution.py:317
  42.4 2.9 %collective-permute-done.10 = f32[2,32,128]{2,1,0:T(8,128)S(1)} collective-permute-done((f32[2,32,128]{2,1,0:T(8,128)S(1)}, f32[2,32,128]{2,1,0:T(8,128)S(1)}, u32[]{:S(2)}, u32[]{:S(2)}) %collective-permute-start.10) | collective-permute-done | bytes 32800 | tf_op jit(solution)/shard_map/ppermute | solution.py:317
  45.4 1.4 %direct.7.y_ref = f32[12,32,128]{2,1,0:T(8,128)S(1)} custom-call(s32[2]{0:T(128)S(1)} %get-tuple-element.27.flag_ref, s32[12,20]{1,0:T(8,128)S(1)} %get-tuple-element.28.ids_ref, bf16[12,32,128]{2,1,0:T(8,128)(2,1)S(1)} %get-tuple-element.49.x_ref, bf16[12,32,128]{2,1,0:T(8,128)(2,1)S(1)} %collective-permute-done.15.e_ref, ...), custom_call_target="tpu_custom_call" | custom-call | flops 251658240 | bytes 7864320 | tf_op jit(solution)/shard_map/direct/pallas_call | solution.py:431
  47.1 2.0 %collective-permute-start.19 = (bf16[12,32,128]{2,1,0:T(8,128)(2,1)S(1)}, bf16[12,32,128]{2,1,0:T(8,128)(2,1)S(1)}, u32[]{:S(2)}, u32[]{:S(2)}) collective-permute-start(bf16[12,32,128]{2,1,0:T(8,128)(2,1)S(1)} %get-tuple-element.43.refs_3_.refs_1_), channel_id=1, source_target_pairs={{0,4},{4,0},{8,12},{12,8},{16,20},{20,16},{24,28},{28,24},{1,5},{5... | collective-permute-start | bytes 294920 | tf_op jit(solution)/shard_map/ppermute | solution.py:311
  49.1 2.7 %near_forces.1 = (f32[37,3,8,128]{3,2,1,0:T(8,128)S(1)}, f32[20,12,32,128]{3,2,1,0:T(8,128)S(1)}) custom-call(s32[2]{0:T(128)S(1)} %get-tuple-element.27.flag_ref, s32[12,20]{1,0:T(8,128)S(1)} %get-tuple-element.28.ids_ref, f32[36,20]{1,0:T(8,128)S(1)} %get-tuple-element.42.bond_ref, bf16[12,32,128]{2,1,0:T(8,128)(2,1)S(1)} %copy-done, ...), custom_call_target="tpu_custom_call" | custom-call | flops 754974720 | bytes 16515072 | tf_op jit(solution)/shard_map/near_forces/pallas_call | solution.py:485
  52.4 2.2 %far_forces.1 = (f32[12,3,128]{2,1,0:T(4,128)S(1)}, f32[12,3,128]{2,1,0:T(4,128)S(1)}, f32[12,3,128]{2,1,0:T(4,128)S(1)}) custom-call(s32[2]{0:T(128)S(1)} %get-tuple-element.27.flag_ref, s32[12,20]{1,0:T(8,128)S(1)} %get-tuple-element.28.ids_ref, f32[36,20]{1,0:T(8,128)S(1)} %get-tuple-element.42.bond_ref, bf16[12,32,128]{2,1,0:T(8,128)(2,1)S(1)} %copy-done, ...), custom_call_target="tpu_custom_call" | custom-call | flops 251658240 | bytes 11796480 | tf_op jit(solution)/shard_map/far_forces/pallas_call | solution.py:542
  54.8 0.8 %collective-permute-start.22 = (f32[12,3,128]{2,1,0:T(4,128)S(1)}, f32[12,3,128]{2,1,0:T(4,128)S(1)}, u32[]{:S(2)}, u32[]{:S(2)}) collective-permute-start(f32[12,3,128]{2,1,0:T(4,128)S(1)} %get-tuple-element.48), channel_id=1, source_target_pairs={{0,28},{4,8},{8,4},{12,16},{16,12},{20,24},{24,20},{28,0},{1,29},{... | collective-permute-start | bytes 55304 | tf_op jit(solution)/shard_map/ppermute | solution.py:310
  55.9 3.0 %collective-permute-done.22.o_ref = f32[12,3,128]{2,1,0:T(4,128)S(1)} collective-permute-done((f32[12,3,128]{2,1,0:T(4,128)S(1)}, f32[12,3,128]{2,1,0:T(4,128)S(1)}, u32[]{:S(2)}, u32[]{:S(2)}) %collective-permute-start.22) | collective-permute-done | bytes 18464 | tf_op jit(solution)/shard_map/ppermute | solution.py:310
  59.2 1.6 %collective-permute-start.23 = (f32[24,128]{1,0:T(8,128)S(1)}, f32[24,128]{1,0:T(8,128)S(1)}, u32[]{:S(2)}, u32[]{:S(2)}) collective-permute-start(f32[24,128]{1,0:T(8,128)S(1)} %packed.1), channel_id=1, source_target_pairs={{0,1},{1,0},{2,3},{3,2},{4,5},{5,4},{6,7},{7,6},{8,9},{9,8},{10,11... | collective-permute-start | bytes 36872 | tf_op jit(solution)/shard_map/ppermute | solution.py:598
  60.8 2.1 %collective-permute-done.23 = f32[24,128]{1,0:T(8,128)S(1)} collective-permute-done((f32[24,128]{1,0:T(8,128)S(1)}, f32[24,128]{1,0:T(8,128)S(1)}, u32[]{:S(2)}, u32[]{:S(2)}) %collective-permute-start.23) | collective-permute-done | bytes 12320 | tf_op jit(solution)/shard_map/ppermute | solution.py:598
  63.0 2.6 %collective-permute-start.24 = (f32[24,128]{1,0:T(8,128)S(1)}, f32[24,128]{1,0:T(8,128)S(1)}, u32[]{:S(2)}, u32[]{:S(2)}) collective-permute-start(f32[24,128]{1,0:T(8,128)S(1)} %add.39.refs_0_), channel_id=1, source_target_pairs={{0,2},{1,3},{2,0},{3,1},{4,6},{5,7},{6,4},{7,5},{8,10},{9,11},{10,... | collective-permute-start | bytes 36872 | tf_op jit(solution)/shard_map/ppermute | solution.py:598
  65.5 2.0 %collective-permute-done.24.refs_1_ = f32[24,128]{1,0:T(8,128)S(1)} collective-permute-done((f32[24,128]{1,0:T(8,128)S(1)}, f32[24,128]{1,0:T(8,128)S(1)}, u32[]{:S(2)}, u32[]{:S(2)}) %collective-permute-start.24) | collective-permute-done | bytes 12320 | tf_op jit(solution)/shard_map/ppermute | solution.py:598
  (48 shorter events, 5.4 us)
Async XLA Ops:
  0.6 8.7 %copy-start = (bf16[12,32,128]{2,1,0:T(8,128)(2,1)S(1)}, bf16[12,32,128]{2,1,0:T(8,128)(2,1)}, u32[]{:S(2)}) copy-start(bf16[12,32,128]{2,1,0:T(8,128)(2,1)} %refs_0_.3) | copy-start | bytes 294916
  0.6 8.7 %copy-start.1 = (f32[12,128]{1,0:T(8,128)S(1)}, f32[12,128]{1,0:T(8,128)}, u32[]{:S(2)}) copy-start(f32[12,128]{1,0:T(8,128)} %site_ref.7) | copy-start | bytes 18436
  0.7 8.7 %collective-permute-start.1 = (bf16[12,32,128]{2,1,0:T(8,128)(2,1)}, bf16[12,32,128]{2,1,0:T(8,128)(2,1)S(1)}, u32[]{:S(2)}, u32[]{:S(2)}) collective-permute-start(bf16[12,32,128]{2,1,0:T(8,128)(2,1)} %refs_0_.3), channel_id=1, source_target_pairs={{0,28},{4,8},{8,4},{12,16},{16,12},{20,24},{24,20},{28,0},{1,29},{... | collective-permute-start | bytes 294920 | tf_op jit(solution)/shard_map/ppermute | solution.py:310
  4.1 5.3 %collective-permute-start = (bf16[12,32,128]{2,1,0:T(8,128)(2,1)}, bf16[12,32,128]{2,1,0:T(8,128)(2,1)S(1)}, u32[]{:S(2)}, u32[]{:S(2)}) collective-permute-start(bf16[12,32,128]{2,1,0:T(8,128)(2,1)} %refs_0_.3), channel_id=1, source_target_pairs={{0,4},{4,0},{8,12},{12,8},{16,20},{20,16},{24,28},{28,24},{1,5},{5... | collective-permute-start | bytes 294920 | tf_op jit(solution)/shard_map/ppermute | solution.py:311
  8.5 2.3 %collective-permute-start.2 = (bf16[12,32,128]{2,1,0:T(8,128)(2,1)S(1)}, bf16[12,32,128]{2,1,0:T(8,128)(2,1)S(1)}, u32[]{:S(2)}, u32[]{:S(2)}) collective-permute-start(bf16[12,32,128]{2,1,0:T(8,128)(2,1)S(1)} %get-tuple-element.31), channel_id=1, source_target_pairs={{0,4},{4,0},{8,12},{12,8},{16,20},{20,16},{24,28},{28,24},{1,5},{5... | collective-permute-start | bytes 294920 | tf_op jit(solution)/shard_map/ppermute | solution.py:311
  9.0 6.0 %collective-permute-start.3 = (bf16[12,32,128]{2,1,0:T(8,128)(2,1)S(1)}, bf16[12,32,128]{2,1,0:T(8,128)(2,1)S(1)}, u32[]{:S(2)}, u32[]{:S(2)}) collective-permute-start(bf16[12,32,128]{2,1,0:T(8,128)(2,1)S(1)} %get-tuple-element.32), channel_id=1, source_target_pairs={{0,28},{4,8},{8,4},{12,16},{16,12},{20,24},{24,20},{28,0},{1,29},{... | collective-permute-start | bytes 294920 | tf_op jit(solution)/shard_map/ppermute | solution.py:310
  15.0 5.5 %collective-permute-start.5 = (bf16[12,32,128]{2,1,0:T(8,128)(2,1)S(1)}, bf16[12,32,128]{2,1,0:T(8,128)(2,1)S(1)}, u32[]{:S(2)}, u32[]{:S(2)}) collective-permute-start(bf16[12,32,128]{2,1,0:T(8,128)(2,1)S(1)} %get-tuple-element.53.x_ref), channel_id=1, source_target_pairs={{0,28},{4,8},{8,4},{12,16},{16,12},{20,24},{24,20},{28,0},{1,29},{... | collective-permute-start | bytes 294920 | tf_op jit(solution)/shard_map/ppermute | solution.py:310
  15.1 5.5 %collective-permute-start.4 = (bf16[12,32,128]{2,1,0:T(8,128)(2,1)S(1)}, bf16[12,32,128]{2,1,0:T(8,128)(2,1)S(1)}, u32[]{:S(2)}, u32[]{:S(2)}) collective-permute-start(bf16[12,32,128]{2,1,0:T(8,128)(2,1)S(1)} %get-tuple-element.53.x_ref), channel_id=1, source_target_pairs={{0,4},{4,0},{8,12},{12,8},{16,20},{20,16},{24,28},{28,24},{1,5},{5... | collective-permute-start | bytes 294920 | tf_op jit(solution)/shard_map/ppermute | solution.py:311
  16.7 5.3 %collective-permute-start.7 = (bf16[12,32,128]{2,1,0:T(8,128)(2,1)S(1)}, bf16[12,32,128]{2,1,0:T(8,128)(2,1)S(1)}, u32[]{:S(2)}, u32[]{:S(2)}) collective-permute-start(bf16[12,32,128]{2,1,0:T(8,128)(2,1)S(1)} %ahead.3), channel_id=1, source_target_pairs={{0,28},{4,8},{8,4},{12,16},{16,12},{20,24},{24,20},{28,0},{1,29},{... | collective-permute-start | bytes 294920 | tf_op jit(solution)/shard_map/ppermute | solution.py:310
  20.5 1.6 %collective-permute-start.6 = (bf16[12,32,128]{2,1,0:T(8,128)(2,1)S(1)}, bf16[12,32,128]{2,1,0:T(8,128)(2,1)S(1)}, u32[]{:S(2)}, u32[]{:S(2)}) collective-permute-start(bf16[12,32,128]{2,1,0:T(8,128)(2,1)S(1)} %get-tuple-element.35), channel_id=1, source_target_pairs={{0,4},{4,0},{8,12},{12,8},{16,20},{20,16},{24,28},{28,24},{1,5},{5... | collective-permute-start | bytes 294920 | tf_op jit(solution)/shard_map/ppermute | solution.py:311
  23.5 5.4 %collective-permute-start.12 = (bf16[12,32,128]{2,1,0:T(8,128)(2,1)S(1)}, bf16[12,32,128]{2,1,0:T(8,128)(2,1)S(1)}, u32[]{:S(2)}, u32[]{:S(2)}) collective-permute-start(bf16[12,32,128]{2,1,0:T(8,128)(2,1)S(1)} %get-tuple-element.51.x_ref), channel_id=1, source_target_pairs={{0,28},{4,8},{8,4},{12,16},{16,12},{20,24},{24,20},{28,0},{1,29},{... | collective-permute-start | bytes 294920 | tf_op jit(solution)/shard_map/ppermute | solution.py:310
  25.7 3.2 %collective-permute-start.11 = (bf16[12,32,128]{2,1,0:T(8,128)(2,1)S(1)}, bf16[12,32,128]{2,1,0:T(8,128)(2,1)S(1)}, u32[]{:S(2)}, u32[]{:S(2)}) collective-permute-start(bf16[12,32,128]{2,1,0:T(8,128)(2,1)S(1)} %get-tuple-element.51.x_ref), channel_id=1, source_target_pairs={{0,4},{4,0},{8,12},{12,8},{16,20},{20,16},{24,28},{28,24},{1,5},{5... | collective-permute-start | bytes 294920 | tf_op jit(solution)/shard_map/ppermute | solution.py:311
  25.8 5.7 %collective-permute-start.14 = (bf16[12,32,128]{2,1,0:T(8,128)(2,1)S(1)}, bf16[12,32,128]{2,1,0:T(8,128)(2,1)S(1)}, u32[]{:S(2)}, u32[]{:S(2)}) collective-permute-start(bf16[12,32,128]{2,1,0:T(8,128)(2,1)S(1)} %ahead.4), channel_id=1, source_target_pairs={{0,28},{4,8},{8,4},{12,16},{16,12},{20,24},{24,20},{28,0},{1,29},{... | collective-permute-start | bytes 294920 | tf_op jit(solution)/shard_map/ppermute | solution.py:310
  28.1 3.5 %collective-permute-start.13 = (bf16[12,32,128]{2,1,0:T(8,128)(2,1)S(1)}, bf16[12,32,128]{2,1,0:T(8,128)(2,1)S(1)}, u32[]{:S(2)}, u32[]{:S(2)}) collective-permute-start(bf16[12,32,128]{2,1,0:T(8,128)(2,1)S(1)} %get-tuple-element.38), channel_id=1, source_target_pairs={{0,4},{4,0},{8,12},{12,8},{16,20},{20,16},{24,28},{28,24},{1,5},{5... | collective-permute-start | bytes 294920 | tf_op jit(solution)/shard_map/ppermute | solution.py:311
  28.7 8.7 %collective-permute-start.8 = (f32[2,32,128]{2,1,0:T(8,128)S(1)}, f32[2,32,128]{2,1,0:T(8,128)S(1)}, u32[]{:S(2)}, u32[]{:S(2)}) collective-permute-start(f32[2,32,128]{2,1,0:T(8,128)S(1)} %moments.1), channel_id=1, source_target_pairs={{0,4},{4,0},{8,12},{12,8},{16,20},{20,16},{24,28},{28,24},{1,5},{5... | collective-permute-start | bytes 98312 | tf_op jit(solution)/shard_map/ppermute | solution.py:317
  32.8 12.6 %collective-permute-start.16 = (bf16[12,32,128]{2,1,0:T(8,128)(2,1)S(1)}, bf16[12,32,128]{2,1,0:T(8,128)(2,1)S(1)}, u32[]{:S(2)}, u32[]{:S(2)}) collective-permute-start(bf16[12,32,128]{2,1,0:T(8,128)(2,1)S(1)} %get-tuple-element.49.x_ref), channel_id=1, source_target_pairs={{0,28},{4,8},{8,4},{12,16},{16,12},{20,24},{24,20},{28,0},{1,29},{... | collective-permute-start | bytes 294920 | tf_op jit(solution)/shard_map/ppermute | solution.py:310
  34.6 10.8 %collective-permute-start.15 = (bf16[12,32,128]{2,1,0:T(8,128)(2,1)S(1)}, bf16[12,32,128]{2,1,0:T(8,128)(2,1)S(1)}, u32[]{:S(2)}, u32[]{:S(2)}) collective-permute-start(bf16[12,32,128]{2,1,0:T(8,128)(2,1)S(1)} %get-tuple-element.49.x_ref), channel_id=1, source_target_pairs={{0,4},{4,0},{8,12},{12,8},{16,20},{20,16},{24,28},{28,24},{1,5},{5... | collective-permute-start | bytes 294920 | tf_op jit(solution)/shard_map/ppermute | solution.py:311
  34.6 12.2 %collective-permute-start.18 = (bf16[12,32,128]{2,1,0:T(8,128)(2,1)S(1)}, bf16[12,32,128]{2,1,0:T(8,128)(2,1)S(1)}, u32[]{:S(2)}, u32[]{:S(2)}) collective-permute-start(bf16[12,32,128]{2,1,0:T(8,128)(2,1)S(1)} %ahead.5), channel_id=1, source_target_pairs={{0,28},{4,8},{8,4},{12,16},{16,12},{20,24},{24,20},{28,0},{1,29},{... | collective-permute-start | bytes 294920 | tf_op jit(solution)/shard_map/ppermute | solution.py:310
  37.0 9.8 %collective-permute-start.17 = (bf16[12,32,128]{2,1,0:T(8,128)(2,1)S(1)}, bf16[12,32,128]{2,1,0:T(8,128)(2,1)S(1)}, u32[]{:S(2)}, u32[]{:S(2)}) collective-permute-start(bf16[12,32,128]{2,1,0:T(8,128)(2,1)S(1)} %get-tuple-element.40), channel_id=1, source_target_pairs={{0,4},{4,0},{8,12},{12,8},{16,20},{20,16},{24,28},{28,24},{1,5},{5... | collective-permute-start | bytes 294920 | tf_op jit(solution)/shard_map/ppermute | solution.py:311
  37.4 4.0 %collective-permute-start.9 = (f32[2,32,128]{2,1,0:T(8,128)S(1)}, f32[2,32,128]{2,1,0:T(8,128)S(1)}, u32[]{:S(2)}, u32[]{:S(2)}) collective-permute-start(f32[2,32,128]{2,1,0:T(8,128)S(1)} %add.34), channel_id=1, source_target_pairs={{0,8},{4,12},{8,0},{12,4},{16,24},{20,28},{24,16},{28,20},{1,9},{5... | collective-permute-start | bytes 98312 | tf_op jit(solution)/shard_map/ppermute | solution.py:317
  41.4 3.9 %collective-permute-start.10 = (f32[2,32,128]{2,1,0:T(8,128)S(1)}, f32[2,32,128]{2,1,0:T(8,128)S(1)}, u32[]{:S(2)}, u32[]{:S(2)}) collective-permute-start(f32[2,32,128]{2,1,0:T(8,128)S(1)} %add.35), channel_id=1, source_target_pairs={{0,16},{4,20},{8,24},{12,28},{16,0},{20,4},{24,8},{28,12},{1,17},{... | collective-permute-start | bytes 98312 | tf_op jit(solution)/shard_map/ppermute | solution.py:317
  47.0 5.4 %collective-permute-start.20 = (bf16[12,32,128]{2,1,0:T(8,128)(2,1)S(1)}, bf16[12,32,128]{2,1,0:T(8,128)(2,1)S(1)}, u32[]{:S(2)}, u32[]{:S(2)}) collective-permute-start(bf16[12,32,128]{2,1,0:T(8,128)(2,1)S(1)} %get-tuple-element.43.refs_3_.refs_1_), channel_id=1, source_target_pairs={{0,28},{4,8},{8,4},{12,16},{16,12},{20,24},{24,20},{28,0},{1,29},{... | collective-permute-start | bytes 294920 | tf_op jit(solution)/shard_map/ppermute | solution.py:310
  47.1 5.3 %collective-permute-start.19 = (bf16[12,32,128]{2,1,0:T(8,128)(2,1)S(1)}, bf16[12,32,128]{2,1,0:T(8,128)(2,1)S(1)}, u32[]{:S(2)}, u32[]{:S(2)}) collective-permute-start(bf16[12,32,128]{2,1,0:T(8,128)(2,1)S(1)} %get-tuple-element.43.refs_3_.refs_1_), channel_id=1, source_target_pairs={{0,4},{4,0},{8,12},{12,8},{16,20},{20,16},{24,28},{28,24},{1,5},{5... | collective-permute-start | bytes 294920 | tf_op jit(solution)/shard_map/ppermute | solution.py:311
  51.8 7.1 %copy-start.2 = (s32[12,128]{1,0:T(8,128)S(1)}, s32[12,128]{1,0:T(8,128)}, u32[]{:S(2)}) copy-start(s32[12,128]{1,0:T(8,128)} %atom_ref.1) | copy-start | bytes 18436
  54.6 1.3 %collective-permute-start.21 = (f32[12,3,128]{2,1,0:T(4,128)S(1)}, f32[12,3,128]{2,1,0:T(4,128)S(1)}, u32[]{:S(2)}, u32[]{:S(2)}) collective-permute-start(f32[12,3,128]{2,1,0:T(4,128)S(1)} %get-tuple-element.47), channel_id=1, source_target_pairs={{0,4},{4,0},{8,12},{12,8},{16,20},{20,16},{24,28},{28,24},{1,5},{5... | collective-permute-start | bytes 55304 | tf_op jit(solution)/shard_map/ppermute | solution.py:311
  54.8 4.2 %collective-permute-start.22 = (f32[12,3,128]{2,1,0:T(4,128)S(1)}, f32[12,3,128]{2,1,0:T(4,128)S(1)}, u32[]{:S(2)}, u32[]{:S(2)}) collective-permute-start(f32[12,3,128]{2,1,0:T(4,128)S(1)} %get-tuple-element.48), channel_id=1, source_target_pairs={{0,28},{4,8},{8,4},{12,16},{16,12},{20,24},{24,20},{28,0},{1,29},{... | collective-permute-start | bytes 55304 | tf_op jit(solution)/shard_map/ppermute | solution.py:310
  59.2 3.7 %collective-permute-start.23 = (f32[24,128]{1,0:T(8,128)S(1)}, f32[24,128]{1,0:T(8,128)S(1)}, u32[]{:S(2)}, u32[]{:S(2)}) collective-permute-start(f32[24,128]{1,0:T(8,128)S(1)} %packed.1), channel_id=1, source_target_pairs={{0,1},{1,0},{2,3},{3,2},{4,5},{5,4},{6,7},{7,6},{8,9},{9,8},{10,11... | collective-permute-start | bytes 36872 | tf_op jit(solution)/shard_map/ppermute | solution.py:598
  63.0 4.6 %collective-permute-start.24 = (f32[24,128]{1,0:T(8,128)S(1)}, f32[24,128]{1,0:T(8,128)S(1)}, u32[]{:S(2)}, u32[]{:S(2)}) collective-permute-start(f32[24,128]{1,0:T(8,128)S(1)} %add.39.refs_0_), channel_id=1, source_target_pairs={{0,2},{1,3},{2,0},{3,1},{4,6},{5,7},{6,4},{7,5},{8,10},{9,11},{10,... | collective-permute-start | bytes 36872 | tf_op jit(solution)/shard_map/ppermute | solution.py:598

commit v6 on v5

--- a/solution.py
+++ b/solution.py
@@ -54,8 +54,8 @@
     height = rows // CHUNKS
 
     def kernel(col_hbm, x_hbm, k_hbm, bond_hbm, table_hbm, mu_ref, *refs):
-        flag_ref, ids_ref, at_ref, out_ref, coeff_ref, own_ref, even_ref, odd_ref, kv_ref, kt_ref = refs[:10]
-        acc, col_sm, col_vm, xv, bond_vm, table_vm, sems, small = refs[10:]
+        flag_ref, ids_ref, at_ref, out_ref, coeff_ref, own_ref, even_ref, odd_ref, kv_ref, kt_ref, image_ref = refs[:11]
+        acc, col_sm, col_vm, xv, bond_vm, table_vm, ids_vm, at_vm, out_vm, sems, small = refs[11:]
         me = lax.axis_index("clus")
 
         def load(index):
@@ -88,18 +88,25 @@
         flag_ref[1] = odd
 
         ids = jnp.where(col >= 0, col - me * rows + REACH, frame)
-        ids_ref[...] = ids
+        ids_vm[...] = ids
         side = lax.broadcasted_iota(jnp.int32, (rows, REACH), 1) + odd * (REACH + rows)
         at = jnp.full((rows, REACH), slots, jnp.int32)
         for m in range(slots):
             at = jnp.where(ids[:, m : m + 1] == side, m, at)
-        at_ref[...] = at
+        at_vm[...] = at
         for c in range(rows):
             kv_ref[slots, c] = jnp.zeros((block, block), kv_ref.dtype)
+            image_ref[slots, c] = jnp.zeros((probes, block), f32)
         for copy in copies[1:]:
             copy.wait()
         for axis in range(3):
-            out_ref[axis * rows : (axis + 1) * rows] = bond_vm[axis].astype(f32)
+            lines = slice(axis * rows, (axis + 1) * rows)
+            out_vm[lines, :slots] = bond_vm[axis].astype(f32)
+            out_vm[lines, slots:] = jnp.zeros((rows, 1), f32)
+        tables = ((ids_vm, ids_ref), (at_vm, at_ref), (out_vm, out_ref))
+        placed = [pltpu.make_async_copy(a, b, small.at[5 + i]) for i, (a, b) in enumerate(tables)]
+        for copy in placed:
+            copy.start()
         energy = (table_vm[7:8] - mu_ref[0]) / SMEARING_TEMP
         occupied = 1.0 / (1.0 + jnp.exp(energy))
         total = jnp.sum(table_vm[...] * occupied, axis=1, keepdims=True)
@@ -125,6 +132,8 @@
                             for slot in (m, m + 1):
                                 at = col_sm[c, slot]
                                 targets.append(jnp.where(at >= 0, at - me * rows + REACH, frame))
+                            image_ref[m, c] = parts[-2]
+                            image_ref[m + 1, c] = parts[-1]
                             kt_ref[m, c] = pair[0].T
                             kt_ref[m + 1, c] = pair[1].T
                         values = [acc[t] + part for t, part in zip(targets, parts)]
@@ -142,6 +151,8 @@
         own_ref[...] = acc[pl.ds(REACH, rows)]
         even_ref[...] = acc[pl.ds((1 - odd) * (REACH + rows), REACH)].astype(bf16)
         odd_ref[...] = acc[pl.ds(odd * (REACH + rows), REACH)].astype(bf16)
+        for copy in placed:
+            copy.wait()
 
     side = jax.ShapeDtypeStruct((REACH, probes, block), bf16)
     hbm = pl.BlockSpec(memory_space=pltpu.HBM)
@@ -149,19 +160,20 @@
     return pl.pallas_call(
         kernel,
         out_shape=[
-            jax.ShapeDtypeStruct((2,), jnp.int32),
-            jax.ShapeDtypeStruct((rows, slots), jnp.int32),
-            jax.ShapeDtypeStruct((rows, REACH), jnp.int32),
-            jax.ShapeDtypeStruct((3 * rows, slots), f32),
+            pltpu.SMEM((2,), jnp.int32),
+            pltpu.SMEM((rows, slots), jnp.int32),
+            pltpu.SMEM((rows, REACH), jnp.int32),
+            pltpu.SMEM((3 * rows, slots + 1), f32),
             jax.ShapeDtypeStruct((8, 128), f32),
             jax.ShapeDtypeStruct((rows, probes, block), f32),
             side,
             side,
             jax.ShapeDtypeStruct((slots + 1, *k.shape[1:]), k.dtype),
             jax.ShapeDtypeStruct(k.shape, k.dtype),
+            jax.ShapeDtypeStruct((slots + 1, rows, probes, block), f32),
         ],
         in_specs=[hbm] * 5 + [SM],
-        out_specs=[SM] + [VM] * 9,
+        out_specs=[SM] * 4 + [VM] * 7,
         scratch_shapes=[
             pltpu.VMEM((frame + 1, probes, block), f32),
             pltpu.SMEM((rows, slots), jnp.int32),
@@ -169,8 +181,11 @@
             pltpu.VMEM(x.shape, x.dtype),
             pltpu.VMEM(bond_dir.shape, bond_dir.dtype),
             pltpu.VMEM((8, 128), f32),
+            pltpu.VMEM((rows, slots), jnp.int32),
+            pltpu.VMEM((rows, REACH), jnp.int32),
+            pltpu.VMEM((3 * rows, slots + 1), f32),
             pltpu.SemaphoreType.DMA((2 * CHUNKS,)),
-            pltpu.SemaphoreType.DMA((5,)),
+            pltpu.SemaphoreType.DMA((8,)),
         ],
         name="opening",
         **params(2 * slots * rows * probes * block * block, k.size * 2),
@@ -446,33 +461,58 @@
     return parts[0]
 
 
-def near_forces(flag, ids, bond, v, v_even, v_crossed, w, k, kt):
+def turned_images(flag, ids, v, v_even, v_crossed, kt):
     slots, rows, block, _ = kt.shape
     probes = v.shape[1]
+
+    def kernel(flag_ref, ids_ref, v_ref, ve_ref, vo_ref, kt_ref, out_ref, vf):
+        fill_frame(vf, flag_ref[1], v_ref, ve_ref, vo_ref)
+
+        def body(count):
+            for c in range(rows):
+                for m in range(0, count, 2):
+                    two = (m, m + 1)
+                    left = jnp.concatenate([vf[ids_ref[c, slot]] for slot in two], axis=0)
+                    weights = jnp.concatenate([kt_ref[slot, c] for slot in two], axis=1)
+                    back = dot(left, weights, NN)
+                    out_ref[m, c] = back[:probes, :block]
+                    out_ref[m + 1, c] = back[probes:, block:]
+
+        by_size(flag_ref, slots, body)
+
+    return pl.pallas_call(
+        kernel,
+        out_shape=jax.ShapeDtypeStruct((slots, rows, probes, block), f32),
+        in_specs=[SM, SM] + [VM] * 4,
+        out_specs=VM,
+        scratch_shapes=[pltpu.VMEM((rows + 2 * REACH + 1, probes, block), bf16)],
+        name="turned_images",
+        **params(2 * slots * rows * probes * block * block, kt.size * 2),
+    )(flag, ids, v, v_even, v_crossed, kt)
+
+
+def near_forces(flag, ids, bond, v, v_even, v_crossed, w, k, turned):
+    slots, rows, probes, block = turned.shape
     frame = rows + 2 * REACH
 
     def kernel(flag_ref, ids_ref, bond_ref, *refs):
-        v_ref, ve_ref, vo_ref, w_ref, k_ref, kt_ref, acc, image_ref, vf = refs
+        v_ref, ve_ref, vo_ref, w_ref, k_ref, turned_ref, acc, vf = refs
         fill_frame(vf, flag_ref[1], v_ref, ve_ref, vo_ref)
         acc[...] = jnp.zeros_like(acc)
 
         def body(count):
             for c in range(rows):
                 mine = w_ref[c].astype(f32)
-                left = jnp.concatenate([w_ref[c], v_ref[c]], axis=0)
                 row = [jnp.zeros((8, block), f32)] * 3
                 for m in range(0, count, 2):
                     two = (m, m + 1)
-                    far = [vf[ids_ref[c, slot]] for slot in two]
-                    out = dot(left, jnp.concatenate([k_ref[slot, c] for slot in two], axis=1), NN)
-                    weights = jnp.concatenate([kt_ref[slot, c] for slot in two], axis=1)
-                    back = dot(jnp.concatenate(far, axis=0), weights, NN)
+                    weights = jnp.concatenate([k_ref[slot, c] for slot in two], axis=1)
+                    out = dot(w_ref[c], weights, NN)
                     for i, slot in enumerate(two):
                         d = ids_ref[c, slot]
-                        lanes = slice(i * block, (i + 1) * block)
-                        image_ref[slot, c] = out[probes:, lanes]
-                        col_part = folded(far[i].astype(f32) * out[:probes, lanes])
-                        row_part = folded(mine * back[i * probes : (i + 1) * probes, lanes])
+                        image = out[:, i * block : (i + 1) * block]
+                        col_part = folded(vf[d].astype(f32) * image)
+                        row_part = folded(mine * turned_ref[slot, c])
                         for axis in range(3):
                             b = bond_ref[axis * rows + c, slot]
                             row[axis] = row[axis] + b * row_part
@@ -484,16 +524,49 @@
 
     return pl.pallas_call(
         kernel,
-        out_shape=[
-            jax.ShapeDtypeStruct((frame + 1, 3, 8, block), f32),
-            jax.ShapeDtypeStruct((slots, rows, probes, block), f32),
-        ],
+        out_shape=jax.ShapeDtypeStruct((frame + 1, 3, 8, block), f32),
         in_specs=[SM, SM, SM] + [VM] * 6,
-        out_specs=[VM] * 2,
+        out_specs=VM,
         scratch_shapes=[pltpu.VMEM((frame + 1, probes, block), bf16)],
         name="near_forces",
-        **params(6 * slots * rows * probes * block * block, k.size * 4),
-    )(flag, ids, bond, v, v_even, v_crossed, w, k, kt)
+        **params(2 * slots * rows * probes * block * block, k.size * 4),
+    )(flag, ids, bond, v, v_even, v_crossed, w, k, turned)
+
+
+def ahead_forces(flag, at, bond, w_crossed, image, started):
+    rows = at.shape[0]
+    block = image.shape[3]
+
+    def kernel(flag_ref, at_ref, bond_ref, w_ref, image_ref, start_ref, out_ref):
+        def body(above):
+            base = REACH + rows if above else 0
+            for j in range(REACH):
+                theirs = w_ref[j].astype(f32)
+                total = [start_ref[base + j, axis] for axis in range(3)]
+                for c in range(j, rows) if above else range(min(j + 1, rows)):
+                    slot = at_ref[c, j]
+                    part = folded(theirs * image_ref[slot, c])
+                    for axis in range(3):
+                        total[axis] = total[axis] + bond_ref[axis * rows + c, slot] * part
+                for axis in range(3):
+                    out_ref[j, axis : axis + 1] = DECAY * jnp.sum(total[axis], axis=0, keepdims=True)
+
+        @pl.when(flag_ref[1] == 0)
+        def _():
+            body(False)
+
+        @pl.when(flag_ref[1] != 0)
+        def _():
+            body(True)
+
+    return pl.pallas_call(
+        kernel,
+        out_shape=jax.ShapeDtypeStruct((REACH, 3, block), f32),
+        in_specs=[SM, SM, SM] + [VM] * 3,
+        out_specs=VM,
+        name="ahead_forces",
+        **params(1000000, 2000000),
+    )(flag, at, bond, w_crossed, image, started)
 
 
 def far_forces(flag, ids, bond, v, w, w_even, w_crossed, kt, image, started):
@@ -503,7 +576,7 @@
 
     def kernel(flag_ref, ids_ref, bond_ref, *refs):
         v_ref, w_ref, we_ref, wo_ref, kt_ref, image_ref, start_ref = refs[:7]
-        own_ref, even_ref, odd_ref, wf, acc = refs[7:]
+        own_ref, even_ref, wf, acc = refs[7:]
         odd = flag_ref[1]
         fill_frame(wf, odd, w_ref, we_ref, wo_ref)
         acc[...] = start_ref[...]
@@ -536,14 +609,15 @@
 
         own_ref[...] = taken(REACH, rows)
         even_ref[...] = taken((1 - odd) * (REACH + rows), REACH)
-        odd_ref[...] = taken(odd * (REACH + rows), REACH)
-
-    side = jax.ShapeDtypeStruct((REACH, 3, block), f32)
-    return pl.pallas_call(
-        kernel,
-        out_shape=[jax.ShapeDtypeStruct((rows, 3, block), f32), side, side],
+
+    return pl.pallas_call(
+        kernel,
+        out_shape=[
+            jax.ShapeDtypeStruct((rows, 3, block), f32),
+            jax.ShapeDtypeStruct((REACH, 3, block), f32),
+        ],
         in_specs=[SM, SM, SM] + [VM] * 7,
-        out_specs=[VM] * 3,
+        out_specs=[VM] * 2,
         scratch_shapes=[
             pltpu.VMEM((frame + 1, probes, block), bf16),
             pltpu.VMEM((frame + 1, 3, 8, block), f32),
@@ -559,8 +633,11 @@
     x = probes
     even, crossed = exchange(x, x)
     v_even, v_crossed = even, crossed
-    flag, ids, at, bond, coeffs, own, to_even, to_odd, k, kt = opening(
+    flag, ids, at, bond, coeffs, own, to_even, to_odd, k, kt, kept = opening(
         block_col.T, x, hopping, jnp.transpose(bond_dir, (0, 2, 1)), chemical_potential
+    )
+    flag, ids, at, bond = (
+        pltpu.with_memory_space_constraint(a, pltpu.SMEM) for a in (flag, ids, at, bond)
     )
     rounds = (lax.axis_size("clus") - 1).bit_length()
     cheb = [probes]
@@ -573,6 +650,8 @@
         back_even, back_crossed = exchange(to_even, to_odd)
         if term > 2:
             sums = doubled(term - 2, sums, "clus")
+        if term == 1:
+            turned = turned_images(flag, ids, x, even, crossed, kt)
         image = direct(flag, ids, x, even, crossed, kt, own, onsite)
         if term == ORDER:
             break
@@ -584,9 +663,10 @@
         sums = doubled(index, sums, "clus")
     weighted, head = closed(coeffs, sums, orbitals, cheb, image, back_even, back_crossed)
     w_even, w_crossed = exchange(weighted, weighted)
-    started, image = near_forces(flag, ids, bond, probes, v_even, v_crossed, weighted, k, kt)
-    own, to_even, to_odd = far_forces(
-        flag, ids, bond, probes, weighted, w_even, w_crossed, kt, image, started
+    started = near_forces(flag, ids, bond, probes, v_even, v_crossed, weighted, k, turned)
+    to_odd = ahead_forces(flag, at, bond, w_crossed, kept, started)
+    own, to_even = far_forces(
+        flag, ids, bond, probes, weighted, w_even, w_crossed, kt, kept, started
     )
     from_even, from_odd = exchange(to_even, to_odd)
     part = packed(head, own, from_even, from_odd, atom_of)

time: 68.6 us -> 63.4 us (0.924)
  Pallas kernels: 23.6 us -> 15.1 us
  waiting for transfers between devices: 19.1 us -> 23.2 us
  starting transfers between devices: 23.7 us -> 23 us
    ppermute x10, waiting for transfers between devices: 9.08 us -> 12.7 us  [exchange(): crossed = lax.ppermute(odd_side, 'clus', shifted)]
    pallas_call x4, Pallas kernels: 5.72 us -> 3.05 us  [direct(): pl.pallas_call(kernel, out_shape=jax.ShapeDtypeStruct((rows, probes, bloc...]
    pallas_call x3, Pallas kernels: 3.73 us -> 1.66 us  [ahead(): pl.pallas_call(kernel, out_shape=jax.ShapeDtypeStruct((REACH, probes, blo...]
    pallas_call x3, Pallas kernels: 4.36 us -> 2.33 us  [spread(): pl.pallas_call(kernel, out_shape=[jax.ShapeDtypeStruct((rows, probes, blo...]
    ppermute x3, waiting for transfers between devices: 5.55 us -> 7.04 us  [doubled(): lax.ppermute(part, axis, [(i, i ^ 1 << index) for i in range(count)])]
    ppermute x2, starting transfers between devices: 4.18 us -> 5.5 us  [local(): lax.ppermute(part, 'probe', [(i, i ^ step) for i in range(count)])]
    ppermute x3, starting transfers between devices: 2.43 us -> 1.42 us  [doubled(): lax.ppermute(part, axis, [(i, i ^ 1 << index) for i in range(count)])]
    pallas_call x1, Pallas kernels: 2.21 us -> 1.2 us  [far_forces(): pl.pallas_call(kernel, out_shape=[jax.ShapeDtypeStruct((rows, 3, block),...]
  transfers between devices with their start and end apart: 25 -> 25, of which waited for: 10 -> 11; matrix products, arithmetic and copies ran while one was open for 0% -> 0% of each run, Pallas kernels for 28% -> 21%
where the time goes in v6:
time: 63.4 us; the launch traced here: 63.2 us
  waiting for transfers between devices  23.2 us (37%)
  starting transfers between devices  23 us (36%)
  Pallas kernels  15.1 us (24%)
  between operations  1.75 us (3%)
    ppermute x10, waiting for transfers between devices, exchange(): crossed = lax.ppermute(odd_side, 'clus', shifted)  12.7 us
    ppermute x10, starting transfers between devices, exchange(): crossed = lax.ppermute(odd_side, 'clus', shifted)  12.6 us
    ppermute x3, waiting for transfers between devices, doubled(): lax.ppermute(part, axis, [(i, i ^ 1 << index) for i in range(count)])  7.04 us
    ppermute x2, starting transfers between devices, local(): lax.ppermute(part, 'probe', [(i, i ^ step) for i in range(count)])  5.5 us
    ppermute x10, starting transfers between devices, exchange(): even = lax.ppermute(even_side, 'clus', paired)  3.53 us
    ppermute x2, waiting for transfers between devices, local(): lax.ppermute(part, 'probe', [(i, i ^ step) for i in range(count)])  3.34 us
    pallas_call x1, Pallas kernels, opening(): pl.pallas_call(kernel, out_shape=[pltpu.SMEM((2,), jnp.int32), pltpu.SMEM...  3.23 us
    pallas_call x4, Pallas kernels, direct(): pl.pallas_call(kernel, out_shape=jax.ShapeDtypeStruct((rows, probes, bloc...  3.05 us
  transfers between devices with their start and end apart: 25, of which 11 were waited for; matrix products, arithmetic and copies ran while one was open for 0% of the time, Pallas kernels for 21%

profile of v6, /device:TPU:0, one launch (start us, length us, event | category | flops | bytes accessed | tf_op | source)
XLA Modules:
  0.0 63.2 jit_solution(13875878137242366002)
XLA Ops:
  1.2 3.5 %collective-permute-start.1 = (bf16[12,32,128]{2,1,0:T(8,128)(2,1)}, bf16[12,32,128]{2,1,0:T(8,128)(2,1)S(1)}, u32[]{:S(2)}, u32[]{:S(2)}) collective-permute-start(bf16[12,32,128]{2,1,0:T(8,128)(2,1)} %refs_0_.3), channel_id=1, source_target_pairs={{0,28},{4,8},{8,4},{12,16},{16,12},{20,24},{24,20},{28,0},{1,29},{... | collective-permute-start | bytes 294920 | tf_op jit(solution)/shard_map/ppermute | solution.py:325
  5.4 3.2 %opening.1 = (s32[2]{0:T(128)S(4)}, s32[12,20]{1,0:T(8,128)S(4)}, s32[12,12]{1,0:T(8,128)S(4)}, f32[36,21]{1,0:T(8,128)S(4)}, f32[8,128]{1,0:T(8,128)S(1)}, /*in...) custom-call(s32[12,20]{1,0:T(8,128)} %bitcast.3, ...), custom_call_target="tpu_custom_call" | custom-call | flops 251658240 | bytes 7864320 | tf_op jit(solution)/shard_map/opening/pallas_call | solution.py:160
  9.4 0.8 %direct.4 = f32[12,32,128]{2,1,0:T(8,128)S(1)} custom-call(s32[2]{0:T(128)S(4)} %get-tuple-element.25.flag_ref, s32[12,20]{1,0:T(8,128)S(4)} %get-tuple-element.26.ids_ref, bf16[12,32,128]{2,1,0:T(8,128)(2,1)S(1)} %copy-done, bf16[12,32,128]{2,1,0:T(8,128)(2,1)S(1)} %collective-permute-done.e_ref.ve_ref.refs_1_, ...), custom_call_target="tpu_custom_call" | custom-call | flops 251658240 | bytes 7864320 | tf_op jit(solution)/shard_map/direct/pallas_call | solution.py:446
  10.2 4.3 %collective-permute-done.3 = bf16[12,32,128]{2,1,0:T(8,128)(2,1)S(1)} collective-permute-done((bf16[12,32,128]{2,1,0:T(8,128)(2,1)S(1)}, bf16[12,32,128]{2,1,0:T(8,128)(2,1)S(1)}, u32[]{:S(2)}, u32[]{:S(2)}) %collective-permute-start.3) | collective-permute-done | bytes 98336 | tf_op jit(solution)/shard_map/ppermute | solution.py:325
  15.4 2.4 %collective-permute-start.7 = (bf16[12,32,128]{2,1,0:T(8,128)(2,1)S(1)}, bf16[12,32,128]{2,1,0:T(8,128)(2,1)S(1)}, u32[]{:S(2)}, u32[]{:S(2)}) collective-permute-start(bf16[12,32,128]{2,1,0:T(8,128)(2,1)S(1)} %ahead.3), channel_id=1, source_target_pairs={{0,28},{4,8},{8,4},{12,16},{16,12},{20,24},{24,20},{28,0},{1,29},{... | collective-permute-start | bytes 294920 | tf_op jit(solution)/shard_map/ppermute | solution.py:325
  17.8 0.8 %spread.3 = (f32[12,32,128]{2,1,0:T(8,128)S(1)}, bf16[12,32,128]{2,1,0:T(8,128)(2,1)S(1)}) custom-call(s32[2]{0:T(128)S(4)} %get-tuple-element.25.flag_ref, s32[12,20]{1,0:T(8,128)S(4)} %get-tuple-element.26.ids_ref, bf16[12,32,128]{2,1,0:T(8,128)(2,1)S(1)} %get-tuple-element.49.x_ref, bf16[21,12,128,128]{3,2,1,0:T(8,128)(2,1)S(1)} %get-tuple-element.31.k_ref.refs_4_), custom_call_target="tpu_custom_call" | custom-call | flops 251658240 | bytes 8257536 | tf_op jit(solution)/shard_map/spread/pallas_call | solution.py:409
  18.7 1.9 %collective-permute-done.5.o_ref = bf16[12,32,128]{2,1,0:T(8,128)(2,1)S(1)} collective-permute-done((bf16[12,32,128]{2,1,0:T(8,128)(2,1)S(1)}, bf16[12,32,128]{2,1,0:T(8,128)(2,1)S(1)}, u32[]{:S(2)}, u32[]{:S(2)}) %collective-permute-start.5) | collective-permute-done | bytes 98336 | tf_op jit(solution)/shard_map/ppermute | solution.py:325
  20.6 0.8 %direct.5 = f32[12,32,128]{2,1,0:T(8,128)S(1)} custom-call(s32[2]{0:T(128)S(4)} %get-tuple-element.25.flag_ref, s32[12,20]{1,0:T(8,128)S(4)} %get-tuple-element.26.ids_ref, bf16[12,32,128]{2,1,0:T(8,128)(2,1)S(1)} %get-tuple-element.49.x_ref, bf16[12,32,128]{2,1,0:T(8,128)(2,1)S(1)} %collective-permute-done.4.e_ref, ...), custom_call_target="tpu_custom_call" | custom-call | flops 251658240 | bytes 7864320 | tf_op jit(solution)/shard_map/direct/pallas_call | solution.py:446
  21.4 0.8 %collective-permute-done.7 = bf16[12,32,128]{2,1,0:T(8,128)(2,1)S(1)} collective-permute-done((bf16[12,32,128]{2,1,0:T(8,128)(2,1)S(1)}, bf16[12,32,128]{2,1,0:T(8,128)(2,1)S(1)}, u32[]{:S(2)}, u32[]{:S(2)}) %collective-permute-start.7) | collective-permute-done | bytes 98336 | tf_op jit(solution)/shard_map/ppermute | solution.py:325
  22.2 0.7 %ahead.4 = bf16[12,32,128]{2,1,0:T(8,128)(2,1)S(1)} custom-call(s32[2]{0:T(128)S(4)} %get-tuple-element.25.flag_ref, s32[12,12]{1,0:T(8,128)S(4)} %get-tuple-element.34.at_ref, bf16[12,32,128]{2,1,0:T(8,128)(2,1)S(1)} %get-tuple-element.47.x_ref, bf16[21,12,128,128]{3,2,1,0:T(8,128)(2,1)S(1)} %get-tuple-element.31.k_ref.refs_4_), custom_call_target="tpu_custom_call" | custom-call | flops 83886080 | bytes 2621440 | tf_op jit(solution)/shard_map/ahead/pallas_call | solution.py:371
  23.0 0.7 %collective-permute-start.12 = (bf16[12,32,128]{2,1,0:T(8,128)(2,1)S(1)}, bf16[12,32,128]{2,1,0:T(8,128)(2,1)S(1)}, u32[]{:S(2)}, u32[]{:S(2)}) collective-permute-start(bf16[12,32,128]{2,1,0:T(8,128)(2,1)S(1)} %get-tuple-element.47.x_ref), channel_id=1, source_target_pairs={{0,28},{4,8},{8,4},{12,16},{16,12},{20,24},{24,20},{28,0},{1,29},{... | collective-permute-start | bytes 294920 | tf_op jit(solution)/shard_map/ppermute | solution.py:325
  23.7 2.0 %collective-permute-start.14 = (bf16[12,32,128]{2,1,0:T(8,128)(2,1)S(1)}, bf16[12,32,128]{2,1,0:T(8,128)(2,1)S(1)}, u32[]{:S(2)}, u32[]{:S(2)}) collective-permute-start(bf16[12,32,128]{2,1,0:T(8,128)(2,1)S(1)} %ahead.4), channel_id=1, source_target_pairs={{0,28},{4,8},{8,4},{12,16},{16,12},{20,24},{24,20},{28,0},{1,29},{... | collective-permute-start | bytes 294920 | tf_op jit(solution)/shard_map/ppermute | solution.py:325
  25.7 0.8 %spread.4 = (f32[12,32,128]{2,1,0:T(8,128)S(1)}, bf16[12,32,128]{2,1,0:T(8,128)(2,1)S(1)}) custom-call(s32[2]{0:T(128)S(4)} %get-tuple-element.25.flag_ref, s32[12,20]{1,0:T(8,128)S(4)} %get-tuple-element.26.ids_ref, bf16[12,32,128]{2,1,0:T(8,128)(2,1)S(1)} %get-tuple-element.47.x_ref, bf16[21,12,128,128]{3,2,1,0:T(8,128)(2,1)S(1)} %get-tuple-element.31.k_ref.refs_4_), custom_call_target="tpu_custom_call" | custom-call | flops 251658240 | bytes 8257536 | tf_op jit(solution)/shard_map/spread/pallas_call | solution.py:409
  27.2 1.8 %collective-permute-done.12.o_ref = bf16[12,32,128]{2,1,0:T(8,128)(2,1)S(1)} collective-permute-done((bf16[12,32,128]{2,1,0:T(8,128)(2,1)S(1)}, bf16[12,32,128]{2,1,0:T(8,128)(2,1)S(1)}, u32[]{:S(2)}, u32[]{:S(2)}) %collective-permute-start.12) | collective-permute-done | bytes 98336 | tf_op jit(solution)/shard_map/ppermute | solution.py:325
  29.0 0.8 %direct.6 = f32[12,32,128]{2,1,0:T(8,128)S(1)} custom-call(s32[2]{0:T(128)S(4)} %get-tuple-element.25.flag_ref, s32[12,20]{1,0:T(8,128)S(4)} %get-tuple-element.26.ids_ref, bf16[12,32,128]{2,1,0:T(8,128)(2,1)S(1)} %get-tuple-element.47.x_ref, bf16[12,32,128]{2,1,0:T(8,128)(2,1)S(1)} %collective-permute-done.11.e_ref, ...), custom_call_target="tpu_custom_call" | custom-call | flops 251658240 | bytes 7864320 | tf_op jit(solution)/shard_map/direct/pallas_call | solution.py:446
  29.8 0.7 %collective-permute-done.14 = bf16[12,32,128]{2,1,0:T(8,128)(2,1)S(1)} collective-permute-done((bf16[12,32,128]{2,1,0:T(8,128)(2,1)S(1)}, bf16[12,32,128]{2,1,0:T(8,128)(2,1)S(1)}, u32[]{:S(2)}, u32[]{:S(2)}) %collective-permute-start.14) | collective-permute-done | bytes 98336 | tf_op jit(solution)/shard_map/ppermute | solution.py:325
  31.7 2.1 %collective-permute-start.18 = (bf16[12,32,128]{2,1,0:T(8,128)(2,1)S(1)}, bf16[12,32,128]{2,1,0:T(8,128)(2,1)S(1)}, u32[]{:S(2)}, u32[]{:S(2)}) collective-permute-start(bf16[12,32,128]{2,1,0:T(8,128)(2,1)S(1)} %ahead.5), channel_id=1, source_target_pairs={{0,28},{4,8},{8,4},{12,16},{16,12},{20,24},{24,20},{28,0},{1,29},{... | collective-permute-start | bytes 294920 | tf_op jit(solution)/shard_map/ppermute | solution.py:325
  33.8 0.8 %spread.5 = (f32[12,32,128]{2,1,0:T(8,128)S(1)}, bf16[12,32,128]{2,1,0:T(8,128)(2,1)S(1)}) custom-call(s32[2]{0:T(128)S(4)} %get-tuple-element.25.flag_ref, s32[12,20]{1,0:T(8,128)S(4)} %get-tuple-element.26.ids_ref, bf16[12,32,128]{2,1,0:T(8,128)(2,1)S(1)} %get-tuple-element.45.x_ref, bf16[21,12,128,128]{3,2,1,0:T(8,128)(2,1)S(1)} %get-tuple-element.31.k_ref.refs_4_), custom_call_target="tpu_custom_call" | custom-call | flops 251658240 | bytes 8257536 | tf_op jit(solution)/shard_map/spread/pallas_call | solution.py:409
  35.3 3.4 %collective-permute-done.9 = f32[2,32,128]{2,1,0:T(8,128)S(1)} collective-permute-done((f32[2,32,128]{2,1,0:T(8,128)S(1)}, f32[2,32,128]{2,1,0:T(8,128)S(1)}, u32[]{:S(2)}, u32[]{:S(2)}) %collective-permute-start.9) | collective-permute-done | bytes 32800 | tf_op jit(solution)/shard_map/ppermute | solution.py:332
  39.0 3.7 %collective-permute-done.10 = f32[2,32,128]{2,1,0:T(8,128)S(1)} collective-permute-done((f32[2,32,128]{2,1,0:T(8,128)S(1)}, f32[2,32,128]{2,1,0:T(8,128)S(1)}, u32[]{:S(2)}, u32[]{:S(2)}) %collective-permute-start.10) | collective-permute-done | bytes 32800 | tf_op jit(solution)/shard_map/ppermute | solution.py:332
  42.6 0.8 %direct.7.y_ref = f32[12,32,128]{2,1,0:T(8,128)S(1)} custom-call(s32[2]{0:T(128)S(4)} %get-tuple-element.25.flag_ref, s32[12,20]{1,0:T(8,128)S(4)} %get-tuple-element.26.ids_ref, bf16[12,32,128]{2,1,0:T(8,128)(2,1)S(1)} %get-tuple-element.45.x_ref, bf16[12,32,128]{2,1,0:T(8,128)(2,1)S(1)} %collective-permute-done.15.e_ref, ...), custom_call_target="tpu_custom_call" | custom-call | flops 251658240 | bytes 7864320 | tf_op jit(solution)/shard_map/direct/pallas_call | solution.py:446
  43.7 1.7 %collective-permute-start.19 = (bf16[12,32,128]{2,1,0:T(8,128)(2,1)S(1)}, bf16[12,32,128]{2,1,0:T(8,128)(2,1)S(1)}, u32[]{:S(2)}, u32[]{:S(2)}) collective-permute-start(bf16[12,32,128]{2,1,0:T(8,128)(2,1)S(1)} %get-tuple-element.41.refs_3_.refs_1_), channel_id=1, source_target_pairs={{0,4},{4,0},{8,12},{12,8},{16,20},{20,16},{24,28},{28,24},{1,5},{5... | collective-permute-start | bytes 294920 | tf_op jit(solution)/shard_map/ppermute | solution.py:326
  45.4 1.0 %turned_images.1.refs_5_ = f32[20,12,32,128]{3,2,1,0:T(8,128)S(1)} custom-call(s32[2]{0:T(128)S(4)} %get-tuple-element.25.flag_ref, s32[12,20]{1,0:T(8,128)S(4)} %get-tuple-element.26.ids_ref, bf16[12,32,128]{2,1,0:T(8,128)(2,1)S(1)} %copy-done, bf16[12,32,128]{2,1,0:T(8,128)(2,1)S(1)} %collective-permute-done.e_ref.ve_ref.refs_1_, ...), custom_call_target="tpu_custom_call" | custom-call | flops 251658240 | bytes 7864320 | tf_op jit(solution)/shard_map/turned_images/pallas_call | solution.py:483
  46.3 1.1 %near_forces.1.refs_6_.start_ref = f32[37,3,8,128]{3,2,1,0:T(8,128)S(1)} custom-call(s32[2]{0:T(128)S(4)} %get-tuple-element.25.flag_ref, s32[12,20]{1,0:T(8,128)S(4)} %get-tuple-element.26.ids_ref, f32[36,21]{1,0:T(8,128)S(4)} %get-tuple-element.40.bond_ref, bf16[12,32,128]{2,1,0:T(8,128)(2,1)S(1)} %copy-done, ...), custom_call_target="tpu_custom_call" | custom-call | flops 251658240 | bytes 16515072 | tf_op jit(solution)/shard_map/near_forces/pallas_call | solution.py:525
  47.4 1.2 %collective-permute-done.20.refs_3_.w_ref = bf16[12,32,128]{2,1,0:T(8,128)(2,1)S(1)} collective-permute-done((bf16[12,32,128]{2,1,0:T(8,128)(2,1)S(1)}, bf16[12,32,128]{2,1,0:T(8,128)(2,1)S(1)}, u32[]{:S(2)}, u32[]{:S(2)}) %collective-permute-start.20) | collective-permute-done | bytes 98336 | tf_op jit(solution)/shard_map/ppermute | solution.py:325
  49.2 1.2 %far_forces.1 = (f32[12,3,128]{2,1,0:T(4,128)S(1)}, f32[12,3,128]{2,1,0:T(4,128)S(1)}) custom-call(s32[2]{0:T(128)S(4)} %get-tuple-element.25.flag_ref, s32[12,20]{1,0:T(8,128)S(4)} %get-tuple-element.26.ids_ref, f32[36,21]{1,0:T(8,128)S(4)} %get-tuple-element.40.bond_ref, bf16[12,32,128]{2,1,0:T(8,128)(2,1)S(1)} %copy-done, ...), custom_call_target="tpu_custom_call" | custom-call | flops 251658240 | bytes 11993088 | tf_op jit(solution)/shard_map/far_forces/pallas_call | solution.py:613
  50.4 0.8 %collective-permute-start.21 = (f32[12,3,128]{2,1,0:T(4,128)S(1)}, f32[12,3,128]{2,1,0:T(4,128)S(1)}, u32[]{:S(2)}, u32[]{:S(2)}) collective-permute-start(f32[12,3,128]{2,1,0:T(4,128)S(1)} %get-tuple-element.44), channel_id=1, source_target_pairs={{0,4},{4,0},{8,12},{12,8},{16,20},{20,16},{24,28},{28,24},{1,5},{5... | collective-permute-start | bytes 55304 | tf_op jit(solution)/shard_map/ppermute | solution.py:326
  51.2 2.1 %collective-permute-done.22.o_ref = f32[12,3,128]{2,1,0:T(4,128)S(1)} collective-permute-done((f32[12,3,128]{2,1,0:T(4,128)S(1)}, f32[12,3,128]{2,1,0:T(4,128)S(1)}, u32[]{:S(2)}, u32[]{:S(2)}) %collective-permute-start.22) | collective-permute-done | bytes 18464 | tf_op jit(solution)/shard_map/ppermute | solution.py:325
  53.6 2.5 %collective-permute-start.23 = (f32[24,128]{1,0:T(8,128)S(1)}, f32[24,128]{1,0:T(8,128)S(1)}, u32[]{:S(2)}, u32[]{:S(2)}) collective-permute-start(f32[24,128]{1,0:T(8,128)S(1)} %packed.1), channel_id=1, source_target_pairs={{0,1},{1,0},{2,3},{3,2},{4,5},{5,4},{6,7},{7,6},{8,9},{9,8},{10,11... | collective-permute-start | bytes 36872 | tf_op jit(solution)/shard_map/ppermute | solution.py:678
  56.0 1.7 %collective-permute-done.23 = f32[24,128]{1,0:T(8,128)S(1)} collective-permute-done((f32[24,128]{1,0:T(8,128)S(1)}, f32[24,128]{1,0:T(8,128)S(1)}, u32[]{:S(2)}, u32[]{:S(2)}) %collective-permute-start.23) | collective-permute-done | bytes 12320 | tf_op jit(solution)/shard_map/ppermute | solution.py:678
  57.7 3.0 %collective-permute-start.24 = (f32[24,128]{1,0:T(8,128)S(1)}, f32[24,128]{1,0:T(8,128)S(1)}, u32[]{:S(2)}, u32[]{:S(2)}) collective-permute-start(f32[24,128]{1,0:T(8,128)S(1)} %add.39.refs_0_), channel_id=1, source_target_pairs={{0,2},{1,3},{2,0},{3,1},{4,6},{5,7},{6,4},{7,5},{8,10},{9,11},{10,... | collective-permute-start | bytes 36872 | tf_op jit(solution)/shard_map/ppermute | solution.py:678
  60.7 1.7 %collective-permute-done.24.refs_1_ = f32[24,128]{1,0:T(8,128)S(1)} collective-permute-done((f32[24,128]{1,0:T(8,128)S(1)}, f32[24,128]{1,0:T(8,128)S(1)}, u32[]{:S(2)}, u32[]{:S(2)}) %collective-permute-start.24) | collective-permute-done | bytes 12320 | tf_op jit(solution)/shard_map/ppermute | solution.py:678
  (50 shorter events, 7.1 us)
Async XLA Ops:
  0.6 8.7 %copy-start = (bf16[12,32,128]{2,1,0:T(8,128)(2,1)S(1)}, bf16[12,32,128]{2,1,0:T(8,128)(2,1)}, u32[]{:S(2)}) copy-start(bf16[12,32,128]{2,1,0:T(8,128)(2,1)} %refs_0_.3) | copy-start | bytes 294916
  0.6 8.7 %copy-start.1 = (f32[12,128]{1,0:T(8,128)S(1)}, f32[12,128]{1,0:T(8,128)}, u32[]{:S(2)}) copy-start(f32[12,128]{1,0:T(8,128)} %site_ref.7) | copy-start | bytes 18436
  0.7 8.7 %collective-permute-start = (bf16[12,32,128]{2,1,0:T(8,128)(2,1)}, bf16[12,32,128]{2,1,0:T(8,128)(2,1)S(1)}, u32[]{:S(2)}, u32[]{:S(2)}) collective-permute-start(bf16[12,32,128]{2,1,0:T(8,128)(2,1)} %refs_0_.3), channel_id=1, source_target_pairs={{0,4},{4,0},{8,12},{12,8},{16,20},{20,16},{24,28},{28,24},{1,5},{5... | collective-permute-start | bytes 294920 | tf_op jit(solution)/shard_map/ppermute | solution.py:326
  1.2 8.1 %collective-permute-start.1 = (bf16[12,32,128]{2,1,0:T(8,128)(2,1)}, bf16[12,32,128]{2,1,0:T(8,128)(2,1)S(1)}, u32[]{:S(2)}, u32[]{:S(2)}) collective-permute-start(bf16[12,32,128]{2,1,0:T(8,128)(2,1)} %refs_0_.3), channel_id=1, source_target_pairs={{0,28},{4,8},{8,4},{12,16},{16,12},{20,24},{24,20},{28,0},{1,29},{... | collective-permute-start | bytes 294920 | tf_op jit(solution)/shard_map/ppermute | solution.py:325
  8.6 1.5 %collective-permute-start.2 = (bf16[12,32,128]{2,1,0:T(8,128)(2,1)S(1)}, bf16[12,32,128]{2,1,0:T(8,128)(2,1)S(1)}, u32[]{:S(2)}, u32[]{:S(2)}) collective-permute-start(bf16[12,32,128]{2,1,0:T(8,128)(2,1)S(1)} %get-tuple-element.29), channel_id=1, source_target_pairs={{0,4},{4,0},{8,12},{12,8},{16,20},{20,16},{24,28},{28,24},{1,5},{5... | collective-permute-start | bytes 294920 | tf_op jit(solution)/shard_map/ppermute | solution.py:326
  8.7 5.7 %collective-permute-start.3 = (bf16[12,32,128]{2,1,0:T(8,128)(2,1)S(1)}, bf16[12,32,128]{2,1,0:T(8,128)(2,1)S(1)}, u32[]{:S(2)}, u32[]{:S(2)}) collective-permute-start(bf16[12,32,128]{2,1,0:T(8,128)(2,1)S(1)} %get-tuple-element.30), channel_id=1, source_target_pairs={{0,28},{4,8},{8,4},{12,16},{16,12},{20,24},{24,20},{28,0},{1,29},{... | collective-permute-start | bytes 294920 | tf_op jit(solution)/shard_map/ppermute | solution.py:325
  14.5 4.2 %collective-permute-start.4 = (bf16[12,32,128]{2,1,0:T(8,128)(2,1)S(1)}, bf16[12,32,128]{2,1,0:T(8,128)(2,1)S(1)}, u32[]{:S(2)}, u32[]{:S(2)}) collective-permute-start(bf16[12,32,128]{2,1,0:T(8,128)(2,1)S(1)} %get-tuple-element.49.x_ref), channel_id=1, source_target_pairs={{0,4},{4,0},{8,12},{12,8},{16,20},{20,16},{24,28},{28,24},{1,5},{5... | collective-permute-start | bytes 294920 | tf_op jit(solution)/shard_map/ppermute | solution.py:326
  14.6 6.1 %collective-permute-start.5 = (bf16[12,32,128]{2,1,0:T(8,128)(2,1)S(1)}, bf16[12,32,128]{2,1,0:T(8,128)(2,1)S(1)}, u32[]{:S(2)}, u32[]{:S(2)}) collective-permute-start(bf16[12,32,128]{2,1,0:T(8,128)(2,1)S(1)} %get-tuple-element.49.x_ref), channel_id=1, source_target_pairs={{0,28},{4,8},{8,4},{12,16},{16,12},{20,24},{24,20},{28,0},{1,29},{... | collective-permute-start | bytes 294920 | tf_op jit(solution)/shard_map/ppermute | solution.py:325
  15.4 6.7 %collective-permute-start.7 = (bf16[12,32,128]{2,1,0:T(8,128)(2,1)S(1)}, bf16[12,32,128]{2,1,0:T(8,128)(2,1)S(1)}, u32[]{:S(2)}, u32[]{:S(2)}) collective-permute-start(bf16[12,32,128]{2,1,0:T(8,128)(2,1)S(1)} %ahead.3), channel_id=1, source_target_pairs={{0,28},{4,8},{8,4},{12,16},{16,12},{20,24},{24,20},{28,0},{1,29},{... | collective-permute-start | bytes 294920 | tf_op jit(solution)/shard_map/ppermute | solution.py:325
  18.6 3.5 %collective-permute-start.6 = (bf16[12,32,128]{2,1,0:T(8,128)(2,1)S(1)}, bf16[12,32,128]{2,1,0:T(8,128)(2,1)S(1)}, u32[]{:S(2)}, u32[]{:S(2)}) collective-permute-start(bf16[12,32,128]{2,1,0:T(8,128)(2,1)S(1)} %get-tuple-element.33), channel_id=1, source_target_pairs={{0,4},{4,0},{8,12},{12,8},{16,20},{20,16},{24,28},{28,24},{1,5},{5... | collective-permute-start | bytes 294920 | tf_op jit(solution)/shard_map/ppermute | solution.py:326
  22.9 4.3 %collective-permute-start.11 = (bf16[12,32,128]{2,1,0:T(8,128)(2,1)S(1)}, bf16[12,32,128]{2,1,0:T(8,128)(2,1)S(1)}, u32[]{:S(2)}, u32[]{:S(2)}) collective-permute-start(bf16[12,32,128]{2,1,0:T(8,128)(2,1)S(1)} %get-tuple-element.47.x_ref), channel_id=1, source_target_pairs={{0,4},{4,0},{8,12},{12,8},{16,20},{20,16},{24,28},{28,24},{1,5},{5... | collective-permute-start | bytes 294920 | tf_op jit(solution)/shard_map/ppermute | solution.py:326
  23.0 6.1 %collective-permute-start.12 = (bf16[12,32,128]{2,1,0:T(8,128)(2,1)S(1)}, bf16[12,32,128]{2,1,0:T(8,128)(2,1)S(1)}, u32[]{:S(2)}, u32[]{:S(2)}) collective-permute-start(bf16[12,32,128]{2,1,0:T(8,128)(2,1)S(1)} %get-tuple-element.47.x_ref), channel_id=1, source_target_pairs={{0,28},{4,8},{8,4},{12,16},{16,12},{20,24},{24,20},{28,0},{1,29},{... | collective-permute-start | bytes 294920 | tf_op jit(solution)/shard_map/ppermute | solution.py:325
  23.7 6.8 %collective-permute-start.14 = (bf16[12,32,128]{2,1,0:T(8,128)(2,1)S(1)}, bf16[12,32,128]{2,1,0:T(8,128)(2,1)S(1)}, u32[]{:S(2)}, u32[]{:S(2)}) collective-permute-start(bf16[12,32,128]{2,1,0:T(8,128)(2,1)S(1)} %ahead.4), channel_id=1, source_target_pairs={{0,28},{4,8},{8,4},{12,16},{16,12},{20,24},{24,20},{28,0},{1,29},{... | collective-permute-start | bytes 294920 | tf_op jit(solution)/shard_map/ppermute | solution.py:325
  26.5 4.0 %collective-permute-start.13 = (bf16[12,32,128]{2,1,0:T(8,128)(2,1)S(1)}, bf16[12,32,128]{2,1,0:T(8,128)(2,1)S(1)}, u32[]{:S(2)}, u32[]{:S(2)}) collective-permute-start(bf16[12,32,128]{2,1,0:T(8,128)(2,1)S(1)} %get-tuple-element.36), channel_id=1, source_target_pairs={{0,4},{4,0},{8,12},{12,8},{16,20},{20,16},{24,28},{28,24},{1,5},{5... | collective-permute-start | bytes 294920 | tf_op jit(solution)/shard_map/ppermute | solution.py:326
  26.6 8.1 %collective-permute-start.8 = (f32[2,32,128]{2,1,0:T(8,128)S(1)}, f32[2,32,128]{2,1,0:T(8,128)S(1)}, u32[]{:S(2)}, u32[]{:S(2)}) collective-permute-start(f32[2,32,128]{2,1,0:T(8,128)S(1)} %moments.1), channel_id=1, source_target_pairs={{0,4},{4,0},{8,12},{12,8},{16,20},{20,16},{24,28},{28,24},{1,5},{5... | collective-permute-start | bytes 98312 | tf_op jit(solution)/shard_map/ppermute | solution.py:332
  31.0 11.6 %collective-permute-start.15 = (bf16[12,32,128]{2,1,0:T(8,128)(2,1)S(1)}, bf16[12,32,128]{2,1,0:T(8,128)(2,1)S(1)}, u32[]{:S(2)}, u32[]{:S(2)}) collective-permute-start(bf16[12,32,128]{2,1,0:T(8,128)(2,1)S(1)} %get-tuple-element.45.x_ref), channel_id=1, source_target_pairs={{0,4},{4,0},{8,12},{12,8},{16,20},{20,16},{24,28},{28,24},{1,5},{5... | collective-permute-start | bytes 294920 | tf_op jit(solution)/shard_map/ppermute | solution.py:326
  31.1 11.5 %collective-permute-start.16 = (bf16[12,32,128]{2,1,0:T(8,128)(2,1)S(1)}, bf16[12,32,128]{2,1,0:T(8,128)(2,1)S(1)}, u32[]{:S(2)}, u32[]{:S(2)}) collective-permute-start(bf16[12,32,128]{2,1,0:T(8,128)(2,1)S(1)} %get-tuple-element.45.x_ref), channel_id=1, source_target_pairs={{0,28},{4,8},{8,4},{12,16},{16,12},{20,24},{24,20},{28,0},{1,29},{... | collective-permute-start | bytes 294920 | tf_op jit(solution)/shard_map/ppermute | solution.py:325
  31.7 11.7 %collective-permute-start.18 = (bf16[12,32,128]{2,1,0:T(8,128)(2,1)S(1)}, bf16[12,32,128]{2,1,0:T(8,128)(2,1)S(1)}, u32[]{:S(2)}, u32[]{:S(2)}) collective-permute-start(bf16[12,32,128]{2,1,0:T(8,128)(2,1)S(1)} %ahead.5), channel_id=1, source_target_pairs={{0,28},{4,8},{8,4},{12,16},{16,12},{20,24},{24,20},{28,0},{1,29},{... | collective-permute-start | bytes 294920 | tf_op jit(solution)/shard_map/ppermute | solution.py:325
  34.6 8.8 %collective-permute-start.17 = (bf16[12,32,128]{2,1,0:T(8,128)(2,1)S(1)}, bf16[12,32,128]{2,1,0:T(8,128)(2,1)S(1)}, u32[]{:S(2)}, u32[]{:S(2)}) collective-permute-start(bf16[12,32,128]{2,1,0:T(8,128)(2,1)S(1)} %get-tuple-element.38), channel_id=1, source_target_pairs={{0,4},{4,0},{8,12},{12,8},{16,20},{20,16},{24,28},{28,24},{1,5},{5... | collective-permute-start | bytes 294920 | tf_op jit(solution)/shard_map/ppermute | solution.py:326
  34.7 4.0 %collective-permute-start.9 = (f32[2,32,128]{2,1,0:T(8,128)S(1)}, f32[2,32,128]{2,1,0:T(8,128)S(1)}, u32[]{:S(2)}, u32[]{:S(2)}) collective-permute-start(f32[2,32,128]{2,1,0:T(8,128)S(1)} %add.34), channel_id=1, source_target_pairs={{0,8},{4,12},{8,0},{12,4},{16,24},{20,28},{24,16},{28,20},{1,9},{5... | collective-permute-start | bytes 98312 | tf_op jit(solution)/shard_map/ppermute | solution.py:332
  38.7 3.9 %collective-permute-start.10 = (f32[2,32,128]{2,1,0:T(8,128)S(1)}, f32[2,32,128]{2,1,0:T(8,128)S(1)}, u32[]{:S(2)}, u32[]{:S(2)}) collective-permute-start(f32[2,32,128]{2,1,0:T(8,128)S(1)} %add.35), channel_id=1, source_target_pairs={{0,16},{4,20},{8,24},{12,28},{16,0},{20,4},{24,8},{28,12},{1,17},{... | collective-permute-start | bytes 98312 | tf_op jit(solution)/shard_map/ppermute | solution.py:332
  43.6 5.0 %collective-permute-start.20 = (bf16[12,32,128]{2,1,0:T(8,128)(2,1)S(1)}, bf16[12,32,128]{2,1,0:T(8,128)(2,1)S(1)}, u32[]{:S(2)}, u32[]{:S(2)}) collective-permute-start(bf16[12,32,128]{2,1,0:T(8,128)(2,1)S(1)} %get-tuple-element.41.refs_3_.refs_1_), channel_id=1, source_target_pairs={{0,28},{4,8},{8,4},{12,16},{16,12},{20,24},{24,20},{28,0},{1,29},{... | collective-permute-start | bytes 294920 | tf_op jit(solution)/shard_map/ppermute | solution.py:325
  43.7 5.5 %collective-permute-start.19 = (bf16[12,32,128]{2,1,0:T(8,128)(2,1)S(1)}, bf16[12,32,128]{2,1,0:T(8,128)(2,1)S(1)}, u32[]{:S(2)}, u32[]{:S(2)}) collective-permute-start(bf16[12,32,128]{2,1,0:T(8,128)(2,1)S(1)} %get-tuple-element.41.refs_3_.refs_1_), channel_id=1, source_target_pairs={{0,4},{4,0},{8,12},{12,8},{16,20},{20,16},{24,28},{28,24},{1,5},{5... | collective-permute-start | bytes 294920 | tf_op jit(solution)/shard_map/ppermute | solution.py:326
  48.6 4.6 %copy-start.2 = (s32[12,128]{1,0:T(8,128)S(1)}, s32[12,128]{1,0:T(8,128)}, u32[]{:S(2)}) copy-start(s32[12,128]{1,0:T(8,128)} %atom_ref.1) | copy-start | bytes 18436
  49.0 4.2 %collective-permute-start.22 = (f32[12,3,128]{2,1,0:T(4,128)S(1)}, f32[12,3,128]{2,1,0:T(4,128)S(1)}, u32[]{:S(2)}, u32[]{:S(2)}) collective-permute-start(f32[12,3,128]{2,1,0:T(4,128)S(1)} %ahead_forces.1), channel_id=1, source_target_pairs={{0,28},{4,8},{8,4},{12,16},{16,12},{20,24},{24,20},{28,0},{1,29},{... | collective-permute-start | bytes 55304 | tf_op jit(solution)/shard_map/ppermute | solution.py:325
  50.4 2.9 %collective-permute-start.21 = (f32[12,3,128]{2,1,0:T(4,128)S(1)}, f32[12,3,128]{2,1,0:T(4,128)S(1)}, u32[]{:S(2)}, u32[]{:S(2)}) collective-permute-start(f32[12,3,128]{2,1,0:T(4,128)S(1)} %get-tuple-element.44), channel_id=1, source_target_pairs={{0,4},{4,0},{8,12},{12,8},{16,20},{20,16},{24,28},{28,24},{1,5},{5... | collective-permute-start | bytes 55304 | tf_op jit(solution)/shard_map/ppermute | solution.py:326
  53.6 4.1 %collective-permute-start.23 = (f32[24,128]{1,0:T(8,128)S(1)}, f32[24,128]{1,0:T(8,128)S(1)}, u32[]{:S(2)}, u32[]{:S(2)}) collective-permute-start(f32[24,128]{1,0:T(8,128)S(1)} %packed.1), channel_id=1, source_target_pairs={{0,1},{1,0},{2,3},{3,2},{4,5},{5,4},{6,7},{7,6},{8,9},{9,8},{10,11... | collective-permute-start | bytes 36872 | tf_op jit(solution)/shard_map/ppermute | solution.py:678
  57.7 4.7 %collective-permute-start.24 = (f32[24,128]{1,0:T(8,128)S(1)}, f32[24,128]{1,0:T(8,128)S(1)}, u32[]{:S(2)}, u32[]{:S(2)}) collective-permute-start(f32[24,128]{1,0:T(8,128)S(1)} %add.39.refs_0_), channel_id=1, source_target_pairs={{0,2},{1,3},{2,0},{3,1},{4,6},{5,7},{6,4},{7,5},{8,10},{9,11},{10,... | collective-permute-start | bytes 36872 | tf_op jit(solution)/shard_map/ppermute | solution.py:678

commit v7 on v6

--- a/solution.py
+++ b/solution.py
@@ -46,16 +46,16 @@
     return jnp.asarray(table)
 
 
-def opening(columns, x, k, bond_dir, chemical_potential):
+def opening(columns, x, k, bond_dir):
     rows, slots = columns.shape
     probes, block = x.shape[1:]
     frame = rows + 2 * REACH
     halves = (0, HALF_SLOTS, slots)
     height = rows // CHUNKS
 
-    def kernel(col_hbm, x_hbm, k_hbm, bond_hbm, table_hbm, mu_ref, *refs):
-        flag_ref, ids_ref, at_ref, out_ref, coeff_ref, own_ref, even_ref, odd_ref, kv_ref, kt_ref, image_ref = refs[:11]
-        acc, col_sm, col_vm, xv, bond_vm, table_vm, ids_vm, at_vm, out_vm, sems, small = refs[11:]
+    def kernel(col_hbm, x_hbm, k_hbm, bond_hbm, *refs):
+        flag_ref, ids_ref, at_ref, out_ref, own_ref, even_ref, odd_ref, kv_ref, kt_ref, image_ref = refs[:10]
+        acc, col_sm, col_vm, xv, bond_vm, ids_vm, at_vm, out_vm, sems, small = refs[10:]
         me = lax.axis_index("clus")
 
         def load(index):
@@ -70,7 +70,6 @@
             (col_hbm, col_vm),
             (col_hbm, col_sm),
             (x_hbm, xv),
-            (table_hbm, table_vm),
             (bond_hbm, bond_vm),
         )
         copies = [pltpu.make_async_copy(a, b, small.at[i]) for i, (a, b) in enumerate(pairs)]
@@ -104,13 +103,9 @@
             out_vm[lines, :slots] = bond_vm[axis].astype(f32)
             out_vm[lines, slots:] = jnp.zeros((rows, 1), f32)
         tables = ((ids_vm, ids_ref), (at_vm, at_ref), (out_vm, out_ref))
-        placed = [pltpu.make_async_copy(a, b, small.at[5 + i]) for i, (a, b) in enumerate(tables)]
+        placed = [pltpu.make_async_copy(a, b, small.at[4 + i]) for i, (a, b) in enumerate(tables)]
         for copy in placed:
             copy.start()
-        energy = (table_vm[7:8] - mu_ref[0]) / SMEARING_TEMP
-        occupied = 1.0 / (1.0 + jnp.exp(energy))
-        total = jnp.sum(table_vm[...] * occupied, axis=1, keepdims=True)
-        coeff_ref[...] = jnp.broadcast_to(total, coeff_ref.shape)
 
         def body(last):
             for index in range(last * CHUNKS):
@@ -156,7 +151,7 @@
 
     side = jax.ShapeDtypeStruct((REACH, probes, block), bf16)
     hbm = pl.BlockSpec(memory_space=pltpu.HBM)
-    operands = (columns, x, k, bond_dir, quadrature())
+    operands = (columns, x, k, bond_dir)
     return pl.pallas_call(
         kernel,
         out_shape=[
@@ -164,7 +159,6 @@
             pltpu.SMEM((rows, slots), jnp.int32),
             pltpu.SMEM((rows, REACH), jnp.int32),
             pltpu.SMEM((3 * rows, slots + 1), f32),
-            jax.ShapeDtypeStruct((8, 128), f32),
             jax.ShapeDtypeStruct((rows, probes, block), f32),
             side,
             side,
@@ -172,24 +166,40 @@
             jax.ShapeDtypeStruct(k.shape, k.dtype),
             jax.ShapeDtypeStruct((slots + 1, rows, probes, block), f32),
         ],
-        in_specs=[hbm] * 5 + [SM],
-        out_specs=[SM] * 4 + [VM] * 7,
+        in_specs=[hbm] * 4,
+        out_specs=[SM] * 4 + [VM] * 6,
         scratch_shapes=[
             pltpu.VMEM((frame + 1, probes, block), f32),
             pltpu.SMEM((rows, slots), jnp.int32),
             pltpu.VMEM((rows, slots), jnp.int32),
             pltpu.VMEM(x.shape, x.dtype),
             pltpu.VMEM(bond_dir.shape, bond_dir.dtype),
-            pltpu.VMEM((8, 128), f32),
             pltpu.VMEM((rows, slots), jnp.int32),
             pltpu.VMEM((rows, REACH), jnp.int32),
             pltpu.VMEM((3 * rows, slots + 1), f32),
             pltpu.SemaphoreType.DMA((2 * CHUNKS,)),
-            pltpu.SemaphoreType.DMA((8,)),
+            pltpu.SemaphoreType.DMA((7,)),
         ],
         name="opening",
         **params(2 * slots * rows * probes * block * block, k.size * 2),
-    )(*(pltpu.with_memory_space_constraint(a, pltpu.HBM) for a in operands), chemical_potential)
+    )(*(pltpu.with_memory_space_constraint(a, pltpu.HBM) for a in operands))
+
+
+def coefficients(chemical_potential):
+    def kernel(table_ref, mu_ref, out_ref):
+        energy = (table_ref[7:8] - mu_ref[0]) / SMEARING_TEMP
+        occupied = 1.0 / (1.0 + jnp.exp(energy))
+        total = jnp.sum(table_ref[...] * occupied, axis=1, keepdims=True)
+        out_ref[...] = jnp.broadcast_to(total, out_ref.shape)
+
+    return pl.pallas_call(
+        kernel,
+        out_shape=jax.ShapeDtypeStruct((8, 128), f32),
+        in_specs=[VM, SM],
+        out_specs=VM,
+        name="coefficients",
+        **params(10000, 8192),
+    )(quadrature(), chemical_potential)
 
 
 def moments(coeffs, v, first, second):
@@ -633,8 +643,8 @@
     x = probes
     even, crossed = exchange(x, x)
     v_even, v_crossed = even, crossed
-    flag, ids, at, bond, coeffs, own, to_even, to_odd, k, kt, kept = opening(
-        block_col.T, x, hopping, jnp.transpose(bond_dir, (0, 2, 1)), chemical_potential
+    flag, ids, at, bond, own, to_even, to_odd, k, kt, kept = opening(
+        block_col.T, x, hopping, jnp.transpose(bond_dir, (0, 2, 1))
     )
     flag, ids, at, bond = (
         pltpu.with_memory_space_constraint(a, pltpu.SMEM) for a in (flag, ids, at, bond)
@@ -651,6 +661,7 @@
         if term > 2:
             sums = doubled(term - 2, sums, "clus")
         if term == 1:
+            coeffs = coefficients(chemical_potential)
             turned = turned_images(flag, ids, x, even, crossed, kt)
         image = direct(flag, ids, x, even, crossed, kt, own, onsite)
         if term == ORDER:

time: 63.4 us -> 62.8 us (level)
  no operation moved by 1% of the time
where the time goes in v7:
time: 62.8 us; the launch traced here: 62.7 us
  starting transfers between devices  23 us (37%)
  waiting for transfers between devices  22.7 us (36%)
  Pallas kernels  15 us (24%)
  between operations  1.75 us (3%)
    ppermute x10, starting transfers between devices, exchange(): crossed = lax.ppermute(odd_side, 'clus', shifted)  12.7 us
    ppermute x10, waiting for transfers between devices, exchange(): crossed = lax.ppermute(odd_side, 'clus', shifted)  12.3 us
    ppermute x3, waiting for transfers between devices, doubled(): lax.ppermute(part, axis, [(i, i ^ 1 << index) for i in range(count)])  7.03 us
    ppermute x2, starting transfers between devices, local(): lax.ppermute(part, 'probe', [(i, i ^ step) for i in range(count)])  5.6 us
    ppermute x2, waiting for transfers between devices, local(): lax.ppermute(part, 'probe', [(i, i ^ step) for i in range(count)])  3.34 us
    ppermute x10, starting transfers between devices, exchange(): even = lax.ppermute(even_side, 'clus', paired)  3.33 us
    pallas_call x1, Pallas kernels, opening(): pl.pallas_call(kernel, out_shape=[pltpu.SMEM((2,), jnp.int32), pltpu.SMEM...  3.12 us
    pallas_call x4, Pallas kernels, direct(): pl.pallas_call(kernel, out_shape=jax.ShapeDtypeStruct((rows, probes, bloc...  3.06 us
  transfers between devices with their start and end apart: 25, of which 11 were waited for; matrix products, arithmetic and copies ran while one was open for 0% of the time, Pallas kernels for 21%

profile of v7, /device:TPU:0, one launch (start us, length us, event | category | flops | bytes accessed | tf_op | source)
XLA Modules:
  0.0 62.7 jit_solution(3357913942775112233)
XLA Ops:
  1.2 3.5 %collective-permute-start.1 = (bf16[12,32,128]{2,1,0:T(8,128)(2,1)}, bf16[12,32,128]{2,1,0:T(8,128)(2,1)S(1)}, u32[]{:S(2)}, u32[]{:S(2)}) collective-permute-start(bf16[12,32,128]{2,1,0:T(8,128)(2,1)} %refs_0_.3), channel_id=1, source_target_pairs={{0,28},{4,8},{8,4},{12,16},{16,12},{20,24},{24,20},{28,0},{1,29},{... | collective-permute-start | bytes 294920 | tf_op jit(solution)/shard_map/ppermute | solution.py:335
  4.8 3.1 %opening.1 = (s32[2]{0:T(128)S(4)}, s32[12,20]{1,0:T(8,128)S(4)}, s32[12,12]{1,0:T(8,128)S(4)}, f32[36,21]{1,0:T(8,128)S(4)}, f32[12,32,128]{2,1,0:T(8,128)S(1)}...) custom-call(s32[12,20]{1,0:T(8,128)} %bitcast.3, ...), custom_call_target="tpu_custom_call" | custom-call | flops 251658240 | bytes 7864320 | tf_op jit(solution)/shard_map/opening/pallas_call | solution.py:155
  8.6 0.8 %direct.4 = f32[12,32,128]{2,1,0:T(8,128)S(1)} custom-call(s32[2]{0:T(128)S(4)} %get-tuple-element.23.flag_ref, s32[12,20]{1,0:T(8,128)S(4)} %get-tuple-element.24.ids_ref, bf16[12,32,128]{2,1,0:T(8,128)(2,1)S(1)} %copy-done, bf16[12,32,128]{2,1,0:T(8,128)(2,1)S(1)} %collective-permute-done.e_ref.ve_ref.refs_1_, ...), custom_call_target="tpu_custom_call" | custom-call | flops 251658240 | bytes 7864320 | tf_op jit(solution)/shard_map/direct/pallas_call | solution.py:456
  9.4 4.3 %collective-permute-done.3 = bf16[12,32,128]{2,1,0:T(8,128)(2,1)S(1)} collective-permute-done((bf16[12,32,128]{2,1,0:T(8,128)(2,1)S(1)}, bf16[12,32,128]{2,1,0:T(8,128)(2,1)S(1)}, u32[]{:S(2)}, u32[]{:S(2)}) %collective-permute-start.3) | collective-permute-done | bytes 98336 | tf_op jit(solution)/shard_map/ppermute | solution.py:335
  14.6 2.4 %collective-permute-start.7 = (bf16[12,32,128]{2,1,0:T(8,128)(2,1)S(1)}, bf16[12,32,128]{2,1,0:T(8,128)(2,1)S(1)}, u32[]{:S(2)}, u32[]{:S(2)}) collective-permute-start(bf16[12,32,128]{2,1,0:T(8,128)(2,1)S(1)} %ahead.3), channel_id=1, source_target_pairs={{0,28},{4,8},{8,4},{12,16},{16,12},{20,24},{24,20},{28,0},{1,29},{... | collective-permute-start | bytes 294920 | tf_op jit(solution)/shard_map/ppermute | solution.py:335
  17.1 0.8 %spread.3 = (f32[12,32,128]{2,1,0:T(8,128)S(1)}, bf16[12,32,128]{2,1,0:T(8,128)(2,1)S(1)}) custom-call(s32[2]{0:T(128)S(4)} %get-tuple-element.23.flag_ref, s32[12,20]{1,0:T(8,128)S(4)} %get-tuple-element.24.ids_ref, bf16[12,32,128]{2,1,0:T(8,128)(2,1)S(1)} %get-tuple-element.47.x_ref, bf16[21,12,128,128]{3,2,1,0:T(8,128)(2,1)S(1)} %get-tuple-element.29.k_ref.refs_4_), custom_call_target="tpu_custom_call" | custom-call | flops 251658240 | bytes 8257536 | tf_op jit(solution)/shard_map/spread/pallas_call | solution.py:419
  17.9 1.9 %collective-permute-done.5.o_ref = bf16[12,32,128]{2,1,0:T(8,128)(2,1)S(1)} collective-permute-done((bf16[12,32,128]{2,1,0:T(8,128)(2,1)S(1)}, bf16[12,32,128]{2,1,0:T(8,128)(2,1)S(1)}, u32[]{:S(2)}, u32[]{:S(2)}) %collective-permute-start.5) | collective-permute-done | bytes 98336 | tf_op jit(solution)/shard_map/ppermute | solution.py:335
  19.8 0.8 %direct.5 = f32[12,32,128]{2,1,0:T(8,128)S(1)} custom-call(s32[2]{0:T(128)S(4)} %get-tuple-element.23.flag_ref, s32[12,20]{1,0:T(8,128)S(4)} %get-tuple-element.24.ids_ref, bf16[12,32,128]{2,1,0:T(8,128)(2,1)S(1)} %get-tuple-element.47.x_ref, bf16[12,32,128]{2,1,0:T(8,128)(2,1)S(1)} %collective-permute-done.4.e_ref, ...), custom_call_target="tpu_custom_call" | custom-call | flops 251658240 | bytes 7864320 | tf_op jit(solution)/shard_map/direct/pallas_call | solution.py:456
  20.6 0.8 %collective-permute-done.7 = bf16[12,32,128]{2,1,0:T(8,128)(2,1)S(1)} collective-permute-done((bf16[12,32,128]{2,1,0:T(8,128)(2,1)S(1)}, bf16[12,32,128]{2,1,0:T(8,128)(2,1)S(1)}, u32[]{:S(2)}, u32[]{:S(2)}) %collective-permute-start.7) | collective-permute-done | bytes 98336 | tf_op jit(solution)/shard_map/ppermute | solution.py:335
  21.5 0.7 %ahead.4 = bf16[12,32,128]{2,1,0:T(8,128)(2,1)S(1)} custom-call(s32[2]{0:T(128)S(4)} %get-tuple-element.23.flag_ref, s32[12,12]{1,0:T(8,128)S(4)} %get-tuple-element.32.at_ref, bf16[12,32,128]{2,1,0:T(8,128)(2,1)S(1)} %get-tuple-element.45.x_ref, bf16[21,12,128,128]{3,2,1,0:T(8,128)(2,1)S(1)} %get-tuple-element.29.k_ref.refs_4_), custom_call_target="tpu_custom_call" | custom-call | flops 83886080 | bytes 2621440 | tf_op jit(solution)/shard_map/ahead/pallas_call | solution.py:381
  22.2 0.7 %collective-permute-start.12 = (bf16[12,32,128]{2,1,0:T(8,128)(2,1)S(1)}, bf16[12,32,128]{2,1,0:T(8,128)(2,1)S(1)}, u32[]{:S(2)}, u32[]{:S(2)}) collective-permute-start(bf16[12,32,128]{2,1,0:T(8,128)(2,1)S(1)} %get-tuple-element.45.x_ref), channel_id=1, source_target_pairs={{0,28},{4,8},{8,4},{12,16},{16,12},{20,24},{24,20},{28,0},{1,29},{... | collective-permute-start | bytes 294920 | tf_op jit(solution)/shard_map/ppermute | solution.py:335
  23.0 2.0 %collective-permute-start.14 = (bf16[12,32,128]{2,1,0:T(8,128)(2,1)S(1)}, bf16[12,32,128]{2,1,0:T(8,128)(2,1)S(1)}, u32[]{:S(2)}, u32[]{:S(2)}) collective-permute-start(bf16[12,32,128]{2,1,0:T(8,128)(2,1)S(1)} %ahead.4), channel_id=1, source_target_pairs={{0,28},{4,8},{8,4},{12,16},{16,12},{20,24},{24,20},{28,0},{1,29},{... | collective-permute-start | bytes 294920 | tf_op jit(solution)/shard_map/ppermute | solution.py:335
  24.9 0.8 %spread.4 = (f32[12,32,128]{2,1,0:T(8,128)S(1)}, bf16[12,32,128]{2,1,0:T(8,128)(2,1)S(1)}) custom-call(s32[2]{0:T(128)S(4)} %get-tuple-element.23.flag_ref, s32[12,20]{1,0:T(8,128)S(4)} %get-tuple-element.24.ids_ref, bf16[12,32,128]{2,1,0:T(8,128)(2,1)S(1)} %get-tuple-element.45.x_ref, bf16[21,12,128,128]{3,2,1,0:T(8,128)(2,1)S(1)} %get-tuple-element.29.k_ref.refs_4_), custom_call_target="tpu_custom_call" | custom-call | flops 251658240 | bytes 8257536 | tf_op jit(solution)/shard_map/spread/pallas_call | solution.py:419
  27.2 1.1 %collective-permute-done.12.o_ref = bf16[12,32,128]{2,1,0:T(8,128)(2,1)S(1)} collective-permute-done((bf16[12,32,128]{2,1,0:T(8,128)(2,1)S(1)}, bf16[12,32,128]{2,1,0:T(8,128)(2,1)S(1)}, u32[]{:S(2)}, u32[]{:S(2)}) %collective-permute-start.12) | collective-permute-done | bytes 98336 | tf_op jit(solution)/shard_map/ppermute | solution.py:335
  28.3 0.8 %direct.6 = f32[12,32,128]{2,1,0:T(8,128)S(1)} custom-call(s32[2]{0:T(128)S(4)} %get-tuple-element.23.flag_ref, s32[12,20]{1,0:T(8,128)S(4)} %get-tuple-element.24.ids_ref, bf16[12,32,128]{2,1,0:T(8,128)(2,1)S(1)} %get-tuple-element.45.x_ref, bf16[12,32,128]{2,1,0:T(8,128)(2,1)S(1)} %collective-permute-done.11.e_ref, ...), custom_call_target="tpu_custom_call" | custom-call | flops 251658240 | bytes 7864320 | tf_op jit(solution)/shard_map/direct/pallas_call | solution.py:456
  29.1 0.8 %collective-permute-done.14 = bf16[12,32,128]{2,1,0:T(8,128)(2,1)S(1)} collective-permute-done((bf16[12,32,128]{2,1,0:T(8,128)(2,1)S(1)}, bf16[12,32,128]{2,1,0:T(8,128)(2,1)S(1)}, u32[]{:S(2)}, u32[]{:S(2)}) %collective-permute-start.14) | collective-permute-done | bytes 98336 | tf_op jit(solution)/shard_map/ppermute | solution.py:335
  31.0 2.2 %collective-permute-start.18 = (bf16[12,32,128]{2,1,0:T(8,128)(2,1)S(1)}, bf16[12,32,128]{2,1,0:T(8,128)(2,1)S(1)}, u32[]{:S(2)}, u32[]{:S(2)}) collective-permute-start(bf16[12,32,128]{2,1,0:T(8,128)(2,1)S(1)} %ahead.5), channel_id=1, source_target_pairs={{0,28},{4,8},{8,4},{12,16},{16,12},{20,24},{24,20},{28,0},{1,29},{... | collective-permute-start | bytes 294920 | tf_op jit(solution)/shard_map/ppermute | solution.py:335
  33.2 0.8 %spread.5 = (f32[12,32,128]{2,1,0:T(8,128)S(1)}, bf16[12,32,128]{2,1,0:T(8,128)(2,1)S(1)}) custom-call(s32[2]{0:T(128)S(4)} %get-tuple-element.23.flag_ref, s32[12,20]{1,0:T(8,128)S(4)} %get-tuple-element.24.ids_ref, bf16[12,32,128]{2,1,0:T(8,128)(2,1)S(1)} %get-tuple-element.43.x_ref, bf16[21,12,128,128]{3,2,1,0:T(8,128)(2,1)S(1)} %get-tuple-element.29.k_ref.refs_4_), custom_call_target="tpu_custom_call" | custom-call | flops 251658240 | bytes 8257536 | tf_op jit(solution)/shard_map/spread/pallas_call | solution.py:419
  34.6 3.5 %collective-permute-done.9 = f32[2,32,128]{2,1,0:T(8,128)S(1)} collective-permute-done((f32[2,32,128]{2,1,0:T(8,128)S(1)}, f32[2,32,128]{2,1,0:T(8,128)S(1)}, u32[]{:S(2)}, u32[]{:S(2)}) %collective-permute-start.9) | collective-permute-done | bytes 32800 | tf_op jit(solution)/shard_map/ppermute | solution.py:342
  38.4 3.6 %collective-permute-done.10 = f32[2,32,128]{2,1,0:T(8,128)S(1)} collective-permute-done((f32[2,32,128]{2,1,0:T(8,128)S(1)}, f32[2,32,128]{2,1,0:T(8,128)S(1)}, u32[]{:S(2)}, u32[]{:S(2)}) %collective-permute-start.10) | collective-permute-done | bytes 32800 | tf_op jit(solution)/shard_map/ppermute | solution.py:342
  42.0 0.8 %direct.7.y_ref = f32[12,32,128]{2,1,0:T(8,128)S(1)} custom-call(s32[2]{0:T(128)S(4)} %get-tuple-element.23.flag_ref, s32[12,20]{1,0:T(8,128)S(4)} %get-tuple-element.24.ids_ref, bf16[12,32,128]{2,1,0:T(8,128)(2,1)S(1)} %get-tuple-element.43.x_ref, bf16[12,32,128]{2,1,0:T(8,128)(2,1)S(1)} %collective-permute-done.15.e_ref, ...), custom_call_target="tpu_custom_call" | custom-call | flops 251658240 | bytes 7864320 | tf_op jit(solution)/shard_map/direct/pallas_call | solution.py:456
  43.0 1.6 %collective-permute-start.19 = (bf16[12,32,128]{2,1,0:T(8,128)(2,1)S(1)}, bf16[12,32,128]{2,1,0:T(8,128)(2,1)S(1)}, u32[]{:S(2)}, u32[]{:S(2)}) collective-permute-start(bf16[12,32,128]{2,1,0:T(8,128)(2,1)S(1)} %get-tuple-element.39.refs_3_.refs_1_), channel_id=1, source_target_pairs={{0,4},{4,0},{8,12},{12,8},{16,20},{20,16},{24,28},{28,24},{1,5},{5... | collective-permute-start | bytes 294920 | tf_op jit(solution)/shard_map/ppermute | solution.py:336
  44.6 0.9 %turned_images.1.refs_5_ = f32[20,12,32,128]{3,2,1,0:T(8,128)S(1)} custom-call(s32[2]{0:T(128)S(4)} %get-tuple-element.23.flag_ref, s32[12,20]{1,0:T(8,128)S(4)} %get-tuple-element.24.ids_ref, bf16[12,32,128]{2,1,0:T(8,128)(2,1)S(1)} %copy-done, bf16[12,32,128]{2,1,0:T(8,128)(2,1)S(1)} %collective-permute-done.e_ref.ve_ref.refs_1_, ...), custom_call_target="tpu_custom_call" | custom-call | flops 251658240 | bytes 7864320 | tf_op jit(solution)/shard_map/turned_images/pallas_call | solution.py:493
  45.6 1.0 %near_forces.1.refs_6_.start_ref = f32[37,3,8,128]{3,2,1,0:T(8,128)S(1)} custom-call(s32[2]{0:T(128)S(4)} %get-tuple-element.23.flag_ref, s32[12,20]{1,0:T(8,128)S(4)} %get-tuple-element.24.ids_ref, f32[36,21]{1,0:T(8,128)S(4)} %get-tuple-element.38.bond_ref, bf16[12,32,128]{2,1,0:T(8,128)(2,1)S(1)} %copy-done, ...), custom_call_target="tpu_custom_call" | custom-call | flops 251658240 | bytes 16515072 | tf_op jit(solution)/shard_map/near_forces/pallas_call | solution.py:535
  46.6 1.4 %collective-permute-done.20.refs_3_.w_ref = bf16[12,32,128]{2,1,0:T(8,128)(2,1)S(1)} collective-permute-done((bf16[12,32,128]{2,1,0:T(8,128)(2,1)S(1)}, bf16[12,32,128]{2,1,0:T(8,128)(2,1)S(1)}, u32[]{:S(2)}, u32[]{:S(2)}) %collective-permute-start.20) | collective-permute-done | bytes 98336 | tf_op jit(solution)/shard_map/ppermute | solution.py:335
  48.6 1.2 %far_forces.1 = (f32[12,3,128]{2,1,0:T(4,128)S(1)}, f32[12,3,128]{2,1,0:T(4,128)S(1)}) custom-call(s32[2]{0:T(128)S(4)} %get-tuple-element.23.flag_ref, s32[12,20]{1,0:T(8,128)S(4)} %get-tuple-element.24.ids_ref, f32[36,21]{1,0:T(8,128)S(4)} %get-tuple-element.38.bond_ref, bf16[12,32,128]{2,1,0:T(8,128)(2,1)S(1)} %copy-done, ...), custom_call_target="tpu_custom_call" | custom-call | flops 251658240 | bytes 11993088 | tf_op jit(solution)/shard_map/far_forces/pallas_call | solution.py:623
  49.8 0.7 %collective-permute-start.21 = (f32[12,3,128]{2,1,0:T(4,128)S(1)}, f32[12,3,128]{2,1,0:T(4,128)S(1)}, u32[]{:S(2)}, u32[]{:S(2)}) collective-permute-start(f32[12,3,128]{2,1,0:T(4,128)S(1)} %get-tuple-element.42), channel_id=1, source_target_pairs={{0,4},{4,0},{8,12},{12,8},{16,20},{20,16},{24,28},{28,24},{1,5},{5... | collective-permute-start | bytes 55304 | tf_op jit(solution)/shard_map/ppermute | solution.py:336
  50.5 2.1 %collective-permute-done.22.o_ref = f32[12,3,128]{2,1,0:T(4,128)S(1)} collective-permute-done((f32[12,3,128]{2,1,0:T(4,128)S(1)}, f32[12,3,128]{2,1,0:T(4,128)S(1)}, u32[]{:S(2)}, u32[]{:S(2)}) %collective-permute-start.22) | collective-permute-done | bytes 18464 | tf_op jit(solution)/shard_map/ppermute | solution.py:335
  52.9 2.6 %collective-permute-start.23 = (f32[24,128]{1,0:T(8,128)S(1)}, f32[24,128]{1,0:T(8,128)S(1)}, u32[]{:S(2)}, u32[]{:S(2)}) collective-permute-start(f32[24,128]{1,0:T(8,128)S(1)} %packed.1), channel_id=1, source_target_pairs={{0,1},{1,0},{2,3},{3,2},{4,5},{5,4},{6,7},{7,6},{8,9},{9,8},{10,11... | collective-permute-start | bytes 36872 | tf_op jit(solution)/shard_map/ppermute | solution.py:689
  55.5 1.7 %collective-permute-done.23 = f32[24,128]{1,0:T(8,128)S(1)} collective-permute-done((f32[24,128]{1,0:T(8,128)S(1)}, f32[24,128]{1,0:T(8,128)S(1)}, u32[]{:S(2)}, u32[]{:S(2)}) %collective-permute-start.23) | collective-permute-done | bytes 12320 | tf_op jit(solution)/shard_map/ppermute | solution.py:689
  57.2 3.0 %collective-permute-start.24 = (f32[24,128]{1,0:T(8,128)S(1)}, f32[24,128]{1,0:T(8,128)S(1)}, u32[]{:S(2)}, u32[]{:S(2)}) collective-permute-start(f32[24,128]{1,0:T(8,128)S(1)} %add.39.refs_0_), channel_id=1, source_target_pairs={{0,2},{1,3},{2,0},{3,1},{4,6},{5,7},{6,4},{7,5},{8,10},{9,11},{10,... | collective-permute-start | bytes 36872 | tf_op jit(solution)/shard_map/ppermute | solution.py:689
  60.2 1.7 %collective-permute-done.24.refs_1_ = f32[24,128]{1,0:T(8,128)S(1)} collective-permute-done((f32[24,128]{1,0:T(8,128)S(1)}, f32[24,128]{1,0:T(8,128)S(1)}, u32[]{:S(2)}, u32[]{:S(2)}) %collective-permute-start.24) | collective-permute-done | bytes 12320 | tf_op jit(solution)/shard_map/ppermute | solution.py:689
  (53 shorter events, 7.2 us)
Async XLA Ops:
  0.6 8.0 %copy-start = (bf16[12,32,128]{2,1,0:T(8,128)(2,1)S(1)}, bf16[12,32,128]{2,1,0:T(8,128)(2,1)}, u32[]{:S(2)}) copy-start(bf16[12,32,128]{2,1,0:T(8,128)(2,1)} %refs_0_.3) | copy-start | bytes 294916
  0.6 8.0 %copy-start.1 = (f32[12,128]{1,0:T(8,128)S(1)}, f32[12,128]{1,0:T(8,128)}, u32[]{:S(2)}) copy-start(f32[12,128]{1,0:T(8,128)} %site_ref.7) | copy-start | bytes 18436
  0.7 7.9 %collective-permute-start = (bf16[12,32,128]{2,1,0:T(8,128)(2,1)}, bf16[12,32,128]{2,1,0:T(8,128)(2,1)S(1)}, u32[]{:S(2)}, u32[]{:S(2)}) collective-permute-start(bf16[12,32,128]{2,1,0:T(8,128)(2,1)} %refs_0_.3), channel_id=1, source_target_pairs={{0,4},{4,0},{8,12},{12,8},{16,20},{20,16},{24,28},{28,24},{1,5},{5... | collective-permute-start | bytes 294920 | tf_op jit(solution)/shard_map/ppermute | solution.py:336
  1.2 7.4 %collective-permute-start.1 = (bf16[12,32,128]{2,1,0:T(8,128)(2,1)}, bf16[12,32,128]{2,1,0:T(8,128)(2,1)S(1)}, u32[]{:S(2)}, u32[]{:S(2)}) collective-permute-start(bf16[12,32,128]{2,1,0:T(8,128)(2,1)} %refs_0_.3), channel_id=1, source_target_pairs={{0,28},{4,8},{8,4},{12,16},{16,12},{20,24},{24,20},{28,0},{1,29},{... | collective-permute-start | bytes 294920 | tf_op jit(solution)/shard_map/ppermute | solution.py:335
  7.9 1.5 %collective-permute-start.2 = (bf16[12,32,128]{2,1,0:T(8,128)(2,1)S(1)}, bf16[12,32,128]{2,1,0:T(8,128)(2,1)S(1)}, u32[]{:S(2)}, u32[]{:S(2)}) collective-permute-start(bf16[12,32,128]{2,1,0:T(8,128)(2,1)S(1)} %get-tuple-element.27), channel_id=1, source_target_pairs={{0,4},{4,0},{8,12},{12,8},{16,20},{20,16},{24,28},{28,24},{1,5},{5... | collective-permute-start | bytes 294920 | tf_op jit(solution)/shard_map/ppermute | solution.py:336
  8.0 5.7 %collective-permute-start.3 = (bf16[12,32,128]{2,1,0:T(8,128)(2,1)S(1)}, bf16[12,32,128]{2,1,0:T(8,128)(2,1)S(1)}, u32[]{:S(2)}, u32[]{:S(2)}) collective-permute-start(bf16[12,32,128]{2,1,0:T(8,128)(2,1)S(1)} %get-tuple-element.28), channel_id=1, source_target_pairs={{0,28},{4,8},{8,4},{12,16},{16,12},{20,24},{24,20},{28,0},{1,29},{... | collective-permute-start | bytes 294920 | tf_op jit(solution)/shard_map/ppermute | solution.py:335
  13.7 4.2 %collective-permute-start.4 = (bf16[12,32,128]{2,1,0:T(8,128)(2,1)S(1)}, bf16[12,32,128]{2,1,0:T(8,128)(2,1)S(1)}, u32[]{:S(2)}, u32[]{:S(2)}) collective-permute-start(bf16[12,32,128]{2,1,0:T(8,128)(2,1)S(1)} %get-tuple-element.47.x_ref), channel_id=1, source_target_pairs={{0,4},{4,0},{8,12},{12,8},{16,20},{20,16},{24,28},{28,24},{1,5},{5... | collective-permute-start | bytes 294920 | tf_op jit(solution)/shard_map/ppermute | solution.py:336
  13.8 6.1 %collective-permute-start.5 = (bf16[12,32,128]{2,1,0:T(8,128)(2,1)S(1)}, bf16[12,32,128]{2,1,0:T(8,128)(2,1)S(1)}, u32[]{:S(2)}, u32[]{:S(2)}) collective-permute-start(bf16[12,32,128]{2,1,0:T(8,128)(2,1)S(1)} %get-tuple-element.47.x_ref), channel_id=1, source_target_pairs={{0,28},{4,8},{8,4},{12,16},{16,12},{20,24},{24,20},{28,0},{1,29},{... | collective-permute-start | bytes 294920 | tf_op jit(solution)/shard_map/ppermute | solution.py:335
  14.6 6.7 %collective-permute-start.7 = (bf16[12,32,128]{2,1,0:T(8,128)(2,1)S(1)}, bf16[12,32,128]{2,1,0:T(8,128)(2,1)S(1)}, u32[]{:S(2)}, u32[]{:S(2)}) collective-permute-start(bf16[12,32,128]{2,1,0:T(8,128)(2,1)S(1)} %ahead.3), channel_id=1, source_target_pairs={{0,28},{4,8},{8,4},{12,16},{16,12},{20,24},{24,20},{28,0},{1,29},{... | collective-permute-start | bytes 294920 | tf_op jit(solution)/shard_map/ppermute | solution.py:335
  17.8 3.5 %collective-permute-start.6 = (bf16[12,32,128]{2,1,0:T(8,128)(2,1)S(1)}, bf16[12,32,128]{2,1,0:T(8,128)(2,1)S(1)}, u32[]{:S(2)}, u32[]{:S(2)}) collective-permute-start(bf16[12,32,128]{2,1,0:T(8,128)(2,1)S(1)} %get-tuple-element.31), channel_id=1, source_target_pairs={{0,4},{4,0},{8,12},{12,8},{16,20},{20,16},{24,28},{28,24},{1,5},{5... | collective-permute-start | bytes 294920 | tf_op jit(solution)/shard_map/ppermute | solution.py:336
  21.5 5.0 %copy-start.3 = (f32[8,128]{1,0:T(8,128)S(1)}, f32[8,128]{1,0:T(8,128)}, u32[]{:S(2)}) copy-start(f32[8,128]{1,0:T(8,128)} %constant.4.clone.table_ref) | copy-start | bytes 12292
  22.2 5.0 %collective-permute-start.11 = (bf16[12,32,128]{2,1,0:T(8,128)(2,1)S(1)}, bf16[12,32,128]{2,1,0:T(8,128)(2,1)S(1)}, u32[]{:S(2)}, u32[]{:S(2)}) collective-permute-start(bf16[12,32,128]{2,1,0:T(8,128)(2,1)S(1)} %get-tuple-element.45.x_ref), channel_id=1, source_target_pairs={{0,4},{4,0},{8,12},{12,8},{16,20},{20,16},{24,28},{28,24},{1,5},{5... | collective-permute-start | bytes 294920 | tf_op jit(solution)/shard_map/ppermute | solution.py:336
  22.2 6.1 %collective-permute-start.12 = (bf16[12,32,128]{2,1,0:T(8,128)(2,1)S(1)}, bf16[12,32,128]{2,1,0:T(8,128)(2,1)S(1)}, u32[]{:S(2)}, u32[]{:S(2)}) collective-permute-start(bf16[12,32,128]{2,1,0:T(8,128)(2,1)S(1)} %get-tuple-element.45.x_ref), channel_id=1, source_target_pairs={{0,28},{4,8},{8,4},{12,16},{16,12},{20,24},{24,20},{28,0},{1,29},{... | collective-permute-start | bytes 294920 | tf_op jit(solution)/shard_map/ppermute | solution.py:335
  23.0 6.9 %collective-permute-start.14 = (bf16[12,32,128]{2,1,0:T(8,128)(2,1)S(1)}, bf16[12,32,128]{2,1,0:T(8,128)(2,1)S(1)}, u32[]{:S(2)}, u32[]{:S(2)}) collective-permute-start(bf16[12,32,128]{2,1,0:T(8,128)(2,1)S(1)} %ahead.4), channel_id=1, source_target_pairs={{0,28},{4,8},{8,4},{12,16},{16,12},{20,24},{24,20},{28,0},{1,29},{... | collective-permute-start | bytes 294920 | tf_op jit(solution)/shard_map/ppermute | solution.py:335
  25.7 4.1 %collective-permute-start.13 = (bf16[12,32,128]{2,1,0:T(8,128)(2,1)S(1)}, bf16[12,32,128]{2,1,0:T(8,128)(2,1)S(1)}, u32[]{:S(2)}, u32[]{:S(2)}) collective-permute-start(bf16[12,32,128]{2,1,0:T(8,128)(2,1)S(1)} %get-tuple-element.34), channel_id=1, source_target_pairs={{0,4},{4,0},{8,12},{12,8},{16,20},{20,16},{24,28},{28,24},{1,5},{5... | collective-permute-start | bytes 294920 | tf_op jit(solution)/shard_map/ppermute | solution.py:336
  26.6 7.4 %collective-permute-start.8 = (f32[2,32,128]{2,1,0:T(8,128)S(1)}, f32[2,32,128]{2,1,0:T(8,128)S(1)}, u32[]{:S(2)}, u32[]{:S(2)}) collective-permute-start(f32[2,32,128]{2,1,0:T(8,128)S(1)} %moments.1), channel_id=1, source_target_pairs={{0,4},{4,0},{8,12},{12,8},{16,20},{20,16},{24,28},{28,24},{1,5},{5... | collective-permute-start | bytes 98312 | tf_op jit(solution)/shard_map/ppermute | solution.py:342
  30.4 11.6 %collective-permute-start.15 = (bf16[12,32,128]{2,1,0:T(8,128)(2,1)S(1)}, bf16[12,32,128]{2,1,0:T(8,128)(2,1)S(1)}, u32[]{:S(2)}, u32[]{:S(2)}) collective-permute-start(bf16[12,32,128]{2,1,0:T(8,128)(2,1)S(1)} %get-tuple-element.43.x_ref), channel_id=1, source_target_pairs={{0,4},{4,0},{8,12},{12,8},{16,20},{20,16},{24,28},{28,24},{1,5},{5... | collective-permute-start | bytes 294920 | tf_op jit(solution)/shard_map/ppermute | solution.py:336
  30.5 11.5 %collective-permute-start.16 = (bf16[12,32,128]{2,1,0:T(8,128)(2,1)S(1)}, bf16[12,32,128]{2,1,0:T(8,128)(2,1)S(1)}, u32[]{:S(2)}, u32[]{:S(2)}) collective-permute-start(bf16[12,32,128]{2,1,0:T(8,128)(2,1)S(1)} %get-tuple-element.43.x_ref), channel_id=1, source_target_pairs={{0,28},{4,8},{8,4},{12,16},{16,12},{20,24},{24,20},{28,0},{1,29},{... | collective-permute-start | bytes 294920 | tf_op jit(solution)/shard_map/ppermute | solution.py:335
  31.0 11.8 %collective-permute-start.18 = (bf16[12,32,128]{2,1,0:T(8,128)(2,1)S(1)}, bf16[12,32,128]{2,1,0:T(8,128)(2,1)S(1)}, u32[]{:S(2)}, u32[]{:S(2)}) collective-permute-start(bf16[12,32,128]{2,1,0:T(8,128)(2,1)S(1)} %ahead.5), channel_id=1, source_target_pairs={{0,28},{4,8},{8,4},{12,16},{16,12},{20,24},{24,20},{28,0},{1,29},{... | collective-permute-start | bytes 294920 | tf_op jit(solution)/shard_map/ppermute | solution.py:335
  34.0 8.8 %collective-permute-start.17 = (bf16[12,32,128]{2,1,0:T(8,128)(2,1)S(1)}, bf16[12,32,128]{2,1,0:T(8,128)(2,1)S(1)}, u32[]{:S(2)}, u32[]{:S(2)}) collective-permute-start(bf16[12,32,128]{2,1,0:T(8,128)(2,1)S(1)} %get-tuple-element.36), channel_id=1, source_target_pairs={{0,4},{4,0},{8,12},{12,8},{16,20},{20,16},{24,28},{28,24},{1,5},{5... | collective-permute-start | bytes 294920 | tf_op jit(solution)/shard_map/ppermute | solution.py:336
  34.1 4.0 %collective-permute-start.9 = (f32[2,32,128]{2,1,0:T(8,128)S(1)}, f32[2,32,128]{2,1,0:T(8,128)S(1)}, u32[]{:S(2)}, u32[]{:S(2)}) collective-permute-start(f32[2,32,128]{2,1,0:T(8,128)S(1)} %add.34), channel_id=1, source_target_pairs={{0,8},{4,12},{8,0},{12,4},{16,24},{20,28},{24,16},{28,20},{1,9},{5... | collective-permute-start | bytes 98312 | tf_op jit(solution)/shard_map/ppermute | solution.py:342
  38.1 3.9 %collective-permute-start.10 = (f32[2,32,128]{2,1,0:T(8,128)S(1)}, f32[2,32,128]{2,1,0:T(8,128)S(1)}, u32[]{:S(2)}, u32[]{:S(2)}) collective-permute-start(f32[2,32,128]{2,1,0:T(8,128)S(1)} %add.35), channel_id=1, source_target_pairs={{0,16},{4,20},{8,24},{12,28},{16,0},{20,4},{24,8},{28,12},{1,17},{... | collective-permute-start | bytes 98312 | tf_op jit(solution)/shard_map/ppermute | solution.py:342
  43.0 5.0 %collective-permute-start.20 = (bf16[12,32,128]{2,1,0:T(8,128)(2,1)S(1)}, bf16[12,32,128]{2,1,0:T(8,128)(2,1)S(1)}, u32[]{:S(2)}, u32[]{:S(2)}) collective-permute-start(bf16[12,32,128]{2,1,0:T(8,128)(2,1)S(1)} %get-tuple-element.39.refs_3_.refs_1_), channel_id=1, source_target_pairs={{0,28},{4,8},{8,4},{12,16},{16,12},{20,24},{24,20},{28,0},{1,29},{... | collective-permute-start | bytes 294920 | tf_op jit(solution)/shard_map/ppermute | solution.py:335
  43.0 5.6 %collective-permute-start.19 = (bf16[12,32,128]{2,1,0:T(8,128)(2,1)S(1)}, bf16[12,32,128]{2,1,0:T(8,128)(2,1)S(1)}, u32[]{:S(2)}, u32[]{:S(2)}) collective-permute-start(bf16[12,32,128]{2,1,0:T(8,128)(2,1)S(1)} %get-tuple-element.39.refs_3_.refs_1_), channel_id=1, source_target_pairs={{0,4},{4,0},{8,12},{12,8},{16,20},{20,16},{24,28},{28,24},{1,5},{5... | collective-permute-start | bytes 294920 | tf_op jit(solution)/shard_map/ppermute | solution.py:336
  48.0 4.6 %copy-start.2 = (s32[12,128]{1,0:T(8,128)S(1)}, s32[12,128]{1,0:T(8,128)}, u32[]{:S(2)}) copy-start(s32[12,128]{1,0:T(8,128)} %atom_ref.1) | copy-start | bytes 18436
  48.4 4.2 %collective-permute-start.22 = (f32[12,3,128]{2,1,0:T(4,128)S(1)}, f32[12,3,128]{2,1,0:T(4,128)S(1)}, u32[]{:S(2)}, u32[]{:S(2)}) collective-permute-start(f32[12,3,128]{2,1,0:T(4,128)S(1)} %ahead_forces.1), channel_id=1, source_target_pairs={{0,28},{4,8},{8,4},{12,16},{16,12},{20,24},{24,20},{28,0},{1,29},{... | collective-permute-start | bytes 55304 | tf_op jit(solution)/shard_map/ppermute | solution.py:335
  49.8 2.8 %collective-permute-start.21 = (f32[12,3,128]{2,1,0:T(4,128)S(1)}, f32[12,3,128]{2,1,0:T(4,128)S(1)}, u32[]{:S(2)}, u32[]{:S(2)}) collective-permute-start(f32[12,3,128]{2,1,0:T(4,128)S(1)} %get-tuple-element.42), channel_id=1, source_target_pairs={{0,4},{4,0},{8,12},{12,8},{16,20},{20,16},{24,28},{28,24},{1,5},{5... | collective-permute-start | bytes 55304 | tf_op jit(solution)/shard_map/ppermute | solution.py:336
  52.9 4.3 %collective-permute-start.23 = (f32[24,128]{1,0:T(8,128)S(1)}, f32[24,128]{1,0:T(8,128)S(1)}, u32[]{:S(2)}, u32[]{:S(2)}) collective-permute-start(f32[24,128]{1,0:T(8,128)S(1)} %packed.1), channel_id=1, source_target_pairs={{0,1},{1,0},{2,3},{3,2},{4,5},{5,4},{6,7},{7,6},{8,9},{9,8},{10,11... | collective-permute-start | bytes 36872 | tf_op jit(solution)/shard_map/ppermute | solution.py:689
  57.2 4.7 %collective-permute-start.24 = (f32[24,128]{1,0:T(8,128)S(1)}, f32[24,128]{1,0:T(8,128)S(1)}, u32[]{:S(2)}, u32[]{:S(2)}) collective-permute-start(f32[24,128]{1,0:T(8,128)S(1)} %add.39.refs_0_), channel_id=1, source_target_pairs={{0,2},{1,3},{2,0},{3,1},{4,6},{5,7},{6,4},{7,5},{8,10},{9,11},{10,... | collective-permute-start | bytes 36872 | tf_op jit(solution)/shard_map/ppermute | solution.py:689
